TPU v7x, 128 devices: a whole 4x4x4 slice. The times are simulated.
128 devices in a mesh: tm: 16 (over x_hi, y, core), height: 8 (over x_lo, z).
Axes of the slice: x: 4 (x_hi: 2, x_lo: 2; x = x_hi * 2 + x_lo), y: 4, z: 4, core: 2. Of those that a mesh axis runs over, the one named last changes fastest.
Arguments:
- tokens: bfloat16 [32, 32, 80, 3072], P('tm', 'height'), may hold values from -6 to 6
- mod_scale: float32 [3072], replicated, may hold values from -3 to 3
- mod_shift: float32 [3072], replicated, may hold values from -3 to 3
- w_qkv: bfloat16 [3072, 4608], P(('tm', 'height')), may hold values from -0.109375 to 0.109375
- q_gain: float32 [128], replicated, may hold values from 0.25 to 1.75
- k_gain: float32 [128], replicated, may hold values from 0.25 to 1.75
- window: int32 [12, 3], replicated, may hold values from 0 to 2, as said below
- valid: int32 [32, 32, 80], replicated, may hold values from 0 to 1, as said below
Outputs:
- attended: bfloat16 [32, 32, 80, 1536], P('tm', 'height')
Inputs may be any that keep to these rules, and one draw needn't show every extreme that they name: `window`: column 0 is at most 1, column 1 at most 1, column 2 at most 2; some head has all three at these most values. `valid`: the last frames, rows and columns of the grid may be padding with 0; scattered tokens elsewhere are 0 too.
All inputs are finite; a program needn't handle non-finite values.
Results may differ from a plain program's by a relative error of at most 0.0055.
Values may be sent and summed in bfloat16 or wider, within the bound.
A program may use at most 128 MiB of HBM per device.

v0:
```python
import jax
import jax.numpy as jnp
from jax import lax
from jax.sharding import PartitionSpec as P

HDIM = 128
HEADS = 12
TT = 1
TH = 2
TW = 8


EPS = 1e-06


def with_halo(cells, sides, width):
    for axis, dim in sides:
        count = lax.axis_size(axis)
        ends = count - 1
        head = lax.slice_in_dim(cells, 0, width, axis=dim)
        tail = lax.slice_in_dim(cells, cells.shape[dim] - width, cells.shape[dim], axis=dim)
        cells = jnp.concatenate(
            [
                lax.ppermute(tail, axis, [(i, (i + 1) % count) for i in range(ends)]),
                cells,
                lax.ppermute(head, axis, [((i + 1) % count, i) for i in range(ends)]),
            ],
            axis=dim,
        )
    return cells


def modulate(tokens, mod_scale, mod_shift):
    values = tokens.astype(jnp.float32)
    mean = jnp.mean(values, axis=-1, keepdims=True)
    centred = values - mean
    variance = jnp.mean(centred * centred, axis=-1, keepdims=True)
    normed = centred * lax.rsqrt(variance + EPS)
    return (normed * (1.0 + mod_scale) + mod_shift).astype(jnp.bfloat16)


def head_norm(values, gain):
    power = jnp.mean(values * values, axis=-1, keepdims=True)
    return (values * lax.rsqrt(power + EPS) * gain).astype(jnp.bfloat16)


def tile_coords(frames, rows, width):
    shape = (frames.shape[0], rows.shape[0], width)
    columns = jnp.arange(width, dtype=jnp.int32)
    frame_tiles = jnp.broadcast_to((frames // TT)[:, None, None], shape).reshape(-1)
    row_tiles = jnp.broadcast_to((rows // TH)[None, :, None], shape).reshape(-1)
    column_tiles = jnp.broadcast_to((columns // TW)[None, None, :], shape).reshape(-1)
    return (frame_tiles, row_tiles, column_tiles)


def per_device(tokens, mod_scale, mod_shift, w_qkv, q_gain, k_gain, window, valid):
    frame_count, row_count, width, features = tokens.shape
    token_count = frame_count * row_count * width
    modulated = modulate(tokens.reshape(token_count, features), mod_scale, mod_shift)
    full_weight = lax.all_gather(w_qkv, ("tm", "height"), axis=0, tiled=True)
    qkv = jnp.dot(modulated, full_weight, preferred_element_type=jnp.float32)
    inner = qkv.shape[1] // 3
    query = head_norm(qkv[:, :inner].reshape(token_count, HEADS, HDIM), q_gain)
    key = head_norm(qkv[:, inner : 2 * inner].reshape(token_count, HEADS, HDIM), k_gain)
    value = qkv[:, 2 * inner :].astype(jnp.bfloat16)
    tiled = (frame_count // TT, TT, row_count // TH, TH, width, inner)
    stacked = jnp.stack([key.reshape(tiled), value.reshape(tiled)])
    extended = with_halo(stacked, (("tm", 1), ("height", 3)), 1)
    frames_ext = frame_count + 2 * TT
    rows_ext = row_count + 2 * TH
    key_count = frames_ext * rows_ext * width
    extended = extended.reshape(2, key_count, HEADS, HDIM)
    key_heads = jnp.transpose(extended[0], (1, 0, 2))
    value_heads = jnp.transpose(extended[1], (1, 0, 2))
    query_heads = jnp.transpose(query, (1, 0, 2))
    frame_block = lax.axis_index("tm")
    row_block = lax.axis_index("height")
    first_frame = frame_block * frame_count
    first_row = row_block * row_count
    zero = jnp.int32(0)
    valid_pad = jnp.pad(valid, ((TT, TT), (TH, TH), (0, 0)))
    key_valid = (
        lax.dynamic_slice(
            valid_pad, (first_frame, first_row, zero), (frames_ext, rows_ext, width)
        ).reshape(-1)
        > 0
    )
    query_valid = (
        lax.dynamic_slice(
            valid, (first_frame, first_row, zero), (frame_count, row_count, width)
        ).reshape(-1)
        > 0
    )
    query_coords = tile_coords(
        first_frame + jnp.arange(frame_count, dtype=jnp.int32),
        first_row + jnp.arange(row_count, dtype=jnp.int32),
        width,
    )
    key_coords = tile_coords(
        first_frame - TT + jnp.arange(frames_ext, dtype=jnp.int32),
        first_row - TH + jnp.arange(rows_ext, dtype=jnp.int32),
        width,
    )
    apart_t, apart_h, apart_w = (
        jnp.abs(qa[:, None] - ka[None, :]) for qa, ka in zip(query_coords, key_coords)
    )
    seen = key_valid[None, :]
    scale = 1.0 / jnp.sqrt(jnp.float32(HDIM))

    def per_head(inputs):
        query_one, key_one, value_one, reach = inputs
        allowed = (apart_t <= reach[0]) & (apart_h <= reach[1]) & (apart_w <= reach[2]) & seen
        scores = (
            jnp.einsum("qd,kd->qk", query_one, key_one, preferred_element_type=jnp.float32) * scale
        )
        terms = jnp.where(allowed, jnp.exp(scores), jnp.float32(0.0))
        total = jnp.sum(terms, axis=-1, keepdims=True)
        total = jnp.where(query_valid[:, None], total, jnp.float32(1.0))
        weights = (terms / total).astype(jnp.bfloat16)
        result = jnp.dot(weights, value_one, preferred_element_type=jnp.float32)
        return jnp.where(query_valid[:, None], result, jnp.float32(0.0)).astype(jnp.bfloat16)

    heads_out = lax.map(per_head, (query_heads, key_heads, value_heads, window))
    attended = jnp.transpose(heads_out, (1, 0, 2)).reshape(frame_count, row_count, width, inner)
    return attended


def solution(mesh):
    in_specs = (
        P("tm", "height", None, None),
        P(),
        P(),
        P(("tm", "height"), None),
        P(),
        P(),
        P(),
        P(),
    )
    out_specs = P("tm", "height", None, None)
    return jax.shard_map(
        per_device, mesh=mesh, in_specs=in_specs, out_specs=out_specs, check_vma=False
    )
```

profile of v0, /device:TPU:6, one launch (start us, length us, event | category | flops | bytes accessed | tf_op | source)
XLA Modules:
  0.0 749.2 jit_solution(9672114326475516388)
XLA Ops:
  18.4 334.3 %all-gather.2.cloned.1.call-done = bf16[3072,4608]{1,0:T(8,128)(2,1)} async-done(((bf16[24,4608]{1,0:T(8,128)(2,1)}), bf16[3072,4608]{1,0:T(8,128)(2,1)}) %all-gather.2.cloned.1.call-update) | async-done | bytes 28311568 | tf_op jit(solution)/shard_map/all_gather | solution.py:60
  352.7 23.6 %fusion.33 = f32[640,4608]{1,0:T(8,128)S(1)} fusion(bf16[640,3072]{1,0:T(8,128)(2,1)} %fusion.25, bf16[3072,4608]{1,0:T(8,128)(2,1)} %all-gather.2.cloned.1.call-done), kind=kOutput, calls=%fused_computation.72 | convolution fusion | flops 18119393280 | bytes 44040192 | tf_op jit(solution)/shard_map/dot_general | solution.py:61
  407.1 6.1 collective-permute-start.1
  413.3 20.4 %collective-permute-done = bf16[2,1,1,2,2,80,1536]{6,5,4,3,1,2,0:T(8,128)(2,1)S(1)} collective-permute-done((bf16[2,1,1,2,2,80,1536]{6,5,4,3,1,2,0:T(8,128)(2,1)S(1)}, bf16[2,1,1,2,2,80,1536]{6,5,4,3,1,2,0:T(8,128)(2,1)S(1)}, u32[]{:S(2)}, u32[]{:S(2)}) %collective-permute-start) | collective-permute-done | bytes 1966112 | tf_op jit(solution)/shard_map/ppermute | solution.py:24
  461.1 69.3 %collective-permute-done.2 = bf16[2,4,1,1,2,80,1536]{6,5,4,3,1,2,0:T(8,128)(2,1)} collective-permute-done((bf16[2,4,1,1,2,80,1536]{6,5,4,3,1,2,0:T(8,128)(2,1)}, bf16[2,4,1,1,2,80,1536]{6,5,4,3,1,2,0:T(8,128)(2,1)}, u32[]{:S(2)}, u32[]{:S(2)}) %collective-permute-start.2) | collective-permute-done | bytes 3932192 | tf_op jit(solution)/shard_map/ppermute | solution.py:24
  531.9 6.5 pad_maximum_fusion
  538.3 5.8 fusion.31
  544.1 15.1 %squeeze.28 = bf16[2560,12,128]{2,1,0:T(8,128)(2,1)} reshape(bf16[1,4,1,4,2,80,1536]{6,5,4,3,1,2,0:T(8,128)(2,1)} %get-tuple-element.149) | data formatting | bytes 15728640 | tf_op jit(solution)/shard_map/squeeze | solution.py:73
  559.2 9.2 %copy.16 = bf16[12,2560,128]{2,1,0:T(8,128)(2,1)} copy(bf16[12,2560,128]{2,0,1:T(8,128)(2,1)} %bitcast.66) | data formatting | bytes 15728640
  568.4 15.1 %squeeze.29 = bf16[2560,12,128]{2,1,0:T(8,128)(2,1)} reshape(bf16[1,4,1,4,2,80,1536]{6,5,4,3,1,2,0:T(8,128)(2,1)} %get-tuple-element.148) | data formatting | bytes 15728640 | tf_op jit(solution)/shard_map/squeeze | solution.py:74
  583.5 9.3 %copy.17 = bf16[12,2560,128]{2,1,0:T(8,128)(2,1)} copy(bf16[12,2560,128]{2,0,1:T(8,128)(2,1)} %bitcast.67) | data formatting | bytes 15728640
  592.7 142.9 %while.11 = (s32[]{:T(128)}, bf16[12,640,128]{2,1,0:T(8,128)(2,1)S(1)}, pred[640]{0:T(1024)(128)(4,1)S(1)}, s32[12,3]{0,1:T(4,128)S(1)}, pred[1,2560]{1,0:T(4,12...) while((s32[]{:T(128)}, ...), condition=%wide.region_6.7_spmd.clone, body=%wide.region_4.6_spmd.clone.sunk | while | flops 866877440 | bytes 14808906 | solution.py:123
  593.4 8.9 %fusion.42 = (f32[640]{0:T(1024)S(1)}, f32[640,2560]{1,0:T(8,128)S(1)}) fusion(bf16[12,2560,128]{2,1,0:T(8,128)(2,1)} %get-tuple-element.290, s32[]{:T(128)} %get-tuple-element.268, bf16[12,640,128]{1,2,0:T(8,128)(2,1)} %get-tuple-element.289, pred[2560]{0:T(1024)(128)(4,1)S(1)} %reduce.4, s32[]{:T(128)} %bitcast.63, ...), kind=kOutput, calls=%fused_computation.69.clone.1 | convolution fusion | flops 444005760 | bytes 7418880 | tf_op jit(solution)/shard_map/while/body/eval_jaxpr/qd,kd->qk/dot_general | solution.py:114
  605.3 8.9 %fusion.42 = (f32[640]{0:T(1024)S(1)}, f32[640,2560]{1,0:T(8,128)S(1)}) fusion(bf16[12,2560,128]{2,1,0:T(8,128)(2,1)} %get-tuple-element.290, s32[]{:T(128)} %get-tuple-element.268, bf16[12,640,128]{1,2,0:T(8,128)(2,1)} %get-tuple-element.289, pred[2560]{0:T(1024)(128)(4,1)S(1)} %reduce.4, s32[]{:T(128)} %bitcast.63, ...), kind=kOutput, calls=%fused_computation.69.clone.1 | convolution fusion | flops 444005760 | bytes 7418880 | tf_op jit(solution)/shard_map/while/body/eval_jaxpr/qd,kd->qk/dot_general | solution.py:114
  617.2 8.9 %fusion.42 = (f32[640]{0:T(1024)S(1)}, f32[640,2560]{1,0:T(8,128)S(1)}) fusion(bf16[12,2560,128]{2,1,0:T(8,128)(2,1)} %get-tuple-element.290, s32[]{:T(128)} %get-tuple-element.268, bf16[12,640,128]{1,2,0:T(8,128)(2,1)} %get-tuple-element.289, pred[2560]{0:T(1024)(128)(4,1)S(1)} %reduce.4, s32[]{:T(128)} %bitcast.63, ...), kind=kOutput, calls=%fused_computation.69.clone.1 | convolution fusion | flops 444005760 | bytes 7418880 | tf_op jit(solution)/shard_map/while/body/eval_jaxpr/qd,kd->qk/dot_general | solution.py:114
  629.1 8.9 %fusion.42 = (f32[640]{0:T(1024)S(1)}, f32[640,2560]{1,0:T(8,128)S(1)}) fusion(bf16[12,2560,128]{2,1,0:T(8,128)(2,1)} %get-tuple-element.290, s32[]{:T(128)} %get-tuple-element.268, bf16[12,640,128]{1,2,0:T(8,128)(2,1)} %get-tuple-element.289, pred[2560]{0:T(1024)(128)(4,1)S(1)} %reduce.4, s32[]{:T(128)} %bitcast.63, ...), kind=kOutput, calls=%fused_computation.69.clone.1 | convolution fusion | flops 444005760 | bytes 7418880 | tf_op jit(solution)/shard_map/while/body/eval_jaxpr/qd,kd->qk/dot_general | solution.py:114
  641.1 8.9 %fusion.42 = (f32[640]{0:T(1024)S(1)}, f32[640,2560]{1,0:T(8,128)S(1)}) fusion(bf16[12,2560,128]{2,1,0:T(8,128)(2,1)} %get-tuple-element.290, s32[]{:T(128)} %get-tuple-element.268, bf16[12,640,128]{1,2,0:T(8,128)(2,1)} %get-tuple-element.289, pred[2560]{0:T(1024)(128)(4,1)S(1)} %reduce.4, s32[]{:T(128)} %bitcast.63, ...), kind=kOutput, calls=%fused_computation.69.clone.1 | convolution fusion | flops 444005760 | bytes 7418880 | tf_op jit(solution)/shard_map/while/body/eval_jaxpr/qd,kd->qk/dot_general | solution.py:114
  653.0 8.9 %fusion.42 = (f32[640]{0:T(1024)S(1)}, f32[640,2560]{1,0:T(8,128)S(1)}) fusion(bf16[12,2560,128]{2,1,0:T(8,128)(2,1)} %get-tuple-element.290, s32[]{:T(128)} %get-tuple-element.268, bf16[12,640,128]{1,2,0:T(8,128)(2,1)} %get-tuple-element.289, pred[2560]{0:T(1024)(128)(4,1)S(1)} %reduce.4, s32[]{:T(128)} %bitcast.63, ...), kind=kOutput, calls=%fused_computation.69.clone.1 | convolution fusion | flops 444005760 | bytes 7418880 | tf_op jit(solution)/shard_map/while/body/eval_jaxpr/qd,kd->qk/dot_general | solution.py:114
  664.9 8.9 %fusion.42 = (f32[640]{0:T(1024)S(1)}, f32[640,2560]{1,0:T(8,128)S(1)}) fusion(bf16[12,2560,128]{2,1,0:T(8,128)(2,1)} %get-tuple-element.290, s32[]{:T(128)} %get-tuple-element.268, bf16[12,640,128]{1,2,0:T(8,128)(2,1)} %get-tuple-element.289, pred[2560]{0:T(1024)(128)(4,1)S(1)} %reduce.4, s32[]{:T(128)} %bitcast.63, ...), kind=kOutput, calls=%fused_computation.69.clone.1 | convolution fusion | flops 444005760 | bytes 7418880 | tf_op jit(solution)/shard_map/while/body/eval_jaxpr/qd,kd->qk/dot_general | solution.py:114
  676.8 8.9 %fusion.42 = (f32[640]{0:T(1024)S(1)}, f32[640,2560]{1,0:T(8,128)S(1)}) fusion(bf16[12,2560,128]{2,1,0:T(8,128)(2,1)} %get-tuple-element.290, s32[]{:T(128)} %get-tuple-element.268, bf16[12,640,128]{1,2,0:T(8,128)(2,1)} %get-tuple-element.289, pred[2560]{0:T(1024)(128)(4,1)S(1)} %reduce.4, s32[]{:T(128)} %bitcast.63, ...), kind=kOutput, calls=%fused_computation.69.clone.1 | convolution fusion | flops 444005760 | bytes 7418880 | tf_op jit(solution)/shard_map/while/body/eval_jaxpr/qd,kd->qk/dot_general | solution.py:114
  688.7 8.9 %fusion.42 = (f32[640]{0:T(1024)S(1)}, f32[640,2560]{1,0:T(8,128)S(1)}) fusion(bf16[12,2560,128]{2,1,0:T(8,128)(2,1)} %get-tuple-element.290, s32[]{:T(128)} %get-tuple-element.268, bf16[12,640,128]{1,2,0:T(8,128)(2,1)} %get-tuple-element.289, pred[2560]{0:T(1024)(128)(4,1)S(1)} %reduce.4, s32[]{:T(128)} %bitcast.63, ...), kind=kOutput, calls=%fused_computation.69.clone.1 | convolution fusion | flops 444005760 | bytes 7418880 | tf_op jit(solution)/shard_map/while/body/eval_jaxpr/qd,kd->qk/dot_general | solution.py:114
  700.6 8.9 %fusion.42 = (f32[640]{0:T(1024)S(1)}, f32[640,2560]{1,0:T(8,128)S(1)}) fusion(bf16[12,2560,128]{2,1,0:T(8,128)(2,1)} %get-tuple-element.290, s32[]{:T(128)} %get-tuple-element.268, bf16[12,640,128]{1,2,0:T(8,128)(2,1)} %get-tuple-element.289, pred[2560]{0:T(1024)(128)(4,1)S(1)} %reduce.4, s32[]{:T(128)} %bitcast.63, ...), kind=kOutput, calls=%fused_computation.69.clone.1 | convolution fusion | flops 444005760 | bytes 7418880 | tf_op jit(solution)/shard_map/while/body/eval_jaxpr/qd,kd->qk/dot_general | solution.py:114
  712.5 8.9 %fusion.42 = (f32[640]{0:T(1024)S(1)}, f32[640,2560]{1,0:T(8,128)S(1)}) fusion(bf16[12,2560,128]{2,1,0:T(8,128)(2,1)} %get-tuple-element.290, s32[]{:T(128)} %get-tuple-element.268, bf16[12,640,128]{1,2,0:T(8,128)(2,1)} %get-tuple-element.289, pred[2560]{0:T(1024)(128)(4,1)S(1)} %reduce.4, s32[]{:T(128)} %bitcast.63, ...), kind=kOutput, calls=%fused_computation.69.clone.1 | convolution fusion | flops 444005760 | bytes 7418880 | tf_op jit(solution)/shard_map/while/body/eval_jaxpr/qd,kd->qk/dot_general | solution.py:114
  724.4 8.9 %fusion.42 = (f32[640]{0:T(1024)S(1)}, f32[640,2560]{1,0:T(8,128)S(1)}) fusion(bf16[12,2560,128]{2,1,0:T(8,128)(2,1)} %get-tuple-element.290, s32[]{:T(128)} %get-tuple-element.268, bf16[12,640,128]{1,2,0:T(8,128)(2,1)} %get-tuple-element.289, pred[2560]{0:T(1024)(128)(4,1)S(1)} %reduce.4, s32[]{:T(128)} %bitcast.63, ...), kind=kOutput, calls=%fused_computation.69.clone.1 | convolution fusion | flops 444005760 | bytes 7418880 | tf_op jit(solution)/shard_map/while/body/eval_jaxpr/qd,kd->qk/dot_general | solution.py:114
  (148 shorter events, 113.4 us)
Async XLA Ops:
  6.5 7.0 copy-start
  6.5 346.2 %all-gather.2.cloned.1.call-start = ((), (), s32[]{:S(2)}) async-start(), calls=%async_computation | async-start | bytes 28532736 | tf_op jit(solution)/shard_map/all_gather | solution.py:60
  7.3 6.3 copy-start.13
  7.3 6.3 copy-start.14
  403.7 31.7 %copy-start.3 = (bf16[1,2,1,2,2,80,1536]{6,5,4,3,1,2,0:T(8,128)(2,1)}, bf16[1,2,1,2,2,80,1536]{6,5,4,3,1,2,0:T(8,128)(2,1)S(1)}, u32[]{:S(2)}) copy-start(bf16[1,2,1,2,2,80,1536]{6,5,4,3,1,2,0:T(8,128)(2,1)S(1)} %multiply_convert_fusion) | copy-start | bytes 5898244
  404.1 29.6 %collective-permute-start = (bf16[2,1,1,2,2,80,1536]{6,5,4,3,1,2,0:T(8,128)(2,1)S(1)}, bf16[2,1,1,2,2,80,1536]{6,5,4,3,1,2,0:T(8,128)(2,1)S(1)}, u32[]{:S(2)}, u32[]{:S(2)}) collective-permute-start(bf16[2,1,1,2,2,80,1536]{6,5,4,3,1,2,0:T(8,128)(2,1)S(1)} %get-tuple-element.155), channel_id=1, source_target_pairs={{0,8},{8,16},{16,24},{24,32},{32,40},{40,48},{48,56},{56,64},{64,7... | collective-permute-start | bytes 5898248 | tf_op jit(solution)/shard_map/ppermute | solution.py:24
  407.1 28.3 %collective-permute-start.1 = (bf16[2,1,1,2,2,80,1536]{6,5,4,3,1,2,0:T(8,128)(2,1)S(1)}, bf16[2,1,1,2,2,80,1536]{6,5,4,3,1,2,0:T(8,128)(2,1)S(1)}, u32[]{:S(2)}, u32[]{:S(2)}) collective-permute-start(bf16[2,1,1,2,2,80,1536]{6,5,4,3,1,2,0:T(8,128)(2,1)S(1)} %get-tuple-element.156), channel_id=1, source_target_pairs={{8,0},{16,8},{24,16},{32,24},{40,32},{48,40},{56,48},{64,56},{72,6... | collective-permute-start | bytes 5898248 | tf_op jit(solution)/shard_map/ppermute | solution.py:26
  433.6 1.8 copy-start.5
  435.4 1.3 copy-start.7
  437.7 11.6 %copy-start.11 = (s32[32,32,80]{2,1,0:T(8,128)S(1)}, s32[32,32,80]{2,1,0:T(8,128)}, u32[]{:S(2)}) copy-start(s32[32,32,80]{2,1,0:T(8,128)} %param.17) | copy-start | bytes 983044
  441.2 89.3 %collective-permute-start.2 = (bf16[2,4,1,1,2,80,1536]{6,5,4,3,1,2,0:T(8,128)(2,1)}, bf16[2,4,1,1,2,80,1536]{6,5,4,3,1,2,0:T(8,128)(2,1)}, u32[]{:S(2)}, u32[]{:S(2)}) collective-permute-start(bf16[2,4,1,1,2,80,1536]{6,5,4,3,1,2,0:T(8,128)(2,1)} %get-tuple-element.153), channel_id=1, source_target_pairs={{0,1},{1,2},{2,3},{3,4},{4,5},{5,6},{6,7},{8,9},{9,10},{10,11},{11... | collective-permute-start | bytes 11796488 | tf_op jit(solution)/shard_map/ppermute | solution.py:24
  445.2 86.6 %collective-permute-start.3 = (bf16[2,4,1,1,2,80,1536]{6,5,4,3,1,2,0:T(8,128)(2,1)}, bf16[2,4,1,1,2,80,1536]{6,5,4,3,1,2,0:T(8,128)(2,1)}, u32[]{:S(2)}, u32[]{:S(2)}) collective-permute-start(bf16[2,4,1,1,2,80,1536]{6,5,4,3,1,2,0:T(8,128)(2,1)} %get-tuple-element.154), channel_id=1, source_target_pairs={{1,0},{2,1},{3,2},{4,3},{5,4},{6,5},{7,6},{9,8},{10,9},{11,10},{12... | collective-permute-start | bytes 11796488 | tf_op jit(solution)/shard_map/ppermute | solution.py:26
  455.9 3.3 copy-start.2
  455.9 3.3 copy-start.15
  458.5 73.4 %copy-start.4 = (bf16[1,2,1,2,2,80,1536]{6,5,4,3,1,2,0:T(8,128)(2,1)S(1)}, bf16[1,2,1,2,2,80,1536]{6,5,4,3,1,2,0:T(8,128)(2,1)}, u32[]{:S(2)}) copy-start(bf16[1,2,1,2,2,80,1536]{6,5,4,3,1,2,0:T(8,128)(2,1)} %copy-done.3) | copy-start | bytes 5898244
  458.5 73.4 %copy-start.6 = (bf16[2,1,1,2,2,80,1536]{6,5,4,3,1,2,0:T(8,128)(2,1)S(1)}, bf16[2,1,1,2,2,80,1536]{6,5,4,3,1,2,0:T(8,128)(2,1)}, u32[]{:S(2)}) copy-start(bf16[2,1,1,2,2,80,1536]{6,5,4,3,1,2,0:T(8,128)(2,1)} %copy-done.5) | copy-start | bytes 5898244
  458.5 73.4 %copy-start.8 = (bf16[2,1,1,2,2,80,1536]{6,5,4,3,1,2,0:T(8,128)(2,1)S(1)}, bf16[2,1,1,2,2,80,1536]{6,5,4,3,1,2,0:T(8,128)(2,1)}, u32[]{:S(2)}) copy-start(bf16[2,1,1,2,2,80,1536]{6,5,4,3,1,2,0:T(8,128)(2,1)} %copy-done.7) | copy-start | bytes 5898244
  583.4 9.3 %copy-start.9 = (bf16[12,640,128]{2,1,0:T(8,128)(2,1)S(1)}, bf16[12,640,128]{2,1,0:T(8,128)(2,1)}, u32[]{:S(2)}) copy-start(bf16[12,640,128]{2,1,0:T(8,128)(2,1)} %custom-call) | copy-start | bytes 5898244
  583.4 9.3 %copy-start.12 = (s32[12,3]{0,1:T(4,128)S(1)}, s32[12,3]{0,1:T(4,128)}, u32[]{:S(2)}) copy-start(s32[12,3]{0,1:T(4,128)} %param.16) | copy-start | bytes 436
  735.6 1.3 copy-start.10
  736.9 5.5 copy-start.1
Sparse Core Ops, SparseCore 0:
  9.1 343.6 all-gather.1
where the time goes:
time: 753 us; the launch traced here: 749 us
  waiting for transfers between devices  428 us (57%)
  matrix products  158 us (21%)
  local copies, waits for them, and re-layouts  96.6 us (13%)
  other arithmetic  35.8 us (5%)
  starting transfers between devices  17.3 us (2%)
  between operations  13.7 us (2%)
    all_gather x1, waiting for transfers between devices, per_device(): full_weight = lax.all_gather(w_qkv, ('tm', 'height'), axis=0, tiled=True)  334 us
    dot_general x12, matrix products, per_head(): jnp.einsum('qd,kd->qk', query_one, key_one, preferred_element_type=jnp.fl...  107 us
    ppermute x2, waiting for transfers between devices, with_halo(): lax.ppermute(tail, axis, [(i, (i + 1) % count) for i in range(ends)])  89.7 us
    dot_general x12, matrix products, per_head(): result = jnp.dot(weights, value_one, preferred_element_type=jnp.float32)  26.8 us
    dot_general x1, matrix products, per_device(): qkv = jnp.dot(modulated, full_weight, preferred_element_type=jnp.float32)  23.6 us
    unnamed x34, local copies, waits for them, and re-layouts  21.7 us
    squeeze x1, local copies, waits for them, and re-layouts, per_device(): value_heads = jnp.transpose(extended[1], (1, 0, 2))  15.1 us
    squeeze x1, local copies, waits for them, and re-layouts, per_device(): key_heads = jnp.transpose(extended[0], (1, 0, 2))  15.1 us
  transfers between devices with their start and end apart: 5, of which 5 were waited for; matrix products, arithmetic and copies ran while one was open for 3% of the time, Pallas kernels for 0%

commit v1 on v0

--- a/solution.py
+++ b/solution.py
@@ -57,7 +57,8 @@
     frame_count, row_count, width, features = tokens.shape
     token_count = frame_count * row_count * width
     modulated = modulate(tokens.reshape(token_count, features), mod_scale, mod_shift)
-    full_weight = lax.all_gather(w_qkv, ("tm", "height"), axis=0, tiled=True)
+    band_weight = lax.all_gather(w_qkv, "height", axis=0, tiled=True)
+    full_weight = lax.all_gather(band_weight, "tm", axis=0, tiled=True)
     qkv = jnp.dot(modulated, full_weight, preferred_element_type=jnp.float32)
     inner = qkv.shape[1] // 3
     query = head_norm(qkv[:, :inner].reshape(token_count, HEADS, HDIM), q_gain)

time: 753 us -> 615 us (0.82)
  waiting for transfers between devices: 428 us -> 288 us
    all_gather x1 -> x2, waiting for transfers between devices: 334 us -> 196 us  [the longest x1 152 us: per_device(): full_weight = lax.all_gather(band_weight, 'tm', axis=0, tiled=True)]
  transfers between devices with their start and end apart: 5 -> 6, of which waited for: 5 -> 6; matrix products, arithmetic and copies ran while one was open for 3% -> 4% of each run, Pallas kernels for 0% -> 0%
where the time goes in v1:
time: 615 us; the launch traced here: 609 us
  waiting for transfers between devices  288 us (47%)
  matrix products  157 us (26%)
  local copies, waits for them, and re-layouts  96.4 us (16%)
  other arithmetic  35.9 us (6%)
  starting transfers between devices  17.3 us (3%)
  between operations  13.7 us (2%)
    all_gather x1, waiting for transfers between devices, per_device(): full_weight = lax.all_gather(band_weight, 'tm', axis=0, tiled=True)  152 us
    dot_general x12, matrix products, per_head(): jnp.einsum('qd,kd->qk', query_one, key_one, preferred_element_type=jnp.fl...  107 us
    ppermute x2, waiting for transfers between devices, with_halo(): lax.ppermute(tail, axis, [(i, (i + 1) % count) for i in range(ends)])  88.7 us
    all_gather x1, waiting for transfers between devices, per_device(): band_weight = lax.all_gather(w_qkv, 'height', axis=0, tiled=True)  44.5 us
    dot_general x12, matrix products, per_head(): result = jnp.dot(weights, value_one, preferred_element_type=jnp.float32)  26.7 us
    dot_general x1, matrix products, per_device(): qkv = jnp.dot(modulated, full_weight, preferred_element_type=jnp.float32)  23.6 us
    unnamed x34, local copies, waits for them, and re-layouts  21.7 us
    squeeze x1, local copies, waits for them, and re-layouts, per_device(): key_heads = jnp.transpose(extended[0], (1, 0, 2))  15.1 us
  transfers between devices with their start and end apart: 6, of which 6 were waited for; matrix products, arithmetic and copies ran while one was open for 4% of the time, Pallas kernels for 0%

profile of v1, /device:TPU:6, one launch (start us, length us, event | category | flops | bytes accessed | tf_op | source)
XLA Modules:
  0.0 609.4 jit_solution(14593037930837388068)
XLA Ops:
  7.3 44.5 %all-gather.3.cloned.1.call-done = bf16[192,4608]{1,0:T(8,128)(2,1)} async-done(((bf16[24,4608]{1,0:T(8,128)(2,1)}), bf16[192,4608]{1,0:T(8,128)(2,1)}) %all-gather.3.cloned.1.call-update) | async-done | bytes 1769488 | tf_op jit(solution)/shard_map/all_gather | solution.py:60
  63.0 151.5 %all-gather.5.cloned.1.call-done = bf16[3072,4608]{1,0:T(8,128)(2,1)} async-done(((bf16[192,4608]{1,0:T(8,128)(2,1)}), bf16[3072,4608]{1,0:T(8,128)(2,1)}) %all-gather.5.cloned.1.call-update) | async-done | bytes 28311568 | tf_op jit(solution)/shard_map/all_gather | solution.py:61
  214.5 23.6 %fusion.33 = f32[640,4608]{1,0:T(8,128)S(1)} fusion(bf16[640,3072]{1,0:T(8,128)(2,1)} %fusion.25, bf16[3072,4608]{1,0:T(8,128)(2,1)} %all-gather.5.cloned.1.call-done), kind=kOutput, calls=%fused_computation.72 | convolution fusion | flops 18119393280 | bytes 44040192 | tf_op jit(solution)/shard_map/dot_general | solution.py:62
  268.1 7.0 %collective-permute-start.1 = (bf16[2,1,1,2,2,80,1536]{6,5,4,3,1,2,0:T(8,128)(2,1)S(1)}, bf16[2,1,1,2,2,80,1536]{6,5,4,3,1,2,0:T(8,128)(2,1)S(1)}, u32[]{:S(2)}, u32[]{:S(2)}) collective-permute-start(bf16[2,1,1,2,2,80,1536]{6,5,4,3,1,2,0:T(8,128)(2,1)S(1)} %get-tuple-element.156), channel_id=1, source_target_pairs={{8,0},{16,8},{24,16},{32,24},{40,32},{48,40},{56,48},{64,56},{72,6... | collective-permute-start | bytes 5898248 | tf_op jit(solution)/shard_map/ppermute | solution.py:26
  275.1 20.4 %collective-permute-done = bf16[2,1,1,2,2,80,1536]{6,5,4,3,1,2,0:T(8,128)(2,1)S(1)} collective-permute-done((bf16[2,1,1,2,2,80,1536]{6,5,4,3,1,2,0:T(8,128)(2,1)S(1)}, bf16[2,1,1,2,2,80,1536]{6,5,4,3,1,2,0:T(8,128)(2,1)S(1)}, u32[]{:S(2)}, u32[]{:S(2)}) %collective-permute-start) | collective-permute-done | bytes 1966112 | tf_op jit(solution)/shard_map/ppermute | solution.py:24
  323.0 68.3 %collective-permute-done.2 = bf16[2,4,1,1,2,80,1536]{6,5,4,3,1,2,0:T(8,128)(2,1)} collective-permute-done((bf16[2,4,1,1,2,80,1536]{6,5,4,3,1,2,0:T(8,128)(2,1)}, bf16[2,4,1,1,2,80,1536]{6,5,4,3,1,2,0:T(8,128)(2,1)}, u32[]{:S(2)}, u32[]{:S(2)}) %collective-permute-start.2) | collective-permute-done | bytes 3932192 | tf_op jit(solution)/shard_map/ppermute | solution.py:24
  392.5 6.5 %pad_maximum_fusion = bf16[2,4,1,4,2,80,1536]{6,5,4,3,1,2,0:T(8,128)(2,1)S(1)} fusion(bf16[2,4,1,1,2,80,1536]{6,5,4,3,1,2,0:T(8,128)(2,1)} %collective-permute-done.3, bf16[2,1,1,2,2,80,1536]{6,5,4,3,1,2,0:T(8,128)(2,1)S(1)} %copy-done.8, bf16[1,2,1,2,2,80,1536]{6,5,4,3,1,2,0:T(8,128)(2,1)S(1)} %bitcast.72, ...), kind=kLoop, calls=%fused_computation.26 | loop fusion | flops 39321600 | bytes 31457280 | tf_op jit(solution)/shard_map/concatenate | solution.py:22
  404.7 15.1 %squeeze.28 = bf16[2560,12,128]{2,1,0:T(8,128)(2,1)} reshape(bf16[1,4,1,4,2,80,1536]{6,5,4,3,1,2,0:T(8,128)(2,1)} %get-tuple-element.149) | data formatting | bytes 15728640 | tf_op jit(solution)/shard_map/squeeze | solution.py:74
  419.8 9.2 %copy.16 = bf16[12,2560,128]{2,1,0:T(8,128)(2,1)} copy(bf16[12,2560,128]{2,0,1:T(8,128)(2,1)} %bitcast.66) | data formatting | bytes 15728640
  428.9 15.1 %squeeze.29 = bf16[2560,12,128]{2,1,0:T(8,128)(2,1)} reshape(bf16[1,4,1,4,2,80,1536]{6,5,4,3,1,2,0:T(8,128)(2,1)} %get-tuple-element.148) | data formatting | bytes 15728640 | tf_op jit(solution)/shard_map/squeeze | solution.py:75
  444.0 9.3 %copy.17 = bf16[12,2560,128]{2,1,0:T(8,128)(2,1)} copy(bf16[12,2560,128]{2,0,1:T(8,128)(2,1)} %bitcast.67) | data formatting | bytes 15728640
  453.3 142.5 %while.11 = (s32[]{:T(128)}, bf16[12,640,128]{2,1,0:T(8,128)(2,1)S(1)}, pred[640]{0:T(1024)(128)(4,1)S(1)}, s32[12,3]{0,1:T(4,128)S(1)}, pred[1,2560]{1,0:T(4,12...) while((s32[]{:T(128)}, ...), condition=%wide.region_6.7_spmd.clone, body=%wide.region_4.6_spmd.clone.sunk | while | flops 866877440 | bytes 14808906 | solution.py:124
  454.0 8.9 %fusion.42 = (f32[640]{0:T(1024)S(1)}, f32[640,2560]{1,0:T(8,128)S(1)}) fusion(bf16[12,2560,128]{2,1,0:T(8,128)(2,1)} %get-tuple-element.290, s32[]{:T(128)} %get-tuple-element.268, bf16[12,640,128]{1,2,0:T(8,128)(2,1)} %get-tuple-element.289, pred[2560]{0:T(1024)(128)(4,1)S(1)} %reduce.4, s32[]{:T(128)} %bitcast.63, ...), kind=kOutput, calls=%fused_computation.69.clone.1 | convolution fusion | flops 444005760 | bytes 7418880 | tf_op jit(solution)/shard_map/while/body/eval_jaxpr/qd,kd->qk/dot_general | solution.py:115
  465.9 8.9 %fusion.42 = (f32[640]{0:T(1024)S(1)}, f32[640,2560]{1,0:T(8,128)S(1)}) fusion(bf16[12,2560,128]{2,1,0:T(8,128)(2,1)} %get-tuple-element.290, s32[]{:T(128)} %get-tuple-element.268, bf16[12,640,128]{1,2,0:T(8,128)(2,1)} %get-tuple-element.289, pred[2560]{0:T(1024)(128)(4,1)S(1)} %reduce.4, s32[]{:T(128)} %bitcast.63, ...), kind=kOutput, calls=%fused_computation.69.clone.1 | convolution fusion | flops 444005760 | bytes 7418880 | tf_op jit(solution)/shard_map/while/body/eval_jaxpr/qd,kd->qk/dot_general | solution.py:115
  477.7 8.9 %fusion.42 = (f32[640]{0:T(1024)S(1)}, f32[640,2560]{1,0:T(8,128)S(1)}) fusion(bf16[12,2560,128]{2,1,0:T(8,128)(2,1)} %get-tuple-element.290, s32[]{:T(128)} %get-tuple-element.268, bf16[12,640,128]{1,2,0:T(8,128)(2,1)} %get-tuple-element.289, pred[2560]{0:T(1024)(128)(4,1)S(1)} %reduce.4, s32[]{:T(128)} %bitcast.63, ...), kind=kOutput, calls=%fused_computation.69.clone.1 | convolution fusion | flops 444005760 | bytes 7418880 | tf_op jit(solution)/shard_map/while/body/eval_jaxpr/qd,kd->qk/dot_general | solution.py:115
  489.6 8.9 %fusion.42 = (f32[640]{0:T(1024)S(1)}, f32[640,2560]{1,0:T(8,128)S(1)}) fusion(bf16[12,2560,128]{2,1,0:T(8,128)(2,1)} %get-tuple-element.290, s32[]{:T(128)} %get-tuple-element.268, bf16[12,640,128]{1,2,0:T(8,128)(2,1)} %get-tuple-element.289, pred[2560]{0:T(1024)(128)(4,1)S(1)} %reduce.4, s32[]{:T(128)} %bitcast.63, ...), kind=kOutput, calls=%fused_computation.69.clone.1 | convolution fusion | flops 444005760 | bytes 7418880 | tf_op jit(solution)/shard_map/while/body/eval_jaxpr/qd,kd->qk/dot_general | solution.py:115
  501.5 8.9 %fusion.42 = (f32[640]{0:T(1024)S(1)}, f32[640,2560]{1,0:T(8,128)S(1)}) fusion(bf16[12,2560,128]{2,1,0:T(8,128)(2,1)} %get-tuple-element.290, s32[]{:T(128)} %get-tuple-element.268, bf16[12,640,128]{1,2,0:T(8,128)(2,1)} %get-tuple-element.289, pred[2560]{0:T(1024)(128)(4,1)S(1)} %reduce.4, s32[]{:T(128)} %bitcast.63, ...), kind=kOutput, calls=%fused_computation.69.clone.1 | convolution fusion | flops 444005760 | bytes 7418880 | tf_op jit(solution)/shard_map/while/body/eval_jaxpr/qd,kd->qk/dot_general | solution.py:115
  513.4 8.9 %fusion.42 = (f32[640]{0:T(1024)S(1)}, f32[640,2560]{1,0:T(8,128)S(1)}) fusion(bf16[12,2560,128]{2,1,0:T(8,128)(2,1)} %get-tuple-element.290, s32[]{:T(128)} %get-tuple-element.268, bf16[12,640,128]{1,2,0:T(8,128)(2,1)} %get-tuple-element.289, pred[2560]{0:T(1024)(128)(4,1)S(1)} %reduce.4, s32[]{:T(128)} %bitcast.63, ...), kind=kOutput, calls=%fused_computation.69.clone.1 | convolution fusion | flops 444005760 | bytes 7418880 | tf_op jit(solution)/shard_map/while/body/eval_jaxpr/qd,kd->qk/dot_general | solution.py:115
  525.2 8.9 %fusion.42 = (f32[640]{0:T(1024)S(1)}, f32[640,2560]{1,0:T(8,128)S(1)}) fusion(bf16[12,2560,128]{2,1,0:T(8,128)(2,1)} %get-tuple-element.290, s32[]{:T(128)} %get-tuple-element.268, bf16[12,640,128]{1,2,0:T(8,128)(2,1)} %get-tuple-element.289, pred[2560]{0:T(1024)(128)(4,1)S(1)} %reduce.4, s32[]{:T(128)} %bitcast.63, ...), kind=kOutput, calls=%fused_computation.69.clone.1 | convolution fusion | flops 444005760 | bytes 7418880 | tf_op jit(solution)/shard_map/while/body/eval_jaxpr/qd,kd->qk/dot_general | solution.py:115
  537.1 8.9 %fusion.42 = (f32[640]{0:T(1024)S(1)}, f32[640,2560]{1,0:T(8,128)S(1)}) fusion(bf16[12,2560,128]{2,1,0:T(8,128)(2,1)} %get-tuple-element.290, s32[]{:T(128)} %get-tuple-element.268, bf16[12,640,128]{1,2,0:T(8,128)(2,1)} %get-tuple-element.289, pred[2560]{0:T(1024)(128)(4,1)S(1)} %reduce.4, s32[]{:T(128)} %bitcast.63, ...), kind=kOutput, calls=%fused_computation.69.clone.1 | convolution fusion | flops 444005760 | bytes 7418880 | tf_op jit(solution)/shard_map/while/body/eval_jaxpr/qd,kd->qk/dot_general | solution.py:115
  549.0 8.9 %fusion.42 = (f32[640]{0:T(1024)S(1)}, f32[640,2560]{1,0:T(8,128)S(1)}) fusion(bf16[12,2560,128]{2,1,0:T(8,128)(2,1)} %get-tuple-element.290, s32[]{:T(128)} %get-tuple-element.268, bf16[12,640,128]{1,2,0:T(8,128)(2,1)} %get-tuple-element.289, pred[2560]{0:T(1024)(128)(4,1)S(1)} %reduce.4, s32[]{:T(128)} %bitcast.63, ...), kind=kOutput, calls=%fused_computation.69.clone.1 | convolution fusion | flops 444005760 | bytes 7418880 | tf_op jit(solution)/shard_map/while/body/eval_jaxpr/qd,kd->qk/dot_general | solution.py:115
  560.9 8.9 %fusion.42 = (f32[640]{0:T(1024)S(1)}, f32[640,2560]{1,0:T(8,128)S(1)}) fusion(bf16[12,2560,128]{2,1,0:T(8,128)(2,1)} %get-tuple-element.290, s32[]{:T(128)} %get-tuple-element.268, bf16[12,640,128]{1,2,0:T(8,128)(2,1)} %get-tuple-element.289, pred[2560]{0:T(1024)(128)(4,1)S(1)} %reduce.4, s32[]{:T(128)} %bitcast.63, ...), kind=kOutput, calls=%fused_computation.69.clone.1 | convolution fusion | flops 444005760 | bytes 7418880 | tf_op jit(solution)/shard_map/while/body/eval_jaxpr/qd,kd->qk/dot_general | solution.py:115
  572.7 8.9 %fusion.42 = (f32[640]{0:T(1024)S(1)}, f32[640,2560]{1,0:T(8,128)S(1)}) fusion(bf16[12,2560,128]{2,1,0:T(8,128)(2,1)} %get-tuple-element.290, s32[]{:T(128)} %get-tuple-element.268, bf16[12,640,128]{1,2,0:T(8,128)(2,1)} %get-tuple-element.289, pred[2560]{0:T(1024)(128)(4,1)S(1)} %reduce.4, s32[]{:T(128)} %bitcast.63, ...), kind=kOutput, calls=%fused_computation.69.clone.1 | convolution fusion | flops 444005760 | bytes 7418880 | tf_op jit(solution)/shard_map/while/body/eval_jaxpr/qd,kd->qk/dot_general | solution.py:115
  584.6 8.9 %fusion.42 = (f32[640]{0:T(1024)S(1)}, f32[640,2560]{1,0:T(8,128)S(1)}) fusion(bf16[12,2560,128]{2,1,0:T(8,128)(2,1)} %get-tuple-element.290, s32[]{:T(128)} %get-tuple-element.268, bf16[12,640,128]{1,2,0:T(8,128)(2,1)} %get-tuple-element.289, pred[2560]{0:T(1024)(128)(4,1)S(1)} %reduce.4, s32[]{:T(128)} %bitcast.63, ...), kind=kOutput, calls=%fused_computation.69.clone.1 | convolution fusion | flops 444005760 | bytes 7418880 | tf_op jit(solution)/shard_map/while/body/eval_jaxpr/qd,kd->qk/dot_general | solution.py:115
  (151 shorter events, 117.9 us)
Async XLA Ops:
  6.5 51.5 %copy-start = (f32[128]{0:T(128)S(1)}, f32[128]{0:T(128)}, u32[]{:S(2)}) copy-start(f32[128]{0:T(128)} %param.15) | copy-start | bytes 1540
  6.5 45.3 %all-gather.3.cloned.1.call-start = ((), (), s32[]{:S(2)}) async-start(), calls=%async_computation | async-start | bytes 1990656 | tf_op jit(solution)/shard_map/all_gather | solution.py:60
  7.3 207.3 %all-gather.5.cloned.1.call-start = ((), (), s32[]{:S(2)}) async-start(), calls=%async_computation.1 | async-start | bytes 30081024 | tf_op jit(solution)/shard_map/all_gather | solution.py:61
  51.8 6.3 %copy-start.13 = (f32[3072]{0:T(1024)S(1)}, f32[3072]{0:T(1024)}, u32[]{:S(2)}) copy-start(f32[3072]{0:T(1024)} %param.11) | copy-start | bytes 36868
  51.8 6.3 %copy-start.14 = (f32[3072]{0:T(1024)S(1)}, f32[3072]{0:T(1024)}, u32[]{:S(2)}) copy-start(f32[3072]{0:T(1024)} %param.12) | copy-start | bytes 36868
  265.5 31.7 %copy-start.3 = (bf16[1,2,1,2,2,80,1536]{6,5,4,3,1,2,0:T(8,128)(2,1)}, bf16[1,2,1,2,2,80,1536]{6,5,4,3,1,2,0:T(8,128)(2,1)S(1)}, u32[]{:S(2)}) copy-start(bf16[1,2,1,2,2,80,1536]{6,5,4,3,1,2,0:T(8,128)(2,1)S(1)} %multiply_convert_fusion) | copy-start | bytes 5898244
  265.9 29.6 %collective-permute-start = (bf16[2,1,1,2,2,80,1536]{6,5,4,3,1,2,0:T(8,128)(2,1)S(1)}, bf16[2,1,1,2,2,80,1536]{6,5,4,3,1,2,0:T(8,128)(2,1)S(1)}, u32[]{:S(2)}, u32[]{:S(2)}) collective-permute-start(bf16[2,1,1,2,2,80,1536]{6,5,4,3,1,2,0:T(8,128)(2,1)S(1)} %get-tuple-element.155), channel_id=1, source_target_pairs={{0,8},{8,16},{16,24},{24,32},{32,40},{40,48},{48,56},{56,64},{64,7... | collective-permute-start | bytes 5898248 | tf_op jit(solution)/shard_map/ppermute | solution.py:24
  268.1 29.1 %collective-permute-start.1 = (bf16[2,1,1,2,2,80,1536]{6,5,4,3,1,2,0:T(8,128)(2,1)S(1)}, bf16[2,1,1,2,2,80,1536]{6,5,4,3,1,2,0:T(8,128)(2,1)S(1)}, u32[]{:S(2)}, u32[]{:S(2)}) collective-permute-start(bf16[2,1,1,2,2,80,1536]{6,5,4,3,1,2,0:T(8,128)(2,1)S(1)} %get-tuple-element.156), channel_id=1, source_target_pairs={{8,0},{16,8},{24,16},{32,24},{40,32},{48,40},{56,48},{64,56},{72,6... | collective-permute-start | bytes 5898248 | tf_op jit(solution)/shard_map/ppermute | solution.py:26
  295.5 1.8 copy-start.5
  297.2 1.3 copy-start.7
  299.6 11.6 %copy-start.11 = (s32[32,32,80]{2,1,0:T(8,128)S(1)}, s32[32,32,80]{2,1,0:T(8,128)}, u32[]{:S(2)}) copy-start(s32[32,32,80]{2,1,0:T(8,128)} %param.17) | copy-start | bytes 983044
  303.0 88.3 %collective-permute-start.2 = (bf16[2,4,1,1,2,80,1536]{6,5,4,3,1,2,0:T(8,128)(2,1)}, bf16[2,4,1,1,2,80,1536]{6,5,4,3,1,2,0:T(8,128)(2,1)}, u32[]{:S(2)}, u32[]{:S(2)}) collective-permute-start(bf16[2,4,1,1,2,80,1536]{6,5,4,3,1,2,0:T(8,128)(2,1)} %get-tuple-element.153), channel_id=1, source_target_pairs={{0,1},{1,2},{2,3},{3,4},{4,5},{5,6},{6,7},{8,9},{9,10},{10,11},{11... | collective-permute-start | bytes 11796488 | tf_op jit(solution)/shard_map/ppermute | solution.py:24
  306.5 86.0 %collective-permute-start.3 = (bf16[2,4,1,1,2,80,1536]{6,5,4,3,1,2,0:T(8,128)(2,1)}, bf16[2,4,1,1,2,80,1536]{6,5,4,3,1,2,0:T(8,128)(2,1)}, u32[]{:S(2)}, u32[]{:S(2)}) collective-permute-start(bf16[2,4,1,1,2,80,1536]{6,5,4,3,1,2,0:T(8,128)(2,1)} %get-tuple-element.154), channel_id=1, source_target_pairs={{1,0},{2,1},{3,2},{4,3},{5,4},{6,5},{7,6},{9,8},{10,9},{11,10},{12... | collective-permute-start | bytes 11796488 | tf_op jit(solution)/shard_map/ppermute | solution.py:26
  317.8 3.3 copy-start.2
  317.8 3.3 copy-start.15
  320.3 72.1 %copy-start.4 = (bf16[1,2,1,2,2,80,1536]{6,5,4,3,1,2,0:T(8,128)(2,1)S(1)}, bf16[1,2,1,2,2,80,1536]{6,5,4,3,1,2,0:T(8,128)(2,1)}, u32[]{:S(2)}) copy-start(bf16[1,2,1,2,2,80,1536]{6,5,4,3,1,2,0:T(8,128)(2,1)} %copy-done.3) | copy-start | bytes 5898244
  320.3 72.1 %copy-start.6 = (bf16[2,1,1,2,2,80,1536]{6,5,4,3,1,2,0:T(8,128)(2,1)S(1)}, bf16[2,1,1,2,2,80,1536]{6,5,4,3,1,2,0:T(8,128)(2,1)}, u32[]{:S(2)}) copy-start(bf16[2,1,1,2,2,80,1536]{6,5,4,3,1,2,0:T(8,128)(2,1)} %copy-done.5) | copy-start | bytes 5898244
  320.4 72.1 %copy-start.8 = (bf16[2,1,1,2,2,80,1536]{6,5,4,3,1,2,0:T(8,128)(2,1)S(1)}, bf16[2,1,1,2,2,80,1536]{6,5,4,3,1,2,0:T(8,128)(2,1)}, u32[]{:S(2)}) copy-start(bf16[2,1,1,2,2,80,1536]{6,5,4,3,1,2,0:T(8,128)(2,1)} %copy-done.7) | copy-start | bytes 5898244
  444.0 9.3 %copy-start.9 = (bf16[12,640,128]{2,1,0:T(8,128)(2,1)S(1)}, bf16[12,640,128]{2,1,0:T(8,128)(2,1)}, u32[]{:S(2)}) copy-start(bf16[12,640,128]{2,1,0:T(8,128)(2,1)} %custom-call) | copy-start | bytes 5898244
  444.0 9.3 %copy-start.12 = (s32[12,3]{0,1:T(4,128)S(1)}, s32[12,3]{0,1:T(4,128)}, u32[]{:S(2)}) copy-start(s32[12,3]{0,1:T(4,128)} %param.16) | copy-start | bytes 436
  595.8 1.3 copy-start.10
  597.1 5.5 copy-start.1
Sparse Core Ops, SparseCore 0:
  9.0 42.7 all-gather.2
  54.3 160.2 all-gather.4

commit v2 on v1

--- a/solution.py
+++ b/solution.py
@@ -2,6 +2,8 @@
 import jax.numpy as jnp
 from jax import lax
 from jax.sharding import PartitionSpec as P
+from jax.experimental import pallas as pl
+from jax.experimental.pallas import tpu as pltpu
 
 HDIM = 128
 HEADS = 12
@@ -69,61 +71,105 @@
     extended = with_halo(stacked, (("tm", 1), ("height", 3)), 1)
     frames_ext = frame_count + 2 * TT
     rows_ext = row_count + 2 * TH
-    key_count = frames_ext * rows_ext * width
-    extended = extended.reshape(2, key_count, HEADS, HDIM)
-    key_heads = jnp.transpose(extended[0], (1, 0, 2))
-    value_heads = jnp.transpose(extended[1], (1, 0, 2))
-    query_heads = jnp.transpose(query, (1, 0, 2))
+    extended = extended.reshape(2, frames_ext, rows_ext, width, inner)
     frame_block = lax.axis_index("tm")
     row_block = lax.axis_index("height")
     first_frame = frame_block * frame_count
     first_row = row_block * row_count
     zero = jnp.int32(0)
     valid_pad = jnp.pad(valid, ((TT, TT), (TH, TH), (0, 0)))
-    key_valid = (
-        lax.dynamic_slice(
-            valid_pad, (first_frame, first_row, zero), (frames_ext, rows_ext, width)
-        ).reshape(-1)
-        > 0
+    key_valid = lax.dynamic_slice(
+        valid_pad, (first_frame, first_row, zero), (frames_ext, rows_ext, width)
     )
-    query_valid = (
-        lax.dynamic_slice(
-            valid, (first_frame, first_row, zero), (frame_count, row_count, width)
-        ).reshape(-1)
-        > 0
+    query_valid = lax.dynamic_slice(
+        valid, (first_frame, first_row, zero), (frame_count, row_count, width)
     )
-    query_coords = tile_coords(
-        first_frame + jnp.arange(frame_count, dtype=jnp.int32),
-        first_row + jnp.arange(row_count, dtype=jnp.int32),
-        width,
+    row_tiles = row_count // TH
+    blocks = frame_count * row_tiles
+    span_t = 2 * TT + 1
+    span_h = 3 * TH
+    query_n = TH * width
+    key_n = span_t * span_h * width
+    block_valid = jnp.stack(
+        [
+            key_valid[f : f + span_t, TH * rt : TH * rt + span_h].reshape(-1)
+            for f in range(frame_count)
+            for rt in range(row_tiles)
+        ]
     )
-    key_coords = tile_coords(
-        first_frame - TT + jnp.arange(frames_ext, dtype=jnp.int32),
-        first_row - TH + jnp.arange(rows_ext, dtype=jnp.int32),
-        width,
+    apart_t = jnp.abs(jnp.arange(span_t, dtype=jnp.int32) - TT)
+    apart_h = jnp.abs(jnp.arange(span_h, dtype=jnp.int32) // TH - 1)
+    near = (apart_t[None, :, None, None] <= window[:, 0, None, None, None]) & (
+        apart_h[None, None, :, None] <= window[:, 1, None, None, None]
     )
-    apart_t, apart_h, apart_w = (
-        jnp.abs(qa[:, None] - ka[None, :]) for qa, ka in zip(query_coords, key_coords)
+    near = jnp.broadcast_to(near, (HEADS, span_t, span_h, width)).reshape(HEADS, 1, key_n)
+    key_mask = (near & (block_valid[None] > 0)).astype(jnp.float32).reshape(HEADS, blocks, 1, key_n)
+    column_tiles = jnp.arange(width, dtype=jnp.int32) // TW
+    key_cols = jnp.tile(column_tiles, span_t * span_h).reshape(1, key_n)
+    query_cols = jnp.tile(column_tiles, TH)
+    query_lo = (query_cols[None, :] - window[:, 2, None]).reshape(HEADS, query_n, 1)
+    query_hi = (query_cols[None, :] + window[:, 2, None]).reshape(HEADS, query_n, 1)
+    query_ok = query_valid.reshape(blocks, query_n, 1).astype(jnp.float32)
+    query_grid = query.reshape(frame_count, row_count, width, inner)
+    return tile_attention(query_grid, extended, key_mask, query_lo, query_hi, key_cols, query_ok)
+
+
+def attention_kernel(q_ref, k_ref, v_ref, km_ref, lo_ref, hi_ref, kc_ref, qv_ref, o_ref):
+    block = pl.program_id(1)
+    span_t = 2 * TT + 1
+    span_h = 3 * TH
+    frame = block // ROW_TILES
+    row = (block % ROW_TILES) * TH
+    width = q_ref.shape[2]
+    query = q_ref[0].reshape(TH * width, HDIM)
+    key = k_ref[0, pl.ds(frame, span_t), pl.ds(row, span_h)].reshape(-1, HDIM)
+    value = v_ref[0, pl.ds(frame, span_t), pl.ds(row, span_h)].reshape(-1, HDIM)
+    scores = lax.dot_general(
+        query, key, (((1,), (1,)), ((), ())), preferred_element_type=jnp.float32
+    ) * (1.0 / float(HDIM) ** 0.5)
+    key_cols = kc_ref[...]
+    allowed = (key_cols >= lo_ref[0]) & (key_cols <= hi_ref[0]) & (km_ref[0, 0] > 0.0)
+    terms = jnp.where(allowed, jnp.exp(scores), jnp.float32(0.0))
+    total = jnp.sum(terms, axis=-1, keepdims=True)
+    seen = qv_ref[0] > 0.0
+    total = jnp.where(seen, total, jnp.float32(1.0))
+    weights = (terms / total).astype(jnp.bfloat16)
+    result = jnp.dot(weights, value, preferred_element_type=jnp.float32)
+    result = jnp.where(seen, result, jnp.float32(0.0)).astype(jnp.bfloat16)
+    o_ref[0] = result.reshape(TH, width, HDIM)
+
+
+ROW_TILES = 2
+
+
+def tile_attention(query, extended, key_mask, query_lo, query_hi, key_cols, query_ok):
+    frames, rows, width, inner = query.shape
+    heads = inner // HDIM
+    row_tiles = rows // TH
+    assert row_tiles == ROW_TILES
+    blocks = frames * row_tiles
+    _, frames_ext, rows_ext, _, _ = extended.shape
+    key_n = key_mask.shape[-1]
+    query_n = TH * width
+    q_spec = pl.BlockSpec(
+        (1, TH, width, HDIM), lambda h, b: (b // row_tiles, b % row_tiles, 0, h)
     )
-    seen = key_valid[None, :]
-    scale = 1.0 / jnp.sqrt(jnp.float32(HDIM))
-
-    def per_head(inputs):
-        query_one, key_one, value_one, reach = inputs
-        allowed = (apart_t <= reach[0]) & (apart_h <= reach[1]) & (apart_w <= reach[2]) & seen
-        scores = (
-            jnp.einsum("qd,kd->qk", query_one, key_one, preferred_element_type=jnp.float32) * scale
-        )
-        terms = jnp.where(allowed, jnp.exp(scores), jnp.float32(0.0))
-        total = jnp.sum(terms, axis=-1, keepdims=True)
-        total = jnp.where(query_valid[:, None], total, jnp.float32(1.0))
-        weights = (terms / total).astype(jnp.bfloat16)
-        result = jnp.dot(weights, value_one, preferred_element_type=jnp.float32)
-        return jnp.where(query_valid[:, None], result, jnp.float32(0.0)).astype(jnp.bfloat16)
-
-    heads_out = lax.map(per_head, (query_heads, key_heads, value_heads, window))
-    attended = jnp.transpose(heads_out, (1, 0, 2)).reshape(frame_count, row_count, width, inner)
-    return attended
+    return pl.pallas_call(
+        attention_kernel,
+        grid=(heads, blocks),
+        in_specs=[
+            q_spec,
+            pl.BlockSpec((1, frames_ext, rows_ext, width, HDIM), lambda h, b: (0, 0, 0, 0, h)),
+            pl.BlockSpec((1, frames_ext, rows_ext, width, HDIM), lambda h, b: (1, 0, 0, 0, h)),
+            pl.BlockSpec((1, 1, 1, key_n), lambda h, b: (h, b, 0, 0)),
+            pl.BlockSpec((1, query_n, 1), lambda h, b: (h, 0, 0)),
+            pl.BlockSpec((1, query_n, 1), lambda h, b: (h, 0, 0)),
+            pl.BlockSpec((1, key_n), lambda h, b: (0, 0)),
+            pl.BlockSpec((1, query_n, 1), lambda h, b: (b, 0, 0)),
+        ],
+        out_specs=q_spec,
+        out_shape=jax.ShapeDtypeStruct(query.shape, jnp.bfloat16),
+    )(query, extended, extended, key_mask, query_lo, query_hi, key_cols, query_ok)
 
 
 def solution(mesh):

time: 615 us -> 476 us (0.77)
  matrix products: 157 us -> 25.5 us
  local copies, waits for them, and re-layouts: 96.4 us -> 40.1 us
  Pallas kernels: 0 us -> 53.1 us
  waiting for transfers between devices: 288 us -> 272 us
  other arithmetic: 35.9 us -> 50.5 us
    dot_general x24 -> x0, matrix products: 134 us -> none  [the longest x12 107 us: per_head(): jnp.einsum('qd,kd->qk', query_one, key_one, preferred_element_type=jnp.fl...]
    pallas_call x0 -> x1, Pallas kernels: none -> 53.1 us  [tile_attention(): pl.pallas_call(attention_kernel, grid=(heads, blocks), in_specs=[q_spec,...]
    squeeze x2 -> x0, local copies, waits for them, and re-layouts: 30.1 us -> none  [the longest x1 15.1 us: per_device(): key_heads = jnp.transpose(extended[0], (1, 0, 2))]
    unnamed x34 -> x26, local copies, waits for them, and re-layouts: 21.7 us -> 1.33 us
    slice x14 -> x1, local copies, waits for them, and re-layouts: 18.1 us -> 0.06 us  [per_device(): key_valid[f:f + span_t, TH * rt:TH * rt + span_h].reshape(-1)]
    ppermute x2, waiting for transfers between devices: 88.7 us -> 72 us  [with_halo(): lax.ppermute(tail, axis, [(i, (i + 1) % count) for i in range(ends)])]
    mul x3 -> x6, local copies, waits for them, and re-layouts: 9.66 us -> 19.2 us  [head_norm(): return (values * lax.rsqrt(power + EPS) * gain).astype(jnp.bfloat16)]
  transfers between devices with their start and end apart: 6 -> 6, of which waited for: 6 -> 6; matrix products, arithmetic and copies ran while one was open for 4% -> 8% of each run, Pallas kernels for 0% -> 0%
where the time goes in v2:
time: 476 us; the launch traced here: 472 us
  waiting for transfers between devices  272 us (57%)
  Pallas kernels  53.1 us (11%)
  other arithmetic  50.5 us (11%)
  local copies, waits for them, and re-layouts  40.1 us (8%)
  matrix products  25.5 us (5%)
  starting transfers between devices  17.3 us (4%)
  between operations  13.7 us (3%)
    all_gather x1, waiting for transfers between devices, per_device(): full_weight = lax.all_gather(band_weight, 'tm', axis=0, tiled=True)  151 us
    ppermute x2, waiting for transfers between devices, with_halo(): lax.ppermute(tail, axis, [(i, (i + 1) % count) for i in range(ends)])  72 us
    pallas_call x1, Pallas kernels, tile_attention(): pl.pallas_call(attention_kernel, grid=(heads, blocks), in_specs=[q_spec,...  53.1 us
    all_gather x1, waiting for transfers between devices, per_device(): band_weight = lax.all_gather(w_qkv, 'height', axis=0, tiled=True)  44.5 us
    dot_general x1, matrix products, per_device(): qkv = jnp.dot(modulated, full_weight, preferred_element_type=jnp.float32)  25.5 us
    mul x6, local copies, waits for them, and re-layouts, head_norm(): return (values * lax.rsqrt(power + EPS) * gain).astype(jnp.bfloat16)  19.2 us
    ppermute x2, starting transfers between devices, with_halo(): lax.ppermute(head, axis, [((i + 1) % count, i) for i in range(ends)])  11.7 us
    concatenate x2, other arithmetic, with_halo(): jnp.concatenate([lax.ppermute(tail, axis, [(i, (i + 1) % count) for i in...  11.6 us
  transfers between devices with their start and end apart: 6, of which 6 were waited for; matrix products, arithmetic and copies ran while one was open for 8% of the time, Pallas kernels for 0%

profile of v2, /device:TPU:6, one launch (start us, length us, event | category | flops | bytes accessed | tf_op | source)
XLA Modules:
  0.0 471.8 jit_solution(7120424117115140677)
XLA Ops:
  7.3 44.5 %all-gather.3.cloned.1.call-done = bf16[192,4608]{1,0:T(8,128)(2,1)} async-done(((bf16[24,4608]{1,0:T(8,128)(2,1)}), bf16[192,4608]{1,0:T(8,128)(2,1)}) %all-gather.3.cloned.1.call-update) | async-done | bytes 1769488 | tf_op jit(solution)/shard_map/all_gather | solution.py:62
  51.9 2.7 convert_reduce_fusion
  54.7 3.3 multiply_reduce_fusion
  58.1 5.0 %fusion.3 = bf16[640,3072]{1,0:T(8,128)(2,1)} fusion(bf16[2,4,80,3072]{3,2,1,0:T(8,128)(2,1)} %param.8, f32[3072]{0:T(1024)S(1)} %copy-done.10, f32[3072]{0:T(1024)S(1)} %broadcast_add_fusion.1, f32[640]{0:T(1024)S(1)} %rsqrt.28, f32[640]{0:T(1024)S(1)} %div.33), kind=kLoop, calls=%fused_computation.6 | loop fusion | flops 11796480 | bytes 7894016 | tf_op jit(solution)/shard_map/convert_element_type | solution.py:41
  63.1 151.4 %all-gather.5.cloned.1.call-done = bf16[3072,4608]{1,0:T(8,128)(2,1)} async-done(((bf16[192,4608]{1,0:T(8,128)(2,1)}), bf16[3072,4608]{1,0:T(8,128)(2,1)}) %all-gather.5.cloned.1.call-update) | async-done | bytes 28311568 | tf_op jit(solution)/shard_map/all_gather | solution.py:63
  214.5 25.5 %fusion.8 = f32[640,4608]{1,0:T(8,128)} fusion(bf16[640,3072]{1,0:T(8,128)(2,1)} %fusion.3, bf16[3072,4608]{1,0:T(8,128)(2,1)} %all-gather.5.cloned.1.call-done), kind=kOutput, calls=%fused_computation.52 | convolution fusion | flops 18119393280 | bytes 44040192 | tf_op jit(solution)/shard_map/dot_general | solution.py:64
  240.0 10.0 %slice_multiply_fusion = (f32[640,1536]{1,0:T(8,128)}, f32[640,1536]{1,0:T(8,128)}, f32[640,1536]{1,0:T(8,128)}, f32[640,1536]{1,0:T(8,128)}) fusion(f32[640,4608]{1,0:T(8,128)} %fusion.8), kind=kLoop, calls=%fused_computation.49 | loop fusion | flops 1966080 | bytes 23592960 | tf_op jit(solution)/shard_map/mul | solution.py:45
  252.4 5.5 %copy.21 = f32[640,1536]{0,1:T(8,128)} copy(f32[640,1536]{1,0:T(8,128)} %get-tuple-element.5) | data formatting | bytes 7864320 | tf_op jit(solution)/shard_map/mul | solution.py:45
  257.8 2.3 reduce_sum.39
  260.4 4.0 mul.114
  264.4 5.5 %mul.115 = f32[1,2,1,2,2,80,1536]{6,5,4,3,1,2,0:T(8,128)} reshape(f32[640,12,128]{2,1,0:T(8,128)} %mul.114) | data formatting | bytes 7864320 | tf_op jit(solution)/shard_map/mul | solution.py:46
  270.0 4.3 multiply_convert_fusion
  276.8 7.2 %collective-permute-start.1 = (bf16[2,1,1,2,2,80,1536]{6,5,4,3,1,2,0:T(8,128)(2,1)S(1)}, bf16[2,1,1,2,2,80,1536]{6,5,4,3,1,2,0:T(8,128)(2,1)S(1)}, u32[]{:S(2)}, u32[]{:S(2)}) collective-permute-start(bf16[2,1,1,2,2,80,1536]{6,5,4,3,1,2,0:T(8,128)(2,1)S(1)} %get-tuple-element.12), channel_id=1, source_target_pairs={{8,0},{16,8},{24,16},{32,24},{40,32},{48,40},{56,48},{64,56},{72,6... | collective-permute-start | bytes 5898248 | tf_op jit(solution)/shard_map/ppermute | solution.py:28
  284.0 20.2 %collective-permute-done = bf16[2,1,1,2,2,80,1536]{6,5,4,3,1,2,0:T(8,128)(2,1)S(1)} collective-permute-done((bf16[2,1,1,2,2,80,1536]{6,5,4,3,1,2,0:T(8,128)(2,1)S(1)}, bf16[2,1,1,2,2,80,1536]{6,5,4,3,1,2,0:T(8,128)(2,1)S(1)}, u32[]{:S(2)}, u32[]{:S(2)}) %collective-permute-start) | collective-permute-done | bytes 1966112 | tf_op jit(solution)/shard_map/ppermute | solution.py:26
  308.3 3.5 fusion.7
  311.8 3.5 collective-permute-start.2
  315.3 4.5 collective-permute-start.3
  325.0 5.5 %copy.19 = f32[640,1536]{0,1:T(8,128)} copy(f32[640,1536]{1,0:T(8,128)} %get-tuple-element.6) | data formatting | bytes 7864320 | tf_op jit(solution)/shard_map/mul | solution.py:45
  333.0 4.0 mul.105
  337.0 5.5 %mul.106 = f32[2,4,80,1536]{3,2,1,0:T(8,128)} reshape(f32[640,12,128]{2,1,0:T(8,128)} %mul.105) | data formatting | bytes 7864320 | tf_op jit(solution)/shard_map/mul | solution.py:46
  342.6 5.7 %multiply_convert_fusion.1.q_ref = bf16[2,4,80,1536]{3,2,1,0:T(8,128)(2,1)} fusion(f32[2,4,80,1536]{3,2,1,0:T(8,128)} %bitcast.33, f32[2,4,80,1536]{3,2,1,0:T(8,128)} %mul.106, f32[1536]{0:T(1024)S(1)} %broadcast_bitcast_fusion.1), kind=kLoop, calls=%fused_computation.13 | loop fusion | flops 2949120 | bytes 9836544 | tf_op jit(solution)/shard_map/convert_element_type | solution.py:46
  348.3 51.8 %collective-permute-done.2 = bf16[2,4,1,1,2,80,1536]{6,5,4,3,1,2,0:T(8,128)(2,1)} collective-permute-done((bf16[2,4,1,1,2,80,1536]{6,5,4,3,1,2,0:T(8,128)(2,1)}, bf16[2,4,1,1,2,80,1536]{6,5,4,3,1,2,0:T(8,128)(2,1)}, u32[]{:S(2)}, u32[]{:S(2)}) %collective-permute-start.2) | collective-permute-done | bytes 3932192 | tf_op jit(solution)/shard_map/ppermute | solution.py:26
  401.3 10.5 %pad_maximum_fusion = bf16[2,4,1,4,2,80,1536]{6,5,4,3,1,2,0:T(8,128)(2,1)} fusion(bf16[2,4,1,1,2,80,1536]{6,5,4,3,1,2,0:T(8,128)(2,1)} %collective-permute-done.3, bf16[2,1,1,2,2,80,1536]{6,5,4,3,1,2,0:T(8,128)(2,1)S(1)} %copy-done.7, bf16[1,2,1,2,2,80,1536]{6,5,4,3,1,2,0:T(8,128)(2,1)S(1)} %bitcast.32, bf16[1,2,1,2,2,80,1536]{6,5,4,3,1,2,0:T(8,128)(2,1)S(1)} %copy-done.3, ...), kind=kLoop, calls=%fused_computation | loop fusion | flops 39321600 | bytes 31457280 | tf_op jit(solution)/shard_map/concatenate | solution.py:24
  411.8 53.1 %shard_map.82 = bf16[2,4,80,1536]{3,2,1,0:T(8,128)(2,1)} custom-call(bf16[2,4,80,1536]{3,2,1,0:T(8,128)(2,1)} %multiply_convert_fusion.1.q_ref, bf16[2,4,8,80,1536]{4,3,2,1,0:T(8,128)(2,1)} %bitcast.28, bf16[2,4,8,80,1536]{4,3,2,1,0:T(8,128)(2,1)} %bitcast.29, f32[12,4,1,1440]{3,2,1,0:T(1,128)} %and_convert_fusion.km_ref, ...), custom_call_target="tpu_custom_call" | custom-call | tf_op jit(solution)/shard_map/pallas_call | solution.py:157
  (71 shorter events, 18.9 us)
Async XLA Ops:
  6.5 51.5 %copy-start = (f32[128]{0:T(128)S(1)}, f32[128]{0:T(128)}, u32[]{:S(2)}) copy-start(f32[128]{0:T(128)} %param.13) | copy-start | bytes 1540
  6.5 45.3 %all-gather.3.cloned.1.call-start = ((), (), s32[]{:S(2)}) async-start(), calls=%async_computation | async-start | bytes 1990656 | tf_op jit(solution)/shard_map/all_gather | solution.py:62
  7.3 207.3 %all-gather.5.cloned.1.call-start = ((), (), s32[]{:S(2)}) async-start(), calls=%async_computation.1 | async-start | bytes 30081024 | tf_op jit(solution)/shard_map/all_gather | solution.py:63
  51.8 6.3 %copy-start.9 = (f32[3072]{0:T(1024)S(1)}, f32[3072]{0:T(1024)}, u32[]{:S(2)}) copy-start(f32[3072]{0:T(1024)} %param.9) | copy-start | bytes 36868
  51.8 6.3 %copy-start.10 = (f32[3072]{0:T(1024)S(1)}, f32[3072]{0:T(1024)}, u32[]{:S(2)}) copy-start(f32[3072]{0:T(1024)} %param.10) | copy-start | bytes 36868
  274.2 31.7 %copy-start.2 = (bf16[1,2,1,2,2,80,1536]{6,5,4,3,1,2,0:T(8,128)(2,1)}, bf16[1,2,1,2,2,80,1536]{6,5,4,3,1,2,0:T(8,128)(2,1)S(1)}, u32[]{:S(2)}) copy-start(bf16[1,2,1,2,2,80,1536]{6,5,4,3,1,2,0:T(8,128)(2,1)S(1)} %multiply_convert_fusion) | copy-start | bytes 5898244
  274.6 29.6 %collective-permute-start = (bf16[2,1,1,2,2,80,1536]{6,5,4,3,1,2,0:T(8,128)(2,1)S(1)}, bf16[2,1,1,2,2,80,1536]{6,5,4,3,1,2,0:T(8,128)(2,1)S(1)}, u32[]{:S(2)}, u32[]{:S(2)}) collective-permute-start(bf16[2,1,1,2,2,80,1536]{6,5,4,3,1,2,0:T(8,128)(2,1)S(1)} %get-tuple-element.11), channel_id=1, source_target_pairs={{0,8},{8,16},{16,24},{24,32},{32,40},{40,48},{48,56},{56,64},{64,7... | collective-permute-start | bytes 5898248 | tf_op jit(solution)/shard_map/ppermute | solution.py:26
  276.8 29.1 %collective-permute-start.1 = (bf16[2,1,1,2,2,80,1536]{6,5,4,3,1,2,0:T(8,128)(2,1)S(1)}, bf16[2,1,1,2,2,80,1536]{6,5,4,3,1,2,0:T(8,128)(2,1)S(1)}, u32[]{:S(2)}, u32[]{:S(2)}) collective-permute-start(bf16[2,1,1,2,2,80,1536]{6,5,4,3,1,2,0:T(8,128)(2,1)S(1)} %get-tuple-element.12), channel_id=1, source_target_pairs={{8,0},{16,8},{24,16},{32,24},{40,32},{48,40},{56,48},{64,56},{72,6... | collective-permute-start | bytes 5898248 | tf_op jit(solution)/shard_map/ppermute | solution.py:28
  304.2 1.8 copy-start.4
  306.0 1.3 copy-start.6
  308.3 11.5 %copy-start.8 = (s32[32,32,80]{2,1,0:T(8,128)S(1)}, s32[32,32,80]{2,1,0:T(8,128)}, u32[]{:S(2)}) copy-start(s32[32,32,80]{2,1,0:T(8,128)} %param.15) | copy-start | bytes 983044
  308.3 11.9 %copy-start.11 = (s32[12,3]{0,1:T(4,128)S(1)}, s32[12,3]{0,1:T(4,128)}, u32[]{:S(2)}) copy-start(s32[12,3]{0,1:T(4,128)} %param.14) | copy-start | bytes 436
  308.3 14.2 %copy-start.12 = (f32[128]{0:T(128)S(1)}, f32[128]{0:T(128)}, u32[]{:S(2)}) copy-start(f32[128]{0:T(128)} %param.12) | copy-start | bytes 1540
  311.8 88.3 %collective-permute-start.2 = (bf16[2,4,1,1,2,80,1536]{6,5,4,3,1,2,0:T(8,128)(2,1)}, bf16[2,4,1,1,2,80,1536]{6,5,4,3,1,2,0:T(8,128)(2,1)}, u32[]{:S(2)}, u32[]{:S(2)}) collective-permute-start(bf16[2,4,1,1,2,80,1536]{6,5,4,3,1,2,0:T(8,128)(2,1)} %get-tuple-element.9), channel_id=1, source_target_pairs={{0,1},{1,2},{2,3},{3,4},{4,5},{5,6},{6,7},{8,9},{9,10},{10,11},{11... | collective-permute-start | bytes 11796488 | tf_op jit(solution)/shard_map/ppermute | solution.py:26
  315.3 86.0 %collective-permute-start.3 = (bf16[2,4,1,1,2,80,1536]{6,5,4,3,1,2,0:T(8,128)(2,1)}, bf16[2,4,1,1,2,80,1536]{6,5,4,3,1,2,0:T(8,128)(2,1)}, u32[]{:S(2)}, u32[]{:S(2)}) collective-permute-start(bf16[2,4,1,1,2,80,1536]{6,5,4,3,1,2,0:T(8,128)(2,1)} %get-tuple-element.10), channel_id=1, source_target_pairs={{1,0},{2,1},{3,2},{4,3},{5,4},{6,5},{7,6},{9,8},{10,9},{11,10},{12... | collective-permute-start | bytes 11796488 | tf_op jit(solution)/shard_map/ppermute | solution.py:28
  342.6 58.7 %copy-start.3 = (bf16[1,2,1,2,2,80,1536]{6,5,4,3,1,2,0:T(8,128)(2,1)S(1)}, bf16[1,2,1,2,2,80,1536]{6,5,4,3,1,2,0:T(8,128)(2,1)}, u32[]{:S(2)}) copy-start(bf16[1,2,1,2,2,80,1536]{6,5,4,3,1,2,0:T(8,128)(2,1)} %copy-done.2) | copy-start | bytes 5898244
  342.6 58.7 %copy-start.5 = (bf16[2,1,1,2,2,80,1536]{6,5,4,3,1,2,0:T(8,128)(2,1)S(1)}, bf16[2,1,1,2,2,80,1536]{6,5,4,3,1,2,0:T(8,128)(2,1)}, u32[]{:S(2)}) copy-start(bf16[2,1,1,2,2,80,1536]{6,5,4,3,1,2,0:T(8,128)(2,1)} %copy-done.4) | copy-start | bytes 5898244
  342.6 58.7 %copy-start.7 = (bf16[2,1,1,2,2,80,1536]{6,5,4,3,1,2,0:T(8,128)(2,1)S(1)}, bf16[2,1,1,2,2,80,1536]{6,5,4,3,1,2,0:T(8,128)(2,1)}, u32[]{:S(2)}) copy-start(bf16[2,1,1,2,2,80,1536]{6,5,4,3,1,2,0:T(8,128)(2,1)} %copy-done.6) | copy-start | bytes 5898244
  411.8 53.1 %copy-start.1 = (f32[128]{0:T(128)S(1)}, f32[128]{0:T(128)}, u32[]{:S(2)}) copy-start(f32[128]{0:T(128)} %param.13) | copy-start | bytes 1540
Sparse Core Ops, SparseCore 0:
  9.0 42.7 all-gather.2
  54.3 160.2 all-gather.4

commit v3 on v2

--- a/solution.py
+++ b/solution.py
@@ -1,3 +1,5 @@
+import functools
+
 import jax
 import jax.numpy as jnp
 from jax import lax
@@ -10,6 +12,7 @@
 TT = 1
 TH = 2
 TW = 8
+GROUPS = 2
 
 
 EPS = 1e-06
@@ -61,17 +64,20 @@
     modulated = modulate(tokens.reshape(token_count, features), mod_scale, mod_shift)
     band_weight = lax.all_gather(w_qkv, "height", axis=0, tiled=True)
     full_weight = lax.all_gather(band_weight, "tm", axis=0, tiled=True)
-    qkv = jnp.dot(modulated, full_weight, preferred_element_type=jnp.float32)
-    inner = qkv.shape[1] // 3
-    query = head_norm(qkv[:, :inner].reshape(token_count, HEADS, HDIM), q_gain)
-    key = head_norm(qkv[:, inner : 2 * inner].reshape(token_count, HEADS, HDIM), k_gain)
-    value = qkv[:, 2 * inner :].astype(jnp.bfloat16)
-    tiled = (frame_count // TT, TT, row_count // TH, TH, width, inner)
-    stacked = jnp.stack([key.reshape(tiled), value.reshape(tiled)])
-    extended = with_halo(stacked, (("tm", 1), ("height", 3)), 1)
+    inner = full_weight.shape[1] // 3
+    group_cols = inner // GROUPS
+    tiled = (frame_count // TT, TT, row_count // TH, TH, width, group_cols)
+    groups = []
+    for group in range(GROUPS):
+        start = group * group_cols
+        key = project(modulated, full_weight, inner + start, group_cols, k_gain)
+        value = project(modulated, full_weight, 2 * inner + start, group_cols, None)
+        stacked = jnp.stack([key.reshape(tiled), value.reshape(tiled)])
+        groups.append(with_halo(stacked, (("tm", 1), ("height", 3)), 1))
+    query = project(modulated, full_weight, 0, inner, q_gain)
     frames_ext = frame_count + 2 * TT
     rows_ext = row_count + 2 * TH
-    extended = extended.reshape(2, frames_ext, rows_ext, width, inner)
+    groups = [g.reshape(2, frames_ext, rows_ext, width, group_cols) for g in groups]
     frame_block = lax.axis_index("tm")
     row_block = lax.axis_index("height")
     first_frame = frame_block * frame_count
@@ -111,7 +117,12 @@
     query_hi = (query_cols[None, :] + window[:, 2, None]).reshape(HEADS, query_n, 1)
     query_ok = query_valid.reshape(blocks, query_n, 1).astype(jnp.float32)
     query_grid = query.reshape(frame_count, row_count, width, inner)
-    return tile_attention(query_grid, extended, key_mask, query_lo, query_hi, key_cols, query_ok)
+    out = None
+    for group, extended in enumerate(groups):
+        out = tile_attention(
+            query_grid, extended, key_mask, query_lo, query_hi, key_cols, query_ok, group, out
+        )
+    return out
 
 
 def attention_kernel(q_ref, k_ref, v_ref, km_ref, lo_ref, hi_ref, kc_ref, qv_ref, o_ref):
@@ -142,9 +153,10 @@
 ROW_TILES = 2
 
 
-def tile_attention(query, extended, key_mask, query_lo, query_hi, key_cols, query_ok):
+def tile_attention(query, extended, key_mask, query_lo, query_hi, key_cols, query_ok, group, out):
     frames, rows, width, inner = query.shape
-    heads = inner // HDIM
+    heads = extended.shape[-1] // HDIM
+    first = group * heads
     row_tiles = rows // TH
     assert row_tiles == ROW_TILES
     blocks = frames * row_tiles
@@ -152,24 +164,66 @@
     key_n = key_mask.shape[-1]
     query_n = TH * width
     q_spec = pl.BlockSpec(
-        (1, TH, width, HDIM), lambda h, b: (b // row_tiles, b % row_tiles, 0, h)
-    )
+        (1, TH, width, HDIM), lambda h, b: (b // row_tiles, b % row_tiles, 0, first + h)
+    )
+    in_specs = [
+        q_spec,
+        pl.BlockSpec((1, frames_ext, rows_ext, width, HDIM), lambda h, b: (0, 0, 0, 0, h)),
+        pl.BlockSpec((1, frames_ext, rows_ext, width, HDIM), lambda h, b: (1, 0, 0, 0, h)),
+        pl.BlockSpec((1, 1, 1, key_n), lambda h, b: (first + h, b, 0, 0)),
+        pl.BlockSpec((1, query_n, 1), lambda h, b: (first + h, 0, 0)),
+        pl.BlockSpec((1, query_n, 1), lambda h, b: (first + h, 0, 0)),
+        pl.BlockSpec((1, key_n), lambda h, b: (0, 0)),
+        pl.BlockSpec((1, query_n, 1), lambda h, b: (b, 0, 0)),
+    ]
+    operands = [query, extended, extended, key_mask, query_lo, query_hi, key_cols, query_ok]
+    aliases = {}
+    kernel = attention_kernel
+    if out is not None:
+        in_specs.append(pl.BlockSpec(memory_space=pl.ANY))
+        operands.append(out)
+        aliases = {len(operands) - 1: 0}
+        kernel = lambda *refs: attention_kernel(*refs[:8], refs[9])
     return pl.pallas_call(
-        attention_kernel,
+        kernel,
         grid=(heads, blocks),
-        in_specs=[
-            q_spec,
-            pl.BlockSpec((1, frames_ext, rows_ext, width, HDIM), lambda h, b: (0, 0, 0, 0, h)),
-            pl.BlockSpec((1, frames_ext, rows_ext, width, HDIM), lambda h, b: (1, 0, 0, 0, h)),
-            pl.BlockSpec((1, 1, 1, key_n), lambda h, b: (h, b, 0, 0)),
-            pl.BlockSpec((1, query_n, 1), lambda h, b: (h, 0, 0)),
-            pl.BlockSpec((1, query_n, 1), lambda h, b: (h, 0, 0)),
-            pl.BlockSpec((1, key_n), lambda h, b: (0, 0)),
-            pl.BlockSpec((1, query_n, 1), lambda h, b: (b, 0, 0)),
-        ],
+        in_specs=in_specs,
         out_specs=q_spec,
         out_shape=jax.ShapeDtypeStruct(query.shape, jnp.bfloat16),
-    )(query, extended, extended, key_mask, query_lo, query_hi, key_cols, query_ok)
+        input_output_aliases=aliases,
+    )(*operands)
+
+
+PROJECT_COLS = 256
+
+
+def projection_kernel(x_ref, w_ref, g_ref, o_ref, *, normalize):
+    acc = jnp.dot(x_ref[...], w_ref[...], preferred_element_type=jnp.float32)
+    for part in range(acc.shape[1] // HDIM):
+        piece = acc[:, part * HDIM : (part + 1) * HDIM]
+        if normalize:
+            power = jnp.mean(piece * piece, axis=-1, keepdims=True)
+            piece = piece * lax.rsqrt(power + EPS) * g_ref[...]
+        o_ref[:, part * HDIM : (part + 1) * HDIM] = piece.astype(o_ref.dtype)
+
+
+def project(x, w, start, count, gain):
+    tokens, features = x.shape
+    cols = PROJECT_COLS
+    normalize = gain is not None
+    gain = gain.reshape(1, HDIM) if normalize else jnp.ones((1, HDIM), jnp.float32)
+    first = start // cols
+    return pl.pallas_call(
+        functools.partial(projection_kernel, normalize=normalize),
+        grid=(count // cols,),
+        in_specs=[
+            pl.BlockSpec((tokens, features), lambda j: (0, 0)),
+            pl.BlockSpec((features, cols), lambda j: (0, first + j)),
+            pl.BlockSpec((1, HDIM), lambda j: (0, 0)),
+        ],
+        out_specs=pl.BlockSpec((tokens, cols), lambda j: (0, j)),
+        out_shape=jax.ShapeDtypeStruct((tokens, count), jnp.bfloat16),
+    )(x, w, gain)
 
 
 def solution(mesh):

time: 476 us -> 410 us (0.86)
  waiting for transfers between devices: 272 us -> 218 us
  Pallas kernels: 53.1 us -> 96.2 us
  local copies, waits for them, and re-layouts: 40.1 us -> 8.56 us
  matrix products: 25.5 us -> 0 us
  starting transfers between devices: 17.3 us -> 36.6 us
  other arithmetic: 50.5 us -> 35.9 us
    ppermute x2 -> x4, waiting for transfers between devices: 72 us -> 20 us  [with_halo(): lax.ppermute(tail, axis, [(i, (i + 1) % count) for i in range(ends)])]
    pallas_call x1 -> x7, Pallas kernels: 53.1 us -> 96.2 us  [the longest x2 55 us: tile_attention(): pl.pallas_call(kernel, grid=(heads, blocks), in_specs=in_specs, out_specs...]
    mul x8 -> x0, local copies, waits for them, and re-layouts: 30.1 us -> none  [the longest x6 19.2 us: head_norm(): return (values * lax.rsqrt(power + EPS) * gain).astype(jnp.bfloat16)]
    dot_general x1 -> x0, matrix products: 25.5 us -> none  [per_device(): qkv = jnp.dot(modulated, full_weight, preferred_element_type=jnp.float32)]
    ppermute x2 -> x4, starting transfers between devices: 11.7 us -> 27.1 us  [with_halo(): lax.ppermute(head, axis, [((i + 1) % count, i) for i in range(ends)])]
    mul x1 -> x0, other arithmetic: 9.98 us -> none  [head_norm(): power = jnp.mean(values * values, axis=-1, keepdims=True)]
    convert_element_type x2 -> x0, other arithmetic: 9.98 us -> none  [head_norm(): return (values * lax.rsqrt(power + EPS) * gain).astype(jnp.bfloat16)]
    concatenate x2 -> x4, other arithmetic: 11.6 us -> 16.8 us  [with_halo(): jnp.concatenate([lax.ppermute(tail, axis, [(i, (i + 1) % count) for i in...]
  transfers between devices with their start and end apart: 6 -> 10, of which waited for: 6 -> 4; matrix products, arithmetic and copies ran while one was open for 8% -> 9% of each run, Pallas kernels for 0% -> 13%
where the time goes in v3:
time: 410 us; the launch traced here: 409 us
  waiting for transfers between devices  218 us (53%)
  Pallas kernels  96.2 us (23%)
  starting transfers between devices  36.6 us (9%)
  other arithmetic  35.9 us (9%)
  between operations  13.7 us (3%)
  local copies, waits for them, and re-layouts  8.56 us (2%)
    all_gather x1, waiting for transfers between devices, per_device(): full_weight = lax.all_gather(band_weight, 'tm', axis=0, tiled=True)  151 us
    pallas_call x2, Pallas kernels, tile_attention(): pl.pallas_call(kernel, grid=(heads, blocks), in_specs=in_specs, out_specs...  55 us
    all_gather x1, waiting for transfers between devices, per_device(): band_weight = lax.all_gather(w_qkv, 'height', axis=0, tiled=True)  44.5 us
    pallas_call x5, Pallas kernels, project(): pl.pallas_call(functools.partial(projection_kernel, normalize=normalize),...  41.3 us
    ppermute x4, starting transfers between devices, with_halo(): lax.ppermute(head, axis, [((i + 1) % count, i) for i in range(ends)])  27.1 us
    ppermute x4, waiting for transfers between devices, with_halo(): lax.ppermute(tail, axis, [(i, (i + 1) % count) for i in range(ends)])  20 us
    concatenate x4, other arithmetic, with_halo(): jnp.concatenate([lax.ppermute(tail, axis, [(i, (i + 1) % count) for i in...  16.8 us
    ppermute x4, starting transfers between devices, with_halo(): lax.ppermute(tail, axis, [(i, (i + 1) % count) for i in range(ends)])  9.44 us
  transfers between devices with their start and end apart: 10, of which 4 were waited for; matrix products, arithmetic and copies ran while one was open for 9% of the time, Pallas kernels for 13%

profile of v3, /device:TPU:6, one launch (start us, length us, event | category | flops | bytes accessed | tf_op | source)
XLA Modules:
  0.0 408.9 jit_solution(878878404556433286)
XLA Ops:
  7.3 44.5 %all-gather.3.cloned.1.call-done = bf16[192,4608]{1,0:T(8,128)(2,1)} async-done(((bf16[24,4608]{1,0:T(8,128)(2,1)}), bf16[192,4608]{1,0:T(8,128)(2,1)}) %all-gather.3.cloned.1.call-update) | async-done | bytes 1769488 | tf_op jit(solution)/shard_map/all_gather | solution.py:65
  51.9 2.7 convert_reduce_fusion
  54.7 3.3 multiply_reduce_fusion
  58.6 4.9 %fusion.3.x_ref = bf16[640,3072]{1,0:T(8,128)(2,1)} fusion(bf16[2,4,80,3072]{3,2,1,0:T(8,128)(2,1)} %param.8, f32[3072]{0:T(1024)S(1)} %copy-done.6, f32[3072]{0:T(1024)S(1)} %broadcast_add_fusion.1, f32[640]{0:T(1024)S(1)} %rsqrt.12, f32[640]{0:T(1024)S(1)} %div.29), kind=kLoop, calls=%fused_computation.6 | loop fusion | flops 11796480 | bytes 7894016 | tf_op jit(solution)/shard_map/convert_element_type | solution.py:44
  63.5 151.0 %all-gather.5.cloned.1.call-done.w_ref = bf16[3072,4608]{1,0:T(8,128)(2,1)} async-done(((bf16[192,4608]{1,0:T(8,128)(2,1)}), bf16[3072,4608]{1,0:T(8,128)(2,1)}) %all-gather.5.cloned.1.call-update) | async-done | bytes 28311568 | tf_op jit(solution)/shard_map/all_gather | solution.py:66
  215.0 7.2 %shard_map.86 = bf16[640,768]{1,0:T(8,128)(2,1)} custom-call(bf16[640,3072]{1,0:T(8,128)(2,1)} %fusion.3.x_ref, bf16[3072,4608]{1,0:T(8,128)(2,1)} %all-gather.5.cloned.1.call-done.w_ref, f32[1,128]{1,0:T(1,128)} %broadcast_10_g_ref.2.g_ref), custom_call_target="tpu_custom_call" | custom-call | tf_op jit(solution)/shard_map/pallas_call | solution.py:216
  222.3 7.6 %shard_map.85 = bf16[640,768]{1,0:T(8,128)(2,1)} custom-call(bf16[640,3072]{1,0:T(8,128)(2,1)} %fusion.3.x_ref, bf16[3072,4608]{1,0:T(8,128)(2,1)} %all-gather.5.cloned.1.call-done.w_ref, f32[1,128]{1,0:T(1,128)} %bitcast.51), custom_call_target="tpu_custom_call" | custom-call | tf_op jit(solution)/shard_map/pallas_call | solution.py:216
  229.8 2.7 fusion.4
  234.7 7.0 %collective-permute-start.5 = (bf16[2,1,1,2,2,80,768]{6,5,4,3,1,0,2:T(8,128)(2,1)}, bf16[2,1,1,2,2,80,768]{6,5,4,3,1,0,2:T(8,128)(2,1)}, u32[]{:S(2)}, u32[]{:S(2)}) collective-permute-start(bf16[2,1,1,2,2,80,768]{6,5,4,3,1,0,2:T(8,128)(2,1)} %get-tuple-element.10), channel_id=1, source_target_pairs={{8,0},{16,8},{24,16},{32,24},{40,32},{48,40},{56,48},{64,56},{72,6... | collective-permute-start | bytes 2949128 | tf_op jit(solution)/shard_map/ppermute | solution.py:31
  241.9 7.3 %shard_map.84 = bf16[640,768]{1,0:T(8,128)(2,1)} custom-call(bf16[640,3072]{1,0:T(8,128)(2,1)} %fusion.3.x_ref, bf16[3072,4608]{1,0:T(8,128)(2,1)} %all-gather.5.cloned.1.call-done.w_ref, f32[1,128]{1,0:T(1,128)} %broadcast_10_g_ref.2.g_ref), custom_call_target="tpu_custom_call" | custom-call | tf_op jit(solution)/shard_map/pallas_call | solution.py:216
  249.2 7.5 %shard_map.83 = bf16[640,768]{1,0:T(8,128)(2,1)} custom-call(bf16[640,3072]{1,0:T(8,128)(2,1)} %fusion.3.x_ref, bf16[3072,4608]{1,0:T(8,128)(2,1)} %all-gather.5.cloned.1.call-done.w_ref, f32[1,128]{1,0:T(1,128)} %bitcast.52), custom_call_target="tpu_custom_call" | custom-call | tf_op jit(solution)/shard_map/pallas_call | solution.py:216
  256.8 2.7 fusion.5
  261.4 7.3 %collective-permute-start.1 = (bf16[2,1,1,2,2,80,768]{6,5,4,3,1,0,2:T(8,128)(2,1)}, bf16[2,1,1,2,2,80,768]{6,5,4,3,1,0,2:T(8,128)(2,1)}, u32[]{:S(2)}, u32[]{:S(2)}) collective-permute-start(bf16[2,1,1,2,2,80,768]{6,5,4,3,1,0,2:T(8,128)(2,1)} %get-tuple-element.12), channel_id=1, source_target_pairs={{8,0},{16,8},{24,16},{32,24},{40,32},{48,40},{56,48},{64,56},{72,6... | collective-permute-start | bytes 2949128 | tf_op jit(solution)/shard_map/ppermute | solution.py:31
  270.5 2.2 fusion.8
  272.7 3.5 collective-permute-start.6
  276.2 4.5 %collective-permute-start.7 = (bf16[2,4,1,1,2,80,768]{6,5,4,3,1,0,2:T(8,128)(2,1)}, bf16[2,4,1,1,2,80,768]{6,5,4,3,1,0,2:T(8,128)(2,1)}, u32[]{:S(2)}, u32[]{:S(2)}) collective-permute-start(bf16[2,4,1,1,2,80,768]{6,5,4,3,1,0,2:T(8,128)(2,1)} %get-tuple-element.6), channel_id=1, source_target_pairs={{1,0},{2,1},{3,2},{4,3},{5,4},{6,5},{7,6},{9,8},{10,9},{11,10},{12... | collective-permute-start | bytes 5898248 | tf_op jit(solution)/shard_map/ppermute | solution.py:31
  287.2 2.3 fusion.9
  291.4 8.4 %collective-permute-start.3 = (bf16[2,4,1,1,2,80,768]{6,5,4,3,1,0,2:T(8,128)(2,1)}, bf16[2,4,1,1,2,80,768]{6,5,4,3,1,0,2:T(8,128)(2,1)}, u32[]{:S(2)}, u32[]{:S(2)}) collective-permute-start(bf16[2,4,1,1,2,80,768]{6,5,4,3,1,0,2:T(8,128)(2,1)} %get-tuple-element.8), channel_id=1, source_target_pairs={{1,0},{2,1},{3,2},{4,3},{5,4},{6,5},{7,6},{9,8},{10,9},{11,10},{12... | collective-permute-start | bytes 5898248 | tf_op jit(solution)/shard_map/ppermute | solution.py:31
  302.3 11.7 %shard_map.82 = bf16[640,1536]{1,0:T(8,128)(2,1)} custom-call(bf16[640,3072]{1,0:T(8,128)(2,1)} %fusion.3.x_ref, bf16[3072,4608]{1,0:T(8,128)(2,1)} %all-gather.5.cloned.1.call-done.w_ref, f32[1,128]{1,0:T(1,128)} %bitcast.53), custom_call_target="tpu_custom_call" | custom-call | tf_op jit(solution)/shard_map/pallas_call | solution.py:216
  314.0 20.0 %collective-permute-done.6 = bf16[2,4,1,1,2,80,768]{6,5,4,3,1,0,2:T(8,128)(2,1)} collective-permute-done((bf16[2,4,1,1,2,80,768]{6,5,4,3,1,0,2:T(8,128)(2,1)}, bf16[2,4,1,1,2,80,768]{6,5,4,3,1,0,2:T(8,128)(2,1)}, u32[]{:S(2)}, u32[]{:S(2)}) %collective-permute-start.6) | collective-permute-done | bytes 1966112 | tf_op jit(solution)/shard_map/ppermute | solution.py:29
  334.0 6.5 %pad_maximum_fusion.1 = bf16[2,4,1,4,2,80,768]{6,5,4,3,1,0,2:T(8,128)(2,1)} fusion(bf16[2,4,1,1,2,80,768]{6,5,4,3,1,0,2:T(8,128)(2,1)} %collective-permute-done.7, bf16[2,1,1,2,2,80,768]{6,5,4,3,1,0,2:T(8,128)(2,1)} %collective-permute-done.5, bf16[1,2,1,2,2,80,768]{6,5,4,3,1,0,2:T(8,128)(2,1)S(1)} %bitcast.41, ...), kind=kLoop, calls=%fused_computation.1 | loop fusion | flops 19660800 | bytes 15728640 | tf_op jit(solution)/shard_map/concatenate | solution.py:27
  340.5 27.5 %shard_map.87.refs_8_ = bf16[2,4,80,1536]{3,2,1,0:T(8,128)(2,1)} custom-call(bf16[2,4,80,1536]{3,2,1,0:T(8,128)(2,1)} %bitcast.37, bf16[2,4,8,80,768]{4,3,2,1,0:T(8,128)(2,1)} %bitcast.33, bf16[2,4,8,80,768]{4,3,2,1,0:T(8,128)(2,1)} %bitcast.34, f32[12,4,1,1440]{3,2,1,0:T(1,128)} %and_convert_fusion.km_ref.refs_3_, ...), custom_call_target="tpu_custom_call" | custom-call | tf_op jit(solution)/shard_map/pallas_call | solution.py:187
  368.0 6.5 %pad_maximum_fusion = bf16[2,4,1,4,2,80,768]{6,5,4,3,1,0,2:T(8,128)(2,1)} fusion(bf16[2,4,1,1,2,80,768]{6,5,4,3,1,0,2:T(8,128)(2,1)} %collective-permute-done.3, bf16[2,1,1,2,2,80,768]{6,5,4,3,1,0,2:T(8,128)(2,1)} %collective-permute-done.1, bf16[1,2,1,2,2,80,768]{6,5,4,3,1,0,2:T(8,128)(2,1)S(1)} %bitcast.47, ...), kind=kLoop, calls=%fused_computation | loop fusion | flops 19660800 | bytes 15728640 | tf_op jit(solution)/shard_map/concatenate | solution.py:27
  374.5 27.5 %shard_map.88 = bf16[2,4,80,1536]{3,2,1,0:T(8,128)(2,1)} custom-call(bf16[2,4,80,1536]{3,2,1,0:T(8,128)(2,1)} %bitcast.38, bf16[2,4,8,80,768]{4,3,2,1,0:T(8,128)(2,1)} %bitcast.35, bf16[2,4,8,80,768]{4,3,2,1,0:T(8,128)(2,1)} %bitcast.36, f32[12,4,1,1440]{3,2,1,0:T(1,128)} %and_convert_fusion.km_ref.refs_3_, ...), custom_call_target="tpu_custom_call", output_to_operand_aliasing={{}: (8, {})} | custom-call | tf_op jit(solution)/shard_map/pallas_call | solution.py:187
  (65 shorter events, 18.9 us)
Async XLA Ops:
  6.5 45.3 %all-gather.3.cloned.1.call-start = ((), (), s32[]{:S(2)}) async-start(), calls=%async_computation | async-start | bytes 1990656 | tf_op jit(solution)/shard_map/all_gather | solution.py:65
  7.3 207.3 %all-gather.5.cloned.1.call-start = ((), (), s32[]{:S(2)}) async-start(), calls=%async_computation.1 | async-start | bytes 30081024 | tf_op jit(solution)/shard_map/all_gather | solution.py:66
  51.8 6.2 %copy-start.9 = (s32[12,3]{0,1:T(4,128)S(1)}, s32[12,3]{0,1:T(4,128)}, u32[]{:S(2)}) copy-start(s32[12,3]{0,1:T(4,128)} %param.14) | copy-start | bytes 436
  51.8 6.8 %copy-start.5 = (f32[3072]{0:T(1024)S(1)}, f32[3072]{0:T(1024)}, u32[]{:S(2)}) copy-start(f32[3072]{0:T(1024)} %param.9) | copy-start | bytes 36868
  51.9 6.8 %copy-start.6 = (f32[3072]{0:T(1024)S(1)}, f32[3072]{0:T(1024)}, u32[]{:S(2)}) copy-start(f32[3072]{0:T(1024)} %param.10) | copy-start | bytes 36868
  222.3 7.6 %copy-start = (bf16[640,768]{1,0:T(8,128)(2,1)S(1)}, bf16[640,768]{1,0:T(8,128)(2,1)}, u32[]{:S(2)}) copy-start(bf16[640,768]{1,0:T(8,128)(2,1)} %shard_map.86) | copy-start | bytes 2949124
  232.5 36.2 %collective-permute-start.4 = (bf16[2,1,1,2,2,80,768]{6,5,4,3,1,0,2:T(8,128)(2,1)}, bf16[2,1,1,2,2,80,768]{6,5,4,3,1,0,2:T(8,128)(2,1)}, u32[]{:S(2)}, u32[]{:S(2)}) collective-permute-start(bf16[2,1,1,2,2,80,768]{6,5,4,3,1,0,2:T(8,128)(2,1)} %get-tuple-element.9), channel_id=1, source_target_pairs={{0,8},{8,16},{16,24},{24,32},{32,40},{40,48},{48,56},{56,64},{64,7... | collective-permute-start | bytes 2949128 | tf_op jit(solution)/shard_map/ppermute | solution.py:29
  234.7 34.0 %collective-permute-start.5 = (bf16[2,1,1,2,2,80,768]{6,5,4,3,1,0,2:T(8,128)(2,1)}, bf16[2,1,1,2,2,80,768]{6,5,4,3,1,0,2:T(8,128)(2,1)}, u32[]{:S(2)}, u32[]{:S(2)}) collective-permute-start(bf16[2,1,1,2,2,80,768]{6,5,4,3,1,0,2:T(8,128)(2,1)} %get-tuple-element.10), channel_id=1, source_target_pairs={{8,0},{16,8},{24,16},{32,24},{40,32},{48,40},{56,48},{64,56},{72,6... | collective-permute-start | bytes 2949128 | tf_op jit(solution)/shard_map/ppermute | solution.py:31
  249.2 7.5 %copy-start.2 = (bf16[640,768]{1,0:T(8,128)(2,1)S(1)}, bf16[640,768]{1,0:T(8,128)(2,1)}, u32[]{:S(2)}) copy-start(bf16[640,768]{1,0:T(8,128)(2,1)} %shard_map.84) | copy-start | bytes 2949124
  256.7 11.9 %copy-start.1 = (bf16[640,768]{1,0:T(8,128)(2,1)S(1)}, bf16[640,768]{1,0:T(8,128)(2,1)}, u32[]{:S(2)}) copy-start(bf16[640,768]{1,0:T(8,128)(2,1)} %shard_map.85) | copy-start | bytes 2949124
  259.5 24.2 %collective-permute-start = (bf16[2,1,1,2,2,80,768]{6,5,4,3,1,0,2:T(8,128)(2,1)}, bf16[2,1,1,2,2,80,768]{6,5,4,3,1,0,2:T(8,128)(2,1)}, u32[]{:S(2)}, u32[]{:S(2)}) collective-permute-start(bf16[2,1,1,2,2,80,768]{6,5,4,3,1,0,2:T(8,128)(2,1)} %get-tuple-element.11), channel_id=1, source_target_pairs={{0,8},{8,16},{16,24},{24,32},{32,40},{40,48},{48,56},{56,64},{64,7... | collective-permute-start | bytes 2949128 | tf_op jit(solution)/shard_map/ppermute | solution.py:29
  261.4 23.7 %collective-permute-start.1 = (bf16[2,1,1,2,2,80,768]{6,5,4,3,1,0,2:T(8,128)(2,1)}, bf16[2,1,1,2,2,80,768]{6,5,4,3,1,0,2:T(8,128)(2,1)}, u32[]{:S(2)}, u32[]{:S(2)}) collective-permute-start(bf16[2,1,1,2,2,80,768]{6,5,4,3,1,0,2:T(8,128)(2,1)} %get-tuple-element.12), channel_id=1, source_target_pairs={{8,0},{16,8},{24,16},{32,24},{40,32},{48,40},{56,48},{64,56},{72,6... | collective-permute-start | bytes 2949128 | tf_op jit(solution)/shard_map/ppermute | solution.py:31
  270.5 11.8 %copy-start.4 = (s32[32,32,80]{2,1,0:T(8,128)S(1)}, s32[32,32,80]{2,1,0:T(8,128)}, u32[]{:S(2)}) copy-start(s32[32,32,80]{2,1,0:T(8,128)} %param.15) | copy-start | bytes 983044
  272.7 61.3 %collective-permute-start.6 = (bf16[2,4,1,1,2,80,768]{6,5,4,3,1,0,2:T(8,128)(2,1)}, bf16[2,4,1,1,2,80,768]{6,5,4,3,1,0,2:T(8,128)(2,1)}, u32[]{:S(2)}, u32[]{:S(2)}) collective-permute-start(bf16[2,4,1,1,2,80,768]{6,5,4,3,1,0,2:T(8,128)(2,1)} %get-tuple-element.5), channel_id=1, source_target_pairs={{0,1},{1,2},{2,3},{3,4},{4,5},{5,6},{6,7},{8,9},{9,10},{10,11},{11... | collective-permute-start | bytes 5898248 | tf_op jit(solution)/shard_map/ppermute | solution.py:29
  276.2 57.8 %collective-permute-start.7 = (bf16[2,4,1,1,2,80,768]{6,5,4,3,1,0,2:T(8,128)(2,1)}, bf16[2,4,1,1,2,80,768]{6,5,4,3,1,0,2:T(8,128)(2,1)}, u32[]{:S(2)}, u32[]{:S(2)}) collective-permute-start(bf16[2,4,1,1,2,80,768]{6,5,4,3,1,0,2:T(8,128)(2,1)} %get-tuple-element.6), channel_id=1, source_target_pairs={{1,0},{2,1},{3,2},{4,3},{5,4},{6,5},{7,6},{9,8},{10,9},{11,10},{12... | collective-permute-start | bytes 5898248 | tf_op jit(solution)/shard_map/ppermute | solution.py:31
  287.2 12.7 %copy-start.7 = (s32[160]{0:T(256)S(1)}, s32[160]{0:T(256)}, u32[]{:S(2)}) copy-start(s32[160]{0:T(256)} %sub.71) | copy-start | bytes 1924
  287.2 12.7 %copy-start.8 = (s32[12]{0:T(128)S(1)}, s32[12]{0:T(128)}, u32[]{:S(2)}) copy-start(s32[12]{0:T(128)} %get-tuple-element.17) | copy-start | bytes 148
  289.4 78.5 %collective-permute-start.2 = (bf16[2,4,1,1,2,80,768]{6,5,4,3,1,0,2:T(8,128)(2,1)}, bf16[2,4,1,1,2,80,768]{6,5,4,3,1,0,2:T(8,128)(2,1)}, u32[]{:S(2)}, u32[]{:S(2)}) collective-permute-start(bf16[2,4,1,1,2,80,768]{6,5,4,3,1,0,2:T(8,128)(2,1)} %get-tuple-element.7), channel_id=1, source_target_pairs={{0,1},{1,2},{2,3},{3,4},{4,5},{5,6},{6,7},{8,9},{9,10},{10,11},{11... | collective-permute-start | bytes 5898248 | tf_op jit(solution)/shard_map/ppermute | solution.py:29
  291.4 76.6 %collective-permute-start.3 = (bf16[2,4,1,1,2,80,768]{6,5,4,3,1,0,2:T(8,128)(2,1)}, bf16[2,4,1,1,2,80,768]{6,5,4,3,1,0,2:T(8,128)(2,1)}, u32[]{:S(2)}, u32[]{:S(2)}) collective-permute-start(bf16[2,4,1,1,2,80,768]{6,5,4,3,1,0,2:T(8,128)(2,1)} %get-tuple-element.8), channel_id=1, source_target_pairs={{1,0},{2,1},{3,2},{4,3},{5,4},{6,5},{7,6},{9,8},{10,9},{11,10},{12... | collective-permute-start | bytes 5898248 | tf_op jit(solution)/shard_map/ppermute | solution.py:31
  340.5 27.5 %copy-start.3 = (bf16[640,768]{1,0:T(8,128)(2,1)S(1)}, bf16[640,768]{1,0:T(8,128)(2,1)}, u32[]{:S(2)}) copy-start(bf16[640,768]{1,0:T(8,128)(2,1)} %shard_map.83) | copy-start | bytes 2949124
Sparse Core Ops, SparseCore 0:
  9.0 42.7 all-gather.2
  54.3 160.2 all-gather.4

commit v4 on v3

--- a/solution.py
+++ b/solution.py
@@ -63,21 +63,16 @@
     token_count = frame_count * row_count * width
     modulated = modulate(tokens.reshape(token_count, features), mod_scale, mod_shift)
     band_weight = lax.all_gather(w_qkv, "height", axis=0, tiled=True)
-    full_weight = lax.all_gather(band_weight, "tm", axis=0, tiled=True)
-    inner = full_weight.shape[1] // 3
+    band_rows = band_weight.shape[0]
+    inner = band_weight.shape[1] // 3
     group_cols = inner // GROUPS
-    tiled = (frame_count // TT, TT, row_count // TH, TH, width, group_cols)
-    groups = []
-    for group in range(GROUPS):
-        start = group * group_cols
-        key = project(modulated, full_weight, inner + start, group_cols, k_gain)
-        value = project(modulated, full_weight, 2 * inner + start, group_cols, None)
-        stacked = jnp.stack([key.reshape(tiled), value.reshape(tiled)])
-        groups.append(with_halo(stacked, (("tm", 1), ("height", 3)), 1))
-    query = project(modulated, full_weight, 0, inner, q_gain)
+    band_parts = (
+        band_weight.reshape(band_rows, 3, GROUPS, group_cols)
+        .transpose(2, 0, 1, 3)
+        .reshape(GROUPS, band_rows, 3 * group_cols)
+    )
     frames_ext = frame_count + 2 * TT
     rows_ext = row_count + 2 * TH
-    groups = [g.reshape(2, frames_ext, rows_ext, width, group_cols) for g in groups]
     frame_block = lax.axis_index("tm")
     row_block = lax.axis_index("height")
     first_frame = frame_block * frame_count
@@ -116,11 +111,21 @@
     query_lo = (query_cols[None, :] - window[:, 2, None]).reshape(HEADS, query_n, 1)
     query_hi = (query_cols[None, :] + window[:, 2, None]).reshape(HEADS, query_n, 1)
     query_ok = query_valid.reshape(blocks, query_n, 1).astype(jnp.float32)
-    query_grid = query.reshape(frame_count, row_count, width, inner)
+    tiled = (frame_count // TT, TT, row_count // TH, TH, width, group_cols)
     out = None
-    for group, extended in enumerate(groups):
+    for group in range(GROUPS):
+        group_weight = lax.all_gather(band_parts[group], "tm", axis=0, tiled=True)
+        if out is not None:
+            group_weight, out = lax.optimization_barrier((group_weight, out))
+        key = project(modulated, group_weight, group_cols, group_cols, k_gain)
+        value = project(modulated, group_weight, 2 * group_cols, group_cols, None)
+        stacked = jnp.stack([key.reshape(tiled), value.reshape(tiled)])
+        extended = with_halo(stacked, (("tm", 1), ("height", 3)), 1)
+        extended = extended.reshape(2, frames_ext, rows_ext, width, group_cols)
+        query = project(modulated, group_weight, 0, group_cols, q_gain)
+        query = query.reshape(frame_count, row_count, width, group_cols)
         out = tile_attention(
-            query_grid, extended, key_mask, query_lo, query_hi, key_cols, query_ok, group, out
+            query, extended, key_mask, query_lo, query_hi, key_cols, query_ok, group, out
         )
     return out
 
@@ -154,8 +159,9 @@
 
 
 def tile_attention(query, extended, key_mask, query_lo, query_hi, key_cols, query_ok, group, out):
-    frames, rows, width, inner = query.shape
-    heads = extended.shape[-1] // HDIM
+    frames, rows, width, group_cols = query.shape
+    heads = group_cols // HDIM
+    out_shape = (frames, rows, width, key_mask.shape[0] * HDIM)
     first = group * heads
     row_tiles = rows // TH
     assert row_tiles == ROW_TILES
@@ -164,6 +170,9 @@
     key_n = key_mask.shape[-1]
     query_n = TH * width
     q_spec = pl.BlockSpec(
+        (1, TH, width, HDIM), lambda h, b: (b // row_tiles, b % row_tiles, 0, h)
+    )
+    o_spec = pl.BlockSpec(
         (1, TH, width, HDIM), lambda h, b: (b // row_tiles, b % row_tiles, 0, first + h)
     )
     in_specs = [
@@ -188,8 +197,8 @@
         kernel,
         grid=(heads, blocks),
         in_specs=in_specs,
-        out_specs=q_spec,
-        out_shape=jax.ShapeDtypeStruct(query.shape, jnp.bfloat16),
+        out_specs=o_spec,
+        out_shape=jax.ShapeDtypeStruct(out_shape, jnp.bfloat16),
         input_output_aliases=aliases,
     )(*operands)
 

time: 410 us -> 451 us (1.10)
  waiting for transfers between devices: 218 us -> 264 us
  starting transfers between devices: 36.6 us -> 23.6 us
  local copies, waits for them, and re-layouts: 8.56 us -> 15.9 us
    ppermute x4, waiting for transfers between devices: 1.49 us -> 111 us  [with_halo(): lax.ppermute(head, axis, [((i + 1) % count, i) for i in range(ends)])]
    all_gather x1 -> x2, waiting for transfers between devices: 151 us -> 83.5 us  [per_device(): group_weight = lax.all_gather(band_parts[group], 'tm', axis=0, tiled=True)]
    ppermute x4, starting transfers between devices: 27.1 us -> 13.1 us  [with_halo(): lax.ppermute(head, axis, [((i + 1) % count, i) for i in range(ends)])]
    pallas_call x5 -> x6, Pallas kernels: 41.3 us -> 44.8 us  [project(): pl.pallas_call(functools.partial(projection_kernel, normalize=normalize),...]
  transfers between devices with their start and end apart: 10 -> 11, of which waited for: 4 -> 10; matrix products, arithmetic and copies ran while one was open for 9% -> 7% of each run, Pallas kernels for 13% -> 13%
where the time goes in v4:
time: 451 us; the launch traced here: 450 us
  waiting for transfers between devices  264 us (59%)
  Pallas kernels  99.7 us (22%)
  other arithmetic  33.3 us (7%)
  starting transfers between devices  23.6 us (5%)
  local copies, waits for them, and re-layouts  15.9 us (4%)
  between operations  13.4 us (3%)
    ppermute x4, waiting for transfers between devices, with_halo(): lax.ppermute(head, axis, [((i + 1) % count, i) for i in range(ends)])  111 us
    all_gather x2, waiting for transfers between devices, per_device(): group_weight = lax.all_gather(band_parts[group], 'tm', axis=0, tiled=True)  83.5 us
    pallas_call x2, Pallas kernels, tile_attention(): pl.pallas_call(kernel, grid=(heads, blocks), in_specs=in_specs, out_specs...  55 us
    pallas_call x6, Pallas kernels, project(): pl.pallas_call(functools.partial(projection_kernel, normalize=normalize),...  44.8 us
    all_gather x1, waiting for transfers between devices, per_device(): band_weight = lax.all_gather(w_qkv, 'height', axis=0, tiled=True)  44.5 us
    ppermute x4, waiting for transfers between devices, with_halo(): lax.ppermute(tail, axis, [(i, (i + 1) % count) for i in range(ends)])  24.1 us
    concatenate x4, other arithmetic, with_halo(): jnp.concatenate([lax.ppermute(tail, axis, [(i, (i + 1) % count) for i in...  14.6 us
    ppermute x4, starting transfers between devices, with_halo(): lax.ppermute(head, axis, [((i + 1) % count, i) for i in range(ends)])  13.1 us
  transfers between devices with their start and end apart: 11, of which 10 were waited for; matrix products, arithmetic and copies ran while one was open for 7% of the time, Pallas kernels for 13%

profile of v4, /device:TPU:6, one launch (start us, length us, event | category | flops | bytes accessed | tf_op | source)
XLA Modules:
  0.0 449.7 jit_solution(2298144760100994629)
XLA Ops:
  7.3 44.5 %all-gather.4.cloned.1.call-done = bf16[192,4608]{1,0:T(8,128)(2,1)} async-done(((bf16[24,4608]{1,0:T(8,128)(2,1)}), bf16[192,4608]{1,0:T(8,128)(2,1)}) %all-gather.4.cloned.1.call-update) | async-done | bytes 1769488 | tf_op jit(solution)/shard_map/all_gather | solution.py:65
  64.4 4.9 %fusion.3.x_ref = bf16[640,3072]{1,0:T(8,128)(2,1)} fusion(bf16[2,4,80,3072]{3,2,1,0:T(8,128)(2,1)} %param.8, f32[3072]{0:T(1024)S(1)} %copy-done.7, f32[3072]{0:T(1024)S(1)} %broadcast_add_fusion.1, f32[640]{0:T(1024)S(1)} %rsqrt.12, f32[640]{0:T(1024)S(1)} %div.29), kind=kLoop, calls=%fused_computation.6 | loop fusion | flops 11796480 | bytes 7894016 | tf_op jit(solution)/shard_map/convert_element_type | solution.py:44
  69.3 83.5 %all-gather.8.cloned.1.call-done.w_ref = bf16[3072,2304]{1,0:T(8,128)(2,1)} async-done(((bf16[192,2304]{1,0:T(8,128)(2,1)}), bf16[3072,2304]{1,0:T(8,128)(2,1)}) %all-gather.8.cloned.1.call-update) | async-done | bytes 14155792 | tf_op jit(solution)/shard_map/all_gather | solution.py:117
  152.8 7.4 %shard_map.83 = bf16[640,768]{1,0:T(8,128)(2,1)} custom-call(bf16[640,3072]{1,0:T(8,128)(2,1)} %fusion.3.x_ref, bf16[3072,2304]{1,0:T(8,128)(2,1)} %all-gather.8.cloned.1.call-done.w_ref, f32[1,128]{1,0:T(1,128)} %bitcast.66), custom_call_target="tpu_custom_call" | custom-call | tf_op jit(solution)/shard_map/pallas_call | solution.py:225
  160.8 7.5 %shard_map.84 = bf16[640,768]{1,0:T(8,128)(2,1)} custom-call(bf16[640,3072]{1,0:T(8,128)(2,1)} %fusion.3.x_ref, bf16[3072,2304]{1,0:T(8,128)(2,1)} %all-gather.8.cloned.1.call-done.w_ref, f32[1,128]{1,0:T(1,128)} %broadcast_8_g_ref.2.g_ref), custom_call_target="tpu_custom_call" | custom-call | tf_op jit(solution)/shard_map/pallas_call | solution.py:225
  171.0 4.2 collective-permute-start.1
  178.8 8.4 %collective-permute-done.1 = bf16[2,1,1,2,2,80,768]{6,5,4,3,1,0,2:T(8,128)(2,1)S(1)} collective-permute-done((bf16[2,1,1,2,2,80,768]{6,5,4,3,1,0,2:T(8,128)(2,1)}, bf16[2,1,1,2,2,80,768]{6,5,4,3,1,0,2:T(8,128)(2,1)S(1)}, u32[]{:S(2)}, u32[]{:S(2)}) %collective-permute-start.1) | collective-permute-done | bytes 983072 | tf_op jit(solution)/shard_map/ppermute | solution.py:31
  187.1 7.5 %collective-permute-done = bf16[2,1,1,2,2,80,768]{6,5,4,3,1,0,2:T(8,128)(2,1)} collective-permute-done((bf16[2,1,1,2,2,80,768]{6,5,4,3,1,0,2:T(8,128)(2,1)}, bf16[2,1,1,2,2,80,768]{6,5,4,3,1,0,2:T(8,128)(2,1)}, u32[]{:S(2)}, u32[]{:S(2)}) %collective-permute-start) | collective-permute-done | bytes 983072 | tf_op jit(solution)/shard_map/ppermute | solution.py:29
  198.5 5.1 %collective-permute-start.3 = (bf16[2,4,1,1,2,80,768]{6,5,4,3,1,0,2:T(8,128)(2,1)}, bf16[2,4,1,1,2,80,768]{6,5,4,3,1,0,2:T(8,128)(2,1)}, u32[]{:S(2)}, u32[]{:S(2)}) collective-permute-start(bf16[2,4,1,1,2,80,768]{6,5,4,3,1,0,2:T(8,128)(2,1)} %get-tuple-element.12), channel_id=1, source_target_pairs={{1,0},{2,1},{3,2},{4,3},{5,4},{6,5},{7,6},{9,8},{10,9},{11,10},{12... | collective-permute-start | bytes 5898248 | tf_op jit(solution)/shard_map/ppermute | solution.py:31
  211.2 7.5 %shard_map.82 = bf16[640,768]{1,0:T(8,128)(2,1)} custom-call(bf16[640,3072]{1,0:T(8,128)(2,1)} %fusion.3.x_ref, bf16[3072,2304]{1,0:T(8,128)(2,1)} %all-gather.8.cloned.1.call-done.w_ref, f32[1,128]{1,0:T(1,128)} %bitcast.68), custom_call_target="tpu_custom_call" | custom-call | tf_op jit(solution)/shard_map/pallas_call | solution.py:225
  218.6 64.4 %collective-permute-done.3 = bf16[2,4,1,1,2,80,768]{6,5,4,3,1,0,2:T(8,128)(2,1)} collective-permute-done((bf16[2,4,1,1,2,80,768]{6,5,4,3,1,0,2:T(8,128)(2,1)}, bf16[2,4,1,1,2,80,768]{6,5,4,3,1,0,2:T(8,128)(2,1)}, u32[]{:S(2)}, u32[]{:S(2)}) %collective-permute-start.3) | collective-permute-done | bytes 1966112 | tf_op jit(solution)/shard_map/ppermute | solution.py:31
  283.0 5.0 %collective-permute-done.2 = bf16[2,4,1,1,2,80,768]{6,5,4,3,1,0,2:T(8,128)(2,1)} collective-permute-done((bf16[2,4,1,1,2,80,768]{6,5,4,3,1,0,2:T(8,128)(2,1)}, bf16[2,4,1,1,2,80,768]{6,5,4,3,1,0,2:T(8,128)(2,1)}, u32[]{:S(2)}, u32[]{:S(2)}) %collective-permute-start.2) | collective-permute-done | bytes 1966112 | tf_op jit(solution)/shard_map/ppermute | solution.py:29
  288.1 6.3 %pad_maximum_fusion = bf16[2,4,1,4,2,80,768]{6,5,4,3,1,0,2:T(8,128)(2,1)} fusion(bf16[2,4,1,1,2,80,768]{6,5,4,3,1,0,2:T(8,128)(2,1)} %collective-permute-done.3, bf16[2,1,1,2,2,80,768]{6,5,4,3,1,0,2:T(8,128)(2,1)S(1)} %collective-permute-done.1, bf16[1,2,1,2,2,80,768]{6,5,4,3,1,0,2:T(8,128)(2,1)S(1)} %bitcast.52, ...), kind=kLoop, calls=%fused_computation | loop fusion | flops 19660800 | bytes 15728640 | tf_op jit(solution)/shard_map/concatenate | solution.py:27
  294.4 27.4 %shard_map.85.refs_8_ = bf16[2,4,80,1536]{3,2,1,0:T(8,128)(2,1)} custom-call(bf16[2,4,80,768]{3,2,1,0:T(8,128)(2,1)} %bitcast.63, bf16[2,4,8,80,768]{4,3,2,1,0:T(8,128)(2,1)} %bitcast.45, bf16[2,4,8,80,768]{4,3,2,1,0:T(8,128)(2,1)} %bitcast.46, f32[12,4,1,1440]{3,2,1,0:T(1,128)} %and_convert_fusion.km_ref.refs_3_, ...), custom_call_target="tpu_custom_call" | custom-call | tf_op jit(solution)/shard_map/pallas_call | solution.py:196
  321.7 7.5 %shard_map.87 = bf16[640,768]{1,0:T(8,128)(2,1)} custom-call(bf16[640,3072]{1,0:T(8,128)(2,1)} %fusion.3.x_ref, bf16[3072,2304]{1,0:T(8,128)(2,1)} %all-gather.6.cloned.1.call-done.w_ref, f32[1,128]{1,0:T(1,128)} %bitcast.67), custom_call_target="tpu_custom_call" | custom-call | tf_op jit(solution)/shard_map/pallas_call | solution.py:225
  329.3 7.4 %shard_map.88 = bf16[640,768]{1,0:T(8,128)(2,1)} custom-call(bf16[640,3072]{1,0:T(8,128)(2,1)} %fusion.3.x_ref, bf16[3072,2304]{1,0:T(8,128)(2,1)} %all-gather.6.cloned.1.call-done.w_ref, f32[1,128]{1,0:T(1,128)} %broadcast_8_g_ref.2.g_ref), custom_call_target="tpu_custom_call" | custom-call | tf_op jit(solution)/shard_map/pallas_call | solution.py:225
  342.4 9.2 %collective-permute-done.5 = bf16[2,1,1,2,2,80,768]{6,5,4,3,1,0,2:T(8,128)(2,1)S(1)} collective-permute-done((bf16[2,1,1,2,2,80,768]{6,5,4,3,1,0,2:T(8,128)(2,1)S(1)}, bf16[2,1,1,2,2,80,768]{6,5,4,3,1,0,2:T(8,128)(2,1)S(1)}, u32[]{:S(2)}, u32[]{:S(2)}) %collective-permute-start.5) | collective-permute-done | bytes 983072 | tf_op jit(solution)/shard_map/ppermute | solution.py:31
  351.6 7.4 %collective-permute-done.4 = bf16[2,1,1,2,2,80,768]{6,5,4,3,1,0,2:T(8,128)(2,1)S(1)} collective-permute-done((bf16[2,1,1,2,2,80,768]{6,5,4,3,1,0,2:T(8,128)(2,1)S(1)}, bf16[2,1,1,2,2,80,768]{6,5,4,3,1,0,2:T(8,128)(2,1)S(1)}, u32[]{:S(2)}, u32[]{:S(2)}) %collective-permute-start.4) | collective-permute-done | bytes 983072 | tf_op jit(solution)/shard_map/ppermute | solution.py:29
  364.6 3.9 collective-permute-start.6
  368.6 7.5 %shard_map.86 = bf16[640,768]{1,0:T(8,128)(2,1)} custom-call(bf16[640,3072]{1,0:T(8,128)(2,1)} %fusion.3.x_ref, bf16[3072,2304]{1,0:T(8,128)(2,1)} %all-gather.6.cloned.1.call-done.w_ref, f32[1,128]{1,0:T(1,128)} %bitcast.69), custom_call_target="tpu_custom_call" | custom-call | tf_op jit(solution)/shard_map/pallas_call | solution.py:225
  376.1 29.2 %collective-permute-done.7 = bf16[2,4,1,1,2,80,768]{6,5,4,3,1,0,2:T(8,128)(2,1)} collective-permute-done((bf16[2,4,1,1,2,80,768]{6,5,4,3,1,0,2:T(8,128)(2,1)}, bf16[2,4,1,1,2,80,768]{6,5,4,3,1,0,2:T(8,128)(2,1)}, u32[]{:S(2)}, u32[]{:S(2)}) %collective-permute-start.7) | collective-permute-done | bytes 1966112 | tf_op jit(solution)/shard_map/ppermute | solution.py:31
  405.3 4.0 collective-permute-done.6
  409.3 6.3 %pad_maximum_fusion.1 = bf16[2,4,1,4,2,80,768]{6,5,4,3,1,0,2:T(8,128)(2,1)} fusion(bf16[2,4,1,1,2,80,768]{6,5,4,3,1,0,2:T(8,128)(2,1)} %collective-permute-done.7, bf16[2,1,1,2,2,80,768]{6,5,4,3,1,0,2:T(8,128)(2,1)S(1)} %collective-permute-done.5, bf16[1,2,1,2,2,80,768]{6,5,4,3,1,0,2:T(8,128)(2,1)S(1)} %bitcast.58, ...), kind=kLoop, calls=%fused_computation.1 | loop fusion | flops 19660800 | bytes 15728640 | tf_op jit(solution)/shard_map/concatenate | solution.py:27
  415.6 27.6 %shard_map.89 = bf16[2,4,80,1536]{3,2,1,0:T(8,128)(2,1)} custom-call(bf16[2,4,80,768]{3,2,1,0:T(8,128)(2,1)} %bitcast.62, bf16[2,4,8,80,768]{4,3,2,1,0:T(8,128)(2,1)} %bitcast.43, bf16[2,4,8,80,768]{4,3,2,1,0:T(8,128)(2,1)} %bitcast.44, f32[12,4,1,1440]{3,2,1,0:T(1,128)} %and_convert_fusion.km_ref.refs_3_, ...), custom_call_target="tpu_custom_call", output_to_operand_aliasing={{}: (8, {})} | custom-call | tf_op jit(solution)/shard_map/pallas_call | solution.py:196
  (72 shorter events, 42.7 us)
Async XLA Ops:
  6.5 45.3 %all-gather.4.cloned.1.call-start = ((), (), s32[]{:S(2)}) async-start(), calls=%async_computation | async-start | bytes 1990656 | tf_op jit(solution)/shard_map/all_gather | solution.py:65
  7.3 145.5 %all-gather.8.cloned.1.call-start = ((), (), s32[]{:S(2)}) async-start(), calls=%async_computation.2 | async-start | bytes 15040512 | tf_op jit(solution)/shard_map/all_gather | solution.py:117
  57.0 264.7 %all-gather.6.cloned.1.call-start = ((), (), s32[]{:S(2)}) async-start(), calls=%async_computation.1 | async-start | bytes 15040512 | tf_op jit(solution)/shard_map/all_gather | solution.py:117
  58.1 6.2 %copy-start.6 = (f32[3072]{0:T(1024)S(1)}, f32[3072]{0:T(1024)}, u32[]{:S(2)}) copy-start(f32[3072]{0:T(1024)} %param.9) | copy-start | bytes 36868
  58.2 6.2 %copy-start.7 = (f32[3072]{0:T(1024)S(1)}, f32[3072]{0:T(1024)}, u32[]{:S(2)}) copy-start(f32[3072]{0:T(1024)} %param.10) | copy-start | bytes 36868
  160.8 7.5 %copy-start = (bf16[640,768]{1,0:T(8,128)(2,1)S(1)}, bf16[640,768]{1,0:T(8,128)(2,1)}, u32[]{:S(2)}) copy-start(bf16[640,768]{1,0:T(8,128)(2,1)} %shard_map.83) | copy-start | bytes 2949124
  168.3 8.9 %copy-start.5 = (s32[32,32,80]{2,1,0:T(8,128)S(1)}, s32[32,32,80]{2,1,0:T(8,128)}, u32[]{:S(2)}) copy-start(s32[32,32,80]{2,1,0:T(8,128)} %param.15) | copy-start | bytes 983044
  168.3 10.5 %copy-start.8 = (s32[12,3]{0,1:T(4,128)S(1)}, s32[12,3]{0,1:T(4,128)}, u32[]{:S(2)}) copy-start(s32[12,3]{0,1:T(4,128)} %param.14) | copy-start | bytes 436
  168.3 26.4 %copy-start.1 = (bf16[640,768]{1,0:T(8,128)(2,1)S(1)}, bf16[640,768]{1,0:T(8,128)(2,1)}, u32[]{:S(2)}) copy-start(bf16[640,768]{1,0:T(8,128)(2,1)} %shard_map.84) | copy-start | bytes 2949124
  171.0 16.1 %collective-permute-start.1 = (bf16[2,1,1,2,2,80,768]{6,5,4,3,1,0,2:T(8,128)(2,1)}, bf16[2,1,1,2,2,80,768]{6,5,4,3,1,0,2:T(8,128)(2,1)S(1)}, u32[]{:S(2)}, u32[]{:S(2)}) collective-permute-start(bf16[2,1,1,2,2,80,768]{6,5,4,3,1,0,2:T(8,128)(2,1)} %get-tuple-element.18), channel_id=1, source_target_pairs={{8,0},{16,8},{24,16},{32,24},{40,32},{48,40},{56,48},{64,56},{72,6... | collective-permute-start | bytes 2949128 | tf_op jit(solution)/shard_map/ppermute | solution.py:31
  175.2 19.5 %collective-permute-start = (bf16[2,1,1,2,2,80,768]{6,5,4,3,1,0,2:T(8,128)(2,1)}, bf16[2,1,1,2,2,80,768]{6,5,4,3,1,0,2:T(8,128)(2,1)}, u32[]{:S(2)}, u32[]{:S(2)}) collective-permute-start(bf16[2,1,1,2,2,80,768]{6,5,4,3,1,0,2:T(8,128)(2,1)} %get-tuple-element.17), channel_id=1, source_target_pairs={{0,8},{8,16},{16,24},{24,32},{32,40},{40,48},{48,56},{56,64},{64,7... | collective-permute-start | bytes 2949128 | tf_op jit(solution)/shard_map/ppermute | solution.py:29
  198.5 84.6 %collective-permute-start.3 = (bf16[2,4,1,1,2,80,768]{6,5,4,3,1,0,2:T(8,128)(2,1)}, bf16[2,4,1,1,2,80,768]{6,5,4,3,1,0,2:T(8,128)(2,1)}, u32[]{:S(2)}, u32[]{:S(2)}) collective-permute-start(bf16[2,4,1,1,2,80,768]{6,5,4,3,1,0,2:T(8,128)(2,1)} %get-tuple-element.12), channel_id=1, source_target_pairs={{1,0},{2,1},{3,2},{4,3},{5,4},{6,5},{7,6},{9,8},{10,9},{11,10},{12... | collective-permute-start | bytes 5898248 | tf_op jit(solution)/shard_map/ppermute | solution.py:31
  203.6 84.4 %collective-permute-start.2 = (bf16[2,4,1,1,2,80,768]{6,5,4,3,1,0,2:T(8,128)(2,1)}, bf16[2,4,1,1,2,80,768]{6,5,4,3,1,0,2:T(8,128)(2,1)}, u32[]{:S(2)}, u32[]{:S(2)}) collective-permute-start(bf16[2,4,1,1,2,80,768]{6,5,4,3,1,0,2:T(8,128)(2,1)} %get-tuple-element.11), channel_id=1, source_target_pairs={{0,1},{1,2},{2,3},{3,4},{4,5},{5,6},{6,7},{8,9},{9,10},{10,11},{11... | collective-permute-start | bytes 5898248 | tf_op jit(solution)/shard_map/ppermute | solution.py:29
  329.3 7.4 %copy-start.2 = (bf16[640,768]{1,0:T(8,128)(2,1)S(1)}, bf16[640,768]{1,0:T(8,128)(2,1)}, u32[]{:S(2)}) copy-start(bf16[640,768]{1,0:T(8,128)(2,1)} %shard_map.87) | copy-start | bytes 2949124
  336.6 23.4 %copy-start.3 = (bf16[640,768]{1,0:T(8,128)(2,1)S(1)}, bf16[640,768]{1,0:T(8,128)(2,1)}, u32[]{:S(2)}) copy-start(bf16[640,768]{1,0:T(8,128)(2,1)} %shard_map.88) | copy-start | bytes 2949124
  338.1 13.5 %collective-permute-start.5 = (bf16[2,1,1,2,2,80,768]{6,5,4,3,1,0,2:T(8,128)(2,1)S(1)}, bf16[2,1,1,2,2,80,768]{6,5,4,3,1,0,2:T(8,128)(2,1)S(1)}, u32[]{:S(2)}, u32[]{:S(2)}) collective-permute-start(bf16[2,1,1,2,2,80,768]{6,5,4,3,1,0,2:T(8,128)(2,1)S(1)} %get-tuple-element.16), channel_id=1, source_target_pairs={{8,0},{16,8},{24,16},{32,24},{40,32},{48,40},{56,48},{64,56},{72,6... | collective-permute-start | bytes 2949128 | tf_op jit(solution)/shard_map/ppermute | solution.py:31
  340.0 19.0 %collective-permute-start.4 = (bf16[2,1,1,2,2,80,768]{6,5,4,3,1,0,2:T(8,128)(2,1)S(1)}, bf16[2,1,1,2,2,80,768]{6,5,4,3,1,0,2:T(8,128)(2,1)S(1)}, u32[]{:S(2)}, u32[]{:S(2)}) collective-permute-start(bf16[2,1,1,2,2,80,768]{6,5,4,3,1,0,2:T(8,128)(2,1)S(1)} %get-tuple-element.15), channel_id=1, source_target_pairs={{0,8},{8,16},{16,24},{24,32},{32,40},{40,48},{48,56},{56,64},{64,7... | collective-permute-start | bytes 2949128 | tf_op jit(solution)/shard_map/ppermute | solution.py:29
  359.0 1.0 copy-start.4
  362.7 42.5 %collective-permute-start.7 = (bf16[2,4,1,1,2,80,768]{6,5,4,3,1,0,2:T(8,128)(2,1)}, bf16[2,4,1,1,2,80,768]{6,5,4,3,1,0,2:T(8,128)(2,1)}, u32[]{:S(2)}, u32[]{:S(2)}) collective-permute-start(bf16[2,4,1,1,2,80,768]{6,5,4,3,1,0,2:T(8,128)(2,1)} %get-tuple-element.10), channel_id=1, source_target_pairs={{1,0},{2,1},{3,2},{4,3},{5,4},{6,5},{7,6},{9,8},{10,9},{11,10},{12... | collective-permute-start | bytes 5898248 | tf_op jit(solution)/shard_map/ppermute | solution.py:31
  364.6 44.7 %collective-permute-start.6 = (bf16[2,4,1,1,2,80,768]{6,5,4,3,1,0,2:T(8,128)(2,1)}, bf16[2,4,1,1,2,80,768]{6,5,4,3,1,0,2:T(8,128)(2,1)}, u32[]{:S(2)}, u32[]{:S(2)}) collective-permute-start(bf16[2,4,1,1,2,80,768]{6,5,4,3,1,0,2:T(8,128)(2,1)} %get-tuple-element.9), channel_id=1, source_target_pairs={{0,1},{1,2},{2,3},{3,4},{4,5},{5,6},{6,7},{8,9},{9,10},{10,11},{11... | collective-permute-start | bytes 5898248 | tf_op jit(solution)/shard_map/ppermute | solution.py:29
Sparse Core Ops, SparseCore 0:
  9.0 42.7 all-gather.3
  57.2 95.5 all-gather.7
  155.3 140.6 all-gather.5

commit v5 on v3

--- a/solution.py
+++ b/solution.py
@@ -62,7 +62,7 @@
     frame_count, row_count, width, features = tokens.shape
     token_count = frame_count * row_count * width
     modulated = modulate(tokens.reshape(token_count, features), mod_scale, mod_shift)
-    band_weight = lax.all_gather(w_qkv, "height", axis=0, tiled=True)
+    band_weight = band_gather(w_qkv)
     full_weight = lax.all_gather(band_weight, "tm", axis=0, tiled=True)
     inner = full_weight.shape[1] // 3
     group_cols = inner // GROUPS
@@ -226,6 +226,67 @@
     )(x, w, gain)
 
 
+MESH = pl.DeviceIdType.MESH
+
+
+def band_gather_kernel(w_ref, out_ref, local_sem, send_sem, recv_sem):
+    count = lax.axis_size("height")
+    me = lax.axis_index("height")
+    frame_block = lax.axis_index("tm")
+    barrier = pltpu.get_barrier_semaphore()
+    for step in range(1, count):
+        peer = lax.rem(me + step, count)
+        pl.semaphore_signal(barrier, inc=1, device_id=(frame_block, peer), device_id_type=MESH)
+    pl.semaphore_wait(barrier, count - 1)
+    own = pltpu.make_async_copy(w_ref, out_ref.at[me], local_sem)
+    own.start()
+    copies = []
+    for step in range(1, count):
+        peer = lax.rem(me + step, count)
+        copy = pltpu.make_async_remote_copy(
+            src_ref=w_ref,
+            dst_ref=out_ref.at[me],
+            send_sem=send_sem.at[step],
+            recv_sem=recv_sem.at[me],
+            device_id=(frame_block, peer),
+            device_id_type=MESH,
+        )
+        copy.start()
+        copies.append(copy)
+    for copy in copies:
+        copy.wait_send()
+    for step in range(1, count):
+        source = lax.rem(me + count - step, count)
+        incoming = pltpu.make_async_remote_copy(
+            src_ref=w_ref,
+            dst_ref=out_ref.at[source],
+            send_sem=send_sem.at[step],
+            recv_sem=recv_sem.at[source],
+            device_id=(frame_block, source),
+            device_id_type=MESH,
+        )
+        incoming.wait_recv()
+    own.wait()
+
+
+def band_gather(w):
+    rows, cols = w.shape
+    count = lax.axis_size("height")
+    gathered = pl.pallas_call(
+        band_gather_kernel,
+        in_specs=[pl.BlockSpec(memory_space=pl.ANY)],
+        out_specs=pl.BlockSpec(memory_space=pl.ANY),
+        out_shape=jax.ShapeDtypeStruct((count, rows, cols), w.dtype),
+        scratch_shapes=[
+            pltpu.SemaphoreType.DMA(()),
+            pltpu.SemaphoreType.DMA((count,)),
+            pltpu.SemaphoreType.DMA((count,)),
+        ],
+        compiler_params=pltpu.CompilerParams(collective_id=0, has_side_effects=True),
+    )(w)
+    return gathered.reshape(count * rows, cols)
+
+
 def solution(mesh):
     in_specs = (
         P("tm", "height", None, None),

time: 410 us -> 394 us (0.961)
  waiting for transfers between devices: 218 us -> 175 us
  Pallas kernels: 96.2 us -> 123 us
    all_gather x1 -> x0, waiting for transfers between devices: 44.5 us -> none  [per_device(): band_weight = lax.all_gather(w_qkv, 'height', axis=0, tiled=True)]
    pallas_call x0 -> x1, Pallas kernels: none -> 27 us  [band_gather(): pl.pallas_call(band_gather_kernel, in_specs=[pl.BlockSpec(memory_space=pl...]
  transfers between devices with their start and end apart: 10 -> 9, of which waited for: 4 -> 3; matrix products, arithmetic and copies ran while one was open for 9% -> 9% of each run, Pallas kernels for 13% -> 14%
where the time goes in v5:
time: 394 us; the launch traced here: 393 us
  waiting for transfers between devices  175 us (44%)
  Pallas kernels  123 us (31%)
  starting transfers between devices  36.6 us (9%)
  other arithmetic  35.9 us (9%)
  between operations  13.7 us (3%)
  local copies, waits for them, and re-layouts  8.69 us (2%)
    all_gather x1, waiting for transfers between devices, per_device(): full_weight = lax.all_gather(band_weight, 'tm', axis=0, tiled=True)  153 us
    pallas_call x2, Pallas kernels, tile_attention(): pl.pallas_call(kernel, grid=(heads, blocks), in_specs=in_specs, out_specs...  55 us
    pallas_call x5, Pallas kernels, project(): pl.pallas_call(functools.partial(projection_kernel, normalize=normalize),...  41.3 us
    ppermute x4, starting transfers between devices, with_halo(): lax.ppermute(head, axis, [((i + 1) % count, i) for i in range(ends)])  27.2 us
    pallas_call x1, Pallas kernels, band_gather(): pl.pallas_call(band_gather_kernel, in_specs=[pl.BlockSpec(memory_space=pl...  27 us
    ppermute x4, waiting for transfers between devices, with_halo(): lax.ppermute(tail, axis, [(i, (i + 1) % count) for i in range(ends)])  20 us
    concatenate x4, other arithmetic, with_halo(): jnp.concatenate([lax.ppermute(tail, axis, [(i, (i + 1) % count) for i in...  16.8 us
    ppermute x4, starting transfers between devices, with_halo(): lax.ppermute(tail, axis, [(i, (i + 1) % count) for i in range(ends)])  9.42 us
  transfers between devices with their start and end apart: 9, of which 3 were waited for; matrix products, arithmetic and copies ran while one was open for 9% of the time, Pallas kernels for 14%

profile of v5, /device:TPU:6, one launch (start us, length us, event | category | flops | bytes accessed | tf_op | source)
XLA Modules:
  0.0 392.8 jit_solution(4862958445453425220)
XLA Ops:
  6.5 27.0 %shard_map.82 = bf16[8,24,4608]{2,1,0:T(8,128)(2,1)} custom-call(bf16[24,4608]{1,0:T(8,128)(2,1)} %w_ref.1), custom_call_target="tpu_custom_call" | custom-call | tf_op jit(solution)/shard_map/pallas_call | solution.py:275
  33.6 2.7 convert_reduce_fusion
  36.5 3.3 multiply_reduce_fusion
  40.5 4.9 %fusion.3.x_ref = bf16[640,3072]{1,0:T(8,128)(2,1)} fusion(bf16[2,4,80,3072]{3,2,1,0:T(8,128)(2,1)} %param.8, f32[3072]{0:T(1024)S(1)} %copy-done.6, f32[3072]{0:T(1024)S(1)} %broadcast_add_fusion.1, f32[640]{0:T(1024)S(1)} %rsqrt.12, f32[640]{0:T(1024)S(1)} %div.29), kind=kLoop, calls=%fused_computation.6 | loop fusion | flops 11796480 | bytes 7894016 | tf_op jit(solution)/shard_map/convert_element_type | solution.py:44
  45.4 153.0 %all-gather.2.cloned.1.call-done.w_ref = bf16[3072,4608]{1,0:T(8,128)(2,1)} async-done(((bf16[192,4608]{1,0:T(8,128)(2,1)}), bf16[3072,4608]{1,0:T(8,128)(2,1)}) %all-gather.2.cloned.1.call-update) | async-done | bytes 28311568 | tf_op jit(solution)/shard_map/all_gather | solution.py:66
  199.0 7.2 %shard_map.87 = bf16[640,768]{1,0:T(8,128)(2,1)} custom-call(bf16[640,3072]{1,0:T(8,128)(2,1)} %fusion.3.x_ref, bf16[3072,4608]{1,0:T(8,128)(2,1)} %all-gather.2.cloned.1.call-done.w_ref, f32[1,128]{1,0:T(1,128)} %broadcast_10_g_ref.2.g_ref), custom_call_target="tpu_custom_call" | custom-call | tf_op jit(solution)/shard_map/pallas_call | solution.py:216
  206.2 7.6 %shard_map.86 = bf16[640,768]{1,0:T(8,128)(2,1)} custom-call(bf16[640,3072]{1,0:T(8,128)(2,1)} %fusion.3.x_ref, bf16[3072,4608]{1,0:T(8,128)(2,1)} %all-gather.2.cloned.1.call-done.w_ref, f32[1,128]{1,0:T(1,128)} %bitcast.53), custom_call_target="tpu_custom_call" | custom-call | tf_op jit(solution)/shard_map/pallas_call | solution.py:216
  213.8 2.7 fusion.4
  218.6 7.0 %collective-permute-start.5 = (bf16[2,1,1,2,2,80,768]{6,5,4,3,1,0,2:T(8,128)(2,1)}, bf16[2,1,1,2,2,80,768]{6,5,4,3,1,0,2:T(8,128)(2,1)}, u32[]{:S(2)}, u32[]{:S(2)}) collective-permute-start(bf16[2,1,1,2,2,80,768]{6,5,4,3,1,0,2:T(8,128)(2,1)} %get-tuple-element.10), channel_id=1, source_target_pairs={{8,0},{16,8},{24,16},{32,24},{40,32},{48,40},{56,48},{64,56},{72,6... | collective-permute-start | bytes 2949128 | tf_op jit(solution)/shard_map/ppermute | solution.py:31
  225.9 7.3 %shard_map.85 = bf16[640,768]{1,0:T(8,128)(2,1)} custom-call(bf16[640,3072]{1,0:T(8,128)(2,1)} %fusion.3.x_ref, bf16[3072,4608]{1,0:T(8,128)(2,1)} %all-gather.2.cloned.1.call-done.w_ref, f32[1,128]{1,0:T(1,128)} %broadcast_10_g_ref.2.g_ref), custom_call_target="tpu_custom_call" | custom-call | tf_op jit(solution)/shard_map/pallas_call | solution.py:216
  233.2 7.5 %shard_map.84 = bf16[640,768]{1,0:T(8,128)(2,1)} custom-call(bf16[640,3072]{1,0:T(8,128)(2,1)} %fusion.3.x_ref, bf16[3072,4608]{1,0:T(8,128)(2,1)} %all-gather.2.cloned.1.call-done.w_ref, f32[1,128]{1,0:T(1,128)} %bitcast.54), custom_call_target="tpu_custom_call" | custom-call | tf_op jit(solution)/shard_map/pallas_call | solution.py:216
  240.7 2.7 fusion.5
  245.4 7.3 %collective-permute-start.1 = (bf16[2,1,1,2,2,80,768]{6,5,4,3,1,0,2:T(8,128)(2,1)}, bf16[2,1,1,2,2,80,768]{6,5,4,3,1,0,2:T(8,128)(2,1)}, u32[]{:S(2)}, u32[]{:S(2)}) collective-permute-start(bf16[2,1,1,2,2,80,768]{6,5,4,3,1,0,2:T(8,128)(2,1)} %get-tuple-element.12), channel_id=1, source_target_pairs={{8,0},{16,8},{24,16},{32,24},{40,32},{48,40},{56,48},{64,56},{72,6... | collective-permute-start | bytes 2949128 | tf_op jit(solution)/shard_map/ppermute | solution.py:31
  254.4 2.2 fusion.8
  256.7 3.5 collective-permute-start.6
  260.1 4.5 %collective-permute-start.7 = (bf16[2,4,1,1,2,80,768]{6,5,4,3,1,0,2:T(8,128)(2,1)}, bf16[2,4,1,1,2,80,768]{6,5,4,3,1,0,2:T(8,128)(2,1)}, u32[]{:S(2)}, u32[]{:S(2)}) collective-permute-start(bf16[2,4,1,1,2,80,768]{6,5,4,3,1,0,2:T(8,128)(2,1)} %get-tuple-element.6), channel_id=1, source_target_pairs={{1,0},{2,1},{3,2},{4,3},{5,4},{6,5},{7,6},{9,8},{10,9},{11,10},{12... | collective-permute-start | bytes 5898248 | tf_op jit(solution)/shard_map/ppermute | solution.py:31
  271.1 2.3 fusion.9
  275.3 8.4 %collective-permute-start.3 = (bf16[2,4,1,1,2,80,768]{6,5,4,3,1,0,2:T(8,128)(2,1)}, bf16[2,4,1,1,2,80,768]{6,5,4,3,1,0,2:T(8,128)(2,1)}, u32[]{:S(2)}, u32[]{:S(2)}) collective-permute-start(bf16[2,4,1,1,2,80,768]{6,5,4,3,1,0,2:T(8,128)(2,1)} %get-tuple-element.8), channel_id=1, source_target_pairs={{1,0},{2,1},{3,2},{4,3},{5,4},{6,5},{7,6},{9,8},{10,9},{11,10},{12... | collective-permute-start | bytes 5898248 | tf_op jit(solution)/shard_map/ppermute | solution.py:31
  286.3 11.7 %shard_map.83 = bf16[640,1536]{1,0:T(8,128)(2,1)} custom-call(bf16[640,3072]{1,0:T(8,128)(2,1)} %fusion.3.x_ref, bf16[3072,4608]{1,0:T(8,128)(2,1)} %all-gather.2.cloned.1.call-done.w_ref, f32[1,128]{1,0:T(1,128)} %bitcast.55), custom_call_target="tpu_custom_call" | custom-call | tf_op jit(solution)/shard_map/pallas_call | solution.py:216
  298.0 20.0 %collective-permute-done.6 = bf16[2,4,1,1,2,80,768]{6,5,4,3,1,0,2:T(8,128)(2,1)} collective-permute-done((bf16[2,4,1,1,2,80,768]{6,5,4,3,1,0,2:T(8,128)(2,1)}, bf16[2,4,1,1,2,80,768]{6,5,4,3,1,0,2:T(8,128)(2,1)}, u32[]{:S(2)}, u32[]{:S(2)}) %collective-permute-start.6) | collective-permute-done | bytes 1966112 | tf_op jit(solution)/shard_map/ppermute | solution.py:29
  318.0 6.5 %pad_maximum_fusion.1 = bf16[2,4,1,4,2,80,768]{6,5,4,3,1,0,2:T(8,128)(2,1)} fusion(bf16[2,4,1,1,2,80,768]{6,5,4,3,1,0,2:T(8,128)(2,1)} %collective-permute-done.7, bf16[2,1,1,2,2,80,768]{6,5,4,3,1,0,2:T(8,128)(2,1)} %collective-permute-done.5, bf16[1,2,1,2,2,80,768]{6,5,4,3,1,0,2:T(8,128)(2,1)S(1)} %bitcast.42, ...), kind=kLoop, calls=%fused_computation.1 | loop fusion | flops 19660800 | bytes 15728640 | tf_op jit(solution)/shard_map/concatenate | solution.py:27
  324.5 27.5 %shard_map.88.refs_8_ = bf16[2,4,80,1536]{3,2,1,0:T(8,128)(2,1)} custom-call(bf16[2,4,80,1536]{3,2,1,0:T(8,128)(2,1)} %bitcast.38, bf16[2,4,8,80,768]{4,3,2,1,0:T(8,128)(2,1)} %bitcast.34, bf16[2,4,8,80,768]{4,3,2,1,0:T(8,128)(2,1)} %bitcast.35, f32[12,4,1,1440]{3,2,1,0:T(1,128)} %and_convert_fusion.km_ref.refs_3_, ...), custom_call_target="tpu_custom_call" | custom-call | tf_op jit(solution)/shard_map/pallas_call | solution.py:187
  352.0 6.5 %pad_maximum_fusion = bf16[2,4,1,4,2,80,768]{6,5,4,3,1,0,2:T(8,128)(2,1)} fusion(bf16[2,4,1,1,2,80,768]{6,5,4,3,1,0,2:T(8,128)(2,1)} %collective-permute-done.3, bf16[2,1,1,2,2,80,768]{6,5,4,3,1,0,2:T(8,128)(2,1)} %collective-permute-done.1, bf16[1,2,1,2,2,80,768]{6,5,4,3,1,0,2:T(8,128)(2,1)S(1)} %bitcast.48, ...), kind=kLoop, calls=%fused_computation | loop fusion | flops 19660800 | bytes 15728640 | tf_op jit(solution)/shard_map/concatenate | solution.py:27
  358.5 27.5 %shard_map.89 = bf16[2,4,80,1536]{3,2,1,0:T(8,128)(2,1)} custom-call(bf16[2,4,80,1536]{3,2,1,0:T(8,128)(2,1)} %bitcast.39, bf16[2,4,8,80,768]{4,3,2,1,0:T(8,128)(2,1)} %bitcast.36, bf16[2,4,8,80,768]{4,3,2,1,0:T(8,128)(2,1)} %bitcast.37, f32[12,4,1,1440]{3,2,1,0:T(1,128)} %and_convert_fusion.km_ref.refs_3_, ...), custom_call_target="tpu_custom_call", output_to_operand_aliasing={{}: (8, {})} | custom-call | tf_op jit(solution)/shard_map/pallas_call | solution.py:187
  (63 shorter events, 18.4 us)
Async XLA Ops:
  6.5 191.9 %all-gather.2.cloned.1.call-start = ((), (), s32[]{:S(2)}) async-start(), calls=%async_computation | async-start | bytes 30081024 | tf_op jit(solution)/shard_map/all_gather | solution.py:66
  33.6 6.2 %copy-start.9 = (s32[12,3]{0,1:T(4,128)S(1)}, s32[12,3]{0,1:T(4,128)}, u32[]{:S(2)}) copy-start(s32[12,3]{0,1:T(4,128)} %param.14) | copy-start | bytes 436
  33.6 6.8 %copy-start.5 = (f32[3072]{0:T(1024)S(1)}, f32[3072]{0:T(1024)}, u32[]{:S(2)}) copy-start(f32[3072]{0:T(1024)} %param.9) | copy-start | bytes 36868
  33.6 6.8 %copy-start.6 = (f32[3072]{0:T(1024)S(1)}, f32[3072]{0:T(1024)}, u32[]{:S(2)}) copy-start(f32[3072]{0:T(1024)} %param.10) | copy-start | bytes 36868
  206.2 7.6 %copy-start = (bf16[640,768]{1,0:T(8,128)(2,1)S(1)}, bf16[640,768]{1,0:T(8,128)(2,1)}, u32[]{:S(2)}) copy-start(bf16[640,768]{1,0:T(8,128)(2,1)} %shard_map.87) | copy-start | bytes 2949124
  216.5 36.2 %collective-permute-start.4 = (bf16[2,1,1,2,2,80,768]{6,5,4,3,1,0,2:T(8,128)(2,1)}, bf16[2,1,1,2,2,80,768]{6,5,4,3,1,0,2:T(8,128)(2,1)}, u32[]{:S(2)}, u32[]{:S(2)}) collective-permute-start(bf16[2,1,1,2,2,80,768]{6,5,4,3,1,0,2:T(8,128)(2,1)} %get-tuple-element.9), channel_id=1, source_target_pairs={{0,8},{8,16},{16,24},{24,32},{32,40},{40,48},{48,56},{56,64},{64,7... | collective-permute-start | bytes 2949128 | tf_op jit(solution)/shard_map/ppermute | solution.py:29
  218.6 34.0 %collective-permute-start.5 = (bf16[2,1,1,2,2,80,768]{6,5,4,3,1,0,2:T(8,128)(2,1)}, bf16[2,1,1,2,2,80,768]{6,5,4,3,1,0,2:T(8,128)(2,1)}, u32[]{:S(2)}, u32[]{:S(2)}) collective-permute-start(bf16[2,1,1,2,2,80,768]{6,5,4,3,1,0,2:T(8,128)(2,1)} %get-tuple-element.10), channel_id=1, source_target_pairs={{8,0},{16,8},{24,16},{32,24},{40,32},{48,40},{56,48},{64,56},{72,6... | collective-permute-start | bytes 2949128 | tf_op jit(solution)/shard_map/ppermute | solution.py:31
  233.2 7.5 %copy-start.2 = (bf16[640,768]{1,0:T(8,128)(2,1)S(1)}, bf16[640,768]{1,0:T(8,128)(2,1)}, u32[]{:S(2)}) copy-start(bf16[640,768]{1,0:T(8,128)(2,1)} %shard_map.85) | copy-start | bytes 2949124
  240.7 11.9 %copy-start.1 = (bf16[640,768]{1,0:T(8,128)(2,1)S(1)}, bf16[640,768]{1,0:T(8,128)(2,1)}, u32[]{:S(2)}) copy-start(bf16[640,768]{1,0:T(8,128)(2,1)} %shard_map.86) | copy-start | bytes 2949124
  243.4 24.1 %collective-permute-start = (bf16[2,1,1,2,2,80,768]{6,5,4,3,1,0,2:T(8,128)(2,1)}, bf16[2,1,1,2,2,80,768]{6,5,4,3,1,0,2:T(8,128)(2,1)}, u32[]{:S(2)}, u32[]{:S(2)}) collective-permute-start(bf16[2,1,1,2,2,80,768]{6,5,4,3,1,0,2:T(8,128)(2,1)} %get-tuple-element.11), channel_id=1, source_target_pairs={{0,8},{8,16},{16,24},{24,32},{32,40},{40,48},{48,56},{56,64},{64,7... | collective-permute-start | bytes 2949128 | tf_op jit(solution)/shard_map/ppermute | solution.py:29
  245.4 23.7 %collective-permute-start.1 = (bf16[2,1,1,2,2,80,768]{6,5,4,3,1,0,2:T(8,128)(2,1)}, bf16[2,1,1,2,2,80,768]{6,5,4,3,1,0,2:T(8,128)(2,1)}, u32[]{:S(2)}, u32[]{:S(2)}) collective-permute-start(bf16[2,1,1,2,2,80,768]{6,5,4,3,1,0,2:T(8,128)(2,1)} %get-tuple-element.12), channel_id=1, source_target_pairs={{8,0},{16,8},{24,16},{32,24},{40,32},{48,40},{56,48},{64,56},{72,6... | collective-permute-start | bytes 2949128 | tf_op jit(solution)/shard_map/ppermute | solution.py:31
  254.4 11.8 %copy-start.4 = (s32[32,32,80]{2,1,0:T(8,128)S(1)}, s32[32,32,80]{2,1,0:T(8,128)}, u32[]{:S(2)}) copy-start(s32[32,32,80]{2,1,0:T(8,128)} %param.15) | copy-start | bytes 983044
  256.7 61.3 %collective-permute-start.6 = (bf16[2,4,1,1,2,80,768]{6,5,4,3,1,0,2:T(8,128)(2,1)}, bf16[2,4,1,1,2,80,768]{6,5,4,3,1,0,2:T(8,128)(2,1)}, u32[]{:S(2)}, u32[]{:S(2)}) collective-permute-start(bf16[2,4,1,1,2,80,768]{6,5,4,3,1,0,2:T(8,128)(2,1)} %get-tuple-element.5), channel_id=1, source_target_pairs={{0,1},{1,2},{2,3},{3,4},{4,5},{5,6},{6,7},{8,9},{9,10},{10,11},{11... | collective-permute-start | bytes 5898248 | tf_op jit(solution)/shard_map/ppermute | solution.py:29
  260.1 57.9 %collective-permute-start.7 = (bf16[2,4,1,1,2,80,768]{6,5,4,3,1,0,2:T(8,128)(2,1)}, bf16[2,4,1,1,2,80,768]{6,5,4,3,1,0,2:T(8,128)(2,1)}, u32[]{:S(2)}, u32[]{:S(2)}) collective-permute-start(bf16[2,4,1,1,2,80,768]{6,5,4,3,1,0,2:T(8,128)(2,1)} %get-tuple-element.6), channel_id=1, source_target_pairs={{1,0},{2,1},{3,2},{4,3},{5,4},{6,5},{7,6},{9,8},{10,9},{11,10},{12... | collective-permute-start | bytes 5898248 | tf_op jit(solution)/shard_map/ppermute | solution.py:31
  271.1 12.6 %copy-start.7 = (s32[160]{0:T(256)S(1)}, s32[160]{0:T(256)}, u32[]{:S(2)}) copy-start(s32[160]{0:T(256)} %sub.71) | copy-start | bytes 1924
  271.1 12.6 %copy-start.8 = (s32[12]{0:T(128)S(1)}, s32[12]{0:T(128)}, u32[]{:S(2)}) copy-start(s32[12]{0:T(128)} %get-tuple-element.17) | copy-start | bytes 148
  273.4 78.5 %collective-permute-start.2 = (bf16[2,4,1,1,2,80,768]{6,5,4,3,1,0,2:T(8,128)(2,1)}, bf16[2,4,1,1,2,80,768]{6,5,4,3,1,0,2:T(8,128)(2,1)}, u32[]{:S(2)}, u32[]{:S(2)}) collective-permute-start(bf16[2,4,1,1,2,80,768]{6,5,4,3,1,0,2:T(8,128)(2,1)} %get-tuple-element.7), channel_id=1, source_target_pairs={{0,1},{1,2},{2,3},{3,4},{4,5},{5,6},{6,7},{8,9},{9,10},{10,11},{11... | collective-permute-start | bytes 5898248 | tf_op jit(solution)/shard_map/ppermute | solution.py:29
  275.3 76.6 %collective-permute-start.3 = (bf16[2,4,1,1,2,80,768]{6,5,4,3,1,0,2:T(8,128)(2,1)}, bf16[2,4,1,1,2,80,768]{6,5,4,3,1,0,2:T(8,128)(2,1)}, u32[]{:S(2)}, u32[]{:S(2)}) collective-permute-start(bf16[2,4,1,1,2,80,768]{6,5,4,3,1,0,2:T(8,128)(2,1)} %get-tuple-element.8), channel_id=1, source_target_pairs={{1,0},{2,1},{3,2},{4,3},{5,4},{6,5},{7,6},{9,8},{10,9},{11,10},{12... | collective-permute-start | bytes 5898248 | tf_op jit(solution)/shard_map/ppermute | solution.py:31
  324.5 27.5 %copy-start.3 = (bf16[640,768]{1,0:T(8,128)(2,1)S(1)}, bf16[640,768]{1,0:T(8,128)(2,1)}, u32[]{:S(2)}) copy-start(bf16[640,768]{1,0:T(8,128)(2,1)} %shard_map.84) | copy-start | bytes 2949124
Sparse Core Ops, SparseCore 0:
  33.7 164.6 all-gather.1

commit v6 on v5

--- a/solution.py
+++ b/solution.py
@@ -94,102 +94,117 @@
     blocks = frame_count * row_tiles
     span_t = 2 * TT + 1
     span_h = 3 * TH
-    query_n = TH * width
-    key_n = span_t * span_h * width
-    block_valid = jnp.stack(
-        [
-            key_valid[f : f + span_t, TH * rt : TH * rt + span_h].reshape(-1)
-            for f in range(frame_count)
-            for rt in range(row_tiles)
-        ]
-    )
     apart_t = jnp.abs(jnp.arange(span_t, dtype=jnp.int32) - TT)
     apart_h = jnp.abs(jnp.arange(span_h, dtype=jnp.int32) // TH - 1)
     near = (apart_t[None, :, None, None] <= window[:, 0, None, None, None]) & (
         apart_h[None, None, :, None] <= window[:, 1, None, None, None]
     )
-    near = jnp.broadcast_to(near, (HEADS, span_t, span_h, width)).reshape(HEADS, 1, key_n)
-    key_mask = (near & (block_valid[None] > 0)).astype(jnp.float32).reshape(HEADS, blocks, 1, key_n)
     column_tiles = jnp.arange(width, dtype=jnp.int32) // TW
-    key_cols = jnp.tile(column_tiles, span_t * span_h).reshape(1, key_n)
-    query_cols = jnp.tile(column_tiles, TH)
-    query_lo = (query_cols[None, :] - window[:, 2, None]).reshape(HEADS, query_n, 1)
-    query_hi = (query_cols[None, :] + window[:, 2, None]).reshape(HEADS, query_n, 1)
-    query_ok = query_valid.reshape(blocks, query_n, 1).astype(jnp.float32)
+    masks = []
+    for q0, q1, k0, k1 in COLUMN_PARTS:
+        key_n = span_t * span_h * (k1 - k0)
+        query_n = TH * (q1 - q0)
+        block_valid = jnp.stack(
+            [
+                key_valid[f : f + span_t, TH * rt : TH * rt + span_h, k0:k1].reshape(-1)
+                for f in range(frame_count)
+                for rt in range(row_tiles)
+            ]
+        )
+        part_near = jnp.broadcast_to(near, (HEADS, span_t, span_h, k1 - k0)).reshape(HEADS, 1, key_n)
+        key_mask = (part_near & (block_valid[None] > 0)).astype(jnp.float32)
+        key_mask = key_mask.reshape(HEADS, blocks, 1, key_n)
+        key_cols = jnp.tile(column_tiles[k0:k1], span_t * span_h).reshape(1, key_n)
+        query_cols = jnp.tile(column_tiles[q0:q1], TH)
+        query_lo = (query_cols[None, :] - window[:, 2, None]).reshape(HEADS, query_n, 1)
+        query_hi = (query_cols[None, :] + window[:, 2, None]).reshape(HEADS, query_n, 1)
+        query_ok = query_valid[:, :, q0:q1].reshape(blocks, query_n, 1).astype(jnp.float32)
+        masks.append((key_mask, query_lo, query_hi, key_cols, query_ok))
     query_grid = query.reshape(frame_count, row_count, width, inner)
     out = None
     for group, extended in enumerate(groups):
         out = tile_attention(
-            query_grid, extended, key_mask, query_lo, query_hi, key_cols, query_ok, group, out
+            query_grid, extended, masks, group, out
         )
     return out
 
 
-def attention_kernel(q_ref, k_ref, v_ref, km_ref, lo_ref, hi_ref, kc_ref, qv_ref, o_ref):
+def attention_kernel(q_ref, k_ref, v_ref, *refs):
+    o_ref = refs[-1]
     block = pl.program_id(1)
     span_t = 2 * TT + 1
     span_h = 3 * TH
     frame = block // ROW_TILES
     row = (block % ROW_TILES) * TH
-    width = q_ref.shape[2]
-    query = q_ref[0].reshape(TH * width, HDIM)
-    key = k_ref[0, pl.ds(frame, span_t), pl.ds(row, span_h)].reshape(-1, HDIM)
-    value = v_ref[0, pl.ds(frame, span_t), pl.ds(row, span_h)].reshape(-1, HDIM)
-    scores = lax.dot_general(
-        query, key, (((1,), (1,)), ((), ())), preferred_element_type=jnp.float32
-    ) * (1.0 / float(HDIM) ** 0.5)
-    key_cols = kc_ref[...]
-    allowed = (key_cols >= lo_ref[0]) & (key_cols <= hi_ref[0]) & (km_ref[0, 0] > 0.0)
-    terms = jnp.where(allowed, jnp.exp(scores), jnp.float32(0.0))
-    total = jnp.sum(terms, axis=-1, keepdims=True)
-    seen = qv_ref[0] > 0.0
-    total = jnp.where(seen, total, jnp.float32(1.0))
-    weights = (terms / total).astype(jnp.bfloat16)
-    result = jnp.dot(weights, value, preferred_element_type=jnp.float32)
-    result = jnp.where(seen, result, jnp.float32(0.0)).astype(jnp.bfloat16)
-    o_ref[0] = result.reshape(TH, width, HDIM)
-
-
+    for part, (q0, q1, k0, k1) in enumerate(COLUMN_PARTS):
+        km_ref, lo_ref, hi_ref, kc_ref, qv_ref = refs[5 * part : 5 * part + 5]
+        query = q_ref[0, :, q0:q1].reshape(TH * (q1 - q0), HDIM)
+        key = k_ref[0, pl.ds(frame, span_t), pl.ds(row, span_h), k0:k1].reshape(-1, HDIM)
+        value = v_ref[0, pl.ds(frame, span_t), pl.ds(row, span_h), k0:k1].reshape(-1, HDIM)
+        scores = lax.dot_general(
+            query, key, (((1,), (1,)), ((), ())), preferred_element_type=jnp.float32
+        ) * (1.0 / float(HDIM) ** 0.5)
+        key_cols = kc_ref[...]
+        allowed = (key_cols >= lo_ref[0]) & (key_cols <= hi_ref[0]) & (km_ref[0, 0] > 0.0)
+        terms = jnp.where(allowed, jnp.exp(scores), jnp.float32(0.0))
+        total = jnp.sum(terms, axis=-1, keepdims=True)
+        seen = qv_ref[0] > 0.0
+        total = jnp.where(seen, total, jnp.float32(1.0))
+        weights = (terms / total).astype(jnp.bfloat16)
+        result = jnp.dot(weights, value, preferred_element_type=jnp.float32)
+        result = jnp.where(seen, result, jnp.float32(0.0)).astype(jnp.bfloat16)
+        o_ref[0, :, q0:q1] = result.reshape(TH, q1 - q0, HDIM)
+
+
+COLUMN_PARTS = ((0, 48, 0, 64), (48, 80, 32, 80))
 ROW_TILES = 2
 
 
-def tile_attention(query, extended, key_mask, query_lo, query_hi, key_cols, query_ok, group, out):
+def tile_attention(query, extended, masks, group, out):
     frames, rows, width, inner = query.shape
     heads = extended.shape[-1] // HDIM
+    out_shape = query.shape
     first = group * heads
     row_tiles = rows // TH
     assert row_tiles == ROW_TILES
+    assert COLUMN_PARTS[-1][1] == width
     blocks = frames * row_tiles
     _, frames_ext, rows_ext, _, _ = extended.shape
-    key_n = key_mask.shape[-1]
-    query_n = TH * width
     q_spec = pl.BlockSpec(
         (1, TH, width, HDIM), lambda h, b: (b // row_tiles, b % row_tiles, 0, first + h)
     )
+    o_spec = q_spec
     in_specs = [
         q_spec,
         pl.BlockSpec((1, frames_ext, rows_ext, width, HDIM), lambda h, b: (0, 0, 0, 0, h)),
         pl.BlockSpec((1, frames_ext, rows_ext, width, HDIM), lambda h, b: (1, 0, 0, 0, h)),
-        pl.BlockSpec((1, 1, 1, key_n), lambda h, b: (first + h, b, 0, 0)),
-        pl.BlockSpec((1, query_n, 1), lambda h, b: (first + h, 0, 0)),
-        pl.BlockSpec((1, query_n, 1), lambda h, b: (first + h, 0, 0)),
-        pl.BlockSpec((1, key_n), lambda h, b: (0, 0)),
-        pl.BlockSpec((1, query_n, 1), lambda h, b: (b, 0, 0)),
     ]
-    operands = [query, extended, extended, key_mask, query_lo, query_hi, key_cols, query_ok]
+    operands = [query, extended, extended]
+    for key_mask, query_lo, query_hi, key_cols, query_ok in masks:
+        key_n = key_mask.shape[-1]
+        query_n = query_lo.shape[1]
+        in_specs += [
+            pl.BlockSpec((1, 1, 1, key_n), lambda h, b: (first + h, b, 0, 0)),
+            pl.BlockSpec((1, query_n, 1), lambda h, b: (first + h, 0, 0)),
+            pl.BlockSpec((1, query_n, 1), lambda h, b: (first + h, 0, 0)),
+            pl.BlockSpec((1, key_n), lambda h, b: (0, 0)),
+            pl.BlockSpec((1, query_n, 1), lambda h, b: (b, 0, 0)),
+        ]
+        operands += [key_mask, query_lo, query_hi, key_cols, query_ok]
     aliases = {}
     kernel = attention_kernel
     if out is not None:
         in_specs.append(pl.BlockSpec(memory_space=pl.ANY))
         operands.append(out)
         aliases = {len(operands) - 1: 0}
-        kernel = lambda *refs: attention_kernel(*refs[:8], refs[9])
+        count = len(operands)
+        kernel = lambda *refs: attention_kernel(*refs[: count - 1], refs[count])
     return pl.pallas_call(
         kernel,
         grid=(heads, blocks),
         in_specs=in_specs,
-        out_specs=q_spec,
-        out_shape=jax.ShapeDtypeStruct(query.shape, jnp.bfloat16),
+        out_specs=o_spec,
+        out_shape=jax.ShapeDtypeStruct(out_shape, jnp.bfloat16),
         input_output_aliases=aliases,
     )(*operands)
 

time: 394 us -> 403 us (1.023)
  Pallas kernels: 123 us -> 129 us
    pallas_call x2, Pallas kernels: 55 us -> 60.4 us  [tile_attention(): pl.pallas_call(kernel, grid=(heads, blocks), in_specs=in_specs, out_specs...]
where the time goes in v6:
time: 403 us; the launch traced here: 401 us
  waiting for transfers between devices  175 us (43%)
  Pallas kernels  129 us (32%)
  other arithmetic  37.6 us (9%)
  starting transfers between devices  36.6 us (9%)
  between operations  13.7 us (3%)
  local copies, waits for them, and re-layouts  9.68 us (2%)
    all_gather x1, waiting for transfers between devices, per_device(): full_weight = lax.all_gather(band_weight, 'tm', axis=0, tiled=True)  152 us
    pallas_call x2, Pallas kernels, tile_attention(): pl.pallas_call(kernel, grid=(heads, blocks), in_specs=in_specs, out_specs...  60.4 us
    pallas_call x5, Pallas kernels, project(): pl.pallas_call(functools.partial(projection_kernel, normalize=normalize),...  41.3 us
    ppermute x4, starting transfers between devices, with_halo(): lax.ppermute(head, axis, [((i + 1) % count, i) for i in range(ends)])  27.1 us
    pallas_call x1, Pallas kernels, band_gather(): pl.pallas_call(band_gather_kernel, in_specs=[pl.BlockSpec(memory_space=pl...  27 us
    ppermute x4, waiting for transfers between devices, with_halo(): lax.ppermute(tail, axis, [(i, (i + 1) % count) for i in range(ends)])  20.4 us
    concatenate x4, other arithmetic, with_halo(): jnp.concatenate([lax.ppermute(tail, axis, [(i, (i + 1) % count) for i in...  16.9 us
    ppermute x4, starting transfers between devices, with_halo(): lax.ppermute(tail, axis, [(i, (i + 1) % count) for i in range(ends)])  9.43 us
  transfers between devices with their start and end apart: 9, of which 3 were waited for; matrix products, arithmetic and copies ran while one was open for 9% of the time, Pallas kernels for 14%

profile of v6, /device:TPU:6, one launch (start us, length us, event | category | flops | bytes accessed | tf_op | source)
XLA Modules:
  0.0 401.1 jit_solution(3270938633595196148)
XLA Ops:
  6.5 27.0 %shard_map.82 = bf16[8,24,4608]{2,1,0:T(8,128)(2,1)} custom-call(bf16[24,4608]{1,0:T(8,128)(2,1)} %w_ref.1), custom_call_target="tpu_custom_call" | custom-call | tf_op jit(solution)/shard_map/pallas_call | solution.py:290
  34.0 2.8 convert_reduce_fusion
  36.8 3.3 multiply_reduce_fusion
  41.8 4.9 %fusion.3.x_ref = bf16[640,3072]{1,0:T(8,128)(2,1)} fusion(bf16[2,4,80,3072]{3,2,1,0:T(8,128)(2,1)} %param.8, f32[3072]{0:T(1024)S(1)} %copy-done.6, f32[3072]{0:T(1024)S(1)} %broadcast_add_fusion.2, f32[640]{0:T(1024)S(1)} %rsqrt.12, f32[640]{0:T(1024)S(1)} %div.37), kind=kLoop, calls=%fused_computation.6 | loop fusion | flops 11796480 | bytes 7894016 | tf_op jit(solution)/shard_map/convert_element_type | solution.py:44
  46.7 151.7 %all-gather.2.cloned.1.call-done.w_ref = bf16[3072,4608]{1,0:T(8,128)(2,1)} async-done(((bf16[192,4608]{1,0:T(8,128)(2,1)}), bf16[3072,4608]{1,0:T(8,128)(2,1)}) %all-gather.2.cloned.1.call-update) | async-done | bytes 28311568 | tf_op jit(solution)/shard_map/all_gather | solution.py:66
  198.9 7.2 %shard_map.87 = bf16[640,768]{1,0:T(8,128)(2,1)} custom-call(bf16[640,3072]{1,0:T(8,128)(2,1)} %fusion.3.x_ref, bf16[3072,4608]{1,0:T(8,128)(2,1)} %all-gather.2.cloned.1.call-done.w_ref, f32[1,128]{1,0:T(1,128)} %broadcast_10_g_ref.2.g_ref), custom_call_target="tpu_custom_call" | custom-call | tf_op jit(solution)/shard_map/pallas_call | solution.py:231
  206.1 7.6 %shard_map.86 = bf16[640,768]{1,0:T(8,128)(2,1)} custom-call(bf16[640,3072]{1,0:T(8,128)(2,1)} %fusion.3.x_ref, bf16[3072,4608]{1,0:T(8,128)(2,1)} %all-gather.2.cloned.1.call-done.w_ref, f32[1,128]{1,0:T(1,128)} %bitcast.55), custom_call_target="tpu_custom_call" | custom-call | tf_op jit(solution)/shard_map/pallas_call | solution.py:231
  213.7 2.7 fusion.4
  218.6 7.0 %collective-permute-start.5 = (bf16[2,1,1,2,2,80,768]{6,5,4,3,1,0,2:T(8,128)(2,1)}, bf16[2,1,1,2,2,80,768]{6,5,4,3,1,0,2:T(8,128)(2,1)}, u32[]{:S(2)}, u32[]{:S(2)}) collective-permute-start(bf16[2,1,1,2,2,80,768]{6,5,4,3,1,0,2:T(8,128)(2,1)} %get-tuple-element.10), channel_id=1, source_target_pairs={{8,0},{16,8},{24,16},{32,24},{40,32},{48,40},{56,48},{64,56},{72,6... | collective-permute-start | bytes 2949128 | tf_op jit(solution)/shard_map/ppermute | solution.py:31
  228.7 7.2 %shard_map.85 = bf16[640,768]{1,0:T(8,128)(2,1)} custom-call(bf16[640,3072]{1,0:T(8,128)(2,1)} %fusion.3.x_ref, bf16[3072,4608]{1,0:T(8,128)(2,1)} %all-gather.2.cloned.1.call-done.w_ref, f32[1,128]{1,0:T(1,128)} %broadcast_10_g_ref.2.g_ref), custom_call_target="tpu_custom_call" | custom-call | tf_op jit(solution)/shard_map/pallas_call | solution.py:231
  235.9 7.6 %shard_map.84 = bf16[640,768]{1,0:T(8,128)(2,1)} custom-call(bf16[640,3072]{1,0:T(8,128)(2,1)} %fusion.3.x_ref, bf16[3072,4608]{1,0:T(8,128)(2,1)} %all-gather.2.cloned.1.call-done.w_ref, f32[1,128]{1,0:T(1,128)} %bitcast.56), custom_call_target="tpu_custom_call" | custom-call | tf_op jit(solution)/shard_map/pallas_call | solution.py:231
  243.5 2.7 fusion.5
  248.1 7.3 %collective-permute-start.1 = (bf16[2,1,1,2,2,80,768]{6,5,4,3,1,0,2:T(8,128)(2,1)}, bf16[2,1,1,2,2,80,768]{6,5,4,3,1,0,2:T(8,128)(2,1)}, u32[]{:S(2)}, u32[]{:S(2)}) collective-permute-start(bf16[2,1,1,2,2,80,768]{6,5,4,3,1,0,2:T(8,128)(2,1)} %get-tuple-element.12), channel_id=1, source_target_pairs={{8,0},{16,8},{24,16},{32,24},{40,32},{48,40},{56,48},{64,56},{72,6... | collective-permute-start | bytes 2949128 | tf_op jit(solution)/shard_map/ppermute | solution.py:31
  259.4 3.5 collective-permute-start.6
  262.9 4.5 %collective-permute-start.7 = (bf16[2,4,1,1,2,80,768]{6,5,4,3,1,0,2:T(8,128)(2,1)}, bf16[2,4,1,1,2,80,768]{6,5,4,3,1,0,2:T(8,128)(2,1)}, u32[]{:S(2)}, u32[]{:S(2)}) collective-permute-start(bf16[2,4,1,1,2,80,768]{6,5,4,3,1,0,2:T(8,128)(2,1)} %get-tuple-element.6), channel_id=1, source_target_pairs={{1,0},{2,1},{3,2},{4,3},{5,4},{6,5},{7,6},{9,8},{10,9},{11,10},{12... | collective-permute-start | bytes 5898248 | tf_op jit(solution)/shard_map/ppermute | solution.py:31
  269.3 2.6 collective-permute-done.1
  273.9 2.3 fusion.9
  278.1 8.4 %collective-permute-start.3 = (bf16[2,4,1,1,2,80,768]{6,5,4,3,1,0,2:T(8,128)(2,1)}, bf16[2,4,1,1,2,80,768]{6,5,4,3,1,0,2:T(8,128)(2,1)}, u32[]{:S(2)}, u32[]{:S(2)}) collective-permute-start(bf16[2,4,1,1,2,80,768]{6,5,4,3,1,0,2:T(8,128)(2,1)} %get-tuple-element.8), channel_id=1, source_target_pairs={{1,0},{2,1},{3,2},{4,3},{5,4},{6,5},{7,6},{9,8},{10,9},{11,10},{12... | collective-permute-start | bytes 5898248 | tf_op jit(solution)/shard_map/ppermute | solution.py:31
  288.6 11.7 %shard_map.83 = bf16[640,1536]{1,0:T(8,128)(2,1)} custom-call(bf16[640,3072]{1,0:T(8,128)(2,1)} %fusion.3.x_ref, bf16[3072,4608]{1,0:T(8,128)(2,1)} %all-gather.2.cloned.1.call-done.w_ref, f32[1,128]{1,0:T(1,128)} %bitcast.57), custom_call_target="tpu_custom_call" | custom-call | tf_op jit(solution)/shard_map/pallas_call | solution.py:231
  300.3 20.4 %collective-permute-done.6 = bf16[2,4,1,1,2,80,768]{6,5,4,3,1,0,2:T(8,128)(2,1)} collective-permute-done((bf16[2,4,1,1,2,80,768]{6,5,4,3,1,0,2:T(8,128)(2,1)}, bf16[2,4,1,1,2,80,768]{6,5,4,3,1,0,2:T(8,128)(2,1)}, u32[]{:S(2)}, u32[]{:S(2)}) %collective-permute-start.6) | collective-permute-done | bytes 1966112 | tf_op jit(solution)/shard_map/ppermute | solution.py:29
  320.8 6.5 %pad_maximum_fusion.1 = bf16[2,4,1,4,2,80,768]{6,5,4,3,1,0,2:T(8,128)(2,1)} fusion(bf16[2,4,1,1,2,80,768]{6,5,4,3,1,0,2:T(8,128)(2,1)} %collective-permute-done.7, bf16[2,1,1,2,2,80,768]{6,5,4,3,1,0,2:T(8,128)(2,1)} %collective-permute-done.5, bf16[1,2,1,2,2,80,768]{6,5,4,3,1,0,2:T(8,128)(2,1)S(1)} %bitcast.43, ...), kind=kLoop, calls=%fused_computation.1 | loop fusion | flops 19660800 | bytes 15728640 | tf_op jit(solution)/shard_map/concatenate | solution.py:27
  327.3 30.1 %shard_map.88.refs_13_ = bf16[2,4,80,1536]{3,2,1,0:T(8,128)(2,1)} custom-call(bf16[2,4,80,1536]{3,2,1,0:T(8,128)(2,1)} %bitcast.39, bf16[2,4,8,80,768]{4,3,2,1,0:T(8,128)(2,1)} %bitcast.35, bf16[2,4,8,80,768]{4,3,2,1,0:T(8,128)(2,1)} %bitcast.36, f32[12,4,1,1152]{3,2,1,0:T(1,128)} %and_convert_fusion.refs_0_.refs_3_, ...), custom_call_target="tpu_custom_call" | custom-call | tf_op jit(solution)/shard_map/pallas_call | solution.py:202
  357.4 6.5 %pad_maximum_fusion = bf16[2,4,1,4,2,80,768]{6,5,4,3,1,0,2:T(8,128)(2,1)} fusion(bf16[2,4,1,1,2,80,768]{6,5,4,3,1,0,2:T(8,128)(2,1)} %collective-permute-done.3, bf16[2,1,1,2,2,80,768]{6,5,4,3,1,0,2:T(8,128)(2,1)} %collective-permute-done.1, bf16[1,2,1,2,2,80,768]{6,5,4,3,1,0,2:T(8,128)(2,1)S(1)} %bitcast.49, ...), kind=kLoop, calls=%fused_computation | loop fusion | flops 19660800 | bytes 15728640 | tf_op jit(solution)/shard_map/concatenate | solution.py:27
  363.9 30.3 %shard_map.89 = bf16[2,4,80,1536]{3,2,1,0:T(8,128)(2,1)} custom-call(bf16[2,4,80,1536]{3,2,1,0:T(8,128)(2,1)} %bitcast.40, bf16[2,4,8,80,768]{4,3,2,1,0:T(8,128)(2,1)} %bitcast.37, bf16[2,4,8,80,768]{4,3,2,1,0:T(8,128)(2,1)} %bitcast.38, f32[12,4,1,1152]{3,2,1,0:T(1,128)} %and_convert_fusion.refs_0_.refs_3_, ...), custom_call_target="tpu_custom_call", output_to_operand_aliasing={{}: (13, {})} | custom-call | tf_op jit(solution)/shard_map/pallas_call | solution.py:202
  (77 shorter events, 21.6 us)
Async XLA Ops:
  6.5 191.9 %all-gather.2.cloned.1.call-start = ((), (), s32[]{:S(2)}) async-start(), calls=%async_computation | async-start | bytes 30081024 | tf_op jit(solution)/shard_map/all_gather | solution.py:66
  34.0 7.6 %copy-start.7 = (s32[12,3]{0,1:T(4,128)S(1)}, s32[12,3]{0,1:T(4,128)}, u32[]{:S(2)}) copy-start(s32[12,3]{0,1:T(4,128)} %param.14) | copy-start | bytes 436
  34.0 7.8 %copy-start.5 = (f32[3072]{0:T(1024)S(1)}, f32[3072]{0:T(1024)}, u32[]{:S(2)}) copy-start(f32[3072]{0:T(1024)} %param.9) | copy-start | bytes 36868
  34.0 7.8 %copy-start.6 = (f32[3072]{0:T(1024)S(1)}, f32[3072]{0:T(1024)}, u32[]{:S(2)}) copy-start(f32[3072]{0:T(1024)} %param.10) | copy-start | bytes 36868
  206.1 7.6 %copy-start = (bf16[640,768]{1,0:T(8,128)(2,1)S(1)}, bf16[640,768]{1,0:T(8,128)(2,1)}, u32[]{:S(2)}) copy-start(bf16[640,768]{1,0:T(8,128)(2,1)} %shard_map.87) | copy-start | bytes 2949124
  213.7 12.5 %copy-start.4 = (s32[32,32,80]{2,1,0:T(8,128)S(1)}, s32[32,32,80]{2,1,0:T(8,128)}, u32[]{:S(2)}) copy-start(s32[32,32,80]{2,1,0:T(8,128)} %param.15) | copy-start | bytes 983044
  216.4 39.0 %collective-permute-start.4 = (bf16[2,1,1,2,2,80,768]{6,5,4,3,1,0,2:T(8,128)(2,1)}, bf16[2,1,1,2,2,80,768]{6,5,4,3,1,0,2:T(8,128)(2,1)}, u32[]{:S(2)}, u32[]{:S(2)}) collective-permute-start(bf16[2,1,1,2,2,80,768]{6,5,4,3,1,0,2:T(8,128)(2,1)} %get-tuple-element.9), channel_id=1, source_target_pairs={{0,8},{8,16},{16,24},{24,32},{32,40},{40,48},{48,56},{56,64},{64,7... | collective-permute-start | bytes 2949128 | tf_op jit(solution)/shard_map/ppermute | solution.py:29
  218.6 36.8 %collective-permute-start.5 = (bf16[2,1,1,2,2,80,768]{6,5,4,3,1,0,2:T(8,128)(2,1)}, bf16[2,1,1,2,2,80,768]{6,5,4,3,1,0,2:T(8,128)(2,1)}, u32[]{:S(2)}, u32[]{:S(2)}) collective-permute-start(bf16[2,1,1,2,2,80,768]{6,5,4,3,1,0,2:T(8,128)(2,1)} %get-tuple-element.10), channel_id=1, source_target_pairs={{8,0},{16,8},{24,16},{32,24},{40,32},{48,40},{56,48},{64,56},{72,6... | collective-permute-start | bytes 2949128 | tf_op jit(solution)/shard_map/ppermute | solution.py:31
  235.9 7.6 %copy-start.2 = (bf16[640,768]{1,0:T(8,128)(2,1)S(1)}, bf16[640,768]{1,0:T(8,128)(2,1)}, u32[]{:S(2)}) copy-start(bf16[640,768]{1,0:T(8,128)(2,1)} %shard_map.85) | copy-start | bytes 2949124
  243.5 11.9 %copy-start.1 = (bf16[640,768]{1,0:T(8,128)(2,1)S(1)}, bf16[640,768]{1,0:T(8,128)(2,1)}, u32[]{:S(2)}) copy-start(bf16[640,768]{1,0:T(8,128)(2,1)} %shard_map.86) | copy-start | bytes 2949124
  246.2 23.0 %collective-permute-start = (bf16[2,1,1,2,2,80,768]{6,5,4,3,1,0,2:T(8,128)(2,1)}, bf16[2,1,1,2,2,80,768]{6,5,4,3,1,0,2:T(8,128)(2,1)}, u32[]{:S(2)}, u32[]{:S(2)}) collective-permute-start(bf16[2,1,1,2,2,80,768]{6,5,4,3,1,0,2:T(8,128)(2,1)} %get-tuple-element.11), channel_id=1, source_target_pairs={{0,8},{8,16},{16,24},{24,32},{32,40},{40,48},{48,56},{56,64},{64,7... | collective-permute-start | bytes 2949128 | tf_op jit(solution)/shard_map/ppermute | solution.py:29
  248.1 23.7 %collective-permute-start.1 = (bf16[2,1,1,2,2,80,768]{6,5,4,3,1,0,2:T(8,128)(2,1)}, bf16[2,1,1,2,2,80,768]{6,5,4,3,1,0,2:T(8,128)(2,1)}, u32[]{:S(2)}, u32[]{:S(2)}) collective-permute-start(bf16[2,1,1,2,2,80,768]{6,5,4,3,1,0,2:T(8,128)(2,1)} %get-tuple-element.12), channel_id=1, source_target_pairs={{8,0},{16,8},{24,16},{32,24},{40,32},{48,40},{56,48},{64,56},{72,6... | collective-permute-start | bytes 2949128 | tf_op jit(solution)/shard_map/ppermute | solution.py:31
  259.4 61.3 %collective-permute-start.6 = (bf16[2,4,1,1,2,80,768]{6,5,4,3,1,0,2:T(8,128)(2,1)}, bf16[2,4,1,1,2,80,768]{6,5,4,3,1,0,2:T(8,128)(2,1)}, u32[]{:S(2)}, u32[]{:S(2)}) collective-permute-start(bf16[2,4,1,1,2,80,768]{6,5,4,3,1,0,2:T(8,128)(2,1)} %get-tuple-element.5), channel_id=1, source_target_pairs={{0,1},{1,2},{2,3},{3,4},{4,5},{5,6},{6,7},{8,9},{9,10},{10,11},{11... | collective-permute-start | bytes 5898248 | tf_op jit(solution)/shard_map/ppermute | solution.py:29
  262.9 57.9 %collective-permute-start.7 = (bf16[2,4,1,1,2,80,768]{6,5,4,3,1,0,2:T(8,128)(2,1)}, bf16[2,4,1,1,2,80,768]{6,5,4,3,1,0,2:T(8,128)(2,1)}, u32[]{:S(2)}, u32[]{:S(2)}) collective-permute-start(bf16[2,4,1,1,2,80,768]{6,5,4,3,1,0,2:T(8,128)(2,1)} %get-tuple-element.6), channel_id=1, source_target_pairs={{1,0},{2,1},{3,2},{4,3},{5,4},{6,5},{7,6},{9,8},{10,9},{11,10},{12... | collective-permute-start | bytes 5898248 | tf_op jit(solution)/shard_map/ppermute | solution.py:31
  276.2 81.2 %collective-permute-start.2 = (bf16[2,4,1,1,2,80,768]{6,5,4,3,1,0,2:T(8,128)(2,1)}, bf16[2,4,1,1,2,80,768]{6,5,4,3,1,0,2:T(8,128)(2,1)}, u32[]{:S(2)}, u32[]{:S(2)}) collective-permute-start(bf16[2,4,1,1,2,80,768]{6,5,4,3,1,0,2:T(8,128)(2,1)} %get-tuple-element.7), channel_id=1, source_target_pairs={{0,1},{1,2},{2,3},{3,4},{4,5},{5,6},{6,7},{8,9},{9,10},{10,11},{11... | collective-permute-start | bytes 5898248 | tf_op jit(solution)/shard_map/ppermute | solution.py:29
  278.1 79.3 %collective-permute-start.3 = (bf16[2,4,1,1,2,80,768]{6,5,4,3,1,0,2:T(8,128)(2,1)}, bf16[2,4,1,1,2,80,768]{6,5,4,3,1,0,2:T(8,128)(2,1)}, u32[]{:S(2)}, u32[]{:S(2)}) collective-permute-start(bf16[2,4,1,1,2,80,768]{6,5,4,3,1,0,2:T(8,128)(2,1)} %get-tuple-element.8), channel_id=1, source_target_pairs={{1,0},{2,1},{3,2},{4,3},{5,4},{6,5},{7,6},{9,8},{10,9},{11,10},{12... | collective-permute-start | bytes 5898248 | tf_op jit(solution)/shard_map/ppermute | solution.py:31
  327.3 30.1 %copy-start.3 = (bf16[640,768]{1,0:T(8,128)(2,1)S(1)}, bf16[640,768]{1,0:T(8,128)(2,1)}, u32[]{:S(2)}) copy-start(bf16[640,768]{1,0:T(8,128)(2,1)} %shard_map.84) | copy-start | bytes 2949124
Sparse Core Ops, SparseCore 0:
  33.7 164.6 all-gather.1

commit v7 on v5

--- a/solution.py
+++ b/solution.py
@@ -70,9 +70,8 @@
     groups = []
     for group in range(GROUPS):
         start = group * group_cols
-        key = project(modulated, full_weight, inner + start, group_cols, k_gain)
-        value = project(modulated, full_weight, 2 * inner + start, group_cols, None)
-        stacked = jnp.stack([key.reshape(tiled), value.reshape(tiled)])
+        stacked = project_kv(modulated, full_weight, start, group_cols, k_gain)
+        stacked = stacked.reshape(2, *tiled)
         groups.append(with_halo(stacked, (("tm", 1), ("height", 3)), 1))
     query = project(modulated, full_weight, 0, inner, q_gain)
     frames_ext = frame_count + 2 * TT
@@ -287,6 +286,42 @@
     return gathered.reshape(count * rows, cols)
 
 
+def projection_kv_kernel(x_ref, w_ref, g_ref, o_ref):
+    acc = jnp.dot(x_ref[...], w_ref[...], preferred_element_type=jnp.float32)
+    is_key = pl.program_id(0) < pl.num_programs(0) // 2
+    for part in range(acc.shape[1] // HDIM):
+        piece = acc[:, part * HDIM : (part + 1) * HDIM]
+        power = jnp.mean(piece * piece, axis=-1, keepdims=True)
+        scale = jnp.where(is_key, lax.rsqrt(power + EPS), jnp.float32(1.0))
+        gain = jnp.where(is_key, g_ref[...], jnp.float32(1.0))
+        normed = jnp.where(is_key, piece * scale * gain, piece)
+        o_ref[0, :, part * HDIM : (part + 1) * HDIM] = normed.astype(o_ref.dtype)
+
+
+def project_kv(x, w, start, count, gain):
+    tokens, features = x.shape
+    cols = PROJECT_COLS
+    inner = w.shape[1] // 3
+    steps = count // cols
+    key_first = (inner + start) // cols
+    value_first = (2 * inner + start) // cols
+
+    def weight_block(j):
+        return (0, jnp.where(j < steps, key_first + j, value_first + j - steps))
+
+    return pl.pallas_call(
+        projection_kv_kernel,
+        grid=(2 * steps,),
+        in_specs=[
+            pl.BlockSpec((tokens, features), lambda j: (0, 0)),
+            pl.BlockSpec((features, cols), weight_block),
+            pl.BlockSpec((1, HDIM), lambda j: (0, 0)),
+        ],
+        out_specs=pl.BlockSpec((1, tokens, cols), lambda j: (j // steps, 0, j % steps)),
+        out_shape=jax.ShapeDtypeStruct((2, tokens, count), jnp.bfloat16),
+    )(x, w, gain.reshape(1, HDIM))
+
+
 def solution(mesh):
     in_specs = (
         P("tm", "height", None, None),

time: 394 us -> 388 us (0.985)
  Pallas kernels: 123 us -> 117 us
  other arithmetic: 35.9 us -> 30.3 us
  local copies, waits for them, and re-layouts: 8.69 us -> 14.1 us
    pallas_call x5 -> x1, Pallas kernels: 41.3 us -> 11.7 us  [project(): pl.pallas_call(functools.partial(projection_kernel, normalize=normalize),...]
    pallas_call x0 -> x2, Pallas kernels: none -> 23.6 us  [project_kv(): pl.pallas_call(projection_kv_kernel, grid=(2 * steps,), in_specs=[pl.Bloc...]
    slice x2 -> x4, local copies, waits for them, and re-layouts: 4.48 us -> 10.4 us  [with_halo(): lax.slice_in_dim(cells, cells.shape[dim] - width, cells.shape[dim], axis=...]
    another operation x2 -> x0, other arithmetic: 5.38 us -> none  [per_device(): stacked = jnp.stack([key.reshape(tiled), value.reshape(tiled)])]
  transfers between devices with their start and end apart: 9 -> 9, of which waited for: 3 -> 4; matrix products, arithmetic and copies ran while one was open for 9% -> 9% of each run, Pallas kernels for 14% -> 13%
where the time goes in v7:
time: 388 us; the launch traced here: 386 us
  waiting for transfers between devices  175 us (45%)
  Pallas kernels  117 us (30%)
  starting transfers between devices  36.4 us (9%)
  other arithmetic  30.3 us (8%)
  local copies, waits for them, and re-layouts  14.1 us (4%)
  between operations  13.7 us (4%)
    all_gather x1, waiting for transfers between devices, per_device(): full_weight = lax.all_gather(band_weight, 'tm', axis=0, tiled=True)  153 us
    pallas_call x2, Pallas kernels, tile_attention(): pl.pallas_call(kernel, grid=(heads, blocks), in_specs=in_specs, out_specs...  55 us
    pallas_call x1, Pallas kernels, band_gather(): pl.pallas_call(band_gather_kernel, in_specs=[pl.BlockSpec(memory_space=pl...  27 us
    ppermute x4, starting transfers between devices, with_halo(): lax.ppermute(head, axis, [((i + 1) % count, i) for i in range(ends)])  27 us
    pallas_call x2, Pallas kernels, project_kv(): pl.pallas_call(projection_kv_kernel, grid=(2 * steps,), in_specs=[pl.Bloc...  23.6 us
    ppermute x4, waiting for transfers between devices, with_halo(): lax.ppermute(tail, axis, [(i, (i + 1) % count) for i in range(ends)])  19.8 us
    concatenate x4, other arithmetic, with_halo(): jnp.concatenate([lax.ppermute(tail, axis, [(i, (i + 1) % count) for i in...  16.6 us
    pallas_call x1, Pallas kernels, project(): pl.pallas_call(functools.partial(projection_kernel, normalize=normalize),...  11.7 us
  transfers between devices with their start and end apart: 9, of which 4 were waited for; matrix products, arithmetic and copies ran while one was open for 9% of the time, Pallas kernels for 13%

profile of v7, /device:TPU:6, one launch (start us, length us, event | category | flops | bytes accessed | tf_op | source)
XLA Modules:
  0.0 386.3 jit_solution(4809131793724847376)
XLA Ops:
  6.5 27.0 %shard_map.82 = bf16[8,24,4608]{2,1,0:T(8,128)(2,1)} custom-call(bf16[24,4608]{1,0:T(8,128)(2,1)} %w_ref.1), custom_call_target="tpu_custom_call" | custom-call | tf_op jit(solution)/shard_map/pallas_call | solution.py:274
  33.6 2.7 convert_reduce_fusion
  36.5 3.3 multiply_reduce_fusion
  40.5 4.9 %fusion.3.x_ref = bf16[640,3072]{1,0:T(8,128)(2,1)} fusion(bf16[2,4,80,3072]{3,2,1,0:T(8,128)(2,1)} %param.8, f32[3072]{0:T(1024)S(1)} %copy-done.4, f32[3072]{0:T(1024)S(1)} %broadcast_add_fusion.1, f32[640]{0:T(1024)S(1)} %rsqrt.12, f32[640]{0:T(1024)S(1)} %div.29), kind=kLoop, calls=%fused_computation.6 | loop fusion | flops 11796480 | bytes 7894016 | tf_op jit(solution)/shard_map/convert_element_type | solution.py:44
  45.4 153.0 %all-gather.2.cloned.1.call-done.w_ref = bf16[3072,4608]{1,0:T(8,128)(2,1)} async-done(((bf16[192,4608]{1,0:T(8,128)(2,1)}), bf16[3072,4608]{1,0:T(8,128)(2,1)}) %all-gather.2.cloned.1.call-update) | async-done | bytes 28311568 | tf_op jit(solution)/shard_map/all_gather | solution.py:66
  198.4 11.7 %shard_map.85 = bf16[2,640,768]{2,1,0:T(8,128)(2,1)} custom-call(bf16[640,3072]{1,0:T(8,128)(2,1)} %fusion.3.x_ref, bf16[3072,4608]{1,0:T(8,128)(2,1)} %all-gather.2.cloned.1.call-done.w_ref, f32[1,128]{1,0:T(1,128)} %bitcast.37), custom_call_target="tpu_custom_call" | custom-call | tf_op jit(solution)/shard_map/pallas_call | solution.py:312
  210.1 2.9 fusion.8
  213.1 2.2 collective-permute-start.4
  215.2 7.0 %collective-permute-start.5 = (bf16[2,1,1,2,2,80,768]{6,5,4,3,1,0,2:T(8,128)(2,1)}, bf16[2,1,1,2,2,80,768]{6,5,4,3,1,0,2:T(8,128)(2,1)}, u32[]{:S(2)}, u32[]{:S(2)}) collective-permute-start(bf16[2,1,1,2,2,80,768]{6,5,4,3,1,0,2:T(8,128)(2,1)} %get-tuple-element.10), channel_id=1, source_target_pairs={{8,0},{16,8},{24,16},{32,24},{40,32},{48,40},{56,48},{64,56},{72,6... | collective-permute-start | bytes 2949128 | tf_op jit(solution)/shard_map/ppermute | solution.py:31
  222.4 11.8 %shard_map.84 = bf16[2,640,768]{2,1,0:T(8,128)(2,1)} custom-call(bf16[640,3072]{1,0:T(8,128)(2,1)} %fusion.3.x_ref, bf16[3072,4608]{1,0:T(8,128)(2,1)} %all-gather.2.cloned.1.call-done.w_ref, f32[1,128]{1,0:T(1,128)} %bitcast.38), custom_call_target="tpu_custom_call" | custom-call | tf_op jit(solution)/shard_map/pallas_call | solution.py:312
  234.3 3.0 fusion.9
  239.2 7.3 %collective-permute-start.1 = (bf16[2,1,1,2,2,80,768]{6,5,4,3,1,0,2:T(8,128)(2,1)}, bf16[2,1,1,2,2,80,768]{6,5,4,3,1,0,2:T(8,128)(2,1)}, u32[]{:S(2)}, u32[]{:S(2)}) collective-permute-start(bf16[2,1,1,2,2,80,768]{6,5,4,3,1,0,2:T(8,128)(2,1)} %get-tuple-element.12), channel_id=1, source_target_pairs={{8,0},{16,8},{24,16},{32,24},{40,32},{48,40},{56,48},{64,56},{72,6... | collective-permute-start | bytes 2949128 | tf_op jit(solution)/shard_map/ppermute | solution.py:31
  249.4 2.2 fusion.6
  251.6 3.5 collective-permute-start.6
  255.0 4.5 %collective-permute-start.7 = (bf16[2,4,1,1,2,80,768]{6,5,4,3,1,0,2:T(8,128)(2,1)}, bf16[2,4,1,1,2,80,768]{6,5,4,3,1,0,2:T(8,128)(2,1)}, u32[]{:S(2)}, u32[]{:S(2)}) collective-permute-start(bf16[2,4,1,1,2,80,768]{6,5,4,3,1,0,2:T(8,128)(2,1)} %get-tuple-element.6), channel_id=1, source_target_pairs={{1,0},{2,1},{3,2},{4,3},{5,4},{6,5},{7,6},{9,8},{10,9},{11,10},{12... | collective-permute-start | bytes 5898248 | tf_op jit(solution)/shard_map/ppermute | solution.py:31
  261.9 2.3 pad_maximum_fusion.2
  264.2 2.3 fusion.7
  268.4 8.2 %collective-permute-start.3 = (bf16[2,4,1,1,2,80,768]{6,5,4,3,1,0,2:T(8,128)(2,1)}, bf16[2,4,1,1,2,80,768]{6,5,4,3,1,0,2:T(8,128)(2,1)}, u32[]{:S(2)}, u32[]{:S(2)}) collective-permute-start(bf16[2,4,1,1,2,80,768]{6,5,4,3,1,0,2:T(8,128)(2,1)} %get-tuple-element.8), channel_id=1, source_target_pairs={{1,0},{2,1},{3,2},{4,3},{5,4},{6,5},{7,6},{9,8},{10,9},{11,10},{12... | collective-permute-start | bytes 5898248 | tf_op jit(solution)/shard_map/ppermute | solution.py:31
  280.1 11.7 %shard_map.83 = bf16[640,1536]{1,0:T(8,128)(2,1)} custom-call(bf16[640,3072]{1,0:T(8,128)(2,1)} %fusion.3.x_ref, bf16[3072,4608]{1,0:T(8,128)(2,1)} %all-gather.2.cloned.1.call-done.w_ref, f32[1,128]{1,0:T(1,128)} %bitcast.39), custom_call_target="tpu_custom_call" | custom-call | tf_op jit(solution)/shard_map/pallas_call | solution.py:215
  291.8 19.0 %collective-permute-done.6 = bf16[2,4,1,1,2,80,768]{6,5,4,3,1,0,2:T(8,128)(2,1)} collective-permute-done((bf16[2,4,1,1,2,80,768]{6,5,4,3,1,0,2:T(8,128)(2,1)}, bf16[2,4,1,1,2,80,768]{6,5,4,3,1,0,2:T(8,128)(2,1)}, u32[]{:S(2)}, u32[]{:S(2)}) %collective-permute-start.6) | collective-permute-done | bytes 1966112 | tf_op jit(solution)/shard_map/ppermute | solution.py:29
  310.8 6.3 %pad_maximum_fusion.1 = bf16[2,4,1,4,2,80,768]{6,5,4,3,1,0,2:T(8,128)(2,1)} fusion(bf16[2,4,1,1,2,80,768]{6,5,4,3,1,0,2:T(8,128)(2,1)} %collective-permute-done.7, bf16[2,1,1,2,2,80,768]{6,5,4,3,1,0,2:T(8,128)(2,1)} %collective-permute-done.5, bf16[2,2,1,2,2,80,768]{6,5,4,3,1,0,2:T(8,128)(2,1)S(1)} %bitcast.30, ...), kind=kLoop, calls=%fused_computation.1 | loop fusion | flops 15728640 | bytes 15728640 | tf_op jit(solution)/shard_map/concatenate | solution.py:27
  317.1 27.5 %shard_map.86.refs_8_ = bf16[2,4,80,1536]{3,2,1,0:T(8,128)(2,1)} custom-call(bf16[2,4,80,1536]{3,2,1,0:T(8,128)(2,1)} %bitcast.34, bf16[2,4,8,80,768]{4,3,2,1,0:T(8,128)(2,1)} %bitcast.24, bf16[2,4,8,80,768]{4,3,2,1,0:T(8,128)(2,1)} %bitcast.25, f32[12,4,1,1440]{3,2,1,0:T(1,128)} %and_convert_fusion.km_ref.refs_3_, ...), custom_call_target="tpu_custom_call" | custom-call | tf_op jit(solution)/shard_map/pallas_call | solution.py:186
  345.5 6.5 %pad_maximum_fusion = bf16[2,4,1,4,2,80,768]{6,5,4,3,1,0,2:T(8,128)(2,1)} fusion(bf16[2,4,1,1,2,80,768]{6,5,4,3,1,0,2:T(8,128)(2,1)} %collective-permute-done.3, bf16[2,1,1,2,2,80,768]{6,5,4,3,1,0,2:T(8,128)(2,1)} %collective-permute-done.1, bf16[2,2,1,2,2,80,768]{6,5,4,3,1,0,2:T(8,128)(2,1)S(1)} %bitcast.33, ...), kind=kLoop, calls=%fused_computation | loop fusion | flops 15728640 | bytes 15728640 | tf_op jit(solution)/shard_map/concatenate | solution.py:27
  352.0 27.5 %shard_map.87 = bf16[2,4,80,1536]{3,2,1,0:T(8,128)(2,1)} custom-call(bf16[2,4,80,1536]{3,2,1,0:T(8,128)(2,1)} %bitcast.35, bf16[2,4,8,80,768]{4,3,2,1,0:T(8,128)(2,1)} %bitcast.26, bf16[2,4,8,80,768]{4,3,2,1,0:T(8,128)(2,1)} %bitcast.27, f32[12,4,1,1440]{3,2,1,0:T(1,128)} %and_convert_fusion.km_ref.refs_3_, ...), custom_call_target="tpu_custom_call", output_to_operand_aliasing={{}: (8, {})} | custom-call | tf_op jit(solution)/shard_map/pallas_call | solution.py:186
  (56 shorter events, 14.3 us)
Async XLA Ops:
  6.5 191.9 %all-gather.2.cloned.1.call-start = ((), (), s32[]{:S(2)}) async-start(), calls=%async_computation | async-start | bytes 30081024 | tf_op jit(solution)/shard_map/all_gather | solution.py:66
  33.6 6.2 %copy-start.7 = (s32[12,3]{0,1:T(4,128)S(1)}, s32[12,3]{0,1:T(4,128)}, u32[]{:S(2)}) copy-start(s32[12,3]{0,1:T(4,128)} %param.14) | copy-start | bytes 436
  33.6 6.8 %copy-start.3 = (f32[3072]{0:T(1024)S(1)}, f32[3072]{0:T(1024)}, u32[]{:S(2)}) copy-start(f32[3072]{0:T(1024)} %param.9) | copy-start | bytes 36868
  33.6 6.8 %copy-start.4 = (f32[3072]{0:T(1024)S(1)}, f32[3072]{0:T(1024)}, u32[]{:S(2)}) copy-start(f32[3072]{0:T(1024)} %param.10) | copy-start | bytes 36868
  213.1 34.8 %collective-permute-start.4 = (bf16[2,1,1,2,2,80,768]{6,5,4,3,1,0,2:T(8,128)(2,1)}, bf16[2,1,1,2,2,80,768]{6,5,4,3,1,0,2:T(8,128)(2,1)S(1)}, u32[]{:S(2)}, u32[]{:S(2)}) collective-permute-start(bf16[2,1,1,2,2,80,768]{6,5,4,3,1,0,2:T(8,128)(2,1)} %get-tuple-element.9), channel_id=1, source_target_pairs={{0,8},{8,16},{16,24},{24,32},{32,40},{40,48},{48,56},{56,64},{64,7... | collective-permute-start | bytes 2949128 | tf_op jit(solution)/shard_map/ppermute | solution.py:29
  215.2 32.6 %collective-permute-start.5 = (bf16[2,1,1,2,2,80,768]{6,5,4,3,1,0,2:T(8,128)(2,1)}, bf16[2,1,1,2,2,80,768]{6,5,4,3,1,0,2:T(8,128)(2,1)}, u32[]{:S(2)}, u32[]{:S(2)}) collective-permute-start(bf16[2,1,1,2,2,80,768]{6,5,4,3,1,0,2:T(8,128)(2,1)} %get-tuple-element.10), channel_id=1, source_target_pairs={{8,0},{16,8},{24,16},{32,24},{40,32},{48,40},{56,48},{64,56},{72,6... | collective-permute-start | bytes 2949128 | tf_op jit(solution)/shard_map/ppermute | solution.py:31
  234.3 13.6 %copy-start = (bf16[2,640,768]{2,1,0:T(8,128)(2,1)S(1)}, bf16[2,640,768]{2,1,0:T(8,128)(2,1)}, u32[]{:S(2)}) copy-start(bf16[2,640,768]{2,1,0:T(8,128)(2,1)} %shard_map.85) | copy-start | bytes 5898244
  237.3 23.0 %collective-permute-start = (bf16[2,1,1,2,2,80,768]{6,5,4,3,1,0,2:T(8,128)(2,1)}, bf16[2,1,1,2,2,80,768]{6,5,4,3,1,0,2:T(8,128)(2,1)}, u32[]{:S(2)}, u32[]{:S(2)}) collective-permute-start(bf16[2,1,1,2,2,80,768]{6,5,4,3,1,0,2:T(8,128)(2,1)} %get-tuple-element.11), channel_id=1, source_target_pairs={{0,8},{8,16},{16,24},{24,32},{32,40},{40,48},{48,56},{56,64},{64,7... | collective-permute-start | bytes 2949128 | tf_op jit(solution)/shard_map/ppermute | solution.py:29
  239.2 22.7 %collective-permute-start.1 = (bf16[2,1,1,2,2,80,768]{6,5,4,3,1,0,2:T(8,128)(2,1)}, bf16[2,1,1,2,2,80,768]{6,5,4,3,1,0,2:T(8,128)(2,1)}, u32[]{:S(2)}, u32[]{:S(2)}) collective-permute-start(bf16[2,1,1,2,2,80,768]{6,5,4,3,1,0,2:T(8,128)(2,1)} %get-tuple-element.12), channel_id=1, source_target_pairs={{8,0},{16,8},{24,16},{32,24},{40,32},{48,40},{56,48},{64,56},{72,6... | collective-permute-start | bytes 2949128 | tf_op jit(solution)/shard_map/ppermute | solution.py:31
  249.4 10.5 %copy-start.2 = (s32[32,32,80]{2,1,0:T(8,128)S(1)}, s32[32,32,80]{2,1,0:T(8,128)}, u32[]{:S(2)}) copy-start(s32[32,32,80]{2,1,0:T(8,128)} %param.15) | copy-start | bytes 983044
  251.6 59.2 %collective-permute-start.6 = (bf16[2,4,1,1,2,80,768]{6,5,4,3,1,0,2:T(8,128)(2,1)}, bf16[2,4,1,1,2,80,768]{6,5,4,3,1,0,2:T(8,128)(2,1)}, u32[]{:S(2)}, u32[]{:S(2)}) collective-permute-start(bf16[2,4,1,1,2,80,768]{6,5,4,3,1,0,2:T(8,128)(2,1)} %get-tuple-element.5), channel_id=1, source_target_pairs={{0,1},{1,2},{2,3},{3,4},{4,5},{5,6},{6,7},{8,9},{9,10},{10,11},{11... | collective-permute-start | bytes 5898248 | tf_op jit(solution)/shard_map/ppermute | solution.py:29
  255.0 55.8 %collective-permute-start.7 = (bf16[2,4,1,1,2,80,768]{6,5,4,3,1,0,2:T(8,128)(2,1)}, bf16[2,4,1,1,2,80,768]{6,5,4,3,1,0,2:T(8,128)(2,1)}, u32[]{:S(2)}, u32[]{:S(2)}) collective-permute-start(bf16[2,4,1,1,2,80,768]{6,5,4,3,1,0,2:T(8,128)(2,1)} %get-tuple-element.6), channel_id=1, source_target_pairs={{1,0},{2,1},{3,2},{4,3},{5,4},{6,5},{7,6},{9,8},{10,9},{11,10},{12... | collective-permute-start | bytes 5898248 | tf_op jit(solution)/shard_map/ppermute | solution.py:31
  264.2 13.4 %copy-start.5 = (s32[160]{0:T(256)S(1)}, s32[160]{0:T(256)}, u32[]{:S(2)}) copy-start(s32[160]{0:T(256)} %sub.71) | copy-start | bytes 1924
  264.2 13.4 %copy-start.6 = (s32[12]{0:T(128)S(1)}, s32[12]{0:T(128)}, u32[]{:S(2)}) copy-start(s32[12]{0:T(128)} %get-tuple-element.17) | copy-start | bytes 148
  266.5 79.0 %collective-permute-start.2 = (bf16[2,4,1,1,2,80,768]{6,5,4,3,1,0,2:T(8,128)(2,1)}, bf16[2,4,1,1,2,80,768]{6,5,4,3,1,0,2:T(8,128)(2,1)}, u32[]{:S(2)}, u32[]{:S(2)}) collective-permute-start(bf16[2,4,1,1,2,80,768]{6,5,4,3,1,0,2:T(8,128)(2,1)} %get-tuple-element.7), channel_id=1, source_target_pairs={{0,1},{1,2},{2,3},{3,4},{4,5},{5,6},{6,7},{8,9},{9,10},{10,11},{11... | collective-permute-start | bytes 5898248 | tf_op jit(solution)/shard_map/ppermute | solution.py:29
  268.4 77.0 %collective-permute-start.3 = (bf16[2,4,1,1,2,80,768]{6,5,4,3,1,0,2:T(8,128)(2,1)}, bf16[2,4,1,1,2,80,768]{6,5,4,3,1,0,2:T(8,128)(2,1)}, u32[]{:S(2)}, u32[]{:S(2)}) collective-permute-start(bf16[2,4,1,1,2,80,768]{6,5,4,3,1,0,2:T(8,128)(2,1)} %get-tuple-element.8), channel_id=1, source_target_pairs={{1,0},{2,1},{3,2},{4,3},{5,4},{6,5},{7,6},{9,8},{10,9},{11,10},{12... | collective-permute-start | bytes 5898248 | tf_op jit(solution)/shard_map/ppermute | solution.py:31
  317.1 28.4 %copy-start.1 = (bf16[2,640,768]{2,1,0:T(8,128)(2,1)S(1)}, bf16[2,640,768]{2,1,0:T(8,128)(2,1)}, u32[]{:S(2)}) copy-start(bf16[2,640,768]{2,1,0:T(8,128)(2,1)} %shard_map.84) | copy-start | bytes 5898244
Sparse Core Ops, SparseCore 0:
  33.7 164.6 all-gather.1

commit v8 on v7

--- a/solution.py
+++ b/solution.py
@@ -143,7 +143,7 @@
     total = jnp.sum(terms, axis=-1, keepdims=True)
     seen = qv_ref[0] > 0.0
     total = jnp.where(seen, total, jnp.float32(1.0))
-    weights = (terms / total).astype(jnp.bfloat16)
+    weights = (terms * (1.0 / total)).astype(jnp.bfloat16)
     result = jnp.dot(weights, value, preferred_element_type=jnp.float32)
     result = jnp.where(seen, result, jnp.float32(0.0)).astype(jnp.bfloat16)
     o_ref[0] = result.reshape(TH, width, HDIM)

time: 388 us -> 388 us (level)
  no operation moved by 1% of the time
where the time goes in v8:
time: 388 us; the launch traced here: 386 us
  waiting for transfers between devices  175 us (45%)
  Pallas kernels  117 us (30%)
  starting transfers between devices  36.4 us (9%)
  other arithmetic  30.3 us (8%)
  local copies, waits for them, and re-layouts  14.1 us (4%)
  between operations  13.7 us (4%)
    all_gather x1, waiting for transfers between devices, per_device(): full_weight = lax.all_gather(band_weight, 'tm', axis=0, tiled=True)  153 us
    pallas_call x2, Pallas kernels, tile_attention(): pl.pallas_call(kernel, grid=(heads, blocks), in_specs=in_specs, out_specs...  54.3 us
    pallas_call x1, Pallas kernels, band_gather(): pl.pallas_call(band_gather_kernel, in_specs=[pl.BlockSpec(memory_space=pl...  27 us
    ppermute x4, starting transfers between devices, with_halo(): lax.ppermute(head, axis, [((i + 1) % count, i) for i in range(ends)])  27 us
    pallas_call x2, Pallas kernels, project_kv(): pl.pallas_call(projection_kv_kernel, grid=(2 * steps,), in_specs=[pl.Bloc...  23.6 us
    ppermute x4, waiting for transfers between devices, with_halo(): lax.ppermute(tail, axis, [(i, (i + 1) % count) for i in range(ends)])  20.2 us
    concatenate x4, other arithmetic, with_halo(): jnp.concatenate([lax.ppermute(tail, axis, [(i, (i + 1) % count) for i in...  16.6 us
    pallas_call x1, Pallas kernels, project(): pl.pallas_call(functools.partial(projection_kernel, normalize=normalize),...  11.7 us
  transfers between devices with their start and end apart: 9, of which 4 were waited for; matrix products, arithmetic and copies ran while one was open for 9% of the time, Pallas kernels for 13%

profile of v8, /device:TPU:6, one launch (start us, length us, event | category | flops | bytes accessed | tf_op | source)
XLA Modules:
  0.0 386.0 jit_solution(3902787425126593180)
XLA Ops:
  6.5 27.0 %shard_map.82 = bf16[8,24,4608]{2,1,0:T(8,128)(2,1)} custom-call(bf16[24,4608]{1,0:T(8,128)(2,1)} %w_ref.1), custom_call_target="tpu_custom_call" | custom-call | tf_op jit(solution)/shard_map/pallas_call | solution.py:274
  33.6 2.7 convert_reduce_fusion
  36.5 3.3 multiply_reduce_fusion
  40.5 4.9 %fusion.3.x_ref = bf16[640,3072]{1,0:T(8,128)(2,1)} fusion(bf16[2,4,80,3072]{3,2,1,0:T(8,128)(2,1)} %param.8, f32[3072]{0:T(1024)S(1)} %copy-done.4, f32[3072]{0:T(1024)S(1)} %broadcast_add_fusion.1, f32[640]{0:T(1024)S(1)} %rsqrt.12, f32[640]{0:T(1024)S(1)} %div.29), kind=kLoop, calls=%fused_computation.6 | loop fusion | flops 11796480 | bytes 7894016 | tf_op jit(solution)/shard_map/convert_element_type | solution.py:44
  45.4 153.0 %all-gather.2.cloned.1.call-done.w_ref = bf16[3072,4608]{1,0:T(8,128)(2,1)} async-done(((bf16[192,4608]{1,0:T(8,128)(2,1)}), bf16[3072,4608]{1,0:T(8,128)(2,1)}) %all-gather.2.cloned.1.call-update) | async-done | bytes 28311568 | tf_op jit(solution)/shard_map/all_gather | solution.py:66
  198.4 11.7 %shard_map.85 = bf16[2,640,768]{2,1,0:T(8,128)(2,1)} custom-call(bf16[640,3072]{1,0:T(8,128)(2,1)} %fusion.3.x_ref, bf16[3072,4608]{1,0:T(8,128)(2,1)} %all-gather.2.cloned.1.call-done.w_ref, f32[1,128]{1,0:T(1,128)} %bitcast.37), custom_call_target="tpu_custom_call" | custom-call | tf_op jit(solution)/shard_map/pallas_call | solution.py:312
  210.1 2.9 fusion.8
  213.1 2.2 collective-permute-start.4
  215.2 7.0 %collective-permute-start.5 = (bf16[2,1,1,2,2,80,768]{6,5,4,3,1,0,2:T(8,128)(2,1)}, bf16[2,1,1,2,2,80,768]{6,5,4,3,1,0,2:T(8,128)(2,1)}, u32[]{:S(2)}, u32[]{:S(2)}) collective-permute-start(bf16[2,1,1,2,2,80,768]{6,5,4,3,1,0,2:T(8,128)(2,1)} %get-tuple-element.10), channel_id=1, source_target_pairs={{8,0},{16,8},{24,16},{32,24},{40,32},{48,40},{56,48},{64,56},{72,6... | collective-permute-start | bytes 2949128 | tf_op jit(solution)/shard_map/ppermute | solution.py:31
  222.4 11.8 %shard_map.84 = bf16[2,640,768]{2,1,0:T(8,128)(2,1)} custom-call(bf16[640,3072]{1,0:T(8,128)(2,1)} %fusion.3.x_ref, bf16[3072,4608]{1,0:T(8,128)(2,1)} %all-gather.2.cloned.1.call-done.w_ref, f32[1,128]{1,0:T(1,128)} %bitcast.38), custom_call_target="tpu_custom_call" | custom-call | tf_op jit(solution)/shard_map/pallas_call | solution.py:312
  234.3 3.0 fusion.9
  239.2 7.3 %collective-permute-start.1 = (bf16[2,1,1,2,2,80,768]{6,5,4,3,1,0,2:T(8,128)(2,1)}, bf16[2,1,1,2,2,80,768]{6,5,4,3,1,0,2:T(8,128)(2,1)}, u32[]{:S(2)}, u32[]{:S(2)}) collective-permute-start(bf16[2,1,1,2,2,80,768]{6,5,4,3,1,0,2:T(8,128)(2,1)} %get-tuple-element.12), channel_id=1, source_target_pairs={{8,0},{16,8},{24,16},{32,24},{40,32},{48,40},{56,48},{64,56},{72,6... | collective-permute-start | bytes 2949128 | tf_op jit(solution)/shard_map/ppermute | solution.py:31
  249.4 2.2 fusion.6
  251.6 3.5 collective-permute-start.6
  255.0 4.5 %collective-permute-start.7 = (bf16[2,4,1,1,2,80,768]{6,5,4,3,1,0,2:T(8,128)(2,1)}, bf16[2,4,1,1,2,80,768]{6,5,4,3,1,0,2:T(8,128)(2,1)}, u32[]{:S(2)}, u32[]{:S(2)}) collective-permute-start(bf16[2,4,1,1,2,80,768]{6,5,4,3,1,0,2:T(8,128)(2,1)} %get-tuple-element.6), channel_id=1, source_target_pairs={{1,0},{2,1},{3,2},{4,3},{5,4},{6,5},{7,6},{9,8},{10,9},{11,10},{12... | collective-permute-start | bytes 5898248 | tf_op jit(solution)/shard_map/ppermute | solution.py:31
  261.9 2.3 pad_maximum_fusion.2
  264.2 2.3 fusion.7
  268.4 8.2 %collective-permute-start.3 = (bf16[2,4,1,1,2,80,768]{6,5,4,3,1,0,2:T(8,128)(2,1)}, bf16[2,4,1,1,2,80,768]{6,5,4,3,1,0,2:T(8,128)(2,1)}, u32[]{:S(2)}, u32[]{:S(2)}) collective-permute-start(bf16[2,4,1,1,2,80,768]{6,5,4,3,1,0,2:T(8,128)(2,1)} %get-tuple-element.8), channel_id=1, source_target_pairs={{1,0},{2,1},{3,2},{4,3},{5,4},{6,5},{7,6},{9,8},{10,9},{11,10},{12... | collective-permute-start | bytes 5898248 | tf_op jit(solution)/shard_map/ppermute | solution.py:31
  280.1 11.7 %shard_map.83 = bf16[640,1536]{1,0:T(8,128)(2,1)} custom-call(bf16[640,3072]{1,0:T(8,128)(2,1)} %fusion.3.x_ref, bf16[3072,4608]{1,0:T(8,128)(2,1)} %all-gather.2.cloned.1.call-done.w_ref, f32[1,128]{1,0:T(1,128)} %bitcast.39), custom_call_target="tpu_custom_call" | custom-call | tf_op jit(solution)/shard_map/pallas_call | solution.py:215
  291.8 19.0 %collective-permute-done.6 = bf16[2,4,1,1,2,80,768]{6,5,4,3,1,0,2:T(8,128)(2,1)} collective-permute-done((bf16[2,4,1,1,2,80,768]{6,5,4,3,1,0,2:T(8,128)(2,1)}, bf16[2,4,1,1,2,80,768]{6,5,4,3,1,0,2:T(8,128)(2,1)}, u32[]{:S(2)}, u32[]{:S(2)}) %collective-permute-start.6) | collective-permute-done | bytes 1966112 | tf_op jit(solution)/shard_map/ppermute | solution.py:29
  310.8 6.3 %pad_maximum_fusion.1 = bf16[2,4,1,4,2,80,768]{6,5,4,3,1,0,2:T(8,128)(2,1)} fusion(bf16[2,4,1,1,2,80,768]{6,5,4,3,1,0,2:T(8,128)(2,1)} %collective-permute-done.7, bf16[2,1,1,2,2,80,768]{6,5,4,3,1,0,2:T(8,128)(2,1)} %collective-permute-done.5, bf16[2,2,1,2,2,80,768]{6,5,4,3,1,0,2:T(8,128)(2,1)S(1)} %bitcast.30, ...), kind=kLoop, calls=%fused_computation.1 | loop fusion | flops 15728640 | bytes 15728640 | tf_op jit(solution)/shard_map/concatenate | solution.py:27
  317.1 27.1 %shard_map.86.refs_8_ = bf16[2,4,80,1536]{3,2,1,0:T(8,128)(2,1)} custom-call(bf16[2,4,80,1536]{3,2,1,0:T(8,128)(2,1)} %bitcast.34, bf16[2,4,8,80,768]{4,3,2,1,0:T(8,128)(2,1)} %bitcast.24, bf16[2,4,8,80,768]{4,3,2,1,0:T(8,128)(2,1)} %bitcast.25, f32[12,4,1,1440]{3,2,1,0:T(1,128)} %and_convert_fusion.km_ref.refs_3_, ...), custom_call_target="tpu_custom_call" | custom-call | tf_op jit(solution)/shard_map/pallas_call | solution.py:186
  345.5 6.5 %pad_maximum_fusion = bf16[2,4,1,4,2,80,768]{6,5,4,3,1,0,2:T(8,128)(2,1)} fusion(bf16[2,4,1,1,2,80,768]{6,5,4,3,1,0,2:T(8,128)(2,1)} %collective-permute-done.3, bf16[2,1,1,2,2,80,768]{6,5,4,3,1,0,2:T(8,128)(2,1)} %collective-permute-done.1, bf16[2,2,1,2,2,80,768]{6,5,4,3,1,0,2:T(8,128)(2,1)S(1)} %bitcast.33, ...), kind=kLoop, calls=%fused_computation | loop fusion | flops 15728640 | bytes 15728640 | tf_op jit(solution)/shard_map/concatenate | solution.py:27
  352.0 27.2 %shard_map.87 = bf16[2,4,80,1536]{3,2,1,0:T(8,128)(2,1)} custom-call(bf16[2,4,80,1536]{3,2,1,0:T(8,128)(2,1)} %bitcast.35, bf16[2,4,8,80,768]{4,3,2,1,0:T(8,128)(2,1)} %bitcast.26, bf16[2,4,8,80,768]{4,3,2,1,0:T(8,128)(2,1)} %bitcast.27, f32[12,4,1,1440]{3,2,1,0:T(1,128)} %and_convert_fusion.km_ref.refs_3_, ...), custom_call_target="tpu_custom_call", output_to_operand_aliasing={{}: (8, {})} | custom-call | tf_op jit(solution)/shard_map/pallas_call | solution.py:186
  (56 shorter events, 14.7 us)
Async XLA Ops:
  6.5 191.9 %all-gather.2.cloned.1.call-start = ((), (), s32[]{:S(2)}) async-start(), calls=%async_computation | async-start | bytes 30081024 | tf_op jit(solution)/shard_map/all_gather | solution.py:66
  33.6 6.2 %copy-start.7 = (s32[12,3]{0,1:T(4,128)S(1)}, s32[12,3]{0,1:T(4,128)}, u32[]{:S(2)}) copy-start(s32[12,3]{0,1:T(4,128)} %param.14) | copy-start | bytes 436
  33.6 6.8 %copy-start.3 = (f32[3072]{0:T(1024)S(1)}, f32[3072]{0:T(1024)}, u32[]{:S(2)}) copy-start(f32[3072]{0:T(1024)} %param.9) | copy-start | bytes 36868
  33.6 6.8 %copy-start.4 = (f32[3072]{0:T(1024)S(1)}, f32[3072]{0:T(1024)}, u32[]{:S(2)}) copy-start(f32[3072]{0:T(1024)} %param.10) | copy-start | bytes 36868
  213.1 34.8 %collective-permute-start.4 = (bf16[2,1,1,2,2,80,768]{6,5,4,3,1,0,2:T(8,128)(2,1)}, bf16[2,1,1,2,2,80,768]{6,5,4,3,1,0,2:T(8,128)(2,1)S(1)}, u32[]{:S(2)}, u32[]{:S(2)}) collective-permute-start(bf16[2,1,1,2,2,80,768]{6,5,4,3,1,0,2:T(8,128)(2,1)} %get-tuple-element.9), channel_id=1, source_target_pairs={{0,8},{8,16},{16,24},{24,32},{32,40},{40,48},{48,56},{56,64},{64,7... | collective-permute-start | bytes 2949128 | tf_op jit(solution)/shard_map/ppermute | solution.py:29
  215.2 32.6 %collective-permute-start.5 = (bf16[2,1,1,2,2,80,768]{6,5,4,3,1,0,2:T(8,128)(2,1)}, bf16[2,1,1,2,2,80,768]{6,5,4,3,1,0,2:T(8,128)(2,1)}, u32[]{:S(2)}, u32[]{:S(2)}) collective-permute-start(bf16[2,1,1,2,2,80,768]{6,5,4,3,1,0,2:T(8,128)(2,1)} %get-tuple-element.10), channel_id=1, source_target_pairs={{8,0},{16,8},{24,16},{32,24},{40,32},{48,40},{56,48},{64,56},{72,6... | collective-permute-start | bytes 2949128 | tf_op jit(solution)/shard_map/ppermute | solution.py:31
  234.3 13.6 %copy-start = (bf16[2,640,768]{2,1,0:T(8,128)(2,1)S(1)}, bf16[2,640,768]{2,1,0:T(8,128)(2,1)}, u32[]{:S(2)}) copy-start(bf16[2,640,768]{2,1,0:T(8,128)(2,1)} %shard_map.85) | copy-start | bytes 5898244
  237.3 23.0 %collective-permute-start = (bf16[2,1,1,2,2,80,768]{6,5,4,3,1,0,2:T(8,128)(2,1)}, bf16[2,1,1,2,2,80,768]{6,5,4,3,1,0,2:T(8,128)(2,1)}, u32[]{:S(2)}, u32[]{:S(2)}) collective-permute-start(bf16[2,1,1,2,2,80,768]{6,5,4,3,1,0,2:T(8,128)(2,1)} %get-tuple-element.11), channel_id=1, source_target_pairs={{0,8},{8,16},{16,24},{24,32},{32,40},{40,48},{48,56},{56,64},{64,7... | collective-permute-start | bytes 2949128 | tf_op jit(solution)/shard_map/ppermute | solution.py:29
  239.2 22.7 %collective-permute-start.1 = (bf16[2,1,1,2,2,80,768]{6,5,4,3,1,0,2:T(8,128)(2,1)}, bf16[2,1,1,2,2,80,768]{6,5,4,3,1,0,2:T(8,128)(2,1)}, u32[]{:S(2)}, u32[]{:S(2)}) collective-permute-start(bf16[2,1,1,2,2,80,768]{6,5,4,3,1,0,2:T(8,128)(2,1)} %get-tuple-element.12), channel_id=1, source_target_pairs={{8,0},{16,8},{24,16},{32,24},{40,32},{48,40},{56,48},{64,56},{72,6... | collective-permute-start | bytes 2949128 | tf_op jit(solution)/shard_map/ppermute | solution.py:31
  249.4 10.5 %copy-start.2 = (s32[32,32,80]{2,1,0:T(8,128)S(1)}, s32[32,32,80]{2,1,0:T(8,128)}, u32[]{:S(2)}) copy-start(s32[32,32,80]{2,1,0:T(8,128)} %param.15) | copy-start | bytes 983044
  251.6 59.2 %collective-permute-start.6 = (bf16[2,4,1,1,2,80,768]{6,5,4,3,1,0,2:T(8,128)(2,1)}, bf16[2,4,1,1,2,80,768]{6,5,4,3,1,0,2:T(8,128)(2,1)}, u32[]{:S(2)}, u32[]{:S(2)}) collective-permute-start(bf16[2,4,1,1,2,80,768]{6,5,4,3,1,0,2:T(8,128)(2,1)} %get-tuple-element.5), channel_id=1, source_target_pairs={{0,1},{1,2},{2,3},{3,4},{4,5},{5,6},{6,7},{8,9},{9,10},{10,11},{11... | collective-permute-start | bytes 5898248 | tf_op jit(solution)/shard_map/ppermute | solution.py:29
  255.0 55.8 %collective-permute-start.7 = (bf16[2,4,1,1,2,80,768]{6,5,4,3,1,0,2:T(8,128)(2,1)}, bf16[2,4,1,1,2,80,768]{6,5,4,3,1,0,2:T(8,128)(2,1)}, u32[]{:S(2)}, u32[]{:S(2)}) collective-permute-start(bf16[2,4,1,1,2,80,768]{6,5,4,3,1,0,2:T(8,128)(2,1)} %get-tuple-element.6), channel_id=1, source_target_pairs={{1,0},{2,1},{3,2},{4,3},{5,4},{6,5},{7,6},{9,8},{10,9},{11,10},{12... | collective-permute-start | bytes 5898248 | tf_op jit(solution)/shard_map/ppermute | solution.py:31
  264.2 13.4 %copy-start.5 = (s32[160]{0:T(256)S(1)}, s32[160]{0:T(256)}, u32[]{:S(2)}) copy-start(s32[160]{0:T(256)} %sub.71) | copy-start | bytes 1924
  264.2 13.4 %copy-start.6 = (s32[12]{0:T(128)S(1)}, s32[12]{0:T(128)}, u32[]{:S(2)}) copy-start(s32[12]{0:T(128)} %get-tuple-element.17) | copy-start | bytes 148
  266.5 79.0 %collective-permute-start.2 = (bf16[2,4,1,1,2,80,768]{6,5,4,3,1,0,2:T(8,128)(2,1)}, bf16[2,4,1,1,2,80,768]{6,5,4,3,1,0,2:T(8,128)(2,1)}, u32[]{:S(2)}, u32[]{:S(2)}) collective-permute-start(bf16[2,4,1,1,2,80,768]{6,5,4,3,1,0,2:T(8,128)(2,1)} %get-tuple-element.7), channel_id=1, source_target_pairs={{0,1},{1,2},{2,3},{3,4},{4,5},{5,6},{6,7},{8,9},{9,10},{10,11},{11... | collective-permute-start | bytes 5898248 | tf_op jit(solution)/shard_map/ppermute | solution.py:29
  268.4 77.0 %collective-permute-start.3 = (bf16[2,4,1,1,2,80,768]{6,5,4,3,1,0,2:T(8,128)(2,1)}, bf16[2,4,1,1,2,80,768]{6,5,4,3,1,0,2:T(8,128)(2,1)}, u32[]{:S(2)}, u32[]{:S(2)}) collective-permute-start(bf16[2,4,1,1,2,80,768]{6,5,4,3,1,0,2:T(8,128)(2,1)} %get-tuple-element.8), channel_id=1, source_target_pairs={{1,0},{2,1},{3,2},{4,3},{5,4},{6,5},{7,6},{9,8},{10,9},{11,10},{12... | collective-permute-start | bytes 5898248 | tf_op jit(solution)/shard_map/ppermute | solution.py:31
  317.1 28.4 %copy-start.1 = (bf16[2,640,768]{2,1,0:T(8,128)(2,1)S(1)}, bf16[2,640,768]{2,1,0:T(8,128)(2,1)}, u32[]{:S(2)}) copy-start(bf16[2,640,768]{2,1,0:T(8,128)(2,1)} %shard_map.84) | copy-start | bytes 5898244
Sparse Core Ops, SparseCore 0:
  33.7 164.6 all-gather.1

commit v9 on v8

--- a/solution.py
+++ b/solution.py
@@ -62,21 +62,21 @@
     frame_count, row_count, width, features = tokens.shape
     token_count = frame_count * row_count * width
     modulated = modulate(tokens.reshape(token_count, features), mod_scale, mod_shift)
+    frames_ext = frame_count + 2 * TT
+    rows_ext = row_count + 2 * TH
+    token_tiles = (frame_count // TT, TT, row_count // TH, TH, width, features)
+    halo_tokens = with_halo(modulated.reshape(token_tiles), (("tm", 0), ("height", 2)), 1)
+    halo_tokens = halo_tokens.reshape(frames_ext * rows_ext * width, features)
     band_weight = band_gather(w_qkv)
     full_weight = lax.all_gather(band_weight, "tm", axis=0, tiled=True)
     inner = full_weight.shape[1] // 3
     group_cols = inner // GROUPS
-    tiled = (frame_count // TT, TT, row_count // TH, TH, width, group_cols)
     groups = []
     for group in range(GROUPS):
         start = group * group_cols
-        stacked = project_kv(modulated, full_weight, start, group_cols, k_gain)
-        stacked = stacked.reshape(2, *tiled)
-        groups.append(with_halo(stacked, (("tm", 1), ("height", 3)), 1))
+        stacked = project_kv(halo_tokens, full_weight, start, group_cols, k_gain)
+        groups.append(stacked.reshape(2, frames_ext, rows_ext, width, group_cols))
     query = project(modulated, full_weight, 0, inner, q_gain)
-    frames_ext = frame_count + 2 * TT
-    rows_ext = row_count + 2 * TH
-    groups = [g.reshape(2, frames_ext, rows_ext, width, group_cols) for g in groups]
     frame_block = lax.axis_index("tm")
     row_block = lax.axis_index("height")
     first_frame = frame_block * frame_count
@@ -194,6 +194,7 @@
 
 
 PROJECT_COLS = 256
+TOKEN_BLOCK = 640
 
 
 def projection_kernel(x_ref, w_ref, g_ref, o_ref, *, normalize):
@@ -288,7 +289,7 @@
 
 def projection_kv_kernel(x_ref, w_ref, g_ref, o_ref):
     acc = jnp.dot(x_ref[...], w_ref[...], preferred_element_type=jnp.float32)
-    is_key = pl.program_id(0) < pl.num_programs(0) // 2
+    is_key = pl.program_id(1) < pl.num_programs(1) // 2
     for part in range(acc.shape[1] // HDIM):
         piece = acc[:, part * HDIM : (part + 1) * HDIM]
         power = jnp.mean(piece * piece, axis=-1, keepdims=True)
@@ -309,15 +310,16 @@
     def weight_block(j):
         return (0, jnp.where(j < steps, key_first + j, value_first + j - steps))
 
+    block = TOKEN_BLOCK
     return pl.pallas_call(
         projection_kv_kernel,
-        grid=(2 * steps,),
+        grid=(tokens // block, 2 * steps),
         in_specs=[
-            pl.BlockSpec((tokens, features), lambda j: (0, 0)),
-            pl.BlockSpec((features, cols), weight_block),
-            pl.BlockSpec((1, HDIM), lambda j: (0, 0)),
+            pl.BlockSpec((block, features), lambda t, j: (t, 0)),
+            pl.BlockSpec((features, cols), lambda t, j: weight_block(j)),
+            pl.BlockSpec((1, HDIM), lambda t, j: (0, 0)),
         ],
-        out_specs=pl.BlockSpec((1, tokens, cols), lambda j: (j // steps, 0, j % steps)),
+        out_specs=pl.BlockSpec((1, block, cols), lambda t, j: (j // steps, t, j % steps)),
         out_shape=jax.ShapeDtypeStruct((2, tokens, count), jnp.bfloat16),
     )(x, w, gain.reshape(1, HDIM))
 

time: 388 us -> 450 us (1.16)
  Pallas kernels: 117 us -> 175 us
  waiting for transfers between devices: 175 us -> 202 us
  starting transfers between devices: 36.4 us -> 17.3 us
  local copies, waits for them, and re-layouts: 14.1 us -> 7.62 us
    ppermute x4 -> x2, waiting for transfers between devices: 20.2 us -> 172 us  [with_halo(): lax.ppermute(tail, axis, [(i, (i + 1) % count) for i in range(ends)])]
    all_gather x1, waiting for transfers between devices: 153 us -> 16.9 us  [per_device(): full_weight = lax.all_gather(band_weight, 'tm', axis=0, tiled=True)]
    pallas_call x2, Pallas kernels: 23.6 us -> 82.4 us  [project_kv(): pl.pallas_call(projection_kv_kernel, grid=(tokens // block, 2 * steps), i...]
    ppermute x4 -> x2, starting transfers between devices: 27 us -> 12.6 us  [with_halo(): lax.ppermute(head, axis, [((i + 1) % count, i) for i in range(ends)])]
    ppermute x4 -> x2, waiting for transfers between devices: 1.62 us -> 13 us  [with_halo(): lax.ppermute(head, axis, [((i + 1) % count, i) for i in range(ends)])]
    slice x4 -> x2, local copies, waits for them, and re-layouts: 10.4 us -> 3.89 us  [with_halo(): lax.slice_in_dim(cells, cells.shape[dim] - width, cells.shape[dim], axis=...]
    ppermute x4 -> x2, starting transfers between devices: 9.42 us -> 4.68 us  [with_halo(): lax.ppermute(tail, axis, [(i, (i + 1) % count) for i in range(ends)])]
    concatenate x4 -> x2, other arithmetic: 16.6 us -> 13.9 us  [with_halo(): jnp.concatenate([lax.ppermute(tail, axis, [(i, (i + 1) % count) for i in...]
  transfers between devices with their start and end apart: 9 -> 5, of which waited for: 4 -> 4; matrix products, arithmetic and copies ran while one was open for 9% -> 8% of each run, Pallas kernels for 13% -> 0%
where the time goes in v9:
time: 450 us; the launch traced here: 445 us
  waiting for transfers between devices  202 us (45%)
  Pallas kernels  175 us (39%)
  other arithmetic  28.6 us (6%)
  starting transfers between devices  17.3 us (4%)
  between operations  13.7 us (3%)
  local copies, waits for them, and re-layouts  7.62 us (2%)
    ppermute x2, waiting for transfers between devices, with_halo(): lax.ppermute(tail, axis, [(i, (i + 1) % count) for i in range(ends)])  172 us
    pallas_call x2, Pallas kernels, project_kv(): pl.pallas_call(projection_kv_kernel, grid=(tokens // block, 2 * steps), i...  82.4 us
    pallas_call x2, Pallas kernels, tile_attention(): pl.pallas_call(kernel, grid=(heads, blocks), in_specs=in_specs, out_specs...  54.2 us
    pallas_call x1, Pallas kernels, band_gather(): pl.pallas_call(band_gather_kernel, in_specs=[pl.BlockSpec(memory_space=pl...  27 us
    all_gather x1, waiting for transfers between devices, per_device(): full_weight = lax.all_gather(band_weight, 'tm', axis=0, tiled=True)  16.9 us
    concatenate x2, other arithmetic, with_halo(): jnp.concatenate([lax.ppermute(tail, axis, [(i, (i + 1) % count) for i in...  13.9 us
    ppermute x2, waiting for transfers between devices, with_halo(): lax.ppermute(head, axis, [((i + 1) % count, i) for i in range(ends)])  13 us
    ppermute x2, starting transfers between devices, with_halo(): lax.ppermute(head, axis, [((i + 1) % count, i) for i in range(ends)])  12.6 us
  transfers between devices with their start and end apart: 5, of which 4 were waited for; matrix products, arithmetic and copies ran while one was open for 8% of the time, Pallas kernels for 0%

profile of v9, /device:TPU:6, one launch (start us, length us, event | category | flops | bytes accessed | tf_op | source)
XLA Modules:
  0.0 444.9 jit_solution(11879807644498457326)
XLA Ops:
  6.5 27.0 %shard_map.82 = bf16[8,24,4608]{2,1,0:T(8,128)(2,1)} custom-call(bf16[24,4608]{1,0:T(8,128)(2,1)} %w_ref.1), custom_call_target="tpu_custom_call" | custom-call | tf_op jit(solution)/shard_map/pallas_call | solution.py:275
  33.6 2.7 convert_reduce_fusion
  36.4 3.3 multiply_reduce_fusion
  39.9 3.8 fusion.3.x_ref
  44.0 1.9 collective-permute-start
  45.9 7.3 %collective-permute-start.1 = (bf16[1,1,2,2,80,3072]{5,4,3,2,0,1:T(8,128)(2,1)S(1)}, bf16[1,1,2,2,80,3072]{5,4,3,2,0,1:T(8,128)(2,1)S(1)}, u32[]{:S(2)}, u32[]{:S(2)}) collective-permute-start(bf16[1,1,2,2,80,3072]{5,4,3,2,0,1:T(8,128)(2,1)S(1)} %bitcast.43), channel_id=1, source_target_pairs={{8,0},{16,8},{24,16},{32,24},{40,32},{48,40},{56,48},{64,56},{72,6... | collective-permute-start | bytes 5898248 | tf_op jit(solution)/shard_map/ppermute | solution.py:31
  53.2 2.1 add_convert_fusion
  55.3 37.2 %collective-permute-done = bf16[1,1,2,2,80,3072]{5,4,3,2,0,1:T(8,128)(2,1)S(1)} collective-permute-done((bf16[1,1,2,2,80,3072]{5,4,3,2,0,1:T(8,128)(2,1)S(1)}, bf16[1,1,2,2,80,3072]{5,4,3,2,0,1:T(8,128)(2,1)S(1)}, u32[]{:S(2)}, u32[]{:S(2)}) %collective-permute-start) | collective-permute-done | bytes 1966112 | tf_op jit(solution)/shard_map/ppermute | solution.py:29
  92.6 1.3 copy-done.3
  93.8 0.9 pad_maximum_fusion.1
  94.8 3.6 fusion.6
  98.4 2.8 collective-permute-start.2
  101.2 5.4 %collective-permute-start.3 = (bf16[4,1,1,2,80,3072]{5,4,3,2,0,1:T(8,128)(2,1)}, bf16[4,1,1,2,80,3072]{5,4,3,2,0,1:T(8,128)(2,1)}, u32[]{:S(2)}, u32[]{:S(2)}) collective-permute-start(bf16[4,1,1,2,80,3072]{5,4,3,2,0,1:T(8,128)(2,1)} %get-tuple-element.6), channel_id=1, source_target_pairs={{1,0},{2,1},{3,2},{4,3},{5,4},{6,5},{7,6},{9,8},{10,9},{11,10},{12... | collective-permute-start | bytes 11796488 | tf_op jit(solution)/shard_map/ppermute | solution.py:31
  109.2 1.6 broadcast_add_fusion
  110.8 0.9 and_convert_fusion.km_ref.refs_3_
  111.7 135.1 %collective-permute-done.2 = bf16[4,1,1,2,80,3072]{5,4,3,2,0,1:T(8,128)(2,1)} collective-permute-done((bf16[4,1,1,2,80,3072]{5,4,3,2,0,1:T(8,128)(2,1)}, bf16[4,1,1,2,80,3072]{5,4,3,2,0,1:T(8,128)(2,1)}, u32[]{:S(2)}, u32[]{:S(2)}) %collective-permute-start.2) | collective-permute-done | bytes 3932192 | tf_op jit(solution)/shard_map/ppermute | solution.py:29
  246.8 13.0 %collective-permute-done.3 = bf16[4,1,1,2,80,3072]{5,4,3,2,0,1:T(8,128)(2,1)} collective-permute-done((bf16[4,1,1,2,80,3072]{5,4,3,2,0,1:T(8,128)(2,1)}, bf16[4,1,1,2,80,3072]{5,4,3,2,0,1:T(8,128)(2,1)}, u32[]{:S(2)}, u32[]{:S(2)}) %collective-permute-start.3) | collective-permute-done | bytes 3932192 | tf_op jit(solution)/shard_map/ppermute | solution.py:31
  259.9 12.9 %pad_maximum_fusion = bf16[4,1,4,2,80,3072]{5,4,3,2,0,1:T(8,128)(2,1)} fusion(bf16[4,1,1,2,80,3072]{5,4,3,2,0,1:T(8,128)(2,1)} %collective-permute-done.3, bf16[1,1,2,2,80,3072]{5,4,3,2,0,1:T(8,128)(2,1)} %copy-done.3, bf16[2,1,2,2,80,3072]{5,4,3,2,0,1:T(8,128)(2,1)} %copy-done.2, bf16[1,1,2,2,80,3072]{5,4,3,2,0,1:T(8,128)(2,1)S(1)} %collective-permute-done, ...), kind=kLoop, calls=%fused_computation | loop fusion | flops 31457280 | bytes 31457280 | tf_op jit(solution)/shard_map/concatenate | solution.py:27
  272.8 16.9 %all-gather.2.cloned.1.call-done.w_ref = bf16[3072,4608]{1,0:T(8,128)(2,1)} async-done(((bf16[192,4608]{1,0:T(8,128)(2,1)}), bf16[3072,4608]{1,0:T(8,128)(2,1)}) %all-gather.2.cloned.1.call-update) | async-done | bytes 28311568 | tf_op jit(solution)/shard_map/all_gather | solution.py:71
  289.7 11.7 %shard_map.83 = bf16[640,1536]{1,0:T(8,128)(2,1)} custom-call(bf16[640,3072]{1,0:T(8,128)(2,1)} %copy-done.1, bf16[3072,4608]{1,0:T(8,128)(2,1)} %all-gather.2.cloned.1.call-done.w_ref, f32[1,128]{1,0:T(1,128)} %bitcast.49), custom_call_target="tpu_custom_call" | custom-call | tf_op jit(solution)/shard_map/pallas_call | solution.py:216
  301.4 41.2 %shard_map.85 = bf16[2,2560,768]{2,1,0:T(8,128)(2,1)} custom-call(bf16[2560,3072]{1,0:T(8,128)(2,1)} %bitcast.33, bf16[3072,4608]{1,0:T(8,128)(2,1)} %all-gather.2.cloned.1.call-done.w_ref, f32[1,128]{1,0:T(1,128)} %bitcast.47), custom_call_target="tpu_custom_call" | custom-call | tf_op jit(solution)/shard_map/pallas_call | solution.py:314
  342.6 27.0 %shard_map.86.refs_8_ = bf16[2,4,80,1536]{3,2,1,0:T(8,128)(2,1)} custom-call(bf16[2,4,80,1536]{3,2,1,0:T(8,128)(2,1)} %bitcast.40, bf16[2,4,8,80,768]{4,3,2,1,0:T(8,128)(2,1)} %bitcast.35, bf16[2,4,8,80,768]{4,3,2,1,0:T(8,128)(2,1)} %bitcast.36, f32[12,4,1,1440]{3,2,1,0:T(1,128)} %and_convert_fusion.km_ref.refs_3_, ...), custom_call_target="tpu_custom_call" | custom-call | tf_op jit(solution)/shard_map/pallas_call | solution.py:186
  369.6 41.2 %shard_map.84 = bf16[2,2560,768]{2,1,0:T(8,128)(2,1)} custom-call(bf16[2560,3072]{1,0:T(8,128)(2,1)} %bitcast.34, bf16[3072,4608]{1,0:T(8,128)(2,1)} %all-gather.2.cloned.1.call-done.w_ref, f32[1,128]{1,0:T(1,128)} %bitcast.48), custom_call_target="tpu_custom_call" | custom-call | tf_op jit(solution)/shard_map/pallas_call | solution.py:314
  410.8 27.2 %shard_map.87 = bf16[2,4,80,1536]{3,2,1,0:T(8,128)(2,1)} custom-call(bf16[2,4,80,1536]{3,2,1,0:T(8,128)(2,1)} %bitcast.41, bf16[2,4,8,80,768]{4,3,2,1,0:T(8,128)(2,1)} %bitcast.37, bf16[2,4,8,80,768]{4,3,2,1,0:T(8,128)(2,1)} %bitcast.38, f32[12,4,1,1440]{3,2,1,0:T(1,128)} %and_convert_fusion.km_ref.refs_3_, ...), custom_call_target="tpu_custom_call", output_to_operand_aliasing={{}: (8, {})} | custom-call | tf_op jit(solution)/shard_map/pallas_call | solution.py:186
  (45 shorter events, 3.1 us)
Async XLA Ops:
  6.5 33.3 %copy-start.6 = (f32[3072]{0:T(1024)S(1)}, f32[3072]{0:T(1024)}, u32[]{:S(2)}) copy-start(f32[3072]{0:T(1024)} %param.9) | copy-start | bytes 36868
  6.5 33.3 %copy-start.5 = (f32[3072]{0:T(1024)S(1)}, f32[3072]{0:T(1024)}, u32[]{:S(2)}) copy-start(f32[3072]{0:T(1024)} %param.10) | copy-start | bytes 36868
  6.5 283.1 %all-gather.2.cloned.1.call-start = ((), (), s32[]{:S(2)}) async-start(), calls=%async_computation | async-start | bytes 30081024 | tf_op jit(solution)/shard_map/all_gather | solution.py:71
  39.9 13.3 %copy-start = (bf16[2,4,80,3072]{3,2,1,0:T(8,128)(2,1)S(1)}, bf16[2,4,80,3072]{3,2,1,0:T(8,128)(2,1)}, u32[]{:S(2)}) copy-start(bf16[2,4,80,3072]{3,2,1,0:T(8,128)(2,1)} %param.8) | copy-start | bytes 11796484
  43.7 11.6 %copy-start.1 = (bf16[640,3072]{1,0:T(8,128)(2,1)}, bf16[640,3072]{1,0:T(8,128)(2,1)S(1)}, u32[]{:S(2)}) copy-start(bf16[640,3072]{1,0:T(8,128)(2,1)S(1)} %fusion.3.x_ref) | copy-start | bytes 11796484
  44.0 48.6 %collective-permute-start = (bf16[1,1,2,2,80,3072]{5,4,3,2,0,1:T(8,128)(2,1)S(1)}, bf16[1,1,2,2,80,3072]{5,4,3,2,0,1:T(8,128)(2,1)S(1)}, u32[]{:S(2)}, u32[]{:S(2)}) collective-permute-start(bf16[1,1,2,2,80,3072]{5,4,3,2,0,1:T(8,128)(2,1)S(1)} %bitcast.44), channel_id=1, source_target_pairs={{0,8},{8,16},{16,24},{24,32},{32,40},{40,48},{48,56},{56,64},{64,7... | collective-permute-start | bytes 5898248 | tf_op jit(solution)/shard_map/ppermute | solution.py:29
  45.9 46.7 %collective-permute-start.1 = (bf16[1,1,2,2,80,3072]{5,4,3,2,0,1:T(8,128)(2,1)S(1)}, bf16[1,1,2,2,80,3072]{5,4,3,2,0,1:T(8,128)(2,1)S(1)}, u32[]{:S(2)}, u32[]{:S(2)}) collective-permute-start(bf16[1,1,2,2,80,3072]{5,4,3,2,0,1:T(8,128)(2,1)S(1)} %bitcast.43), channel_id=1, source_target_pairs={{8,0},{16,8},{24,16},{32,24},{40,32},{48,40},{56,48},{64,56},{72,6... | collective-permute-start | bytes 5898248 | tf_op jit(solution)/shard_map/ppermute | solution.py:31
  55.3 37.3 %copy-start.2 = (bf16[2,1,2,2,80,3072]{5,4,3,2,0,1:T(8,128)(2,1)}, bf16[2,1,2,2,80,3072]{5,4,3,2,0,1:T(8,128)(2,1)S(1)}, u32[]{:S(2)}) copy-start(bf16[2,1,2,2,80,3072]{5,4,3,2,0,1:T(8,128)(2,1)S(1)} %add_convert_fusion) | copy-start | bytes 11796484
  92.6 1.3 copy-start.3
  94.8 11.8 %copy-start.4 = (s32[32,32,80]{2,1,0:T(8,128)S(1)}, s32[32,32,80]{2,1,0:T(8,128)}, u32[]{:S(2)}) copy-start(s32[32,32,80]{2,1,0:T(8,128)} %param.15) | copy-start | bytes 983044
  94.8 12.2 %copy-start.7 = (s32[12,3]{0,1:T(4,128)S(1)}, s32[12,3]{0,1:T(4,128)}, u32[]{:S(2)}) copy-start(s32[12,3]{0,1:T(4,128)} %param.14) | copy-start | bytes 436
  98.4 148.4 %collective-permute-start.2 = (bf16[4,1,1,2,80,3072]{5,4,3,2,0,1:T(8,128)(2,1)}, bf16[4,1,1,2,80,3072]{5,4,3,2,0,1:T(8,128)(2,1)}, u32[]{:S(2)}, u32[]{:S(2)}) collective-permute-start(bf16[4,1,1,2,80,3072]{5,4,3,2,0,1:T(8,128)(2,1)} %get-tuple-element.5), channel_id=1, source_target_pairs={{0,1},{1,2},{2,3},{3,4},{4,5},{5,6},{6,7},{8,9},{9,10},{10,11},{11... | collective-permute-start | bytes 11796488 | tf_op jit(solution)/shard_map/ppermute | solution.py:29
  101.2 158.7 %collective-permute-start.3 = (bf16[4,1,1,2,80,3072]{5,4,3,2,0,1:T(8,128)(2,1)}, bf16[4,1,1,2,80,3072]{5,4,3,2,0,1:T(8,128)(2,1)}, u32[]{:S(2)}, u32[]{:S(2)}) collective-permute-start(bf16[4,1,1,2,80,3072]{5,4,3,2,0,1:T(8,128)(2,1)} %get-tuple-element.6), channel_id=1, source_target_pairs={{1,0},{2,1},{3,2},{4,3},{5,4},{6,5},{7,6},{9,8},{10,9},{11,10},{12... | collective-permute-start | bytes 11796488 | tf_op jit(solution)/shard_map/ppermute | solution.py:31
Sparse Core Ops, SparseCore 0:
  33.7 255.8 all-gather.1

commit v10 on v8

--- a/solution.py
+++ b/solution.py
@@ -125,28 +125,29 @@
 
 
 def attention_kernel(q_ref, k_ref, v_ref, km_ref, lo_ref, hi_ref, kc_ref, qv_ref, o_ref):
-    block = pl.program_id(1)
+    frame = pl.program_id(1)
     span_t = 2 * TT + 1
     span_h = 3 * TH
-    frame = block // ROW_TILES
-    row = (block % ROW_TILES) * TH
     width = q_ref.shape[2]
-    query = q_ref[0].reshape(TH * width, HDIM)
-    key = k_ref[0, pl.ds(frame, span_t), pl.ds(row, span_h)].reshape(-1, HDIM)
-    value = v_ref[0, pl.ds(frame, span_t), pl.ds(row, span_h)].reshape(-1, HDIM)
-    scores = lax.dot_general(
-        query, key, (((1,), (1,)), ((), ())), preferred_element_type=jnp.float32
-    ) * (1.0 / float(HDIM) ** 0.5)
     key_cols = kc_ref[...]
-    allowed = (key_cols >= lo_ref[0]) & (key_cols <= hi_ref[0]) & (km_ref[0, 0] > 0.0)
-    terms = jnp.where(allowed, jnp.exp(scores), jnp.float32(0.0))
-    total = jnp.sum(terms, axis=-1, keepdims=True)
-    seen = qv_ref[0] > 0.0
-    total = jnp.where(seen, total, jnp.float32(1.0))
-    weights = (terms * (1.0 / total)).astype(jnp.bfloat16)
-    result = jnp.dot(weights, value, preferred_element_type=jnp.float32)
-    result = jnp.where(seen, result, jnp.float32(0.0)).astype(jnp.bfloat16)
-    o_ref[0] = result.reshape(TH, width, HDIM)
+    width_ok = (key_cols >= lo_ref[0]) & (key_cols <= hi_ref[0])
+    for tile in range(ROW_TILES):
+        row = tile * TH
+        query = q_ref[0, row : row + TH].reshape(TH * width, HDIM)
+        key = k_ref[0, pl.ds(frame, span_t), row : row + span_h].reshape(-1, HDIM)
+        value = v_ref[0, pl.ds(frame, span_t), row : row + span_h].reshape(-1, HDIM)
+        scores = lax.dot_general(
+            query, key, (((1,), (1,)), ((), ())), preferred_element_type=jnp.float32
+        ) * (1.0 / float(HDIM) ** 0.5)
+        allowed = width_ok & (km_ref[0, tile] > 0.0)
+        terms = jnp.where(allowed, jnp.exp(scores), jnp.float32(0.0))
+        total = jnp.sum(terms, axis=-1, keepdims=True)
+        seen = qv_ref[tile] > 0.0
+        total = jnp.where(seen, total, jnp.float32(1.0))
+        weights = (terms * (1.0 / total)).astype(jnp.bfloat16)
+        result = jnp.dot(weights, value, preferred_element_type=jnp.float32)
+        result = jnp.where(seen, result, jnp.float32(0.0)).astype(jnp.bfloat16)
+        o_ref[0, row : row + TH] = result.reshape(TH, width, HDIM)
 
 
 ROW_TILES = 2
@@ -162,18 +163,16 @@
     _, frames_ext, rows_ext, _, _ = extended.shape
     key_n = key_mask.shape[-1]
     query_n = TH * width
-    q_spec = pl.BlockSpec(
-        (1, TH, width, HDIM), lambda h, b: (b // row_tiles, b % row_tiles, 0, first + h)
-    )
+    q_spec = pl.BlockSpec((1, rows, width, HDIM), lambda h, f: (f, 0, 0, first + h))
     in_specs = [
         q_spec,
         pl.BlockSpec((1, frames_ext, rows_ext, width, HDIM), lambda h, b: (0, 0, 0, 0, h)),
         pl.BlockSpec((1, frames_ext, rows_ext, width, HDIM), lambda h, b: (1, 0, 0, 0, h)),
-        pl.BlockSpec((1, 1, 1, key_n), lambda h, b: (first + h, b, 0, 0)),
+        pl.BlockSpec((1, row_tiles, 1, key_n), lambda h, f: (first + h, f, 0, 0)),
         pl.BlockSpec((1, query_n, 1), lambda h, b: (first + h, 0, 0)),
         pl.BlockSpec((1, query_n, 1), lambda h, b: (first + h, 0, 0)),
         pl.BlockSpec((1, key_n), lambda h, b: (0, 0)),
-        pl.BlockSpec((1, query_n, 1), lambda h, b: (b, 0, 0)),
+        pl.BlockSpec((row_tiles, query_n, 1), lambda h, f: (f, 0, 0)),
     ]
     operands = [query, extended, extended, key_mask, query_lo, query_hi, key_cols, query_ok]
     aliases = {}
@@ -185,7 +184,7 @@
         kernel = lambda *refs: attention_kernel(*refs[:8], refs[9])
     return pl.pallas_call(
         kernel,
-        grid=(heads, blocks),
+        grid=(heads, frames),
         in_specs=in_specs,
         out_specs=q_spec,
         out_shape=jax.ShapeDtypeStruct(query.shape, jnp.bfloat16),

time: 388 us -> 381 us (0.982)
  Pallas kernels: 117 us -> 105 us
  waiting for transfers between devices: 175 us -> 181 us
    pallas_call x2, Pallas kernels: 54.3 us -> 42.4 us  [tile_attention(): pl.pallas_call(kernel, grid=(heads, frames), in_specs=in_specs, out_specs...]
    ppermute x4, waiting for transfers between devices: 20.2 us -> 26 us  [with_halo(): lax.ppermute(tail, axis, [(i, (i + 1) % count) for i in range(ends)])]
  transfers between devices with their start and end apart: 9 -> 9, of which waited for: 4 -> 4; matrix products, arithmetic and copies ran while one was open for 9% -> 9% of each run, Pallas kernels for 13% -> 12%
where the time goes in v10:
time: 381 us; the launch traced here: 380 us
  waiting for transfers between devices  181 us (48%)
  Pallas kernels  105 us (28%)
  starting transfers between devices  36.6 us (10%)
  other arithmetic  30.3 us (8%)
  local copies, waits for them, and re-layouts  14.1 us (4%)
  between operations  13.7 us (4%)
    all_gather x1, waiting for transfers between devices, per_device(): full_weight = lax.all_gather(band_weight, 'tm', axis=0, tiled=True)  153 us
    pallas_call x2, Pallas kernels, tile_attention(): pl.pallas_call(kernel, grid=(heads, frames), in_specs=in_specs, out_specs...  42.4 us
    ppermute x4, starting transfers between devices, with_halo(): lax.ppermute(head, axis, [((i + 1) % count, i) for i in range(ends)])  27.2 us
    pallas_call x1, Pallas kernels, band_gather(): pl.pallas_call(band_gather_kernel, in_specs=[pl.BlockSpec(memory_space=pl...  27 us
    ppermute x4, waiting for transfers between devices, with_halo(): lax.ppermute(tail, axis, [(i, (i + 1) % count) for i in range(ends)])  26 us
    pallas_call x2, Pallas kernels, project_kv(): pl.pallas_call(projection_kv_kernel, grid=(2 * steps,), in_specs=[pl.Bloc...  23.6 us
    concatenate x4, other arithmetic, with_halo(): jnp.concatenate([lax.ppermute(tail, axis, [(i, (i + 1) % count) for i in...  16.6 us
    pallas_call x1, Pallas kernels, project(): pl.pallas_call(functools.partial(projection_kernel, normalize=normalize),...  11.7 us
  transfers between devices with their start and end apart: 9, of which 4 were waited for; matrix products, arithmetic and copies ran while one was open for 9% of the time, Pallas kernels for 12%

profile of v10, /device:TPU:6, one launch (start us, length us, event | category | flops | bytes accessed | tf_op | source)
XLA Modules:
  0.0 380.0 jit_solution(8297363310161280622)
XLA Ops:
  6.5 27.0 %shard_map.82 = bf16[8,24,4608]{2,1,0:T(8,128)(2,1)} custom-call(bf16[24,4608]{1,0:T(8,128)(2,1)} %w_ref.1), custom_call_target="tpu_custom_call" | custom-call | tf_op jit(solution)/shard_map/pallas_call | solution.py:273
  33.6 2.7 convert_reduce_fusion
  36.5 3.3 multiply_reduce_fusion
  40.5 4.9 %fusion.3.x_ref = bf16[640,3072]{1,0:T(8,128)(2,1)} fusion(bf16[2,4,80,3072]{3,2,1,0:T(8,128)(2,1)} %param.8, f32[3072]{0:T(1024)S(1)} %copy-done.4, f32[3072]{0:T(1024)S(1)} %broadcast_add_fusion.1, f32[640]{0:T(1024)S(1)} %rsqrt.12, f32[640]{0:T(1024)S(1)} %div.29), kind=kLoop, calls=%fused_computation.6 | loop fusion | flops 11796480 | bytes 7894016 | tf_op jit(solution)/shard_map/convert_element_type | solution.py:44
  45.4 153.0 %all-gather.2.cloned.1.call-done.w_ref = bf16[3072,4608]{1,0:T(8,128)(2,1)} async-done(((bf16[192,4608]{1,0:T(8,128)(2,1)}), bf16[3072,4608]{1,0:T(8,128)(2,1)}) %all-gather.2.cloned.1.call-update) | async-done | bytes 28311568 | tf_op jit(solution)/shard_map/all_gather | solution.py:66
  198.4 11.7 %shard_map.85 = bf16[2,640,768]{2,1,0:T(8,128)(2,1)} custom-call(bf16[640,3072]{1,0:T(8,128)(2,1)} %fusion.3.x_ref, bf16[3072,4608]{1,0:T(8,128)(2,1)} %all-gather.2.cloned.1.call-done.w_ref, f32[1,128]{1,0:T(1,128)} %bitcast.37), custom_call_target="tpu_custom_call" | custom-call | tf_op jit(solution)/shard_map/pallas_call | solution.py:311
  210.1 2.9 fusion.8
  215.2 7.0 %collective-permute-start.5 = (bf16[2,1,1,2,2,80,768]{6,5,4,3,1,0,2:T(8,128)(2,1)}, bf16[2,1,1,2,2,80,768]{6,5,4,3,1,0,2:T(8,128)(2,1)}, u32[]{:S(2)}, u32[]{:S(2)}) collective-permute-start(bf16[2,1,1,2,2,80,768]{6,5,4,3,1,0,2:T(8,128)(2,1)} %get-tuple-element.10), channel_id=1, source_target_pairs={{8,0},{16,8},{24,16},{32,24},{40,32},{48,40},{56,48},{64,56},{72,6... | collective-permute-start | bytes 2949128 | tf_op jit(solution)/shard_map/ppermute | solution.py:31
  222.4 11.8 %shard_map.84 = bf16[2,640,768]{2,1,0:T(8,128)(2,1)} custom-call(bf16[640,3072]{1,0:T(8,128)(2,1)} %fusion.3.x_ref, bf16[3072,4608]{1,0:T(8,128)(2,1)} %all-gather.2.cloned.1.call-done.w_ref, f32[1,128]{1,0:T(1,128)} %bitcast.38), custom_call_target="tpu_custom_call" | custom-call | tf_op jit(solution)/shard_map/pallas_call | solution.py:311
  234.3 3.0 fusion.9
  239.2 7.3 %collective-permute-start.1 = (bf16[2,1,1,2,2,80,768]{6,5,4,3,1,0,2:T(8,128)(2,1)}, bf16[2,1,1,2,2,80,768]{6,5,4,3,1,0,2:T(8,128)(2,1)}, u32[]{:S(2)}, u32[]{:S(2)}) collective-permute-start(bf16[2,1,1,2,2,80,768]{6,5,4,3,1,0,2:T(8,128)(2,1)} %get-tuple-element.12), channel_id=1, source_target_pairs={{8,0},{16,8},{24,16},{32,24},{40,32},{48,40},{56,48},{64,56},{72,6... | collective-permute-start | bytes 2949128 | tf_op jit(solution)/shard_map/ppermute | solution.py:31
  249.4 2.2 fusion.6
  251.6 3.4 collective-permute-start.6
  255.0 4.5 %collective-permute-start.7 = (bf16[2,4,1,1,2,80,768]{6,5,4,3,1,0,2:T(8,128)(2,1)}, bf16[2,4,1,1,2,80,768]{6,5,4,3,1,0,2:T(8,128)(2,1)}, u32[]{:S(2)}, u32[]{:S(2)}) collective-permute-start(bf16[2,4,1,1,2,80,768]{6,5,4,3,1,0,2:T(8,128)(2,1)} %get-tuple-element.6), channel_id=1, source_target_pairs={{1,0},{2,1},{3,2},{4,3},{5,4},{6,5},{7,6},{9,8},{10,9},{11,10},{12... | collective-permute-start | bytes 5898248 | tf_op jit(solution)/shard_map/ppermute | solution.py:31
  261.9 2.3 pad_maximum_fusion.2
  264.2 2.3 fusion.7
  268.4 8.4 %collective-permute-start.3 = (bf16[2,4,1,1,2,80,768]{6,5,4,3,1,0,2:T(8,128)(2,1)}, bf16[2,4,1,1,2,80,768]{6,5,4,3,1,0,2:T(8,128)(2,1)}, u32[]{:S(2)}, u32[]{:S(2)}) collective-permute-start(bf16[2,4,1,1,2,80,768]{6,5,4,3,1,0,2:T(8,128)(2,1)} %get-tuple-element.8), channel_id=1, source_target_pairs={{1,0},{2,1},{3,2},{4,3},{5,4},{6,5},{7,6},{9,8},{10,9},{11,10},{12... | collective-permute-start | bytes 5898248 | tf_op jit(solution)/shard_map/ppermute | solution.py:31
  280.3 11.7 %shard_map.83 = bf16[640,1536]{1,0:T(8,128)(2,1)} custom-call(bf16[640,3072]{1,0:T(8,128)(2,1)} %fusion.3.x_ref, bf16[3072,4608]{1,0:T(8,128)(2,1)} %all-gather.2.cloned.1.call-done.w_ref, f32[1,128]{1,0:T(1,128)} %bitcast.39), custom_call_target="tpu_custom_call" | custom-call | tf_op jit(solution)/shard_map/pallas_call | solution.py:214
  292.0 18.8 %collective-permute-done.6 = bf16[2,4,1,1,2,80,768]{6,5,4,3,1,0,2:T(8,128)(2,1)} collective-permute-done((bf16[2,4,1,1,2,80,768]{6,5,4,3,1,0,2:T(8,128)(2,1)}, bf16[2,4,1,1,2,80,768]{6,5,4,3,1,0,2:T(8,128)(2,1)}, u32[]{:S(2)}, u32[]{:S(2)}) %collective-permute-start.6) | collective-permute-done | bytes 1966112 | tf_op jit(solution)/shard_map/ppermute | solution.py:29
  310.8 6.3 %pad_maximum_fusion.1 = bf16[2,4,1,4,2,80,768]{6,5,4,3,1,0,2:T(8,128)(2,1)} fusion(bf16[2,4,1,1,2,80,768]{6,5,4,3,1,0,2:T(8,128)(2,1)} %collective-permute-done.7, bf16[2,1,1,2,2,80,768]{6,5,4,3,1,0,2:T(8,128)(2,1)} %collective-permute-done.5, bf16[2,2,1,2,2,80,768]{6,5,4,3,1,0,2:T(8,128)(2,1)S(1)} %bitcast.30, ...), kind=kLoop, calls=%fused_computation.1 | loop fusion | flops 15728640 | bytes 15728640 | tf_op jit(solution)/shard_map/concatenate | solution.py:27
  317.1 21.1 %shard_map.86.refs_8_ = bf16[2,4,80,1536]{3,2,1,0:T(8,128)(2,1)} custom-call(bf16[2,4,80,1536]{3,2,1,0:T(8,128)(2,1)} %bitcast.34, bf16[2,4,8,80,768]{4,3,2,1,0:T(8,128)(2,1)} %bitcast.24, bf16[2,4,8,80,768]{4,3,2,1,0:T(8,128)(2,1)} %bitcast.25, f32[12,4,1,1440]{3,2,1,0:T(1,128)} %and_convert_fusion.km_ref.refs_3_, ...), custom_call_target="tpu_custom_call" | custom-call | tf_op jit(solution)/shard_map/pallas_call | solution.py:185
  338.2 7.2 %collective-permute-done.2 = bf16[2,4,1,1,2,80,768]{6,5,4,3,1,0,2:T(8,128)(2,1)} collective-permute-done((bf16[2,4,1,1,2,80,768]{6,5,4,3,1,0,2:T(8,128)(2,1)}, bf16[2,4,1,1,2,80,768]{6,5,4,3,1,0,2:T(8,128)(2,1)}, u32[]{:S(2)}, u32[]{:S(2)}) %collective-permute-start.2) | collective-permute-done | bytes 1966112 | tf_op jit(solution)/shard_map/ppermute | solution.py:29
  345.5 6.5 %pad_maximum_fusion = bf16[2,4,1,4,2,80,768]{6,5,4,3,1,0,2:T(8,128)(2,1)} fusion(bf16[2,4,1,1,2,80,768]{6,5,4,3,1,0,2:T(8,128)(2,1)} %collective-permute-done.3, bf16[2,1,1,2,2,80,768]{6,5,4,3,1,0,2:T(8,128)(2,1)} %collective-permute-done.1, bf16[2,2,1,2,2,80,768]{6,5,4,3,1,0,2:T(8,128)(2,1)S(1)} %bitcast.33, ...), kind=kLoop, calls=%fused_computation | loop fusion | flops 15728640 | bytes 15728640 | tf_op jit(solution)/shard_map/concatenate | solution.py:27
  352.0 21.2 %shard_map.87 = bf16[2,4,80,1536]{3,2,1,0:T(8,128)(2,1)} custom-call(bf16[2,4,80,1536]{3,2,1,0:T(8,128)(2,1)} %bitcast.35, bf16[2,4,8,80,768]{4,3,2,1,0:T(8,128)(2,1)} %bitcast.26, bf16[2,4,8,80,768]{4,3,2,1,0:T(8,128)(2,1)} %bitcast.27, f32[12,4,1,1440]{3,2,1,0:T(1,128)} %and_convert_fusion.km_ref.refs_3_, ...), custom_call_target="tpu_custom_call", output_to_operand_aliasing={{}: (8, {})} | custom-call | tf_op jit(solution)/shard_map/pallas_call | solution.py:185
  (56 shorter events, 15.6 us)
Async XLA Ops:
  6.5 191.9 %all-gather.2.cloned.1.call-start = ((), (), s32[]{:S(2)}) async-start(), calls=%async_computation | async-start | bytes 30081024 | tf_op jit(solution)/shard_map/all_gather | solution.py:66
  33.6 6.2 %copy-start.7 = (s32[12,3]{0,1:T(4,128)S(1)}, s32[12,3]{0,1:T(4,128)}, u32[]{:S(2)}) copy-start(s32[12,3]{0,1:T(4,128)} %param.14) | copy-start | bytes 436
  33.6 6.8 %copy-start.3 = (f32[3072]{0:T(1024)S(1)}, f32[3072]{0:T(1024)}, u32[]{:S(2)}) copy-start(f32[3072]{0:T(1024)} %param.9) | copy-start | bytes 36868
  33.6 6.8 %copy-start.4 = (f32[3072]{0:T(1024)S(1)}, f32[3072]{0:T(1024)}, u32[]{:S(2)}) copy-start(f32[3072]{0:T(1024)} %param.10) | copy-start | bytes 36868
  213.1 34.8 %collective-permute-start.4 = (bf16[2,1,1,2,2,80,768]{6,5,4,3,1,0,2:T(8,128)(2,1)}, bf16[2,1,1,2,2,80,768]{6,5,4,3,1,0,2:T(8,128)(2,1)S(1)}, u32[]{:S(2)}, u32[]{:S(2)}) collective-permute-start(bf16[2,1,1,2,2,80,768]{6,5,4,3,1,0,2:T(8,128)(2,1)} %get-tuple-element.9), channel_id=1, source_target_pairs={{0,8},{8,16},{16,24},{24,32},{32,40},{40,48},{48,56},{56,64},{64,7... | collective-permute-start | bytes 2949128 | tf_op jit(solution)/shard_map/ppermute | solution.py:29
  215.2 32.6 %collective-permute-start.5 = (bf16[2,1,1,2,2,80,768]{6,5,4,3,1,0,2:T(8,128)(2,1)}, bf16[2,1,1,2,2,80,768]{6,5,4,3,1,0,2:T(8,128)(2,1)}, u32[]{:S(2)}, u32[]{:S(2)}) collective-permute-start(bf16[2,1,1,2,2,80,768]{6,5,4,3,1,0,2:T(8,128)(2,1)} %get-tuple-element.10), channel_id=1, source_target_pairs={{8,0},{16,8},{24,16},{32,24},{40,32},{48,40},{56,48},{64,56},{72,6... | collective-permute-start | bytes 2949128 | tf_op jit(solution)/shard_map/ppermute | solution.py:31
  234.3 13.6 %copy-start = (bf16[2,640,768]{2,1,0:T(8,128)(2,1)S(1)}, bf16[2,640,768]{2,1,0:T(8,128)(2,1)}, u32[]{:S(2)}) copy-start(bf16[2,640,768]{2,1,0:T(8,128)(2,1)} %shard_map.85) | copy-start | bytes 5898244
  237.3 23.0 %collective-permute-start = (bf16[2,1,1,2,2,80,768]{6,5,4,3,1,0,2:T(8,128)(2,1)}, bf16[2,1,1,2,2,80,768]{6,5,4,3,1,0,2:T(8,128)(2,1)}, u32[]{:S(2)}, u32[]{:S(2)}) collective-permute-start(bf16[2,1,1,2,2,80,768]{6,5,4,3,1,0,2:T(8,128)(2,1)} %get-tuple-element.11), channel_id=1, source_target_pairs={{0,8},{8,16},{16,24},{24,32},{32,40},{40,48},{48,56},{56,64},{64,7... | collective-permute-start | bytes 2949128 | tf_op jit(solution)/shard_map/ppermute | solution.py:29
  239.2 22.7 %collective-permute-start.1 = (bf16[2,1,1,2,2,80,768]{6,5,4,3,1,0,2:T(8,128)(2,1)}, bf16[2,1,1,2,2,80,768]{6,5,4,3,1,0,2:T(8,128)(2,1)}, u32[]{:S(2)}, u32[]{:S(2)}) collective-permute-start(bf16[2,1,1,2,2,80,768]{6,5,4,3,1,0,2:T(8,128)(2,1)} %get-tuple-element.12), channel_id=1, source_target_pairs={{8,0},{16,8},{24,16},{32,24},{40,32},{48,40},{56,48},{64,56},{72,6... | collective-permute-start | bytes 2949128 | tf_op jit(solution)/shard_map/ppermute | solution.py:31
  249.4 10.5 %copy-start.2 = (s32[32,32,80]{2,1,0:T(8,128)S(1)}, s32[32,32,80]{2,1,0:T(8,128)}, u32[]{:S(2)}) copy-start(s32[32,32,80]{2,1,0:T(8,128)} %param.15) | copy-start | bytes 983044
  251.6 59.2 %collective-permute-start.6 = (bf16[2,4,1,1,2,80,768]{6,5,4,3,1,0,2:T(8,128)(2,1)}, bf16[2,4,1,1,2,80,768]{6,5,4,3,1,0,2:T(8,128)(2,1)}, u32[]{:S(2)}, u32[]{:S(2)}) collective-permute-start(bf16[2,4,1,1,2,80,768]{6,5,4,3,1,0,2:T(8,128)(2,1)} %get-tuple-element.5), channel_id=1, source_target_pairs={{0,1},{1,2},{2,3},{3,4},{4,5},{5,6},{6,7},{8,9},{9,10},{10,11},{11... | collective-permute-start | bytes 5898248 | tf_op jit(solution)/shard_map/ppermute | solution.py:29
  255.0 55.8 %collective-permute-start.7 = (bf16[2,4,1,1,2,80,768]{6,5,4,3,1,0,2:T(8,128)(2,1)}, bf16[2,4,1,1,2,80,768]{6,5,4,3,1,0,2:T(8,128)(2,1)}, u32[]{:S(2)}, u32[]{:S(2)}) collective-permute-start(bf16[2,4,1,1,2,80,768]{6,5,4,3,1,0,2:T(8,128)(2,1)} %get-tuple-element.6), channel_id=1, source_target_pairs={{1,0},{2,1},{3,2},{4,3},{5,4},{6,5},{7,6},{9,8},{10,9},{11,10},{12... | collective-permute-start | bytes 5898248 | tf_op jit(solution)/shard_map/ppermute | solution.py:31
  264.2 13.6 %copy-start.5 = (s32[160]{0:T(256)S(1)}, s32[160]{0:T(256)}, u32[]{:S(2)}) copy-start(s32[160]{0:T(256)} %sub.71) | copy-start | bytes 1924
  264.2 13.6 %copy-start.6 = (s32[12]{0:T(128)S(1)}, s32[12]{0:T(128)}, u32[]{:S(2)}) copy-start(s32[12]{0:T(128)} %get-tuple-element.17) | copy-start | bytes 148
  266.5 79.0 %collective-permute-start.2 = (bf16[2,4,1,1,2,80,768]{6,5,4,3,1,0,2:T(8,128)(2,1)}, bf16[2,4,1,1,2,80,768]{6,5,4,3,1,0,2:T(8,128)(2,1)}, u32[]{:S(2)}, u32[]{:S(2)}) collective-permute-start(bf16[2,4,1,1,2,80,768]{6,5,4,3,1,0,2:T(8,128)(2,1)} %get-tuple-element.7), channel_id=1, source_target_pairs={{0,1},{1,2},{2,3},{3,4},{4,5},{5,6},{6,7},{8,9},{9,10},{10,11},{11... | collective-permute-start | bytes 5898248 | tf_op jit(solution)/shard_map/ppermute | solution.py:29
  268.4 77.0 %collective-permute-start.3 = (bf16[2,4,1,1,2,80,768]{6,5,4,3,1,0,2:T(8,128)(2,1)}, bf16[2,4,1,1,2,80,768]{6,5,4,3,1,0,2:T(8,128)(2,1)}, u32[]{:S(2)}, u32[]{:S(2)}) collective-permute-start(bf16[2,4,1,1,2,80,768]{6,5,4,3,1,0,2:T(8,128)(2,1)} %get-tuple-element.8), channel_id=1, source_target_pairs={{1,0},{2,1},{3,2},{4,3},{5,4},{6,5},{7,6},{9,8},{10,9},{11,10},{12... | collective-permute-start | bytes 5898248 | tf_op jit(solution)/shard_map/ppermute | solution.py:31
  317.1 28.4 %copy-start.1 = (bf16[2,640,768]{2,1,0:T(8,128)(2,1)S(1)}, bf16[2,640,768]{2,1,0:T(8,128)(2,1)}, u32[]{:S(2)}) copy-start(bf16[2,640,768]{2,1,0:T(8,128)(2,1)} %shard_map.84) | copy-start | bytes 5898244
Sparse Core Ops, SparseCore 0:
  33.7 164.6 all-gather.1

commit v11 on v10

--- a/solution.py
+++ b/solution.py
@@ -125,29 +125,29 @@
 
 
 def attention_kernel(q_ref, k_ref, v_ref, km_ref, lo_ref, hi_ref, kc_ref, qv_ref, o_ref):
-    frame = pl.program_id(1)
     span_t = 2 * TT + 1
     span_h = 3 * TH
     width = q_ref.shape[2]
     key_cols = kc_ref[...]
     width_ok = (key_cols >= lo_ref[0]) & (key_cols <= hi_ref[0])
-    for tile in range(ROW_TILES):
+    for block in range(q_ref.shape[0] * ROW_TILES):
+        frame, tile = divmod(block, ROW_TILES)
         row = tile * TH
-        query = q_ref[0, row : row + TH].reshape(TH * width, HDIM)
-        key = k_ref[0, pl.ds(frame, span_t), row : row + span_h].reshape(-1, HDIM)
-        value = v_ref[0, pl.ds(frame, span_t), row : row + span_h].reshape(-1, HDIM)
+        query = q_ref[frame, row : row + TH].reshape(TH * width, HDIM)
+        key = k_ref[0, frame : frame + span_t, row : row + span_h].reshape(-1, HDIM)
+        value = v_ref[0, frame : frame + span_t, row : row + span_h].reshape(-1, HDIM)
         scores = lax.dot_general(
             query, key, (((1,), (1,)), ((), ())), preferred_element_type=jnp.float32
         ) * (1.0 / float(HDIM) ** 0.5)
-        allowed = width_ok & (km_ref[0, tile] > 0.0)
+        allowed = width_ok & (km_ref[0, block] > 0.0)
         terms = jnp.where(allowed, jnp.exp(scores), jnp.float32(0.0))
         total = jnp.sum(terms, axis=-1, keepdims=True)
-        seen = qv_ref[tile] > 0.0
+        seen = qv_ref[block] > 0.0
         total = jnp.where(seen, total, jnp.float32(1.0))
         weights = (terms * (1.0 / total)).astype(jnp.bfloat16)
         result = jnp.dot(weights, value, preferred_element_type=jnp.float32)
         result = jnp.where(seen, result, jnp.float32(0.0)).astype(jnp.bfloat16)
-        o_ref[0, row : row + TH] = result.reshape(TH, width, HDIM)
+        o_ref[frame, row : row + TH] = result.reshape(TH, width, HDIM)
 
 
 ROW_TILES = 2
@@ -163,16 +163,16 @@
     _, frames_ext, rows_ext, _, _ = extended.shape
     key_n = key_mask.shape[-1]
     query_n = TH * width
-    q_spec = pl.BlockSpec((1, rows, width, HDIM), lambda h, f: (f, 0, 0, first + h))
+    q_spec = pl.BlockSpec((frames, rows, width, HDIM), lambda h: (0, 0, 0, first + h))
     in_specs = [
         q_spec,
-        pl.BlockSpec((1, frames_ext, rows_ext, width, HDIM), lambda h, b: (0, 0, 0, 0, h)),
-        pl.BlockSpec((1, frames_ext, rows_ext, width, HDIM), lambda h, b: (1, 0, 0, 0, h)),
-        pl.BlockSpec((1, row_tiles, 1, key_n), lambda h, f: (first + h, f, 0, 0)),
-        pl.BlockSpec((1, query_n, 1), lambda h, b: (first + h, 0, 0)),
-        pl.BlockSpec((1, query_n, 1), lambda h, b: (first + h, 0, 0)),
-        pl.BlockSpec((1, key_n), lambda h, b: (0, 0)),
-        pl.BlockSpec((row_tiles, query_n, 1), lambda h, f: (f, 0, 0)),
+        pl.BlockSpec((1, frames_ext, rows_ext, width, HDIM), lambda h: (0, 0, 0, 0, h)),
+        pl.BlockSpec((1, frames_ext, rows_ext, width, HDIM), lambda h: (1, 0, 0, 0, h)),
+        pl.BlockSpec((1, blocks, 1, key_n), lambda h: (first + h, 0, 0, 0)),
+        pl.BlockSpec((1, query_n, 1), lambda h: (first + h, 0, 0)),
+        pl.BlockSpec((1, query_n, 1), lambda h: (first + h, 0, 0)),
+        pl.BlockSpec((1, key_n), lambda h: (0, 0)),
+        pl.BlockSpec((blocks, query_n, 1), lambda h: (0, 0, 0)),
     ]
     operands = [query, extended, extended, key_mask, query_lo, query_hi, key_cols, query_ok]
     aliases = {}
@@ -184,7 +184,7 @@
         kernel = lambda *refs: attention_kernel(*refs[:8], refs[9])
     return pl.pallas_call(
         kernel,
-        grid=(heads, frames),
+        grid=(heads,),
         in_specs=in_specs,
         out_specs=q_spec,
         out_shape=jax.ShapeDtypeStruct(query.shape, jnp.bfloat16),

time: 381 us -> 379 us (level)
  Pallas kernels: 105 us -> 101 us
  transfers between devices with their start and end apart: 9 -> 9, of which waited for: 4 -> 4; matrix products, arithmetic and copies ran while one was open for 9% -> 9% of each run, Pallas kernels for 12% -> 11%
where the time goes in v11:
time: 379 us; the launch traced here: 378 us
  waiting for transfers between devices  182 us (48%)
  Pallas kernels  101 us (27%)
  starting transfers between devices  36.6 us (10%)
  other arithmetic  30.3 us (8%)
  local copies, waits for them, and re-layouts  14.1 us (4%)
  between operations  13.7 us (4%)
    all_gather x1, waiting for transfers between devices, per_device(): full_weight = lax.all_gather(band_weight, 'tm', axis=0, tiled=True)  153 us
    pallas_call x2, Pallas kernels, tile_attention(): pl.pallas_call(kernel, grid=(heads,), in_specs=in_specs, out_specs=q_spec...  38.8 us
    ppermute x4, waiting for transfers between devices, with_halo(): lax.ppermute(tail, axis, [(i, (i + 1) % count) for i in range(ends)])  27.8 us
    ppermute x4, starting transfers between devices, with_halo(): lax.ppermute(head, axis, [((i + 1) % count, i) for i in range(ends)])  27.2 us
    pallas_call x1, Pallas kernels, band_gather(): pl.pallas_call(band_gather_kernel, in_specs=[pl.BlockSpec(memory_space=pl...  27 us
    pallas_call x2, Pallas kernels, project_kv(): pl.pallas_call(projection_kv_kernel, grid=(2 * steps,), in_specs=[pl.Bloc...  23.6 us
    concatenate x4, other arithmetic, with_halo(): jnp.concatenate([lax.ppermute(tail, axis, [(i, (i + 1) % count) for i in...  16.6 us
    pallas_call x1, Pallas kernels, project(): pl.pallas_call(functools.partial(projection_kernel, normalize=normalize),...  11.7 us
  transfers between devices with their start and end apart: 9, of which 4 were waited for; matrix products, arithmetic and copies ran while one was open for 9% of the time, Pallas kernels for 11%

profile of v11, /device:TPU:6, one launch (start us, length us, event | category | flops | bytes accessed | tf_op | source)
XLA Modules:
  0.0 378.2 jit_solution(2029811555471158669)
XLA Ops:
  6.5 27.0 %shard_map.82 = bf16[8,24,4608]{2,1,0:T(8,128)(2,1)} custom-call(bf16[24,4608]{1,0:T(8,128)(2,1)} %w_ref.1), custom_call_target="tpu_custom_call" | custom-call | tf_op jit(solution)/shard_map/pallas_call | solution.py:273
  33.6 2.7 convert_reduce_fusion
  36.5 3.3 multiply_reduce_fusion
  40.5 4.9 %fusion.3.x_ref = bf16[640,3072]{1,0:T(8,128)(2,1)} fusion(bf16[2,4,80,3072]{3,2,1,0:T(8,128)(2,1)} %param.8, f32[3072]{0:T(1024)S(1)} %copy-done.4, f32[3072]{0:T(1024)S(1)} %broadcast_add_fusion.1, f32[640]{0:T(1024)S(1)} %rsqrt.12, f32[640]{0:T(1024)S(1)} %div.29), kind=kLoop, calls=%fused_computation.6 | loop fusion | flops 11796480 | bytes 7894016 | tf_op jit(solution)/shard_map/convert_element_type | solution.py:44
  45.4 153.0 %all-gather.2.cloned.1.call-done.w_ref = bf16[3072,4608]{1,0:T(8,128)(2,1)} async-done(((bf16[192,4608]{1,0:T(8,128)(2,1)}), bf16[3072,4608]{1,0:T(8,128)(2,1)}) %all-gather.2.cloned.1.call-update) | async-done | bytes 28311568 | tf_op jit(solution)/shard_map/all_gather | solution.py:66
  198.4 11.7 %shard_map.85 = bf16[2,640,768]{2,1,0:T(8,128)(2,1)} custom-call(bf16[640,3072]{1,0:T(8,128)(2,1)} %fusion.3.x_ref, bf16[3072,4608]{1,0:T(8,128)(2,1)} %all-gather.2.cloned.1.call-done.w_ref, f32[1,128]{1,0:T(1,128)} %bitcast.37), custom_call_target="tpu_custom_call" | custom-call | tf_op jit(solution)/shard_map/pallas_call | solution.py:311
  210.1 2.9 fusion.8
  215.2 7.0 %collective-permute-start.5 = (bf16[2,1,1,2,2,80,768]{6,5,4,3,1,0,2:T(8,128)(2,1)}, bf16[2,1,1,2,2,80,768]{6,5,4,3,1,0,2:T(8,128)(2,1)}, u32[]{:S(2)}, u32[]{:S(2)}) collective-permute-start(bf16[2,1,1,2,2,80,768]{6,5,4,3,1,0,2:T(8,128)(2,1)} %get-tuple-element.10), channel_id=1, source_target_pairs={{8,0},{16,8},{24,16},{32,24},{40,32},{48,40},{56,48},{64,56},{72,6... | collective-permute-start | bytes 2949128 | tf_op jit(solution)/shard_map/ppermute | solution.py:31
  222.4 11.8 %shard_map.84 = bf16[2,640,768]{2,1,0:T(8,128)(2,1)} custom-call(bf16[640,3072]{1,0:T(8,128)(2,1)} %fusion.3.x_ref, bf16[3072,4608]{1,0:T(8,128)(2,1)} %all-gather.2.cloned.1.call-done.w_ref, f32[1,128]{1,0:T(1,128)} %bitcast.38), custom_call_target="tpu_custom_call" | custom-call | tf_op jit(solution)/shard_map/pallas_call | solution.py:311
  234.3 3.0 fusion.9
  239.2 7.3 %collective-permute-start.1 = (bf16[2,1,1,2,2,80,768]{6,5,4,3,1,0,2:T(8,128)(2,1)}, bf16[2,1,1,2,2,80,768]{6,5,4,3,1,0,2:T(8,128)(2,1)}, u32[]{:S(2)}, u32[]{:S(2)}) collective-permute-start(bf16[2,1,1,2,2,80,768]{6,5,4,3,1,0,2:T(8,128)(2,1)} %get-tuple-element.12), channel_id=1, source_target_pairs={{8,0},{16,8},{24,16},{32,24},{40,32},{48,40},{56,48},{64,56},{72,6... | collective-permute-start | bytes 2949128 | tf_op jit(solution)/shard_map/ppermute | solution.py:31
  249.4 2.2 fusion.6
  251.6 3.4 collective-permute-start.6
  255.0 4.5 %collective-permute-start.7 = (bf16[2,4,1,1,2,80,768]{6,5,4,3,1,0,2:T(8,128)(2,1)}, bf16[2,4,1,1,2,80,768]{6,5,4,3,1,0,2:T(8,128)(2,1)}, u32[]{:S(2)}, u32[]{:S(2)}) collective-permute-start(bf16[2,4,1,1,2,80,768]{6,5,4,3,1,0,2:T(8,128)(2,1)} %get-tuple-element.6), channel_id=1, source_target_pairs={{1,0},{2,1},{3,2},{4,3},{5,4},{6,5},{7,6},{9,8},{10,9},{11,10},{12... | collective-permute-start | bytes 5898248 | tf_op jit(solution)/shard_map/ppermute | solution.py:31
  261.9 2.3 pad_maximum_fusion.2
  264.2 2.3 fusion.7
  268.4 8.4 %collective-permute-start.3 = (bf16[2,4,1,1,2,80,768]{6,5,4,3,1,0,2:T(8,128)(2,1)}, bf16[2,4,1,1,2,80,768]{6,5,4,3,1,0,2:T(8,128)(2,1)}, u32[]{:S(2)}, u32[]{:S(2)}) collective-permute-start(bf16[2,4,1,1,2,80,768]{6,5,4,3,1,0,2:T(8,128)(2,1)} %get-tuple-element.8), channel_id=1, source_target_pairs={{1,0},{2,1},{3,2},{4,3},{5,4},{6,5},{7,6},{9,8},{10,9},{11,10},{12... | collective-permute-start | bytes 5898248 | tf_op jit(solution)/shard_map/ppermute | solution.py:31
  280.3 11.7 %shard_map.83 = bf16[640,1536]{1,0:T(8,128)(2,1)} custom-call(bf16[640,3072]{1,0:T(8,128)(2,1)} %fusion.3.x_ref, bf16[3072,4608]{1,0:T(8,128)(2,1)} %all-gather.2.cloned.1.call-done.w_ref, f32[1,128]{1,0:T(1,128)} %bitcast.39), custom_call_target="tpu_custom_call" | custom-call | tf_op jit(solution)/shard_map/pallas_call | solution.py:214
  292.0 18.8 %collective-permute-done.6 = bf16[2,4,1,1,2,80,768]{6,5,4,3,1,0,2:T(8,128)(2,1)} collective-permute-done((bf16[2,4,1,1,2,80,768]{6,5,4,3,1,0,2:T(8,128)(2,1)}, bf16[2,4,1,1,2,80,768]{6,5,4,3,1,0,2:T(8,128)(2,1)}, u32[]{:S(2)}, u32[]{:S(2)}) %collective-permute-start.6) | collective-permute-done | bytes 1966112 | tf_op jit(solution)/shard_map/ppermute | solution.py:29
  310.8 6.3 %pad_maximum_fusion.1 = bf16[2,4,1,4,2,80,768]{6,5,4,3,1,0,2:T(8,128)(2,1)} fusion(bf16[2,4,1,1,2,80,768]{6,5,4,3,1,0,2:T(8,128)(2,1)} %collective-permute-done.7, bf16[2,1,1,2,2,80,768]{6,5,4,3,1,0,2:T(8,128)(2,1)} %collective-permute-done.5, bf16[2,2,1,2,2,80,768]{6,5,4,3,1,0,2:T(8,128)(2,1)S(1)} %bitcast.30, ...), kind=kLoop, calls=%fused_computation.1 | loop fusion | flops 15728640 | bytes 15728640 | tf_op jit(solution)/shard_map/concatenate | solution.py:27
  317.1 19.4 %shard_map.86.refs_8_ = bf16[2,4,80,1536]{3,2,1,0:T(8,128)(2,1)} custom-call(bf16[2,4,80,1536]{3,2,1,0:T(8,128)(2,1)} %bitcast.34, bf16[2,4,8,80,768]{4,3,2,1,0:T(8,128)(2,1)} %bitcast.24, bf16[2,4,8,80,768]{4,3,2,1,0:T(8,128)(2,1)} %bitcast.25, f32[12,4,1,1440]{3,2,1,0:T(1,128)} %and_convert_fusion.km_ref.refs_3_, ...), custom_call_target="tpu_custom_call" | custom-call | tf_op jit(solution)/shard_map/pallas_call | solution.py:185
  336.5 9.0 %collective-permute-done.2 = bf16[2,4,1,1,2,80,768]{6,5,4,3,1,0,2:T(8,128)(2,1)} collective-permute-done((bf16[2,4,1,1,2,80,768]{6,5,4,3,1,0,2:T(8,128)(2,1)}, bf16[2,4,1,1,2,80,768]{6,5,4,3,1,0,2:T(8,128)(2,1)}, u32[]{:S(2)}, u32[]{:S(2)}) %collective-permute-start.2) | collective-permute-done | bytes 1966112 | tf_op jit(solution)/shard_map/ppermute | solution.py:29
  345.5 6.5 %pad_maximum_fusion = bf16[2,4,1,4,2,80,768]{6,5,4,3,1,0,2:T(8,128)(2,1)} fusion(bf16[2,4,1,1,2,80,768]{6,5,4,3,1,0,2:T(8,128)(2,1)} %collective-permute-done.3, bf16[2,1,1,2,2,80,768]{6,5,4,3,1,0,2:T(8,128)(2,1)} %collective-permute-done.1, bf16[2,2,1,2,2,80,768]{6,5,4,3,1,0,2:T(8,128)(2,1)S(1)} %bitcast.33, ...), kind=kLoop, calls=%fused_computation | loop fusion | flops 15728640 | bytes 15728640 | tf_op jit(solution)/shard_map/concatenate | solution.py:27
  352.0 19.4 %shard_map.87 = bf16[2,4,80,1536]{3,2,1,0:T(8,128)(2,1)} custom-call(bf16[2,4,80,1536]{3,2,1,0:T(8,128)(2,1)} %bitcast.35, bf16[2,4,8,80,768]{4,3,2,1,0:T(8,128)(2,1)} %bitcast.26, bf16[2,4,8,80,768]{4,3,2,1,0:T(8,128)(2,1)} %bitcast.27, f32[12,4,1,1440]{3,2,1,0:T(1,128)} %and_convert_fusion.km_ref.refs_3_, ...), custom_call_target="tpu_custom_call", output_to_operand_aliasing={{}: (8, {})} | custom-call | tf_op jit(solution)/shard_map/pallas_call | solution.py:185
  (56 shorter events, 15.6 us)
Async XLA Ops:
  6.5 191.9 %all-gather.2.cloned.1.call-start = ((), (), s32[]{:S(2)}) async-start(), calls=%async_computation | async-start | bytes 30081024 | tf_op jit(solution)/shard_map/all_gather | solution.py:66
  33.6 6.2 %copy-start.7 = (s32[12,3]{0,1:T(4,128)S(1)}, s32[12,3]{0,1:T(4,128)}, u32[]{:S(2)}) copy-start(s32[12,3]{0,1:T(4,128)} %param.14) | copy-start | bytes 436
  33.6 6.8 %copy-start.3 = (f32[3072]{0:T(1024)S(1)}, f32[3072]{0:T(1024)}, u32[]{:S(2)}) copy-start(f32[3072]{0:T(1024)} %param.9) | copy-start | bytes 36868
  33.6 6.8 %copy-start.4 = (f32[3072]{0:T(1024)S(1)}, f32[3072]{0:T(1024)}, u32[]{:S(2)}) copy-start(f32[3072]{0:T(1024)} %param.10) | copy-start | bytes 36868
  213.1 34.8 %collective-permute-start.4 = (bf16[2,1,1,2,2,80,768]{6,5,4,3,1,0,2:T(8,128)(2,1)}, bf16[2,1,1,2,2,80,768]{6,5,4,3,1,0,2:T(8,128)(2,1)S(1)}, u32[]{:S(2)}, u32[]{:S(2)}) collective-permute-start(bf16[2,1,1,2,2,80,768]{6,5,4,3,1,0,2:T(8,128)(2,1)} %get-tuple-element.9), channel_id=1, source_target_pairs={{0,8},{8,16},{16,24},{24,32},{32,40},{40,48},{48,56},{56,64},{64,7... | collective-permute-start | bytes 2949128 | tf_op jit(solution)/shard_map/ppermute | solution.py:29
  215.2 32.6 %collective-permute-start.5 = (bf16[2,1,1,2,2,80,768]{6,5,4,3,1,0,2:T(8,128)(2,1)}, bf16[2,1,1,2,2,80,768]{6,5,4,3,1,0,2:T(8,128)(2,1)}, u32[]{:S(2)}, u32[]{:S(2)}) collective-permute-start(bf16[2,1,1,2,2,80,768]{6,5,4,3,1,0,2:T(8,128)(2,1)} %get-tuple-element.10), channel_id=1, source_target_pairs={{8,0},{16,8},{24,16},{32,24},{40,32},{48,40},{56,48},{64,56},{72,6... | collective-permute-start | bytes 2949128 | tf_op jit(solution)/shard_map/ppermute | solution.py:31
  234.3 13.6 %copy-start = (bf16[2,640,768]{2,1,0:T(8,128)(2,1)S(1)}, bf16[2,640,768]{2,1,0:T(8,128)(2,1)}, u32[]{:S(2)}) copy-start(bf16[2,640,768]{2,1,0:T(8,128)(2,1)} %shard_map.85) | copy-start | bytes 5898244
  237.3 23.0 %collective-permute-start = (bf16[2,1,1,2,2,80,768]{6,5,4,3,1,0,2:T(8,128)(2,1)}, bf16[2,1,1,2,2,80,768]{6,5,4,3,1,0,2:T(8,128)(2,1)}, u32[]{:S(2)}, u32[]{:S(2)}) collective-permute-start(bf16[2,1,1,2,2,80,768]{6,5,4,3,1,0,2:T(8,128)(2,1)} %get-tuple-element.11), channel_id=1, source_target_pairs={{0,8},{8,16},{16,24},{24,32},{32,40},{40,48},{48,56},{56,64},{64,7... | collective-permute-start | bytes 2949128 | tf_op jit(solution)/shard_map/ppermute | solution.py:29
  239.2 22.7 %collective-permute-start.1 = (bf16[2,1,1,2,2,80,768]{6,5,4,3,1,0,2:T(8,128)(2,1)}, bf16[2,1,1,2,2,80,768]{6,5,4,3,1,0,2:T(8,128)(2,1)}, u32[]{:S(2)}, u32[]{:S(2)}) collective-permute-start(bf16[2,1,1,2,2,80,768]{6,5,4,3,1,0,2:T(8,128)(2,1)} %get-tuple-element.12), channel_id=1, source_target_pairs={{8,0},{16,8},{24,16},{32,24},{40,32},{48,40},{56,48},{64,56},{72,6... | collective-permute-start | bytes 2949128 | tf_op jit(solution)/shard_map/ppermute | solution.py:31
  249.4 10.5 %copy-start.2 = (s32[32,32,80]{2,1,0:T(8,128)S(1)}, s32[32,32,80]{2,1,0:T(8,128)}, u32[]{:S(2)}) copy-start(s32[32,32,80]{2,1,0:T(8,128)} %param.15) | copy-start | bytes 983044
  251.6 59.2 %collective-permute-start.6 = (bf16[2,4,1,1,2,80,768]{6,5,4,3,1,0,2:T(8,128)(2,1)}, bf16[2,4,1,1,2,80,768]{6,5,4,3,1,0,2:T(8,128)(2,1)}, u32[]{:S(2)}, u32[]{:S(2)}) collective-permute-start(bf16[2,4,1,1,2,80,768]{6,5,4,3,1,0,2:T(8,128)(2,1)} %get-tuple-element.5), channel_id=1, source_target_pairs={{0,1},{1,2},{2,3},{3,4},{4,5},{5,6},{6,7},{8,9},{9,10},{10,11},{11... | collective-permute-start | bytes 5898248 | tf_op jit(solution)/shard_map/ppermute | solution.py:29
  255.0 55.8 %collective-permute-start.7 = (bf16[2,4,1,1,2,80,768]{6,5,4,3,1,0,2:T(8,128)(2,1)}, bf16[2,4,1,1,2,80,768]{6,5,4,3,1,0,2:T(8,128)(2,1)}, u32[]{:S(2)}, u32[]{:S(2)}) collective-permute-start(bf16[2,4,1,1,2,80,768]{6,5,4,3,1,0,2:T(8,128)(2,1)} %get-tuple-element.6), channel_id=1, source_target_pairs={{1,0},{2,1},{3,2},{4,3},{5,4},{6,5},{7,6},{9,8},{10,9},{11,10},{12... | collective-permute-start | bytes 5898248 | tf_op jit(solution)/shard_map/ppermute | solution.py:31
  264.2 13.6 %copy-start.5 = (s32[160]{0:T(256)S(1)}, s32[160]{0:T(256)}, u32[]{:S(2)}) copy-start(s32[160]{0:T(256)} %sub.71) | copy-start | bytes 1924
  264.2 13.6 %copy-start.6 = (s32[12]{0:T(128)S(1)}, s32[12]{0:T(128)}, u32[]{:S(2)}) copy-start(s32[12]{0:T(128)} %get-tuple-element.17) | copy-start | bytes 148
  266.5 79.0 %collective-permute-start.2 = (bf16[2,4,1,1,2,80,768]{6,5,4,3,1,0,2:T(8,128)(2,1)}, bf16[2,4,1,1,2,80,768]{6,5,4,3,1,0,2:T(8,128)(2,1)}, u32[]{:S(2)}, u32[]{:S(2)}) collective-permute-start(bf16[2,4,1,1,2,80,768]{6,5,4,3,1,0,2:T(8,128)(2,1)} %get-tuple-element.7), channel_id=1, source_target_pairs={{0,1},{1,2},{2,3},{3,4},{4,5},{5,6},{6,7},{8,9},{9,10},{10,11},{11... | collective-permute-start | bytes 5898248 | tf_op jit(solution)/shard_map/ppermute | solution.py:29
  268.4 77.0 %collective-permute-start.3 = (bf16[2,4,1,1,2,80,768]{6,5,4,3,1,0,2:T(8,128)(2,1)}, bf16[2,4,1,1,2,80,768]{6,5,4,3,1,0,2:T(8,128)(2,1)}, u32[]{:S(2)}, u32[]{:S(2)}) collective-permute-start(bf16[2,4,1,1,2,80,768]{6,5,4,3,1,0,2:T(8,128)(2,1)} %get-tuple-element.8), channel_id=1, source_target_pairs={{1,0},{2,1},{3,2},{4,3},{5,4},{6,5},{7,6},{9,8},{10,9},{11,10},{12... | collective-permute-start | bytes 5898248 | tf_op jit(solution)/shard_map/ppermute | solution.py:31
  317.1 28.4 %copy-start.1 = (bf16[2,640,768]{2,1,0:T(8,128)(2,1)S(1)}, bf16[2,640,768]{2,1,0:T(8,128)(2,1)}, u32[]{:S(2)}) copy-start(bf16[2,640,768]{2,1,0:T(8,128)(2,1)} %shard_map.84) | copy-start | bytes 5898244
Sparse Core Ops, SparseCore 0:
  33.7 164.6 all-gather.1

commit v12 on v11

--- a/solution.py
+++ b/solution.py
@@ -192,7 +192,7 @@
     )(*operands)
 
 
-PROJECT_COLS = 256
+PROJECT_COLS = 768
 
 
 def projection_kernel(x_ref, w_ref, g_ref, o_ref, *, normalize):

time: 379 us -> 378 us (level)
  no operation moved by 1% of the time
where the time goes in v12:
time: 378 us
  waiting for transfers between devices  183 us (48%)
  Pallas kernels  101 us (27%)
  starting transfers between devices  36.6 us (10%)
  other arithmetic  30.3 us (8%)
  local copies, waits for them, and re-layouts  14.1 us (4%)
  between operations  13.7 us (4%)
    all_gather x1, waiting for transfers between devices, per_device(): full_weight = lax.all_gather(band_weight, 'tm', axis=0, tiled=True)  153 us
    pallas_call x2, Pallas kernels, tile_attention(): pl.pallas_call(kernel, grid=(heads,), in_specs=in_specs, out_specs=q_spec...  38.7 us
    ppermute x4, waiting for transfers between devices, with_halo(): lax.ppermute(tail, axis, [(i, (i + 1) % count) for i in range(ends)])  27.9 us
    ppermute x4, starting transfers between devices, with_halo(): lax.ppermute(head, axis, [((i + 1) % count, i) for i in range(ends)])  27.2 us
    pallas_call x1, Pallas kernels, band_gather(): pl.pallas_call(band_gather_kernel, in_specs=[pl.BlockSpec(memory_space=pl...  27 us
    pallas_call x2, Pallas kernels, project_kv(): pl.pallas_call(projection_kv_kernel, grid=(2 * steps,), in_specs=[pl.Bloc...  23.2 us
    concatenate x4, other arithmetic, with_halo(): jnp.concatenate([lax.ppermute(tail, axis, [(i, (i + 1) % count) for i in...  16.6 us
    pallas_call x1, Pallas kernels, project(): pl.pallas_call(functools.partial(projection_kernel, normalize=normalize),...  11.6 us
  transfers between devices with their start and end apart: 9, of which 4 were waited for; matrix products, arithmetic and copies ran while one was open for 9% of the time, Pallas kernels for 11%

profile of v12, /device:TPU:6, one launch (start us, length us, event | category | flops | bytes accessed | tf_op | source)
XLA Modules:
  0.0 377.7 jit_solution(11025097753452297522)
XLA Ops:
  6.5 27.0 %shard_map.82 = bf16[8,24,4608]{2,1,0:T(8,128)(2,1)} custom-call(bf16[24,4608]{1,0:T(8,128)(2,1)} %w_ref.1), custom_call_target="tpu_custom_call" | custom-call | tf_op jit(solution)/shard_map/pallas_call | solution.py:273
  33.6 2.7 convert_reduce_fusion
  36.5 3.3 multiply_reduce_fusion
  40.5 4.9 %fusion.3.x_ref = bf16[640,3072]{1,0:T(8,128)(2,1)} fusion(bf16[2,4,80,3072]{3,2,1,0:T(8,128)(2,1)} %param.8, f32[3072]{0:T(1024)S(1)} %copy-done.4, f32[3072]{0:T(1024)S(1)} %broadcast_add_fusion.1, f32[640]{0:T(1024)S(1)} %rsqrt.12, f32[640]{0:T(1024)S(1)} %div.29), kind=kLoop, calls=%fused_computation.6 | loop fusion | flops 11796480 | bytes 7894016 | tf_op jit(solution)/shard_map/convert_element_type | solution.py:44
  45.4 153.0 %all-gather.2.cloned.1.call-done.w_ref = bf16[3072,4608]{1,0:T(8,128)(2,1)} async-done(((bf16[192,4608]{1,0:T(8,128)(2,1)}), bf16[3072,4608]{1,0:T(8,128)(2,1)}) %all-gather.2.cloned.1.call-update) | async-done | bytes 28311568 | tf_op jit(solution)/shard_map/all_gather | solution.py:66
  198.4 11.6 %shard_map.85 = bf16[2,640,768]{2,1,0:T(8,128)(2,1)} custom-call(bf16[640,3072]{1,0:T(8,128)(2,1)} %fusion.3.x_ref, bf16[3072,4608]{1,0:T(8,128)(2,1)} %all-gather.2.cloned.1.call-done.w_ref, f32[1,128]{1,0:T(1,128)} %bitcast.37), custom_call_target="tpu_custom_call" | custom-call | tf_op jit(solution)/shard_map/pallas_call | solution.py:311
  210.0 2.9 fusion.8
  215.1 7.0 %collective-permute-start.5 = (bf16[2,1,1,2,2,80,768]{6,5,4,3,1,0,2:T(8,128)(2,1)}, bf16[2,1,1,2,2,80,768]{6,5,4,3,1,0,2:T(8,128)(2,1)}, u32[]{:S(2)}, u32[]{:S(2)}) collective-permute-start(bf16[2,1,1,2,2,80,768]{6,5,4,3,1,0,2:T(8,128)(2,1)} %get-tuple-element.10), channel_id=1, source_target_pairs={{8,0},{16,8},{24,16},{32,24},{40,32},{48,40},{56,48},{64,56},{72,6... | collective-permute-start | bytes 2949128 | tf_op jit(solution)/shard_map/ppermute | solution.py:31
  222.3 11.6 %shard_map.84 = bf16[2,640,768]{2,1,0:T(8,128)(2,1)} custom-call(bf16[640,3072]{1,0:T(8,128)(2,1)} %fusion.3.x_ref, bf16[3072,4608]{1,0:T(8,128)(2,1)} %all-gather.2.cloned.1.call-done.w_ref, f32[1,128]{1,0:T(1,128)} %bitcast.38), custom_call_target="tpu_custom_call" | custom-call | tf_op jit(solution)/shard_map/pallas_call | solution.py:311
  233.9 3.0 fusion.9
  238.8 7.3 %collective-permute-start.1 = (bf16[2,1,1,2,2,80,768]{6,5,4,3,1,0,2:T(8,128)(2,1)}, bf16[2,1,1,2,2,80,768]{6,5,4,3,1,0,2:T(8,128)(2,1)}, u32[]{:S(2)}, u32[]{:S(2)}) collective-permute-start(bf16[2,1,1,2,2,80,768]{6,5,4,3,1,0,2:T(8,128)(2,1)} %get-tuple-element.12), channel_id=1, source_target_pairs={{8,0},{16,8},{24,16},{32,24},{40,32},{48,40},{56,48},{64,56},{72,6... | collective-permute-start | bytes 2949128 | tf_op jit(solution)/shard_map/ppermute | solution.py:31
  249.0 2.2 fusion.6
  251.2 3.4 collective-permute-start.6
  254.6 4.5 %collective-permute-start.7 = (bf16[2,4,1,1,2,80,768]{6,5,4,3,1,0,2:T(8,128)(2,1)}, bf16[2,4,1,1,2,80,768]{6,5,4,3,1,0,2:T(8,128)(2,1)}, u32[]{:S(2)}, u32[]{:S(2)}) collective-permute-start(bf16[2,4,1,1,2,80,768]{6,5,4,3,1,0,2:T(8,128)(2,1)} %get-tuple-element.6), channel_id=1, source_target_pairs={{1,0},{2,1},{3,2},{4,3},{5,4},{6,5},{7,6},{9,8},{10,9},{11,10},{12... | collective-permute-start | bytes 5898248 | tf_op jit(solution)/shard_map/ppermute | solution.py:31
  261.5 2.3 pad_maximum_fusion.2
  263.8 2.3 fusion.7
  268.0 8.4 %collective-permute-start.3 = (bf16[2,4,1,1,2,80,768]{6,5,4,3,1,0,2:T(8,128)(2,1)}, bf16[2,4,1,1,2,80,768]{6,5,4,3,1,0,2:T(8,128)(2,1)}, u32[]{:S(2)}, u32[]{:S(2)}) collective-permute-start(bf16[2,4,1,1,2,80,768]{6,5,4,3,1,0,2:T(8,128)(2,1)} %get-tuple-element.8), channel_id=1, source_target_pairs={{1,0},{2,1},{3,2},{4,3},{5,4},{6,5},{7,6},{9,8},{10,9},{11,10},{12... | collective-permute-start | bytes 5898248 | tf_op jit(solution)/shard_map/ppermute | solution.py:31
  279.9 11.6 %shard_map.83 = bf16[640,1536]{1,0:T(8,128)(2,1)} custom-call(bf16[640,3072]{1,0:T(8,128)(2,1)} %fusion.3.x_ref, bf16[3072,4608]{1,0:T(8,128)(2,1)} %all-gather.2.cloned.1.call-done.w_ref, f32[1,128]{1,0:T(1,128)} %bitcast.39), custom_call_target="tpu_custom_call" | custom-call | tf_op jit(solution)/shard_map/pallas_call | solution.py:214
  291.5 18.9 %collective-permute-done.6 = bf16[2,4,1,1,2,80,768]{6,5,4,3,1,0,2:T(8,128)(2,1)} collective-permute-done((bf16[2,4,1,1,2,80,768]{6,5,4,3,1,0,2:T(8,128)(2,1)}, bf16[2,4,1,1,2,80,768]{6,5,4,3,1,0,2:T(8,128)(2,1)}, u32[]{:S(2)}, u32[]{:S(2)}) %collective-permute-start.6) | collective-permute-done | bytes 1966112 | tf_op jit(solution)/shard_map/ppermute | solution.py:29
  310.4 6.3 %pad_maximum_fusion.1 = bf16[2,4,1,4,2,80,768]{6,5,4,3,1,0,2:T(8,128)(2,1)} fusion(bf16[2,4,1,1,2,80,768]{6,5,4,3,1,0,2:T(8,128)(2,1)} %collective-permute-done.7, bf16[2,1,1,2,2,80,768]{6,5,4,3,1,0,2:T(8,128)(2,1)} %collective-permute-done.5, bf16[2,2,1,2,2,80,768]{6,5,4,3,1,0,2:T(8,128)(2,1)S(1)} %bitcast.30, ...), kind=kLoop, calls=%fused_computation.1 | loop fusion | flops 15728640 | bytes 15728640 | tf_op jit(solution)/shard_map/concatenate | solution.py:27
  316.7 19.4 %shard_map.86.refs_8_ = bf16[2,4,80,1536]{3,2,1,0:T(8,128)(2,1)} custom-call(bf16[2,4,80,1536]{3,2,1,0:T(8,128)(2,1)} %bitcast.34, bf16[2,4,8,80,768]{4,3,2,1,0:T(8,128)(2,1)} %bitcast.24, bf16[2,4,8,80,768]{4,3,2,1,0:T(8,128)(2,1)} %bitcast.25, f32[12,4,1,1440]{3,2,1,0:T(1,128)} %and_convert_fusion.km_ref.refs_3_, ...), custom_call_target="tpu_custom_call" | custom-call | tf_op jit(solution)/shard_map/pallas_call | solution.py:185
  336.1 9.0 %collective-permute-done.2 = bf16[2,4,1,1,2,80,768]{6,5,4,3,1,0,2:T(8,128)(2,1)} collective-permute-done((bf16[2,4,1,1,2,80,768]{6,5,4,3,1,0,2:T(8,128)(2,1)}, bf16[2,4,1,1,2,80,768]{6,5,4,3,1,0,2:T(8,128)(2,1)}, u32[]{:S(2)}, u32[]{:S(2)}) %collective-permute-start.2) | collective-permute-done | bytes 1966112 | tf_op jit(solution)/shard_map/ppermute | solution.py:29
  345.1 6.5 %pad_maximum_fusion = bf16[2,4,1,4,2,80,768]{6,5,4,3,1,0,2:T(8,128)(2,1)} fusion(bf16[2,4,1,1,2,80,768]{6,5,4,3,1,0,2:T(8,128)(2,1)} %collective-permute-done.3, bf16[2,1,1,2,2,80,768]{6,5,4,3,1,0,2:T(8,128)(2,1)} %collective-permute-done.1, bf16[2,2,1,2,2,80,768]{6,5,4,3,1,0,2:T(8,128)(2,1)S(1)} %bitcast.33, ...), kind=kLoop, calls=%fused_computation | loop fusion | flops 15728640 | bytes 15728640 | tf_op jit(solution)/shard_map/concatenate | solution.py:27
  351.6 19.3 %shard_map.87 = bf16[2,4,80,1536]{3,2,1,0:T(8,128)(2,1)} custom-call(bf16[2,4,80,1536]{3,2,1,0:T(8,128)(2,1)} %bitcast.35, bf16[2,4,8,80,768]{4,3,2,1,0:T(8,128)(2,1)} %bitcast.26, bf16[2,4,8,80,768]{4,3,2,1,0:T(8,128)(2,1)} %bitcast.27, f32[12,4,1,1440]{3,2,1,0:T(1,128)} %and_convert_fusion.km_ref.refs_3_, ...), custom_call_target="tpu_custom_call", output_to_operand_aliasing={{}: (8, {})} | custom-call | tf_op jit(solution)/shard_map/pallas_call | solution.py:185
  (56 shorter events, 15.6 us)
Async XLA Ops:
  6.5 191.9 %all-gather.2.cloned.1.call-start = ((), (), s32[]{:S(2)}) async-start(), calls=%async_computation | async-start | bytes 30081024 | tf_op jit(solution)/shard_map/all_gather | solution.py:66
  33.6 6.2 %copy-start.7 = (s32[12,3]{0,1:T(4,128)S(1)}, s32[12,3]{0,1:T(4,128)}, u32[]{:S(2)}) copy-start(s32[12,3]{0,1:T(4,128)} %param.14) | copy-start | bytes 436
  33.6 6.8 %copy-start.3 = (f32[3072]{0:T(1024)S(1)}, f32[3072]{0:T(1024)}, u32[]{:S(2)}) copy-start(f32[3072]{0:T(1024)} %param.9) | copy-start | bytes 36868
  33.6 6.8 %copy-start.4 = (f32[3072]{0:T(1024)S(1)}, f32[3072]{0:T(1024)}, u32[]{:S(2)}) copy-start(f32[3072]{0:T(1024)} %param.10) | copy-start | bytes 36868
  212.9 34.6 %collective-permute-start.4 = (bf16[2,1,1,2,2,80,768]{6,5,4,3,1,0,2:T(8,128)(2,1)}, bf16[2,1,1,2,2,80,768]{6,5,4,3,1,0,2:T(8,128)(2,1)S(1)}, u32[]{:S(2)}, u32[]{:S(2)}) collective-permute-start(bf16[2,1,1,2,2,80,768]{6,5,4,3,1,0,2:T(8,128)(2,1)} %get-tuple-element.9), channel_id=1, source_target_pairs={{0,8},{8,16},{16,24},{24,32},{32,40},{40,48},{48,56},{56,64},{64,7... | collective-permute-start | bytes 2949128 | tf_op jit(solution)/shard_map/ppermute | solution.py:29
  215.1 32.4 %collective-permute-start.5 = (bf16[2,1,1,2,2,80,768]{6,5,4,3,1,0,2:T(8,128)(2,1)}, bf16[2,1,1,2,2,80,768]{6,5,4,3,1,0,2:T(8,128)(2,1)}, u32[]{:S(2)}, u32[]{:S(2)}) collective-permute-start(bf16[2,1,1,2,2,80,768]{6,5,4,3,1,0,2:T(8,128)(2,1)} %get-tuple-element.10), channel_id=1, source_target_pairs={{8,0},{16,8},{24,16},{32,24},{40,32},{48,40},{56,48},{64,56},{72,6... | collective-permute-start | bytes 2949128 | tf_op jit(solution)/shard_map/ppermute | solution.py:31
  233.9 13.6 %copy-start = (bf16[2,640,768]{2,1,0:T(8,128)(2,1)S(1)}, bf16[2,640,768]{2,1,0:T(8,128)(2,1)}, u32[]{:S(2)}) copy-start(bf16[2,640,768]{2,1,0:T(8,128)(2,1)} %shard_map.85) | copy-start | bytes 5898244
  236.9 23.0 %collective-permute-start = (bf16[2,1,1,2,2,80,768]{6,5,4,3,1,0,2:T(8,128)(2,1)}, bf16[2,1,1,2,2,80,768]{6,5,4,3,1,0,2:T(8,128)(2,1)}, u32[]{:S(2)}, u32[]{:S(2)}) collective-permute-start(bf16[2,1,1,2,2,80,768]{6,5,4,3,1,0,2:T(8,128)(2,1)} %get-tuple-element.11), channel_id=1, source_target_pairs={{0,8},{8,16},{16,24},{24,32},{32,40},{40,48},{48,56},{56,64},{64,7... | collective-permute-start | bytes 2949128 | tf_op jit(solution)/shard_map/ppermute | solution.py:29
  238.8 22.7 %collective-permute-start.1 = (bf16[2,1,1,2,2,80,768]{6,5,4,3,1,0,2:T(8,128)(2,1)}, bf16[2,1,1,2,2,80,768]{6,5,4,3,1,0,2:T(8,128)(2,1)}, u32[]{:S(2)}, u32[]{:S(2)}) collective-permute-start(bf16[2,1,1,2,2,80,768]{6,5,4,3,1,0,2:T(8,128)(2,1)} %get-tuple-element.12), channel_id=1, source_target_pairs={{8,0},{16,8},{24,16},{32,24},{40,32},{48,40},{56,48},{64,56},{72,6... | collective-permute-start | bytes 2949128 | tf_op jit(solution)/shard_map/ppermute | solution.py:31
  249.0 10.5 %copy-start.2 = (s32[32,32,80]{2,1,0:T(8,128)S(1)}, s32[32,32,80]{2,1,0:T(8,128)}, u32[]{:S(2)}) copy-start(s32[32,32,80]{2,1,0:T(8,128)} %param.15) | copy-start | bytes 983044
  251.2 59.2 %collective-permute-start.6 = (bf16[2,4,1,1,2,80,768]{6,5,4,3,1,0,2:T(8,128)(2,1)}, bf16[2,4,1,1,2,80,768]{6,5,4,3,1,0,2:T(8,128)(2,1)}, u32[]{:S(2)}, u32[]{:S(2)}) collective-permute-start(bf16[2,4,1,1,2,80,768]{6,5,4,3,1,0,2:T(8,128)(2,1)} %get-tuple-element.5), channel_id=1, source_target_pairs={{0,1},{1,2},{2,3},{3,4},{4,5},{5,6},{6,7},{8,9},{9,10},{10,11},{11... | collective-permute-start | bytes 5898248 | tf_op jit(solution)/shard_map/ppermute | solution.py:29
  254.6 55.8 %collective-permute-start.7 = (bf16[2,4,1,1,2,80,768]{6,5,4,3,1,0,2:T(8,128)(2,1)}, bf16[2,4,1,1,2,80,768]{6,5,4,3,1,0,2:T(8,128)(2,1)}, u32[]{:S(2)}, u32[]{:S(2)}) collective-permute-start(bf16[2,4,1,1,2,80,768]{6,5,4,3,1,0,2:T(8,128)(2,1)} %get-tuple-element.6), channel_id=1, source_target_pairs={{1,0},{2,1},{3,2},{4,3},{5,4},{6,5},{7,6},{9,8},{10,9},{11,10},{12... | collective-permute-start | bytes 5898248 | tf_op jit(solution)/shard_map/ppermute | solution.py:31
  263.8 13.6 %copy-start.5 = (s32[160]{0:T(256)S(1)}, s32[160]{0:T(256)}, u32[]{:S(2)}) copy-start(s32[160]{0:T(256)} %sub.71) | copy-start | bytes 1924
  263.8 13.6 %copy-start.6 = (s32[12]{0:T(128)S(1)}, s32[12]{0:T(128)}, u32[]{:S(2)}) copy-start(s32[12]{0:T(128)} %get-tuple-element.17) | copy-start | bytes 148
  266.1 79.0 %collective-permute-start.2 = (bf16[2,4,1,1,2,80,768]{6,5,4,3,1,0,2:T(8,128)(2,1)}, bf16[2,4,1,1,2,80,768]{6,5,4,3,1,0,2:T(8,128)(2,1)}, u32[]{:S(2)}, u32[]{:S(2)}) collective-permute-start(bf16[2,4,1,1,2,80,768]{6,5,4,3,1,0,2:T(8,128)(2,1)} %get-tuple-element.7), channel_id=1, source_target_pairs={{0,1},{1,2},{2,3},{3,4},{4,5},{5,6},{6,7},{8,9},{9,10},{10,11},{11... | collective-permute-start | bytes 5898248 | tf_op jit(solution)/shard_map/ppermute | solution.py:29
  268.0 77.0 %collective-permute-start.3 = (bf16[2,4,1,1,2,80,768]{6,5,4,3,1,0,2:T(8,128)(2,1)}, bf16[2,4,1,1,2,80,768]{6,5,4,3,1,0,2:T(8,128)(2,1)}, u32[]{:S(2)}, u32[]{:S(2)}) collective-permute-start(bf16[2,4,1,1,2,80,768]{6,5,4,3,1,0,2:T(8,128)(2,1)} %get-tuple-element.8), channel_id=1, source_target_pairs={{1,0},{2,1},{3,2},{4,3},{5,4},{6,5},{7,6},{9,8},{10,9},{11,10},{12... | collective-permute-start | bytes 5898248 | tf_op jit(solution)/shard_map/ppermute | solution.py:31
  316.7 28.4 %copy-start.1 = (bf16[2,640,768]{2,1,0:T(8,128)(2,1)S(1)}, bf16[2,640,768]{2,1,0:T(8,128)(2,1)}, u32[]{:S(2)}) copy-start(bf16[2,640,768]{2,1,0:T(8,128)(2,1)} %shard_map.84) | copy-start | bytes 5898244
Sparse Core Ops, SparseCore 0:
  33.7 164.6 all-gather.1

commit v13 on v11

--- a/solution.py
+++ b/solution.py
@@ -73,7 +73,6 @@
         stacked = project_kv(modulated, full_weight, start, group_cols, k_gain)
         stacked = stacked.reshape(2, *tiled)
         groups.append(with_halo(stacked, (("tm", 1), ("height", 3)), 1))
-    query = project(modulated, full_weight, 0, inner, q_gain)
     frames_ext = frame_count + 2 * TT
     rows_ext = row_count + 2 * TH
     groups = [g.reshape(2, frames_ext, rows_ext, width, group_cols) for g in groups]
@@ -115,11 +114,15 @@
     query_lo = (query_cols[None, :] - window[:, 2, None]).reshape(HEADS, query_n, 1)
     query_hi = (query_cols[None, :] + window[:, 2, None]).reshape(HEADS, query_n, 1)
     query_ok = query_valid.reshape(blocks, query_n, 1).astype(jnp.float32)
-    query_grid = query.reshape(frame_count, row_count, width, inner)
     out = None
     for group, extended in enumerate(groups):
+        source = modulated
+        if out is not None:
+            source, out = lax.optimization_barrier((modulated, out))
+        query = project(source, full_weight, group * group_cols, group_cols, q_gain)
+        query = query.reshape(frame_count, row_count, width, group_cols)
         out = tile_attention(
-            query_grid, extended, key_mask, query_lo, query_hi, key_cols, query_ok, group, out
+            query, extended, key_mask, query_lo, query_hi, key_cols, query_ok, group, out
         )
     return out
 
@@ -154,8 +157,9 @@
 
 
 def tile_attention(query, extended, key_mask, query_lo, query_hi, key_cols, query_ok, group, out):
-    frames, rows, width, inner = query.shape
-    heads = extended.shape[-1] // HDIM
+    frames, rows, width, group_cols = query.shape
+    heads = group_cols // HDIM
+    out_shape = (frames, rows, width, key_mask.shape[0] * HDIM)
     first = group * heads
     row_tiles = rows // TH
     assert row_tiles == ROW_TILES
@@ -163,7 +167,8 @@
     _, frames_ext, rows_ext, _, _ = extended.shape
     key_n = key_mask.shape[-1]
     query_n = TH * width
-    q_spec = pl.BlockSpec((frames, rows, width, HDIM), lambda h: (0, 0, 0, first + h))
+    q_spec = pl.BlockSpec((frames, rows, width, HDIM), lambda h: (0, 0, 0, h))
+    o_spec = pl.BlockSpec((frames, rows, width, HDIM), lambda h: (0, 0, 0, first + h))
     in_specs = [
         q_spec,
         pl.BlockSpec((1, frames_ext, rows_ext, width, HDIM), lambda h: (0, 0, 0, 0, h)),
@@ -186,8 +191,8 @@
         kernel,
         grid=(heads,),
         in_specs=in_specs,
-        out_specs=q_spec,
-        out_shape=jax.ShapeDtypeStruct(query.shape, jnp.bfloat16),
+        out_specs=o_spec,
+        out_shape=jax.ShapeDtypeStruct(out_shape, jnp.bfloat16),
         input_output_aliases=aliases,
     )(*operands)
 

time: 379 us -> 379 us (level)
    pallas_call x1 -> x2, Pallas kernels: 11.7 us -> 15.1 us  [project(): pl.pallas_call(functools.partial(projection_kernel, normalize=normalize),...]
  transfers between devices with their start and end apart: 9 -> 9, of which waited for: 4 -> 4; matrix products, arithmetic and copies ran while one was open for 9% -> 9% of each run, Pallas kernels for 11% -> 12%
where the time goes in v13:
time: 379 us; the launch traced here: 378 us
  waiting for transfers between devices  179 us (47%)
  Pallas kernels  104 us (27%)
  starting transfers between devices  36.6 us (10%)
  other arithmetic  30.4 us (8%)
  local copies, waits for them, and re-layouts  14.2 us (4%)
  between operations  13.7 us (4%)
    all_gather x1, waiting for transfers between devices, per_device(): full_weight = lax.all_gather(band_weight, 'tm', axis=0, tiled=True)  154 us
    pallas_call x2, Pallas kernels, tile_attention(): pl.pallas_call(kernel, grid=(heads,), in_specs=in_specs, out_specs=o_spec...  38.7 us
    ppermute x4, starting transfers between devices, with_halo(): lax.ppermute(head, axis, [((i + 1) % count, i) for i in range(ends)])  27.2 us
    pallas_call x1, Pallas kernels, band_gather(): pl.pallas_call(band_gather_kernel, in_specs=[pl.BlockSpec(memory_space=pl...  27 us
    ppermute x4, waiting for transfers between devices, with_halo(): lax.ppermute(tail, axis, [(i, (i + 1) % count) for i in range(ends)])  25.1 us
    pallas_call x2, Pallas kernels, project_kv(): pl.pallas_call(projection_kv_kernel, grid=(2 * steps,), in_specs=[pl.Bloc...  23.5 us
    concatenate x4, other arithmetic, with_halo(): jnp.concatenate([lax.ppermute(tail, axis, [(i, (i + 1) % count) for i in...  16.6 us
    pallas_call x2, Pallas kernels, project(): pl.pallas_call(functools.partial(projection_kernel, normalize=normalize),...  15.1 us
  transfers between devices with their start and end apart: 9, of which 4 were waited for; matrix products, arithmetic and copies ran while one was open for 9% of the time, Pallas kernels for 12%

profile of v13, /device:TPU:6, one launch (start us, length us, event | category | flops | bytes accessed | tf_op | source)
XLA Modules:
  0.0 378.2 jit_solution(16518119773919010052)
XLA Ops:
  6.5 27.0 %shard_map.82 = bf16[8,24,4608]{2,1,0:T(8,128)(2,1)} custom-call(bf16[24,4608]{1,0:T(8,128)(2,1)} %w_ref.1), custom_call_target="tpu_custom_call" | custom-call | tf_op jit(solution)/shard_map/pallas_call | solution.py:278
  33.6 2.7 convert_reduce_fusion
  36.5 3.3 multiply_reduce_fusion
  39.9 4.9 %fusion.3.x_ref = bf16[640,3072]{1,0:T(8,128)(2,1)} fusion(bf16[2,4,80,3072]{3,2,1,0:T(8,128)(2,1)} %param.8, f32[3072]{0:T(1024)S(1)} %copy-done.6, f32[3072]{0:T(1024)S(1)} %broadcast_add_fusion.1, f32[640]{0:T(1024)S(1)} %rsqrt.12, f32[640]{0:T(1024)S(1)} %div.29), kind=kLoop, calls=%fused_computation.6 | loop fusion | flops 11796480 | bytes 7894016 | tf_op jit(solution)/shard_map/convert_element_type | solution.py:44
  44.8 153.6 %all-gather.2.cloned.1.call-done.w_ref = bf16[3072,4608]{1,0:T(8,128)(2,1)} async-done(((bf16[192,4608]{1,0:T(8,128)(2,1)}), bf16[3072,4608]{1,0:T(8,128)(2,1)}) %all-gather.2.cloned.1.call-update) | async-done | bytes 28311568 | tf_op jit(solution)/shard_map/all_gather | solution.py:66
  198.4 11.7 %shard_map.84 = bf16[2,640,768]{2,1,0:T(8,128)(2,1)} custom-call(bf16[640,3072]{1,0:T(8,128)(2,1)} %fusion.3.x_ref, bf16[3072,4608]{1,0:T(8,128)(2,1)} %all-gather.2.cloned.1.call-done.w_ref, f32[1,128]{1,0:T(1,128)} %bitcast.38), custom_call_target="tpu_custom_call" | custom-call | tf_op jit(solution)/shard_map/pallas_call | solution.py:316
  210.1 3.0 fusion.9
  213.2 2.2 collective-permute-start
  215.3 7.0 %collective-permute-start.1 = (bf16[2,1,1,2,2,80,768]{6,5,4,3,1,0,2:T(8,128)(2,1)}, bf16[2,1,1,2,2,80,768]{6,5,4,3,1,0,2:T(8,128)(2,1)}, u32[]{:S(2)}, u32[]{:S(2)}) collective-permute-start(bf16[2,1,1,2,2,80,768]{6,5,4,3,1,0,2:T(8,128)(2,1)} %get-tuple-element.16), channel_id=1, source_target_pairs={{8,0},{16,8},{24,16},{32,24},{40,32},{48,40},{56,48},{64,56},{72,6... | collective-permute-start | bytes 2949128 | tf_op jit(solution)/shard_map/ppermute | solution.py:31
  222.5 11.8 %shard_map.87 = bf16[2,640,768]{2,1,0:T(8,128)(2,1)} custom-call(bf16[640,3072]{1,0:T(8,128)(2,1)} %fusion.3.x_ref, bf16[3072,4608]{1,0:T(8,128)(2,1)} %all-gather.2.cloned.1.call-done.w_ref, f32[1,128]{1,0:T(1,128)} %bitcast.39), custom_call_target="tpu_custom_call" | custom-call | tf_op jit(solution)/shard_map/pallas_call | solution.py:316
  234.3 3.0 fusion.8
  239.3 7.3 %collective-permute-start.5 = (bf16[2,1,1,2,2,80,768]{6,5,4,3,1,0,2:T(8,128)(2,1)}, bf16[2,1,1,2,2,80,768]{6,5,4,3,1,0,2:T(8,128)(2,1)}, u32[]{:S(2)}, u32[]{:S(2)}) collective-permute-start(bf16[2,1,1,2,2,80,768]{6,5,4,3,1,0,2:T(8,128)(2,1)} %get-tuple-element.14), channel_id=1, source_target_pairs={{8,0},{16,8},{24,16},{32,24},{40,32},{48,40},{56,48},{64,56},{72,6... | collective-permute-start | bytes 2949128 | tf_op jit(solution)/shard_map/ppermute | solution.py:31
  249.7 2.3 fusion.7
  252.0 3.4 collective-permute-start.2
  255.4 4.5 %collective-permute-start.3 = (bf16[2,4,1,1,2,80,768]{6,5,4,3,1,0,2:T(8,128)(2,1)}, bf16[2,4,1,1,2,80,768]{6,5,4,3,1,0,2:T(8,128)(2,1)}, u32[]{:S(2)}, u32[]{:S(2)}) collective-permute-start(bf16[2,4,1,1,2,80,768]{6,5,4,3,1,0,2:T(8,128)(2,1)} %get-tuple-element.12), channel_id=1, source_target_pairs={{1,0},{2,1},{3,2},{4,3},{5,4},{6,5},{7,6},{9,8},{10,9},{11,10},{12... | collective-permute-start | bytes 5898248 | tf_op jit(solution)/shard_map/ppermute | solution.py:31
  261.6 2.3 pad_maximum_fusion.3
  268.0 8.4 %collective-permute-start.7 = (bf16[2,4,1,1,2,80,768]{6,5,4,3,1,0,2:T(8,128)(2,1)}, bf16[2,4,1,1,2,80,768]{6,5,4,3,1,0,2:T(8,128)(2,1)}, u32[]{:S(2)}, u32[]{:S(2)}) collective-permute-start(bf16[2,4,1,1,2,80,768]{6,5,4,3,1,0,2:T(8,128)(2,1)} %get-tuple-element.10), channel_id=1, source_target_pairs={{1,0},{2,1},{3,2},{4,3},{5,4},{6,5},{7,6},{9,8},{10,9},{11,10},{12... | collective-permute-start | bytes 5898248 | tf_op jit(solution)/shard_map/ppermute | solution.py:31
  279.7 7.5 %shard_map.83 = bf16[640,768]{1,0:T(8,128)(2,1)} custom-call(bf16[640,3072]{1,0:T(8,128)(2,1)} %fusion.3.x_ref, bf16[3072,4608]{1,0:T(8,128)(2,1)} %all-gather.2.cloned.1.call-done.w_ref, f32[1,128]{1,0:T(1,128)} %bitcast.40), custom_call_target="tpu_custom_call" | custom-call | tf_op jit(solution)/shard_map/pallas_call | solution.py:219
  287.2 23.3 %collective-permute-done.2 = bf16[2,4,1,1,2,80,768]{6,5,4,3,1,0,2:T(8,128)(2,1)} collective-permute-done((bf16[2,4,1,1,2,80,768]{6,5,4,3,1,0,2:T(8,128)(2,1)}, bf16[2,4,1,1,2,80,768]{6,5,4,3,1,0,2:T(8,128)(2,1)}, u32[]{:S(2)}, u32[]{:S(2)}) %collective-permute-start.2) | collective-permute-done | bytes 1966112 | tf_op jit(solution)/shard_map/ppermute | solution.py:29
  310.5 6.3 %pad_maximum_fusion = bf16[2,4,1,4,2,80,768]{6,5,4,3,1,0,2:T(8,128)(2,1)} fusion(bf16[2,4,1,1,2,80,768]{6,5,4,3,1,0,2:T(8,128)(2,1)} %collective-permute-done.3, bf16[2,1,1,2,2,80,768]{6,5,4,3,1,0,2:T(8,128)(2,1)} %collective-permute-done.1, bf16[2,2,1,2,2,80,768]{6,5,4,3,1,0,2:T(8,128)(2,1)S(1)} %bitcast.31, ...), kind=kLoop, calls=%fused_computation | loop fusion | flops 15728640 | bytes 15728640 | tf_op jit(solution)/shard_map/concatenate | solution.py:27
  316.8 19.3 %shard_map.85.refs_8_ = bf16[2,4,80,1536]{3,2,1,0:T(8,128)(2,1)} custom-call(bf16[2,4,80,768]{3,2,1,0:T(8,128)(2,1)} %bitcast.37, bf16[2,4,8,80,768]{4,3,2,1,0:T(8,128)(2,1)} %bitcast.27, bf16[2,4,8,80,768]{4,3,2,1,0:T(8,128)(2,1)} %bitcast.28, f32[12,4,1,1440]{3,2,1,0:T(1,128)} %and_convert_fusion.km_ref.refs_3_, ...), custom_call_target="tpu_custom_call" | custom-call | tf_op jit(solution)/shard_map/pallas_call | solution.py:190
  336.1 7.6 %shard_map.86 = bf16[640,768]{1,0:T(8,128)(2,1)} custom-call(bf16[640,3072]{1,0:T(8,128)(2,1)} %fusion.3.x_ref, bf16[3072,4608]{1,0:T(8,128)(2,1)} %all-gather.2.cloned.1.call-done.w_ref, f32[1,128]{1,0:T(1,128)} %bitcast.41), custom_call_target="tpu_custom_call" | custom-call | tf_op jit(solution)/shard_map/pallas_call | solution.py:219
  345.5 6.5 %pad_maximum_fusion.1 = bf16[2,4,1,4,2,80,768]{6,5,4,3,1,0,2:T(8,128)(2,1)} fusion(bf16[2,4,1,1,2,80,768]{6,5,4,3,1,0,2:T(8,128)(2,1)} %collective-permute-done.7, bf16[2,1,1,2,2,80,768]{6,5,4,3,1,0,2:T(8,128)(2,1)} %collective-permute-done.5, bf16[2,2,1,2,2,80,768]{6,5,4,3,1,0,2:T(8,128)(2,1)S(1)} %bitcast.34, ...), kind=kLoop, calls=%fused_computation.1 | loop fusion | flops 15728640 | bytes 15728640 | tf_op jit(solution)/shard_map/concatenate | solution.py:27
  352.0 19.4 %shard_map.88 = bf16[2,4,80,1536]{3,2,1,0:T(8,128)(2,1)} custom-call(bf16[2,4,80,768]{3,2,1,0:T(8,128)(2,1)} %bitcast.36, bf16[2,4,8,80,768]{4,3,2,1,0:T(8,128)(2,1)} %bitcast.25, bf16[2,4,8,80,768]{4,3,2,1,0:T(8,128)(2,1)} %bitcast.26, f32[12,4,1,1440]{3,2,1,0:T(1,128)} %and_convert_fusion.km_ref.refs_3_, ...), custom_call_target="tpu_custom_call", output_to_operand_aliasing={{}: (8, {})} | custom-call | tf_op jit(solution)/shard_map/pallas_call | solution.py:190
  (57 shorter events, 16.2 us)
Async XLA Ops:
  6.5 191.9 %all-gather.2.cloned.1.call-start = ((), (), s32[]{:S(2)}) async-start(), calls=%async_computation | async-start | bytes 30081024 | tf_op jit(solution)/shard_map/all_gather | solution.py:66
  33.6 6.2 %copy-start.7 = (s32[12,3]{0,1:T(4,128)S(1)}, s32[12,3]{0,1:T(4,128)}, u32[]{:S(2)}) copy-start(s32[12,3]{0,1:T(4,128)} %param.14) | copy-start | bytes 436
  33.6 6.3 %copy-start.5 = (f32[3072]{0:T(1024)S(1)}, f32[3072]{0:T(1024)}, u32[]{:S(2)}) copy-start(f32[3072]{0:T(1024)} %param.9) | copy-start | bytes 36868
  33.6 6.3 %copy-start.6 = (f32[3072]{0:T(1024)S(1)}, f32[3072]{0:T(1024)}, u32[]{:S(2)}) copy-start(f32[3072]{0:T(1024)} %param.10) | copy-start | bytes 36868
  213.2 35.0 %collective-permute-start = (bf16[2,1,1,2,2,80,768]{6,5,4,3,1,0,2:T(8,128)(2,1)}, bf16[2,1,1,2,2,80,768]{6,5,4,3,1,0,2:T(8,128)(2,1)S(1)}, u32[]{:S(2)}, u32[]{:S(2)}) collective-permute-start(bf16[2,1,1,2,2,80,768]{6,5,4,3,1,0,2:T(8,128)(2,1)} %get-tuple-element.15), channel_id=1, source_target_pairs={{0,8},{8,16},{16,24},{24,32},{32,40},{40,48},{48,56},{56,64},{64,7... | collective-permute-start | bytes 2949128 | tf_op jit(solution)/shard_map/ppermute | solution.py:29
  215.3 32.8 %collective-permute-start.1 = (bf16[2,1,1,2,2,80,768]{6,5,4,3,1,0,2:T(8,128)(2,1)}, bf16[2,1,1,2,2,80,768]{6,5,4,3,1,0,2:T(8,128)(2,1)}, u32[]{:S(2)}, u32[]{:S(2)}) collective-permute-start(bf16[2,1,1,2,2,80,768]{6,5,4,3,1,0,2:T(8,128)(2,1)} %get-tuple-element.16), channel_id=1, source_target_pairs={{8,0},{16,8},{24,16},{32,24},{40,32},{48,40},{56,48},{64,56},{72,6... | collective-permute-start | bytes 2949128 | tf_op jit(solution)/shard_map/ppermute | solution.py:31
  234.3 12.2 %copy-start.2 = (s32[32,32,80]{2,1,0:T(8,128)S(1)}, s32[32,32,80]{2,1,0:T(8,128)}, u32[]{:S(2)}) copy-start(s32[32,32,80]{2,1,0:T(8,128)} %param.15) | copy-start | bytes 983044
  234.3 13.8 %copy-start = (bf16[2,640,768]{2,1,0:T(8,128)(2,1)S(1)}, bf16[2,640,768]{2,1,0:T(8,128)(2,1)}, u32[]{:S(2)}) copy-start(bf16[2,640,768]{2,1,0:T(8,128)(2,1)} %shard_map.84) | copy-start | bytes 5898244
  237.4 23.9 %collective-permute-start.4 = (bf16[2,1,1,2,2,80,768]{6,5,4,3,1,0,2:T(8,128)(2,1)}, bf16[2,1,1,2,2,80,768]{6,5,4,3,1,0,2:T(8,128)(2,1)}, u32[]{:S(2)}, u32[]{:S(2)}) collective-permute-start(bf16[2,1,1,2,2,80,768]{6,5,4,3,1,0,2:T(8,128)(2,1)} %get-tuple-element.13), channel_id=1, source_target_pairs={{0,8},{8,16},{16,24},{24,32},{32,40},{40,48},{48,56},{56,64},{64,7... | collective-permute-start | bytes 2949128 | tf_op jit(solution)/shard_map/ppermute | solution.py:29
  239.3 22.3 %collective-permute-start.5 = (bf16[2,1,1,2,2,80,768]{6,5,4,3,1,0,2:T(8,128)(2,1)}, bf16[2,1,1,2,2,80,768]{6,5,4,3,1,0,2:T(8,128)(2,1)}, u32[]{:S(2)}, u32[]{:S(2)}) collective-permute-start(bf16[2,1,1,2,2,80,768]{6,5,4,3,1,0,2:T(8,128)(2,1)} %get-tuple-element.14), channel_id=1, source_target_pairs={{8,0},{16,8},{24,16},{32,24},{40,32},{48,40},{56,48},{64,56},{72,6... | collective-permute-start | bytes 2949128 | tf_op jit(solution)/shard_map/ppermute | solution.py:31
  252.0 58.5 %collective-permute-start.2 = (bf16[2,4,1,1,2,80,768]{6,5,4,3,1,0,2:T(8,128)(2,1)}, bf16[2,4,1,1,2,80,768]{6,5,4,3,1,0,2:T(8,128)(2,1)}, u32[]{:S(2)}, u32[]{:S(2)}) collective-permute-start(bf16[2,4,1,1,2,80,768]{6,5,4,3,1,0,2:T(8,128)(2,1)} %get-tuple-element.11), channel_id=1, source_target_pairs={{0,1},{1,2},{2,3},{3,4},{4,5},{5,6},{6,7},{8,9},{9,10},{10,11},{11... | collective-permute-start | bytes 5898248 | tf_op jit(solution)/shard_map/ppermute | solution.py:29
  255.4 55.0 %collective-permute-start.3 = (bf16[2,4,1,1,2,80,768]{6,5,4,3,1,0,2:T(8,128)(2,1)}, bf16[2,4,1,1,2,80,768]{6,5,4,3,1,0,2:T(8,128)(2,1)}, u32[]{:S(2)}, u32[]{:S(2)}) collective-permute-start(bf16[2,4,1,1,2,80,768]{6,5,4,3,1,0,2:T(8,128)(2,1)} %get-tuple-element.12), channel_id=1, source_target_pairs={{1,0},{2,1},{3,2},{4,3},{5,4},{6,5},{7,6},{9,8},{10,9},{11,10},{12... | collective-permute-start | bytes 5898248 | tf_op jit(solution)/shard_map/ppermute | solution.py:31
  263.9 13.2 %copy-start.3 = (s32[1,1440]{1,0:T(1,128)S(1)}, s32[1,1440]{1,0:T(1,128)}, u32[]{:S(2)}) copy-start(s32[1,1440]{1,0:T(1,128)} %stack.13) | copy-start | bytes 17284
  263.9 13.2 %copy-start.4 = (s32[1,1440]{1,0:T(1,128)S(1)}, s32[1,1440]{1,0:T(1,128)}, u32[]{:S(2)}) copy-start(s32[1,1440]{1,0:T(1,128)} %stack.14) | copy-start | bytes 17284
  266.0 79.5 %collective-permute-start.6 = (bf16[2,4,1,1,2,80,768]{6,5,4,3,1,0,2:T(8,128)(2,1)}, bf16[2,4,1,1,2,80,768]{6,5,4,3,1,0,2:T(8,128)(2,1)}, u32[]{:S(2)}, u32[]{:S(2)}) collective-permute-start(bf16[2,4,1,1,2,80,768]{6,5,4,3,1,0,2:T(8,128)(2,1)} %get-tuple-element.9), channel_id=1, source_target_pairs={{0,1},{1,2},{2,3},{3,4},{4,5},{5,6},{6,7},{8,9},{9,10},{10,11},{11... | collective-permute-start | bytes 5898248 | tf_op jit(solution)/shard_map/ppermute | solution.py:29
  268.0 77.5 %collective-permute-start.7 = (bf16[2,4,1,1,2,80,768]{6,5,4,3,1,0,2:T(8,128)(2,1)}, bf16[2,4,1,1,2,80,768]{6,5,4,3,1,0,2:T(8,128)(2,1)}, u32[]{:S(2)}, u32[]{:S(2)}) collective-permute-start(bf16[2,4,1,1,2,80,768]{6,5,4,3,1,0,2:T(8,128)(2,1)} %get-tuple-element.10), channel_id=1, source_target_pairs={{1,0},{2,1},{3,2},{4,3},{5,4},{6,5},{7,6},{9,8},{10,9},{11,10},{12... | collective-permute-start | bytes 5898248 | tf_op jit(solution)/shard_map/ppermute | solution.py:31
  336.1 9.4 %copy-start.1 = (bf16[2,640,768]{2,1,0:T(8,128)(2,1)S(1)}, bf16[2,640,768]{2,1,0:T(8,128)(2,1)}, u32[]{:S(2)}) copy-start(bf16[2,640,768]{2,1,0:T(8,128)(2,1)} %shard_map.87) | copy-start | bytes 5898244
Sparse Core Ops, SparseCore 0:
  33.7 164.6 all-gather.1

commit v14 on v11

--- a/solution.py
+++ b/solution.py
@@ -72,11 +72,17 @@
         start = group * group_cols
         stacked = project_kv(modulated, full_weight, start, group_cols, k_gain)
         stacked = stacked.reshape(2, *tiled)
-        groups.append(with_halo(stacked, (("tm", 1), ("height", 3)), 1))
+        middle = with_halo(stacked, (("tm", 1),), 1)
+        middle = middle.reshape(2, frame_count + 2 * TT, row_count, width, group_cols)
+        count = lax.axis_size("height")
+        top = lax.ppermute(
+            middle[:, :, row_count - TH :], "height", [(i, i + 1) for i in range(count - 1)]
+        )
+        bottom = lax.ppermute(middle[:, :, :TH], "height", [(i + 1, i) for i in range(count - 1)])
+        groups.append((middle, top, bottom))
     query = project(modulated, full_weight, 0, inner, q_gain)
     frames_ext = frame_count + 2 * TT
     rows_ext = row_count + 2 * TH
-    groups = [g.reshape(2, frames_ext, rows_ext, width, group_cols) for g in groups]
     frame_block = lax.axis_index("tm")
     row_block = lax.axis_index("height")
     first_frame = frame_block * frame_count
@@ -116,36 +122,59 @@
     query_hi = (query_cols[None, :] + window[:, 2, None]).reshape(HEADS, query_n, 1)
     query_ok = query_valid.reshape(blocks, query_n, 1).astype(jnp.float32)
     query_grid = query.reshape(frame_count, row_count, width, inner)
+    assert row_count == 2 * TH
+    mask_rows = key_mask.reshape(HEADS, blocks, span_t, span_h, width)
+    halo_masks, own_masks = [], []
+    for block in range(blocks):
+        halo_rows = slice(0, TH) if block % row_tiles == 0 else slice(span_h - TH, span_h)
+        own_rows = slice(TH, span_h) if block % row_tiles == 0 else slice(0, row_count)
+        halo_masks.append(mask_rows[:, block, :, halo_rows].reshape(HEADS, 1, -1))
+        own_masks.append(mask_rows[:, block, :, own_rows].reshape(HEADS, 1, -1))
+    halo_mask = jnp.stack(halo_masks, axis=1)
+    own_mask = jnp.stack(own_masks, axis=1)
+    halo_cols = jnp.tile(column_tiles, span_t * TH).reshape(1, -1)
+    own_cols = jnp.tile(column_tiles, span_t * row_count).reshape(1, -1)
     out = None
-    for group, extended in enumerate(groups):
-        out = tile_attention(
-            query_grid, extended, key_mask, query_lo, query_hi, key_cols, query_ok, group, out
-        )
+    for group, pieces in enumerate(groups):
+        masks = (halo_mask, own_mask, query_lo, query_hi, halo_cols, own_cols, query_ok)
+        out = tile_attention(query_grid, pieces, masks, group, out)
     return out
 
 
-def attention_kernel(q_ref, k_ref, v_ref, km_ref, lo_ref, hi_ref, kc_ref, qv_ref, o_ref):
+def attention_kernel(
+    q_ref, mk_ref, mv_ref, tk_ref, tv_ref, bk_ref, bv_ref,
+    hm_ref, om_ref, lo_ref, hi_ref, hc_ref, oc_ref, qv_ref, o_ref,
+):
     span_t = 2 * TT + 1
-    span_h = 3 * TH
     width = q_ref.shape[2]
-    key_cols = kc_ref[...]
-    width_ok = (key_cols >= lo_ref[0]) & (key_cols <= hi_ref[0])
+    scale = 1.0 / float(HDIM) ** 0.5
+    halo_ok = (hc_ref[...] >= lo_ref[0]) & (hc_ref[...] <= hi_ref[0])
+    own_ok = (oc_ref[...] >= lo_ref[0]) & (oc_ref[...] <= hi_ref[0])
     for block in range(q_ref.shape[0] * ROW_TILES):
         frame, tile = divmod(block, ROW_TILES)
         row = tile * TH
+        hk_ref, hv_ref = (tk_ref, tv_ref) if tile == 0 else (bk_ref, bv_ref)
         query = q_ref[frame, row : row + TH].reshape(TH * width, HDIM)
-        key = k_ref[0, frame : frame + span_t, row : row + span_h].reshape(-1, HDIM)
-        value = v_ref[0, frame : frame + span_t, row : row + span_h].reshape(-1, HDIM)
-        scores = lax.dot_general(
-            query, key, (((1,), (1,)), ((), ())), preferred_element_type=jnp.float32
-        ) * (1.0 / float(HDIM) ** 0.5)
-        allowed = width_ok & (km_ref[0, block] > 0.0)
-        terms = jnp.where(allowed, jnp.exp(scores), jnp.float32(0.0))
-        total = jnp.sum(terms, axis=-1, keepdims=True)
+        pieces = (
+            (hk_ref, hv_ref, halo_ok & (hm_ref[0, block] > 0.0)),
+            (mk_ref, mv_ref, own_ok & (om_ref[0, block] > 0.0)),
+        )
+        terms, values = [], []
+        for k_ref, v_ref, allowed in pieces:
+            key = k_ref[0, frame : frame + span_t].reshape(-1, HDIM)
+            values.append(v_ref[0, frame : frame + span_t].reshape(-1, HDIM))
+            scores = lax.dot_general(
+                query, key, (((1,), (1,)), ((), ())), preferred_element_type=jnp.float32
+            ) * scale
+            terms.append(jnp.where(allowed, jnp.exp(scores), jnp.float32(0.0)))
+        total = jnp.sum(terms[0], axis=-1, keepdims=True) + jnp.sum(terms[1], axis=-1, keepdims=True)
         seen = qv_ref[block] > 0.0
-        total = jnp.where(seen, total, jnp.float32(1.0))
-        weights = (terms * (1.0 / total)).astype(jnp.bfloat16)
-        result = jnp.dot(weights, value, preferred_element_type=jnp.float32)
+        inverse = 1.0 / jnp.where(seen, total, jnp.float32(1.0))
+        result = jnp.dot(
+            (terms[0] * inverse).astype(jnp.bfloat16), values[0], preferred_element_type=jnp.float32
+        ) + jnp.dot(
+            (terms[1] * inverse).astype(jnp.bfloat16), values[1], preferred_element_type=jnp.float32
+        )
         result = jnp.where(seen, result, jnp.float32(0.0)).astype(jnp.bfloat16)
         o_ref[frame, row : row + TH] = result.reshape(TH, width, HDIM)
 
@@ -153,35 +182,43 @@
 ROW_TILES = 2
 
 
-def tile_attention(query, extended, key_mask, query_lo, query_hi, key_cols, query_ok, group, out):
+def tile_attention(query, pieces, masks, group, out):
     frames, rows, width, inner = query.shape
-    heads = extended.shape[-1] // HDIM
+    middle, top, bottom = pieces
+    heads = middle.shape[-1] // HDIM
     first = group * heads
-    row_tiles = rows // TH
-    assert row_tiles == ROW_TILES
-    blocks = frames * row_tiles
-    _, frames_ext, rows_ext, _, _ = extended.shape
-    key_n = key_mask.shape[-1]
+    assert rows // TH == ROW_TILES
+    blocks = frames * ROW_TILES
+    halo_mask, own_mask, query_lo, query_hi, halo_cols, own_cols, query_ok = masks
     query_n = TH * width
     q_spec = pl.BlockSpec((frames, rows, width, HDIM), lambda h: (0, 0, 0, first + h))
-    in_specs = [
-        q_spec,
-        pl.BlockSpec((1, frames_ext, rows_ext, width, HDIM), lambda h: (0, 0, 0, 0, h)),
-        pl.BlockSpec((1, frames_ext, rows_ext, width, HDIM), lambda h: (1, 0, 0, 0, h)),
-        pl.BlockSpec((1, blocks, 1, key_n), lambda h: (first + h, 0, 0, 0)),
+
+    def piece_specs(piece):
+        shape = (1, *piece.shape[1:-1], HDIM)
+        return [
+            pl.BlockSpec(shape, lambda h: (0, 0, 0, 0, h)),
+            pl.BlockSpec(shape, lambda h: (1, 0, 0, 0, h)),
+        ]
+
+    in_specs = [q_spec] + piece_specs(middle) + piece_specs(top) + piece_specs(bottom) + [
+        pl.BlockSpec((1, blocks, 1, halo_mask.shape[-1]), lambda h: (first + h, 0, 0, 0)),
+        pl.BlockSpec((1, blocks, 1, own_mask.shape[-1]), lambda h: (first + h, 0, 0, 0)),
         pl.BlockSpec((1, query_n, 1), lambda h: (first + h, 0, 0)),
         pl.BlockSpec((1, query_n, 1), lambda h: (first + h, 0, 0)),
-        pl.BlockSpec((1, key_n), lambda h: (0, 0)),
+        pl.BlockSpec((1, halo_cols.shape[-1]), lambda h: (0, 0)),
+        pl.BlockSpec((1, own_cols.shape[-1]), lambda h: (0, 0)),
         pl.BlockSpec((blocks, query_n, 1), lambda h: (0, 0, 0)),
     ]
-    operands = [query, extended, extended, key_mask, query_lo, query_hi, key_cols, query_ok]
+    operands = [query, middle, middle, top, top, bottom, bottom, halo_mask, own_mask,
+                query_lo, query_hi, halo_cols, own_cols, query_ok]
     aliases = {}
     kernel = attention_kernel
     if out is not None:
+        count = len(operands)
         in_specs.append(pl.BlockSpec(memory_space=pl.ANY))
         operands.append(out)
-        aliases = {len(operands) - 1: 0}
-        kernel = lambda *refs: attention_kernel(*refs[:8], refs[9])
+        aliases = {count: 0}
+        kernel = lambda *refs: attention_kernel(*refs[:count], refs[count + 1])
     return pl.pallas_call(
         kernel,
         grid=(heads,),

time: 379 us -> 372 us (0.982)
  other arithmetic: 30.3 us -> 16.2 us
  waiting for transfers between devices: 182 us -> 194 us
  starting transfers between devices: 36.6 us -> 30.5 us
    ppermute x0 -> x4, waiting for transfers between devices: none -> 37.7 us  [the longest x2 31.6 us: per_device(): lax.ppermute(middle[:, :, :TH], 'height', [(i + 1, i) for i in range(coun...]
    ppermute x4 -> x2, waiting for transfers between devices: 27.8 us -> 0.01 us  [with_halo(): lax.ppermute(tail, axis, [(i, (i + 1) % count) for i in range(ends)])]
    concatenate x4 -> x2, other arithmetic: 16.6 us -> 3.24 us  [with_halo(): jnp.concatenate([lax.ppermute(tail, axis, [(i, (i + 1) % count) for i in...]
    ppermute x4 -> x2, starting transfers between devices: 27.2 us -> 14.3 us  [with_halo(): lax.ppermute(head, axis, [((i + 1) % count, i) for i in range(ends)])]
    ppermute x0 -> x4, starting transfers between devices: none -> 12.2 us  [the longest x2 7.5 us: per_device(): lax.ppermute(middle[:, :, :TH], 'height', [(i + 1, i) for i in range(coun...]
    unnamed x16 -> x30, local copies, waits for them, and re-layouts: 0.04 us -> 7.94 us
    slice x5 -> x4, local copies, waits for them, and re-layouts: 10.5 us -> 4.65 us  [the longest x2 4.51 us: per_device(): middle[:, :, :TH]]
    ppermute x4 -> x2, starting transfers between devices: 9.42 us -> 4.06 us  [with_halo(): lax.ppermute(tail, axis, [(i, (i + 1) % count) for i in range(ends)])]
  transfers between devices with their start and end apart: 9 -> 9, of which waited for: 4 -> 6; matrix products, arithmetic and copies ran while one was open for 9% -> 7% of each run, Pallas kernels for 11% -> 11%
where the time goes in v14:
time: 372 us
  waiting for transfers between devices  194 us (52%)
  Pallas kernels  101 us (27%)
  starting transfers between devices  30.5 us (8%)
  local copies, waits for them, and re-layouts  16.2 us (4%)
  other arithmetic  16.2 us (4%)
  between operations  13.8 us (4%)
    all_gather x1, waiting for transfers between devices, per_device(): full_weight = lax.all_gather(band_weight, 'tm', axis=0, tiled=True)  153 us
    pallas_call x2, Pallas kernels, tile_attention(): pl.pallas_call(kernel, grid=(heads,), in_specs=in_specs, out_specs=q_spec...  38.7 us
    ppermute x2, waiting for transfers between devices, per_device(): lax.ppermute(middle[:, :, :TH], 'height', [(i + 1, i) for i in range(coun...  31.6 us
    pallas_call x1, Pallas kernels, band_gather(): pl.pallas_call(band_gather_kernel, in_specs=[pl.BlockSpec(memory_space=pl...  27 us
    pallas_call x2, Pallas kernels, project_kv(): pl.pallas_call(projection_kv_kernel, grid=(2 * steps,), in_specs=[pl.Bloc...  23.5 us
    ppermute x2, starting transfers between devices, with_halo(): lax.ppermute(head, axis, [((i + 1) % count, i) for i in range(ends)])  14.3 us
    pallas_call x1, Pallas kernels, project(): pl.pallas_call(functools.partial(projection_kernel, normalize=normalize),...  11.7 us
    unnamed x30, local copies, waits for them, and re-layouts  7.94 us
  transfers between devices with their start and end apart: 9, of which 6 were waited for; matrix products, arithmetic and copies ran while one was open for 7% of the time, Pallas kernels for 11%

profile of v14, /device:TPU:6, one launch (start us, length us, event | category | flops | bytes accessed | tf_op | source)
XLA Modules:
  0.0 371.5 jit_solution(15636686096363048566)
XLA Ops:
  6.5 27.0 %shard_map.82 = bf16[8,24,4608]{2,1,0:T(8,128)(2,1)} custom-call(bf16[24,4608]{1,0:T(8,128)(2,1)} %w_ref.1), custom_call_target="tpu_custom_call" | custom-call | tf_op jit(solution)/shard_map/pallas_call | solution.py:310
  33.7 2.8 convert_reduce_fusion
  36.5 3.3 multiply_reduce_fusion
  40.1 4.9 %fusion.3.x_ref = bf16[640,3072]{1,0:T(8,128)(2,1)} fusion(bf16[2,4,80,3072]{3,2,1,0:T(8,128)(2,1)} %param.8, f32[3072]{0:T(1024)S(1)} %copy-done.9, f32[3072]{0:T(1024)S(1)} %broadcast_add_fusion.1, f32[640]{0:T(1024)S(1)} %rsqrt.12, f32[640]{0:T(1024)S(1)} %div.33), kind=kLoop, calls=%fused_computation.4 | loop fusion | flops 11796480 | bytes 7894016 | tf_op jit(solution)/shard_map/convert_element_type | solution.py:44
  45.0 153.4 %all-gather.2.cloned.1.call-done.w_ref = bf16[3072,4608]{1,0:T(8,128)(2,1)} async-done(((bf16[192,4608]{1,0:T(8,128)(2,1)}), bf16[3072,4608]{1,0:T(8,128)(2,1)}) %all-gather.2.cloned.1.call-update) | async-done | bytes 28311568 | tf_op jit(solution)/shard_map/all_gather | solution.py:66
  198.4 11.8 %shard_map.85 = bf16[2,640,768]{2,1,0:T(8,128)(2,1)} custom-call(bf16[640,3072]{1,0:T(8,128)(2,1)} %fusion.3.x_ref, bf16[3072,4608]{1,0:T(8,128)(2,1)} %all-gather.2.cloned.1.call-done.w_ref, f32[1,128]{1,0:T(1,128)} %bitcast.68), custom_call_target="tpu_custom_call" | custom-call | tf_op jit(solution)/shard_map/pallas_call | solution.py:348
  210.2 2.9 slice_bitcast_fusion.1
  215.3 7.0 %collective-permute-start.5 = (bf16[2,1,1,2,2,80,768]{6,5,4,3,0,2,1:T(8,128)(2,1)}, bf16[2,1,1,2,2,80,768]{6,5,4,3,0,2,1:T(8,128)(2,1)}, u32[]{:S(2)}, u32[]{:S(2)}) collective-permute-start(bf16[2,1,1,2,2,80,768]{6,5,4,3,0,2,1:T(8,128)(2,1)} %get-tuple-element.10), channel_id=1, source_target_pairs={{8,0},{16,8},{24,16},{32,24},{40,32},{48,40},{56,48},{64,56},{72,6... | collective-permute-start | bytes 2949128 | tf_op jit(solution)/shard_map/ppermute | solution.py:31
  222.4 11.7 %shard_map.84 = bf16[2,640,768]{2,1,0:T(8,128)(2,1)} custom-call(bf16[640,3072]{1,0:T(8,128)(2,1)} %fusion.3.x_ref, bf16[3072,4608]{1,0:T(8,128)(2,1)} %all-gather.2.cloned.1.call-done.w_ref, f32[1,128]{1,0:T(1,128)} %bitcast.69), custom_call_target="tpu_custom_call" | custom-call | tf_op jit(solution)/shard_map/pallas_call | solution.py:348
  234.1 3.1 slice_bitcast_fusion.3
  239.1 7.3 %collective-permute-start.1 = (bf16[2,1,1,2,2,80,768]{6,5,4,3,0,2,1:T(8,128)(2,1)}, bf16[2,1,1,2,2,80,768]{6,5,4,3,0,2,1:T(8,128)(2,1)}, u32[]{:S(2)}, u32[]{:S(2)}) collective-permute-start(bf16[2,1,1,2,2,80,768]{6,5,4,3,0,2,1:T(8,128)(2,1)} %get-tuple-element.12), channel_id=1, source_target_pairs={{8,0},{16,8},{24,16},{32,24},{40,32},{48,40},{56,48},{64,56},{72,6... | collective-permute-start | bytes 2949128 | tf_op jit(solution)/shard_map/ppermute | solution.py:31
  250.6 2.2 fusion.10
  253.8 4.2 %collective-permute-start.7 = (bf16[2,4,2,80,768]{4,3,2,1,0:T(8,128)(2,1)}, bf16[2,4,2,80,768]{4,3,2,1,0:T(8,128)(2,1)S(1)}, u32[]{:S(2)}, u32[]{:S(2)}) collective-permute-start(bf16[2,4,2,80,768]{4,3,2,1,0:T(8,128)(2,1)} %get-tuple-element.5), channel_id=1, source_target_pairs={{1,0},{2,1},{3,2},{4,3},{5,4},{6,5},{7,6},{9,8},{10,9},{11,10},{12... | collective-permute-start | bytes 5898248 | tf_op jit(solution)/shard_map/ppermute | solution.py:81
  260.0 2.8 collective-permute-done.1
  264.3 2.3 fusion.11
  267.5 3.3 collective-permute-start.3
  270.7 2.7 collective-permute-start.2
  276.6 11.7 %shard_map.83 = bf16[640,1536]{1,0:T(8,128)(2,1)} custom-call(bf16[640,3072]{1,0:T(8,128)(2,1)} %fusion.3.x_ref, bf16[3072,4608]{1,0:T(8,128)(2,1)} %all-gather.2.cloned.1.call-done.w_ref, f32[1,128]{1,0:T(1,128)} %bitcast.70), custom_call_target="tpu_custom_call" | custom-call | tf_op jit(solution)/shard_map/pallas_call | solution.py:251
  288.3 16.6 %collective-permute-done.7.bk_ref.bv_ref = bf16[2,4,2,80,768]{4,3,2,1,0:T(8,128)(2,1)S(1)} collective-permute-done((bf16[2,4,2,80,768]{4,3,2,1,0:T(8,128)(2,1)}, bf16[2,4,2,80,768]{4,3,2,1,0:T(8,128)(2,1)S(1)}, u32[]{:S(2)}, u32[]{:S(2)}) %collective-permute-start.7) | collective-permute-done | bytes 1966112 | tf_op jit(solution)/shard_map/ppermute | solution.py:81
  304.9 3.2 collective-permute-done.6.tk_ref.tv_ref
  308.1 19.3 %shard_map.86.refs_14_ = bf16[2,4,80,1536]{3,2,1,0:T(8,128)(2,1)} custom-call(bf16[2,4,80,1536]{3,2,1,0:T(8,128)(2,1)} %bitcast.64, bf16[2,4,4,80,768]{4,3,2,1,0:T(8,128)(2,1)} %copy-done, bf16[2,4,4,80,768]{4,3,2,1,0:T(8,128)(2,1)} %copy-done, bf16[2,4,2,80,768]{4,3,2,1,0:T(8,128)(2,1)} %collective-permute-done.6.tk_ref.tv_ref, ...), custom_call_target="tpu_custom_call" | custom-call | tf_op jit(solution)/shard_map/pallas_call | solution.py:222
  327.4 15.1 %collective-permute-done.3.refs_5_.refs_6_ = bf16[2,4,2,80,768]{4,3,2,1,0:T(8,128)(2,1)} collective-permute-done((bf16[2,4,2,80,768]{4,3,2,1,0:T(8,128)(2,1)}, bf16[2,4,2,80,768]{4,3,2,1,0:T(8,128)(2,1)}, u32[]{:S(2)}, u32[]{:S(2)}) %collective-permute-start.3) | collective-permute-done | bytes 1966112 | tf_op jit(solution)/shard_map/ppermute | solution.py:81
  342.5 2.8 collective-permute-done.2.refs_3_.refs_4_
  345.3 19.4 %shard_map.87 = bf16[2,4,80,1536]{3,2,1,0:T(8,128)(2,1)} custom-call(bf16[2,4,80,1536]{3,2,1,0:T(8,128)(2,1)} %bitcast.65, bf16[2,4,4,80,768]{4,3,2,1,0:T(8,128)(2,1)} %copy-done.1, bf16[2,4,4,80,768]{4,3,2,1,0:T(8,128)(2,1)} %copy-done.1, bf16[2,4,2,80,768]{4,3,2,1,0:T(8,128)(2,1)} %collective-permute-done.2.refs_3_.refs_4_, ...), custom_call_target="tpu_custom_call", output_to_operand_aliasing={{}: (14, {})} | custom-call | tf_op jit(solution)/shard_map/pallas_call | solution.py:222
  (74 shorter events, 17.0 us)
Async XLA Ops:
  6.5 191.9 %all-gather.2.cloned.1.call-start = ((), (), s32[]{:S(2)}) async-start(), calls=%async_computation | async-start | bytes 30081024 | tf_op jit(solution)/shard_map/all_gather | solution.py:66
  33.6 6.3 %copy-start.6 = (s32[32,32,80]{2,1,0:T(8,128)S(1)}, s32[32,32,80]{2,1,0:T(8,128)}, u32[]{:S(2)}) copy-start(s32[32,32,80]{2,1,0:T(8,128)} %param.15) | copy-start | bytes 983044
  33.6 6.3 %copy-start.10 = (s32[12,3]{0,1:T(4,128)S(1)}, s32[12,3]{0,1:T(4,128)}, u32[]{:S(2)}) copy-start(s32[12,3]{0,1:T(4,128)} %param.14) | copy-start | bytes 436
  33.6 6.4 %copy-start.8 = (f32[3072]{0:T(1024)S(1)}, f32[3072]{0:T(1024)}, u32[]{:S(2)}) copy-start(f32[3072]{0:T(1024)} %param.9) | copy-start | bytes 36868
  33.7 6.4 %copy-start.9 = (f32[3072]{0:T(1024)S(1)}, f32[3072]{0:T(1024)}, u32[]{:S(2)}) copy-start(f32[3072]{0:T(1024)} %param.10) | copy-start | bytes 36868
  213.1 35.7 %collective-permute-start.4 = (bf16[2,1,1,2,2,80,768]{6,5,4,3,0,2,1:T(8,128)(2,1)}, bf16[2,1,1,2,2,80,768]{6,5,4,3,0,2,1:T(8,128)(2,1)}, u32[]{:S(2)}, u32[]{:S(2)}) collective-permute-start(bf16[2,1,1,2,2,80,768]{6,5,4,3,0,2,1:T(8,128)(2,1)} %get-tuple-element.9), channel_id=1, source_target_pairs={{0,8},{8,16},{16,24},{24,32},{32,40},{40,48},{48,56},{56,64},{64,7... | collective-permute-start | bytes 2949128 | tf_op jit(solution)/shard_map/ppermute | solution.py:29
  215.3 33.6 %collective-permute-start.5 = (bf16[2,1,1,2,2,80,768]{6,5,4,3,0,2,1:T(8,128)(2,1)}, bf16[2,1,1,2,2,80,768]{6,5,4,3,0,2,1:T(8,128)(2,1)}, u32[]{:S(2)}, u32[]{:S(2)}) collective-permute-start(bf16[2,1,1,2,2,80,768]{6,5,4,3,0,2,1:T(8,128)(2,1)} %get-tuple-element.10), channel_id=1, source_target_pairs={{8,0},{16,8},{24,16},{32,24},{40,32},{48,40},{56,48},{64,56},{72,6... | collective-permute-start | bytes 2949128 | tf_op jit(solution)/shard_map/ppermute | solution.py:31
  234.1 14.7 %copy-start.3 = (bf16[2,640,768]{2,1,0:T(8,128)(2,1)S(1)}, bf16[2,640,768]{2,1,0:T(8,128)(2,1)}, u32[]{:S(2)}) copy-start(bf16[2,640,768]{2,1,0:T(8,128)(2,1)} %shard_map.85) | copy-start | bytes 5898244
  237.2 22.8 %collective-permute-start = (bf16[2,1,1,2,2,80,768]{6,5,4,3,0,2,1:T(8,128)(2,1)}, bf16[2,1,1,2,2,80,768]{6,5,4,3,0,2,1:T(8,128)(2,1)S(1)}, u32[]{:S(2)}, u32[]{:S(2)}) collective-permute-start(bf16[2,1,1,2,2,80,768]{6,5,4,3,0,2,1:T(8,128)(2,1)} %get-tuple-element.11), channel_id=1, source_target_pairs={{0,8},{8,16},{16,24},{24,32},{32,40},{40,48},{48,56},{56,64},{64,7... | collective-permute-start | bytes 2949128 | tf_op jit(solution)/shard_map/ppermute | solution.py:29
  239.1 23.7 %collective-permute-start.1 = (bf16[2,1,1,2,2,80,768]{6,5,4,3,0,2,1:T(8,128)(2,1)}, bf16[2,1,1,2,2,80,768]{6,5,4,3,0,2,1:T(8,128)(2,1)}, u32[]{:S(2)}, u32[]{:S(2)}) collective-permute-start(bf16[2,1,1,2,2,80,768]{6,5,4,3,0,2,1:T(8,128)(2,1)} %get-tuple-element.12), channel_id=1, source_target_pairs={{8,0},{16,8},{24,16},{32,24},{40,32},{48,40},{56,48},{64,56},{72,6... | collective-permute-start | bytes 2949128 | tf_op jit(solution)/shard_map/ppermute | solution.py:31
  250.6 3.3 copy-start
  250.6 12.2 %copy-start.2 = (bf16[2,640,768]{2,1,0:T(8,128)(2,1)S(1)}, bf16[2,640,768]{2,1,0:T(8,128)(2,1)}, u32[]{:S(2)}) copy-start(bf16[2,640,768]{2,1,0:T(8,128)(2,1)} %shard_map.84) | copy-start | bytes 5898244
  253.8 51.1 %collective-permute-start.7 = (bf16[2,4,2,80,768]{4,3,2,1,0:T(8,128)(2,1)}, bf16[2,4,2,80,768]{4,3,2,1,0:T(8,128)(2,1)S(1)}, u32[]{:S(2)}, u32[]{:S(2)}) collective-permute-start(bf16[2,4,2,80,768]{4,3,2,1,0:T(8,128)(2,1)} %get-tuple-element.5), channel_id=1, source_target_pairs={{1,0},{2,1},{3,2},{4,3},{5,4},{6,5},{7,6},{9,8},{10,9},{11,10},{12... | collective-permute-start | bytes 5898248 | tf_op jit(solution)/shard_map/ppermute | solution.py:81
  258.1 50.1 %collective-permute-start.6 = (bf16[2,4,2,80,768]{4,3,2,1,0:T(8,128)(2,1)}, bf16[2,4,2,80,768]{4,3,2,1,0:T(8,128)(2,1)}, u32[]{:S(2)}, u32[]{:S(2)}) collective-permute-start(bf16[2,4,2,80,768]{4,3,2,1,0:T(8,128)(2,1)} %get-tuple-element.6), channel_id=1, source_target_pairs={{0,1},{1,2},{2,3},{3,4},{4,5},{5,6},{6,7},{8,9},{9,10},{10,11},{11... | collective-permute-start | bytes 5898248 | tf_op jit(solution)/shard_map/ppermute | solution.py:78
  264.3 3.2 copy-start.1
  267.5 75.0 %collective-permute-start.3 = (bf16[2,4,2,80,768]{4,3,2,1,0:T(8,128)(2,1)}, bf16[2,4,2,80,768]{4,3,2,1,0:T(8,128)(2,1)}, u32[]{:S(2)}, u32[]{:S(2)}) collective-permute-start(bf16[2,4,2,80,768]{4,3,2,1,0:T(8,128)(2,1)} %get-tuple-element.7), channel_id=1, source_target_pairs={{1,0},{2,1},{3,2},{4,3},{5,4},{6,5},{7,6},{9,8},{10,9},{11,10},{12... | collective-permute-start | bytes 5898248 | tf_op jit(solution)/shard_map/ppermute | solution.py:81
  270.7 74.6 %collective-permute-start.2 = (bf16[2,4,2,80,768]{4,3,2,1,0:T(8,128)(2,1)}, bf16[2,4,2,80,768]{4,3,2,1,0:T(8,128)(2,1)}, u32[]{:S(2)}, u32[]{:S(2)}) collective-permute-start(bf16[2,4,2,80,768]{4,3,2,1,0:T(8,128)(2,1)} %get-tuple-element.8), channel_id=1, source_target_pairs={{0,1},{1,2},{2,3},{3,4},{4,5},{5,6},{6,7},{8,9},{9,10},{10,11},{11... | collective-permute-start | bytes 5898248 | tf_op jit(solution)/shard_map/ppermute | solution.py:78
  275.0 13.3 %copy-start.7 = (f32[12,4,1,480]{3,2,1,0:T(1,128)}, f32[12,4,1,480]{3,2,1,0:T(1,128)S(1)}, u32[]{:S(2)}) copy-start(f32[12,4,1,480]{3,2,1,0:T(1,128)S(1)} %constant_dynamic-update-slice_fusion.hm_ref.refs_7_) | copy-start | bytes 276484
  275.1 13.3 %copy-start.5 = (f32[12,4,1,960]{3,2,1,0:T(1,128)}, f32[12,4,1,960]{3,2,1,0:T(1,128)S(1)}, u32[]{:S(2)}) copy-start(f32[12,4,1,960]{3,2,1,0:T(1,128)S(1)} %constant_dynamic-update-slice_fusion.4.om_ref.refs_8_) | copy-start | bytes 552964
  304.9 3.2 copy-start.4
Sparse Core Ops, SparseCore 0:
  33.7 164.6 all-gather.1

commit v15 on v14

--- a/solution.py
+++ b/solution.py
@@ -12,7 +12,7 @@
 TT = 1
 TH = 2
 TW = 8
-GROUPS = 2
+GROUPS = 3
 
 
 EPS = 1e-06

time: 372 us -> 386 us (1.038)
  waiting for transfers between devices: 194 us -> 174 us
  starting transfers between devices: 30.5 us -> 50 us
  Pallas kernels: 101 us -> 107 us
  local copies, waits for them, and re-layouts: 16.2 us -> 22.1 us
    ppermute x2 -> x3, waiting for transfers between devices: 31.6 us -> 0.01 us  [per_device(): lax.ppermute(middle[:, :, :TH], 'height', [(i + 1, i) for i in range(coun...]
    ppermute x2 -> x3, waiting for transfers between devices: 0.01 us -> 21.6 us  [with_halo(): lax.ppermute(tail, axis, [(i, (i + 1) % count) for i in range(ends)])]
    ppermute x2 -> x3, starting transfers between devices: 7.5 us -> 16.4 us  [per_device(): lax.ppermute(middle[:, :, :TH], 'height', [(i + 1, i) for i in range(coun...]
    ppermute x2 -> x3, starting transfers between devices: 14.3 us -> 21.7 us  [with_halo(): lax.ppermute(head, axis, [((i + 1) % count, i) for i in range(ends)])]
    ppermute x2 -> x3, waiting for transfers between devices: 6.02 us -> 0.02 us  [per_device(): lax.ppermute(middle[:, :, row_count - TH:], 'height', [(i, i + 1) for i i...]
    pallas_call x2 -> x3, Pallas kernels: 23.5 us -> 26.7 us  [project_kv(): pl.pallas_call(projection_kv_kernel, grid=(2 * steps,), in_specs=[pl.Bloc...]
    pallas_call x2 -> x3, Pallas kernels: 38.7 us -> 41.2 us  [tile_attention(): pl.pallas_call(kernel, grid=(heads,), in_specs=in_specs, out_specs=q_spec...]
    unnamed x30 -> x37, local copies, waits for them, and re-layouts: 7.94 us -> 9.55 us
  transfers between devices with their start and end apart: 9 -> 13, of which waited for: 6 -> 2; matrix products, arithmetic and copies ran while one was open for 7% -> 9% of each run, Pallas kernels for 11% -> 15%
where the time goes in v15:
time: 386 us; the launch traced here: 385 us
  waiting for transfers between devices  174 us (45%)
  Pallas kernels  107 us (28%)
  starting transfers between devices  50 us (13%)
  local copies, waits for them, and re-layouts  22.1 us (6%)
  other arithmetic  18.2 us (5%)
  between operations  13.9 us (4%)
    all_gather x1, waiting for transfers between devices, per_device(): full_weight = lax.all_gather(band_weight, 'tm', axis=0, tiled=True)  153 us
    pallas_call x3, Pallas kernels, tile_attention(): pl.pallas_call(kernel, grid=(heads,), in_specs=in_specs, out_specs=q_spec...  41.2 us
    pallas_call x1, Pallas kernels, band_gather(): pl.pallas_call(band_gather_kernel, in_specs=[pl.BlockSpec(memory_space=pl...  27 us
    pallas_call x3, Pallas kernels, project_kv(): pl.pallas_call(projection_kv_kernel, grid=(2 * steps,), in_specs=[pl.Bloc...  26.7 us
    ppermute x3, starting transfers between devices, with_halo(): lax.ppermute(head, axis, [((i + 1) % count, i) for i in range(ends)])  21.7 us
    ppermute x3, waiting for transfers between devices, with_halo(): lax.ppermute(tail, axis, [(i, (i + 1) % count) for i in range(ends)])  21.6 us
    ppermute x3, starting transfers between devices, per_device(): lax.ppermute(middle[:, :, :TH], 'height', [(i + 1, i) for i in range(coun...  16.4 us
    pallas_call x1, Pallas kernels, project(): pl.pallas_call(functools.partial(projection_kernel, normalize=normalize),...  11.7 us
  transfers between devices with their start and end apart: 13, of which 2 were waited for; matrix products, arithmetic and copies ran while one was open for 9% of the time, Pallas kernels for 15%

profile of v15, /device:TPU:6, one launch (start us, length us, event | category | flops | bytes accessed | tf_op | source)
XLA Modules:
  0.0 385.1 jit_solution(18001935693474618815)
XLA Ops:
  6.5 27.0 %shard_map.82 = bf16[8,24,4608]{2,1,0:T(8,128)(2,1)} custom-call(bf16[24,4608]{1,0:T(8,128)(2,1)} %w_ref.1), custom_call_target="tpu_custom_call" | custom-call | tf_op jit(solution)/shard_map/pallas_call | solution.py:310
  33.6 2.7 convert_reduce_fusion
  36.5 3.4 multiply_reduce_fusion
  40.9 4.9 %fusion.3.x_ref = bf16[640,3072]{1,0:T(8,128)(2,1)} fusion(bf16[2,4,80,3072]{3,2,1,0:T(8,128)(2,1)} %param.8, f32[3072]{0:T(1024)S(1)} %copy-done.12, f32[3072]{0:T(1024)S(1)} %broadcast_add_fusion.1, f32[640]{0:T(1024)S(1)} %rsqrt.12, f32[640]{0:T(1024)S(1)} %div.37), kind=kLoop, calls=%fused_computation.4 | loop fusion | flops 11796480 | bytes 7894016 | tf_op jit(solution)/shard_map/convert_element_type | solution.py:44
  45.8 152.6 %all-gather.2.cloned.1.call-done.w_ref = bf16[3072,4608]{1,0:T(8,128)(2,1)} async-done(((bf16[192,4608]{1,0:T(8,128)(2,1)}), bf16[3072,4608]{1,0:T(8,128)(2,1)}) %all-gather.2.cloned.1.call-update) | async-done | bytes 28311568 | tf_op jit(solution)/shard_map/all_gather | solution.py:66
  198.4 8.9 %shard_map.86 = bf16[2,640,512]{2,1,0:T(8,128)(2,1)} custom-call(bf16[640,3072]{1,0:T(8,128)(2,1)} %fusion.3.x_ref, bf16[3072,4608]{1,0:T(8,128)(2,1)} %all-gather.2.cloned.1.call-done.w_ref, f32[1,128]{1,0:T(1,128)} %bitcast.79), custom_call_target="tpu_custom_call" | custom-call | tf_op jit(solution)/shard_map/pallas_call | solution.py:348
  207.3 2.3 slice_bitcast_fusion.1
  209.6 2.2 collective-permute-start.8
  211.7 7.0 %collective-permute-start.9 = (bf16[2,1,1,2,2,80,512]{6,5,4,3,0,2,1:T(8,128)(2,1)S(1)}, bf16[2,1,1,2,2,80,512]{6,5,4,3,0,2,1:T(8,128)(2,1)}, u32[]{:S(2)}, u32[]{:S(2)}) collective-permute-start(bf16[2,1,1,2,2,80,512]{6,5,4,3,0,2,1:T(8,128)(2,1)S(1)} %get-tuple-element.12), channel_id=1, source_target_pairs={{8,0},{16,8},{24,16},{32,24},{40,32},{48,40},{56,48},{64,56},{72,6... | collective-permute-start | bytes 1966088 | tf_op jit(solution)/shard_map/ppermute | solution.py:31
  221.8 8.9 %shard_map.85 = bf16[2,640,512]{2,1,0:T(8,128)(2,1)} custom-call(bf16[640,3072]{1,0:T(8,128)(2,1)} %fusion.3.x_ref, bf16[3072,4608]{1,0:T(8,128)(2,1)} %all-gather.2.cloned.1.call-done.w_ref, f32[1,128]{1,0:T(1,128)} %bitcast.80), custom_call_target="tpu_custom_call" | custom-call | tf_op jit(solution)/shard_map/pallas_call | solution.py:348
  230.7 2.4 slice_bitcast_fusion.3
  235.1 7.4 %collective-permute-start.5 = (bf16[2,1,1,2,2,80,512]{6,5,4,3,0,2,1:T(8,128)(2,1)}, bf16[2,1,1,2,2,80,512]{6,5,4,3,0,2,1:T(8,128)(2,1)}, u32[]{:S(2)}, u32[]{:S(2)}) collective-permute-start(bf16[2,1,1,2,2,80,512]{6,5,4,3,0,2,1:T(8,128)(2,1)} %get-tuple-element.14), channel_id=1, source_target_pairs={{8,0},{16,8},{24,16},{32,24},{40,32},{48,40},{56,48},{64,56},{72,6... | collective-permute-start | bytes 1966088 | tf_op jit(solution)/shard_map/ppermute | solution.py:31
  242.4 8.9 %shard_map.84 = bf16[2,640,512]{2,1,0:T(8,128)(2,1)} custom-call(bf16[640,3072]{1,0:T(8,128)(2,1)} %fusion.3.x_ref, bf16[3072,4608]{1,0:T(8,128)(2,1)} %all-gather.2.cloned.1.call-done.w_ref, f32[1,128]{1,0:T(1,128)} %bitcast.81), custom_call_target="tpu_custom_call" | custom-call | tf_op jit(solution)/shard_map/pallas_call | solution.py:348
  255.1 4.4 %collective-permute-start.11 = (bf16[2,4,2,80,512]{4,3,2,1,0:T(8,128)(2,1)}, bf16[2,4,2,80,512]{4,3,2,1,0:T(8,128)(2,1)}, u32[]{:S(2)}, u32[]{:S(2)}) collective-permute-start(bf16[2,4,2,80,512]{4,3,2,1,0:T(8,128)(2,1)} %get-tuple-element.5), channel_id=1, source_target_pairs={{1,0},{2,1},{3,2},{4,3},{5,4},{6,5},{7,6},{9,8},{10,9},{11,10},{12... | collective-permute-start | bytes 3932168 | tf_op jit(solution)/shard_map/ppermute | solution.py:81
  262.6 7.3 %collective-permute-start.1 = (bf16[2,1,1,2,2,80,512]{6,5,4,3,0,2,1:T(8,128)(2,1)}, bf16[2,1,1,2,2,80,512]{6,5,4,3,0,2,1:T(8,128)(2,1)}, u32[]{:S(2)}, u32[]{:S(2)}) collective-permute-start(bf16[2,1,1,2,2,80,512]{6,5,4,3,0,2,1:T(8,128)(2,1)} %get-tuple-element.16), channel_id=1, source_target_pairs={{8,0},{16,8},{24,16},{32,24},{40,32},{48,40},{56,48},{64,56},{72,6... | collective-permute-start | bytes 1966088 | tf_op jit(solution)/shard_map/ppermute | solution.py:31
  275.9 6.0 %collective-permute-start.7 = (bf16[2,4,2,80,512]{4,3,2,1,0:T(8,128)(2,1)}, bf16[2,4,2,80,512]{4,3,2,1,0:T(8,128)(2,1)S(1)}, u32[]{:S(2)}, u32[]{:S(2)}) collective-permute-start(bf16[2,4,2,80,512]{4,3,2,1,0:T(8,128)(2,1)} %get-tuple-element.7), channel_id=1, source_target_pairs={{1,0},{2,1},{3,2},{4,3},{5,4},{6,5},{7,6},{9,8},{10,9},{11,10},{12... | collective-permute-start | bytes 3932168 | tf_op jit(solution)/shard_map/ppermute | solution.py:81
  281.9 21.6 %collective-permute-done = bf16[2,1,1,2,2,80,512]{6,5,4,3,0,2,1:T(8,128)(2,1)} collective-permute-done((bf16[2,1,1,2,2,80,512]{6,5,4,3,0,2,1:T(8,128)(2,1)}, bf16[2,1,1,2,2,80,512]{6,5,4,3,0,2,1:T(8,128)(2,1)}, u32[]{:S(2)}, u32[]{:S(2)}) %collective-permute-start) | collective-permute-done | bytes 655392 | tf_op jit(solution)/shard_map/ppermute | solution.py:29
  309.5 6.0 %collective-permute-start.3 = (bf16[2,4,2,80,512]{4,3,2,1,0:T(8,128)(2,1)}, bf16[2,4,2,80,512]{4,3,2,1,0:T(8,128)(2,1)S(1)}, u32[]{:S(2)}, u32[]{:S(2)}) collective-permute-start(bf16[2,4,2,80,512]{4,3,2,1,0:T(8,128)(2,1)} %get-tuple-element.9), channel_id=1, source_target_pairs={{1,0},{2,1},{3,2},{4,3},{5,4},{6,5},{7,6},{9,8},{10,9},{11,10},{12... | collective-permute-start | bytes 3932168 | tf_op jit(solution)/shard_map/ppermute | solution.py:81
  315.5 2.1 collective-permute-start.2
  321.0 2.2 broadcast_add_fusion
  323.2 11.7 %shard_map.83 = bf16[640,1536]{1,0:T(8,128)(2,1)} custom-call(bf16[640,3072]{1,0:T(8,128)(2,1)} %fusion.3.x_ref, bf16[3072,4608]{1,0:T(8,128)(2,1)} %all-gather.2.cloned.1.call-done.w_ref, f32[1,128]{1,0:T(1,128)} %bitcast.82), custom_call_target="tpu_custom_call" | custom-call | tf_op jit(solution)/shard_map/pallas_call | solution.py:251
  334.9 13.7 %shard_map.87.refs_14_ = bf16[2,4,80,1536]{3,2,1,0:T(8,128)(2,1)} custom-call(bf16[2,4,80,1536]{3,2,1,0:T(8,128)(2,1)} %bitcast.68, bf16[2,4,4,80,512]{4,3,2,1,0:T(8,128)(2,1)} %copy-done, bf16[2,4,4,80,512]{4,3,2,1,0:T(8,128)(2,1)} %copy-done, bf16[2,4,2,80,512]{4,3,2,1,0:T(8,128)(2,1)} %collective-permute-done.10.tk_ref.tv_ref, ...), custom_call_target="tpu_custom_call" | custom-call | tf_op jit(solution)/shard_map/pallas_call | solution.py:222
  349.7 13.7 %shard_map.88.refs_14_ = bf16[2,4,80,1536]{3,2,1,0:T(8,128)(2,1)} custom-call(bf16[2,4,80,1536]{3,2,1,0:T(8,128)(2,1)} %bitcast.69, bf16[2,4,4,80,512]{4,3,2,1,0:T(8,128)(2,1)} %copy-done.1, bf16[2,4,4,80,512]{4,3,2,1,0:T(8,128)(2,1)} %copy-done.1, ...), custom_call_target="tpu_custom_call", output_to_operand_aliasing={{}: (14, {})} | custom-call | tf_op jit(solution)/shard_map/pallas_call | solution.py:222
  364.5 13.7 %shard_map.89 = bf16[2,4,80,1536]{3,2,1,0:T(8,128)(2,1)} custom-call(bf16[2,4,80,1536]{3,2,1,0:T(8,128)(2,1)} %bitcast.70, bf16[2,4,4,80,512]{4,3,2,1,0:T(8,128)(2,1)} %copy-done.2, bf16[2,4,4,80,512]{4,3,2,1,0:T(8,128)(2,1)} %copy-done.2, bf16[2,4,2,80,512]{4,3,2,1,0:T(8,128)(2,1)} %collective-permute-done.2.refs_3_.refs_4_, ...), custom_call_target="tpu_custom_call", output_to_operand_aliasing={{}: (14, {})} | custom-call | tf_op jit(solution)/shard_map/pallas_call | solution.py:222
  (93 shorter events, 30.1 us)
Async XLA Ops:
  6.5 191.9 %all-gather.2.cloned.1.call-start = ((), (), s32[]{:S(2)}) async-start(), calls=%async_computation | async-start | bytes 30081024 | tf_op jit(solution)/shard_map/all_gather | solution.py:66
  36.3 3.6 copy-start.10
  36.4 3.7 copy-start.13
  36.4 4.5 %copy-start.11 = (f32[3072]{0:T(1024)S(1)}, f32[3072]{0:T(1024)}, u32[]{:S(2)}) copy-start(f32[3072]{0:T(1024)} %param.9) | copy-start | bytes 36868
  36.4 4.5 %copy-start.12 = (f32[3072]{0:T(1024)S(1)}, f32[3072]{0:T(1024)}, u32[]{:S(2)}) copy-start(f32[3072]{0:T(1024)} %param.10) | copy-start | bytes 36868
  209.6 41.8 %collective-permute-start.8 = (bf16[2,1,1,2,2,80,512]{6,5,4,3,0,2,1:T(8,128)(2,1)}, bf16[2,1,1,2,2,80,512]{6,5,4,3,0,2,1:T(8,128)(2,1)S(1)}, u32[]{:S(2)}, u32[]{:S(2)}) collective-permute-start(bf16[2,1,1,2,2,80,512]{6,5,4,3,0,2,1:T(8,128)(2,1)} %get-tuple-element.11), channel_id=1, source_target_pairs={{0,8},{8,16},{16,24},{24,32},{32,40},{40,48},{48,56},{56,64},{64,7... | collective-permute-start | bytes 1966088 | tf_op jit(solution)/shard_map/ppermute | solution.py:29
  211.7 39.6 %collective-permute-start.9 = (bf16[2,1,1,2,2,80,512]{6,5,4,3,0,2,1:T(8,128)(2,1)S(1)}, bf16[2,1,1,2,2,80,512]{6,5,4,3,0,2,1:T(8,128)(2,1)}, u32[]{:S(2)}, u32[]{:S(2)}) collective-permute-start(bf16[2,1,1,2,2,80,512]{6,5,4,3,0,2,1:T(8,128)(2,1)S(1)} %get-tuple-element.12), channel_id=1, source_target_pairs={{8,0},{16,8},{24,16},{32,24},{40,32},{48,40},{56,48},{64,56},{72,6... | collective-permute-start | bytes 1966088 | tf_op jit(solution)/shard_map/ppermute | solution.py:31
  233.1 36.9 %collective-permute-start.4 = (bf16[2,1,1,2,2,80,512]{6,5,4,3,0,2,1:T(8,128)(2,1)}, bf16[2,1,1,2,2,80,512]{6,5,4,3,0,2,1:T(8,128)(2,1)}, u32[]{:S(2)}, u32[]{:S(2)}) collective-permute-start(bf16[2,1,1,2,2,80,512]{6,5,4,3,0,2,1:T(8,128)(2,1)} %get-tuple-element.13), channel_id=1, source_target_pairs={{0,8},{8,16},{16,24},{24,32},{32,40},{40,48},{48,56},{56,64},{64,7... | collective-permute-start | bytes 1966088 | tf_op jit(solution)/shard_map/ppermute | solution.py:29
  235.0 16.3 %copy-start.5 = (bf16[2,640,512]{2,1,0:T(8,128)(2,1)S(1)}, bf16[2,640,512]{2,1,0:T(8,128)(2,1)}, u32[]{:S(2)}) copy-start(bf16[2,640,512]{2,1,0:T(8,128)(2,1)} %shard_map.86) | copy-start | bytes 3932164
  235.1 37.0 %collective-permute-start.5 = (bf16[2,1,1,2,2,80,512]{6,5,4,3,0,2,1:T(8,128)(2,1)}, bf16[2,1,1,2,2,80,512]{6,5,4,3,0,2,1:T(8,128)(2,1)}, u32[]{:S(2)}, u32[]{:S(2)}) collective-permute-start(bf16[2,1,1,2,2,80,512]{6,5,4,3,0,2,1:T(8,128)(2,1)} %get-tuple-element.14), channel_id=1, source_target_pairs={{8,0},{16,8},{24,16},{32,24},{40,32},{48,40},{56,48},{64,56},{72,6... | collective-permute-start | bytes 1966088 | tf_op jit(solution)/shard_map/ppermute | solution.py:31
  252.7 2.3 copy-start
  252.8 6.7 %copy-start.3 = (bf16[2,640,512]{2,1,0:T(8,128)(2,1)S(1)}, bf16[2,640,512]{2,1,0:T(8,128)(2,1)}, u32[]{:S(2)}) copy-start(bf16[2,640,512]{2,1,0:T(8,128)(2,1)} %shard_map.84) | copy-start | bytes 3932164
  255.1 16.9 %copy-start.4 = (bf16[2,640,512]{2,1,0:T(8,128)(2,1)S(1)}, bf16[2,640,512]{2,1,0:T(8,128)(2,1)}, u32[]{:S(2)}) copy-start(bf16[2,640,512]{2,1,0:T(8,128)(2,1)} %shard_map.85) | copy-start | bytes 3932164
  255.1 60.4 %collective-permute-start.11 = (bf16[2,4,2,80,512]{4,3,2,1,0:T(8,128)(2,1)}, bf16[2,4,2,80,512]{4,3,2,1,0:T(8,128)(2,1)}, u32[]{:S(2)}, u32[]{:S(2)}) collective-permute-start(bf16[2,4,2,80,512]{4,3,2,1,0:T(8,128)(2,1)} %get-tuple-element.5), channel_id=1, source_target_pairs={{1,0},{2,1},{3,2},{4,3},{5,4},{6,5},{7,6},{9,8},{10,9},{11,10},{12... | collective-permute-start | bytes 3932168 | tf_op jit(solution)/shard_map/ppermute | solution.py:81
  260.7 42.9 %collective-permute-start = (bf16[2,1,1,2,2,80,512]{6,5,4,3,0,2,1:T(8,128)(2,1)}, bf16[2,1,1,2,2,80,512]{6,5,4,3,0,2,1:T(8,128)(2,1)}, u32[]{:S(2)}, u32[]{:S(2)}) collective-permute-start(bf16[2,1,1,2,2,80,512]{6,5,4,3,0,2,1:T(8,128)(2,1)} %get-tuple-element.15), channel_id=1, source_target_pairs={{0,8},{8,16},{16,24},{24,32},{32,40},{40,48},{48,56},{56,64},{64,7... | collective-permute-start | bytes 1966088 | tf_op jit(solution)/shard_map/ppermute | solution.py:29
  262.6 42.9 %collective-permute-start.1 = (bf16[2,1,1,2,2,80,512]{6,5,4,3,0,2,1:T(8,128)(2,1)}, bf16[2,1,1,2,2,80,512]{6,5,4,3,0,2,1:T(8,128)(2,1)}, u32[]{:S(2)}, u32[]{:S(2)}) collective-permute-start(bf16[2,1,1,2,2,80,512]{6,5,4,3,0,2,1:T(8,128)(2,1)} %get-tuple-element.16), channel_id=1, source_target_pairs={{8,0},{16,8},{24,16},{32,24},{40,32},{48,40},{56,48},{64,56},{72,6... | collective-permute-start | bytes 1966088 | tf_op jit(solution)/shard_map/ppermute | solution.py:31
  270.1 64.8 %collective-permute-start.10 = (bf16[2,4,2,80,512]{4,3,2,1,0:T(8,128)(2,1)}, bf16[2,4,2,80,512]{4,3,2,1,0:T(8,128)(2,1)}, u32[]{:S(2)}, u32[]{:S(2)}) collective-permute-start(bf16[2,4,2,80,512]{4,3,2,1,0:T(8,128)(2,1)} %get-tuple-element.6), channel_id=1, source_target_pairs={{0,1},{1,2},{2,3},{3,4},{4,5},{5,6},{6,7},{8,9},{9,10},{10,11},{11... | collective-permute-start | bytes 3932168 | tf_op jit(solution)/shard_map/ppermute | solution.py:78
  275.9 72.7 %collective-permute-start.7 = (bf16[2,4,2,80,512]{4,3,2,1,0:T(8,128)(2,1)}, bf16[2,4,2,80,512]{4,3,2,1,0:T(8,128)(2,1)S(1)}, u32[]{:S(2)}, u32[]{:S(2)}) collective-permute-start(bf16[2,4,2,80,512]{4,3,2,1,0:T(8,128)(2,1)} %get-tuple-element.7), channel_id=1, source_target_pairs={{1,0},{2,1},{3,2},{4,3},{5,4},{6,5},{7,6},{9,8},{10,9},{11,10},{12... | collective-permute-start | bytes 3932168 | tf_op jit(solution)/shard_map/ppermute | solution.py:81
  303.5 45.1 %collective-permute-start.6 = (bf16[2,4,2,80,512]{4,3,2,1,0:T(8,128)(2,1)}, bf16[2,4,2,80,512]{4,3,2,1,0:T(8,128)(2,1)}, u32[]{:S(2)}, u32[]{:S(2)}) collective-permute-start(bf16[2,4,2,80,512]{4,3,2,1,0:T(8,128)(2,1)} %get-tuple-element.8), channel_id=1, source_target_pairs={{0,1},{1,2},{2,3},{3,4},{4,5},{5,6},{6,7},{8,9},{9,10},{10,11},{11... | collective-permute-start | bytes 3932168 | tf_op jit(solution)/shard_map/ppermute | solution.py:78
  307.0 2.4 copy-start.2
  309.5 53.9 %collective-permute-start.3 = (bf16[2,4,2,80,512]{4,3,2,1,0:T(8,128)(2,1)}, bf16[2,4,2,80,512]{4,3,2,1,0:T(8,128)(2,1)S(1)}, u32[]{:S(2)}, u32[]{:S(2)}) collective-permute-start(bf16[2,4,2,80,512]{4,3,2,1,0:T(8,128)(2,1)} %get-tuple-element.9), channel_id=1, source_target_pairs={{1,0},{2,1},{3,2},{4,3},{5,4},{6,5},{7,6},{9,8},{10,9},{11,10},{12... | collective-permute-start | bytes 3932168 | tf_op jit(solution)/shard_map/ppermute | solution.py:81
  315.5 47.9 %collective-permute-start.2 = (bf16[2,4,2,80,512]{4,3,2,1,0:T(8,128)(2,1)}, bf16[2,4,2,80,512]{4,3,2,1,0:T(8,128)(2,1)}, u32[]{:S(2)}, u32[]{:S(2)}) collective-permute-start(bf16[2,4,2,80,512]{4,3,2,1,0:T(8,128)(2,1)} %get-tuple-element.10), channel_id=1, source_target_pairs={{0,1},{1,2},{2,3},{3,4},{4,5},{5,6},{6,7},{8,9},{9,10},{10,11},{11... | collective-permute-start | bytes 3932168 | tf_op jit(solution)/shard_map/ppermute | solution.py:78
  320.9 14.0 %copy-start.9 = (f32[12,4,1,480]{3,2,1,0:T(1,128)}, f32[12,4,1,480]{3,2,1,0:T(1,128)S(1)}, u32[]{:S(2)}) copy-start(f32[12,4,1,480]{3,2,1,0:T(1,128)S(1)} %constant_dynamic-update-slice_fusion.hm_ref.refs_7_) | copy-start | bytes 276484
  321.0 13.9 %copy-start.8 = (f32[12,4,1,960]{3,2,1,0:T(1,128)}, f32[12,4,1,960]{3,2,1,0:T(1,128)S(1)}, u32[]{:S(2)}) copy-start(f32[12,4,1,960]{3,2,1,0:T(1,128)S(1)} %constant_dynamic-update-slice_fusion.4.om_ref.refs_8_) | copy-start | bytes 552964
  (3 other events, 4.4 us)
Sparse Core Ops, SparseCore 0:
  33.7 164.6 all-gather.1

commit v16 on v14

--- a/solution.py
+++ b/solution.py
@@ -72,14 +72,14 @@
         start = group * group_cols
         stacked = project_kv(modulated, full_weight, start, group_cols, k_gain)
         stacked = stacked.reshape(2, *tiled)
-        middle = with_halo(stacked, (("tm", 1),), 1)
-        middle = middle.reshape(2, frame_count + 2 * TT, row_count, width, group_cols)
-        count = lax.axis_size("height")
-        top = lax.ppermute(
-            middle[:, :, row_count - TH :], "height", [(i, i + 1) for i in range(count - 1)]
-        )
-        bottom = lax.ppermute(middle[:, :, :TH], "height", [(i + 1, i) for i in range(count - 1)])
-        groups.append((middle, top, bottom))
+        rows_done = with_halo(stacked, (("height", 3),), 1)
+        rows_done = rows_done.reshape(2, frame_count, row_count + 2 * TH, width, group_cols)
+        count = lax.axis_size("tm")
+        before = lax.ppermute(
+            rows_done[:, frame_count - TT :], "tm", [(i, i + 1) for i in range(count - 1)]
+        )
+        after = lax.ppermute(rows_done[:, :TT], "tm", [(i + 1, i) for i in range(count - 1)])
+        groups.append((rows_done, before, after))
     query = project(modulated, full_weight, 0, inner, q_gain)
     frames_ext = frame_count + 2 * TT
     rows_ext = row_count + 2 * TH
@@ -122,18 +122,19 @@
     query_hi = (query_cols[None, :] + window[:, 2, None]).reshape(HEADS, query_n, 1)
     query_ok = query_valid.reshape(blocks, query_n, 1).astype(jnp.float32)
     query_grid = query.reshape(frame_count, row_count, width, inner)
-    assert row_count == 2 * TH
+    assert frame_count == 2 * TT
     mask_rows = key_mask.reshape(HEADS, blocks, span_t, span_h, width)
     halo_masks, own_masks = [], []
     for block in range(blocks):
-        halo_rows = slice(0, TH) if block % row_tiles == 0 else slice(span_h - TH, span_h)
-        own_rows = slice(TH, span_h) if block % row_tiles == 0 else slice(0, row_count)
-        halo_masks.append(mask_rows[:, block, :, halo_rows].reshape(HEADS, 1, -1))
-        own_masks.append(mask_rows[:, block, :, own_rows].reshape(HEADS, 1, -1))
+        first_frame_block = block // row_tiles == 0
+        halo_frames = slice(0, TT) if first_frame_block else slice(span_t - TT, span_t)
+        own_frames = slice(TT, span_t) if first_frame_block else slice(0, frame_count)
+        halo_masks.append(mask_rows[:, block, halo_frames].reshape(HEADS, 1, -1))
+        own_masks.append(mask_rows[:, block, own_frames].reshape(HEADS, 1, -1))
     halo_mask = jnp.stack(halo_masks, axis=1)
     own_mask = jnp.stack(own_masks, axis=1)
-    halo_cols = jnp.tile(column_tiles, span_t * TH).reshape(1, -1)
-    own_cols = jnp.tile(column_tiles, span_t * row_count).reshape(1, -1)
+    halo_cols = jnp.tile(column_tiles, TT * span_h).reshape(1, -1)
+    own_cols = jnp.tile(column_tiles, frame_count * span_h).reshape(1, -1)
     out = None
     for group, pieces in enumerate(groups):
         masks = (halo_mask, own_mask, query_lo, query_hi, halo_cols, own_cols, query_ok)
@@ -145,7 +146,7 @@
     q_ref, mk_ref, mv_ref, tk_ref, tv_ref, bk_ref, bv_ref,
     hm_ref, om_ref, lo_ref, hi_ref, hc_ref, oc_ref, qv_ref, o_ref,
 ):
-    span_t = 2 * TT + 1
+    span_h = 3 * TH
     width = q_ref.shape[2]
     scale = 1.0 / float(HDIM) ** 0.5
     halo_ok = (hc_ref[...] >= lo_ref[0]) & (hc_ref[...] <= hi_ref[0])
@@ -153,7 +154,7 @@
     for block in range(q_ref.shape[0] * ROW_TILES):
         frame, tile = divmod(block, ROW_TILES)
         row = tile * TH
-        hk_ref, hv_ref = (tk_ref, tv_ref) if tile == 0 else (bk_ref, bv_ref)
+        hk_ref, hv_ref = (tk_ref, tv_ref) if frame == 0 else (bk_ref, bv_ref)
         query = q_ref[frame, row : row + TH].reshape(TH * width, HDIM)
         pieces = (
             (hk_ref, hv_ref, halo_ok & (hm_ref[0, block] > 0.0)),
@@ -161,8 +162,8 @@
         )
         terms, values = [], []
         for k_ref, v_ref, allowed in pieces:
-            key = k_ref[0, frame : frame + span_t].reshape(-1, HDIM)
-            values.append(v_ref[0, frame : frame + span_t].reshape(-1, HDIM))
+            key = k_ref[0, :, row : row + span_h].reshape(-1, HDIM)
+            values.append(v_ref[0, :, row : row + span_h].reshape(-1, HDIM))
             scores = lax.dot_general(
                 query, key, (((1,), (1,)), ((), ())), preferred_element_type=jnp.float32
             ) * scale

time: 372 us -> 341 us (0.917)
  waiting for transfers between devices: 194 us -> 162 us
  starting transfers between devices: 30.5 us -> 25.3 us
    ppermute x4, waiting for transfers between devices: 37.7 us -> 0.01 us  [the longest x2 0.01 us: per_device(): lax.ppermute(rows_done[:, :TT], 'tm', [(i + 1, i) for i in range(count -...]
    ppermute x2, waiting for transfers between devices: 0.01 us -> 7.57 us  [with_halo(): lax.ppermute(tail, axis, [(i, (i + 1) % count) for i in range(ends)])]
    slice x4 -> x6, local copies, waits for them, and re-layouts: 4.65 us -> 10.6 us  [the longest x2 6 us: with_halo(): lax.slice_in_dim(cells, cells.shape[dim] - width, cells.shape[dim], axis=...]
    unnamed x30 -> x18, local copies, waits for them, and re-layouts: 7.94 us -> 3.17 us
    ppermute x2, starting transfers between devices: 14.3 us -> 10.5 us  [with_halo(): lax.ppermute(head, axis, [((i + 1) % count, i) for i in range(ends)])]
  transfers between devices with their start and end apart: 9 -> 9, of which waited for: 6 -> 3; matrix products, arithmetic and copies ran while one was open for 7% -> 9% of each run, Pallas kernels for 11% -> 13%
where the time goes in v16:
time: 341 us; the launch traced here: 337 us
  waiting for transfers between devices  162 us (48%)
  Pallas kernels  101 us (30%)
  starting transfers between devices  25.3 us (7%)
  other arithmetic  17.7 us (5%)
  local copies, waits for them, and re-layouts  17.3 us (5%)
  between operations  13.8 us (4%)
    all_gather x1, waiting for transfers between devices, per_device(): full_weight = lax.all_gather(band_weight, 'tm', axis=0, tiled=True)  154 us
    pallas_call x2, Pallas kernels, tile_attention(): pl.pallas_call(kernel, grid=(heads,), in_specs=in_specs, out_specs=q_spec...  38.6 us
    pallas_call x1, Pallas kernels, band_gather(): pl.pallas_call(band_gather_kernel, in_specs=[pl.BlockSpec(memory_space=pl...  27 us
    pallas_call x2, Pallas kernels, project_kv(): pl.pallas_call(projection_kv_kernel, grid=(2 * steps,), in_specs=[pl.Bloc...  23.6 us
    pallas_call x1, Pallas kernels, project(): pl.pallas_call(functools.partial(projection_kernel, normalize=normalize),...  11.7 us
    ppermute x2, starting transfers between devices, with_halo(): lax.ppermute(head, axis, [((i + 1) % count, i) for i in range(ends)])  10.5 us
    ppermute x2, waiting for transfers between devices, with_halo(): lax.ppermute(tail, axis, [(i, (i + 1) % count) for i in range(ends)])  7.57 us
  transfers between devices with their start and end apart: 9, of which 3 were waited for; matrix products, arithmetic and copies ran while one was open for 9% of the time, Pallas kernels for 13%

profile of v16, /device:TPU:6, one launch (start us, length us, event | category | flops | bytes accessed | tf_op | source)
XLA Modules:
  0.0 337.4 jit_solution(10327758396072951905)
XLA Ops:
  6.5 27.0 %shard_map.82 = bf16[8,24,4608]{2,1,0:T(8,128)(2,1)} custom-call(bf16[24,4608]{1,0:T(8,128)(2,1)} %w_ref.1), custom_call_target="tpu_custom_call" | custom-call | tf_op jit(solution)/shard_map/pallas_call | solution.py:311
  33.6 2.7 convert_reduce_fusion
  36.5 3.3 multiply_reduce_fusion
  39.9 4.9 %fusion.3.x_ref = bf16[640,3072]{1,0:T(8,128)(2,1)} fusion(bf16[2,4,80,3072]{3,2,1,0:T(8,128)(2,1)} %param.8, f32[3072]{0:T(1024)S(1)} %copy-done.7, f32[3072]{0:T(1024)S(1)} %broadcast_add_fusion.1, f32[640]{0:T(1024)S(1)} %rsqrt.12, f32[640]{0:T(1024)S(1)} %div.33), kind=kLoop, calls=%fused_computation.4 | loop fusion | flops 11796480 | bytes 7894016 | tf_op jit(solution)/shard_map/convert_element_type | solution.py:44
  44.8 153.6 %all-gather.2.cloned.1.call-done.w_ref = bf16[3072,4608]{1,0:T(8,128)(2,1)} async-done(((bf16[192,4608]{1,0:T(8,128)(2,1)}), bf16[3072,4608]{1,0:T(8,128)(2,1)}) %all-gather.2.cloned.1.call-update) | async-done | bytes 28311568 | tf_op jit(solution)/shard_map/all_gather | solution.py:66
  198.4 11.8 %shard_map.85 = bf16[2,640,768]{2,1,0:T(8,128)(2,1)} custom-call(bf16[640,3072]{1,0:T(8,128)(2,1)} %fusion.3.x_ref, bf16[3072,4608]{1,0:T(8,128)(2,1)} %all-gather.2.cloned.1.call-done.w_ref, f32[1,128]{1,0:T(1,128)} %bitcast.61), custom_call_target="tpu_custom_call" | custom-call | tf_op jit(solution)/shard_map/pallas_call | solution.py:349
  210.2 2.9 fusion.12
  213.2 3.4 %collective-permute-start.4 = (bf16[2,2,1,1,2,80,768]{6,5,4,3,1,0,2:T(8,128)(2,1)}, bf16[2,2,1,1,2,80,768]{6,5,4,3,1,0,2:T(8,128)(2,1)S(1)}, u32[]{:S(2)}, u32[]{:S(2)}) collective-permute-start(bf16[2,2,1,1,2,80,768]{6,5,4,3,1,0,2:T(8,128)(2,1)} %get-tuple-element.9), channel_id=1, source_target_pairs={{0,1},{1,2},{2,3},{3,4},{4,5},{5,6},{6,7},{8,9},{9,10},{10,11},{11... | collective-permute-start | bytes 2949128 | tf_op jit(solution)/shard_map/ppermute | solution.py:29
  216.6 4.5 %collective-permute-start.5 = (bf16[2,2,1,1,2,80,768]{6,5,4,3,1,0,2:T(8,128)(2,1)}, bf16[2,2,1,1,2,80,768]{6,5,4,3,1,0,2:T(8,128)(2,1)}, u32[]{:S(2)}, u32[]{:S(2)}) collective-permute-start(bf16[2,2,1,1,2,80,768]{6,5,4,3,1,0,2:T(8,128)(2,1)} %get-tuple-element.10), channel_id=1, source_target_pairs={{1,0},{2,1},{3,2},{4,3},{5,4},{6,5},{7,6},{9,8},{10,9},{11,10},{12... | collective-permute-start | bytes 2949128 | tf_op jit(solution)/shard_map/ppermute | solution.py:31
  221.2 11.8 %shard_map.84 = bf16[2,640,768]{2,1,0:T(8,128)(2,1)} custom-call(bf16[640,3072]{1,0:T(8,128)(2,1)} %fusion.3.x_ref, bf16[3072,4608]{1,0:T(8,128)(2,1)} %all-gather.2.cloned.1.call-done.w_ref, f32[1,128]{1,0:T(1,128)} %bitcast.62), custom_call_target="tpu_custom_call" | custom-call | tf_op jit(solution)/shard_map/pallas_call | solution.py:349
  233.0 3.1 fusion.13
  236.1 1.9 collective-permute-start
  238.0 6.0 %collective-permute-start.1 = (bf16[2,2,1,1,2,80,768]{6,5,4,3,1,0,2:T(8,128)(2,1)}, bf16[2,2,1,1,2,80,768]{6,5,4,3,1,0,2:T(8,128)(2,1)}, u32[]{:S(2)}, u32[]{:S(2)}) collective-permute-start(bf16[2,2,1,1,2,80,768]{6,5,4,3,1,0,2:T(8,128)(2,1)} %get-tuple-element.12), channel_id=1, source_target_pairs={{1,0},{2,1},{3,2},{4,3},{5,4},{6,5},{7,6},{9,8},{10,9},{11,10},{12... | collective-permute-start | bytes 2949128 | tf_op jit(solution)/shard_map/ppermute | solution.py:31
  248.0 2.2 fusion.10
  251.3 3.0 collective-permute-start.7
  254.2 1.9 collective-permute-start.6
  256.2 7.6 %collective-permute-done = bf16[2,2,1,1,2,80,768]{6,5,4,3,1,0,2:T(8,128)(2,1)} collective-permute-done((bf16[2,2,1,1,2,80,768]{6,5,4,3,1,0,2:T(8,128)(2,1)}, bf16[2,2,1,1,2,80,768]{6,5,4,3,1,0,2:T(8,128)(2,1)}, u32[]{:S(2)}, u32[]{:S(2)}) %collective-permute-start) | collective-permute-done | bytes 983072 | tf_op jit(solution)/shard_map/ppermute | solution.py:29
  264.9 1.7 pad_maximum_fusion
  266.7 2.4 fusion.11
  269.8 2.3 collective-permute-start.3
  272.2 2.2 collective-permute-start.2
  279.0 11.7 %shard_map.83 = bf16[640,1536]{1,0:T(8,128)(2,1)} custom-call(bf16[640,3072]{1,0:T(8,128)(2,1)} %fusion.3.x_ref, bf16[3072,4608]{1,0:T(8,128)(2,1)} %all-gather.2.cloned.1.call-done.w_ref, f32[1,128]{1,0:T(1,128)} %bitcast.63), custom_call_target="tpu_custom_call" | custom-call | tf_op jit(solution)/shard_map/pallas_call | solution.py:252
  292.0 19.3 %shard_map.86.refs_14_ = bf16[2,4,80,1536]{3,2,1,0:T(8,128)(2,1)} custom-call(bf16[2,4,80,1536]{3,2,1,0:T(8,128)(2,1)} %bitcast.50, bf16[2,2,8,80,768]{4,3,2,1,0:T(8,128)(2,1)} %bitcast.41, bf16[2,2,8,80,768]{4,3,2,1,0:T(8,128)(2,1)} %bitcast.42, bf16[2,1,8,80,768]{4,3,2,1,0:T(8,128)(2,1)} %collective-permute-done.6.tk_ref.tv_ref, ...), custom_call_target="tpu_custom_call" | custom-call | tf_op jit(solution)/shard_map/pallas_call | solution.py:223
  311.2 19.3 %shard_map.87 = bf16[2,4,80,1536]{3,2,1,0:T(8,128)(2,1)} custom-call(bf16[2,4,80,1536]{3,2,1,0:T(8,128)(2,1)} %bitcast.51, bf16[2,2,8,80,768]{4,3,2,1,0:T(8,128)(2,1)} %bitcast.44, bf16[2,2,8,80,768]{4,3,2,1,0:T(8,128)(2,1)} %bitcast.45, bf16[2,1,8,80,768]{4,3,2,1,0:T(8,128)(2,1)} %collective-permute-done.2.refs_3_.refs_4_, ...), custom_call_target="tpu_custom_call", output_to_operand_aliasing={{}: (14, {})} | custom-call | tf_op jit(solution)/shard_map/pallas_call | solution.py:223
  (64 shorter events, 13.1 us)
Async XLA Ops:
  6.5 191.9 %all-gather.2.cloned.1.call-start = ((), (), s32[]{:S(2)}) async-start(), calls=%async_computation | async-start | bytes 30081024 | tf_op jit(solution)/shard_map/all_gather | solution.py:66
  33.6 6.2 %copy-start.6 = (f32[3072]{0:T(1024)S(1)}, f32[3072]{0:T(1024)}, u32[]{:S(2)}) copy-start(f32[3072]{0:T(1024)} %param.9) | copy-start | bytes 36868
  33.6 6.2 %copy-start.7 = (f32[3072]{0:T(1024)S(1)}, f32[3072]{0:T(1024)}, u32[]{:S(2)}) copy-start(f32[3072]{0:T(1024)} %param.10) | copy-start | bytes 36868
  210.2 10.9 %copy-start.5 = (s32[32,32,80]{2,1,0:T(8,128)S(1)}, s32[32,32,80]{2,1,0:T(8,128)}, u32[]{:S(2)}) copy-start(s32[32,32,80]{2,1,0:T(8,128)} %param.15) | copy-start | bytes 983044
  213.2 33.2 %collective-permute-start.4 = (bf16[2,2,1,1,2,80,768]{6,5,4,3,1,0,2:T(8,128)(2,1)}, bf16[2,2,1,1,2,80,768]{6,5,4,3,1,0,2:T(8,128)(2,1)S(1)}, u32[]{:S(2)}, u32[]{:S(2)}) collective-permute-start(bf16[2,2,1,1,2,80,768]{6,5,4,3,1,0,2:T(8,128)(2,1)} %get-tuple-element.9), channel_id=1, source_target_pairs={{0,1},{1,2},{2,3},{3,4},{4,5},{5,6},{6,7},{8,9},{9,10},{10,11},{11... | collective-permute-start | bytes 2949128 | tf_op jit(solution)/shard_map/ppermute | solution.py:29
  216.6 29.8 %collective-permute-start.5 = (bf16[2,2,1,1,2,80,768]{6,5,4,3,1,0,2:T(8,128)(2,1)}, bf16[2,2,1,1,2,80,768]{6,5,4,3,1,0,2:T(8,128)(2,1)}, u32[]{:S(2)}, u32[]{:S(2)}) collective-permute-start(bf16[2,2,1,1,2,80,768]{6,5,4,3,1,0,2:T(8,128)(2,1)} %get-tuple-element.10), channel_id=1, source_target_pairs={{1,0},{2,1},{3,2},{4,3},{5,4},{6,5},{7,6},{9,8},{10,9},{11,10},{12... | collective-permute-start | bytes 2949128 | tf_op jit(solution)/shard_map/ppermute | solution.py:31
  233.0 13.4 %copy-start.8 = (s32[12,3]{0,1:T(4,128)S(1)}, s32[12,3]{0,1:T(4,128)}, u32[]{:S(2)}) copy-start(s32[12,3]{0,1:T(4,128)} %param.14) | copy-start | bytes 436
  233.0 13.4 %copy-start.2 = (bf16[2,640,768]{2,1,0:T(8,128)(2,1)S(1)}, bf16[2,640,768]{2,1,0:T(8,128)(2,1)}, u32[]{:S(2)}) copy-start(bf16[2,640,768]{2,1,0:T(8,128)(2,1)} %shard_map.85) | copy-start | bytes 5898244
  236.1 27.7 %collective-permute-start = (bf16[2,2,1,1,2,80,768]{6,5,4,3,1,0,2:T(8,128)(2,1)}, bf16[2,2,1,1,2,80,768]{6,5,4,3,1,0,2:T(8,128)(2,1)}, u32[]{:S(2)}, u32[]{:S(2)}) collective-permute-start(bf16[2,2,1,1,2,80,768]{6,5,4,3,1,0,2:T(8,128)(2,1)} %get-tuple-element.11), channel_id=1, source_target_pairs={{0,1},{1,2},{2,3},{3,4},{4,5},{5,6},{6,7},{8,9},{9,10},{10,11},{11... | collective-permute-start | bytes 2949128 | tf_op jit(solution)/shard_map/ppermute | solution.py:29
  238.0 26.9 %collective-permute-start.1 = (bf16[2,2,1,1,2,80,768]{6,5,4,3,1,0,2:T(8,128)(2,1)}, bf16[2,2,1,1,2,80,768]{6,5,4,3,1,0,2:T(8,128)(2,1)}, u32[]{:S(2)}, u32[]{:S(2)}) collective-permute-start(bf16[2,2,1,1,2,80,768]{6,5,4,3,1,0,2:T(8,128)(2,1)} %get-tuple-element.12), channel_id=1, source_target_pairs={{1,0},{2,1},{3,2},{4,3},{5,4},{6,5},{7,6},{9,8},{10,9},{11,10},{12... | collective-permute-start | bytes 2949128 | tf_op jit(solution)/shard_map/ppermute | solution.py:31
  248.0 3.3 copy-start
  248.0 16.9 %copy-start.3 = (bf16[2,640,768]{2,1,0:T(8,128)(2,1)S(1)}, bf16[2,640,768]{2,1,0:T(8,128)(2,1)}, u32[]{:S(2)}) copy-start(bf16[2,640,768]{2,1,0:T(8,128)(2,1)} %shard_map.84) | copy-start | bytes 5898244
  251.3 39.5 %collective-permute-start.7 = (bf16[2,1,8,80,768]{4,3,2,1,0:T(8,128)(2,1)}, bf16[2,1,8,80,768]{4,3,2,1,0:T(8,128)(2,1)S(1)}, u32[]{:S(2)}, u32[]{:S(2)}) collective-permute-start(bf16[2,1,8,80,768]{4,3,2,1,0:T(8,128)(2,1)} %get-tuple-element.5), channel_id=1, source_target_pairs={{8,0},{16,8},{24,16},{32,24},{40,32},{48,40},{56,48},{64,56},{72,6... | collective-permute-start | bytes 5898248 | tf_op jit(solution)/shard_map/ppermute | solution.py:81
  254.2 36.5 %collective-permute-start.6 = (bf16[2,1,8,80,768]{4,3,2,1,0:T(8,128)(2,1)}, bf16[2,1,8,80,768]{4,3,2,1,0:T(8,128)(2,1)}, u32[]{:S(2)}, u32[]{:S(2)}) collective-permute-start(bf16[2,1,8,80,768]{4,3,2,1,0:T(8,128)(2,1)} %get-tuple-element.6), channel_id=1, source_target_pairs={{0,8},{8,16},{16,24},{24,32},{32,40},{40,48},{48,56},{56,64},{64,7... | collective-permute-start | bytes 5898248 | tf_op jit(solution)/shard_map/ppermute | solution.py:78
  266.7 3.2 copy-start.1
  269.8 41.4 %collective-permute-start.3 = (bf16[2,1,8,80,768]{4,3,2,1,0:T(8,128)(2,1)}, bf16[2,1,8,80,768]{4,3,2,1,0:T(8,128)(2,1)}, u32[]{:S(2)}, u32[]{:S(2)}) collective-permute-start(bf16[2,1,8,80,768]{4,3,2,1,0:T(8,128)(2,1)} %get-tuple-element.7), channel_id=1, source_target_pairs={{8,0},{16,8},{24,16},{32,24},{40,32},{48,40},{56,48},{64,56},{72,6... | collective-permute-start | bytes 5898248 | tf_op jit(solution)/shard_map/ppermute | solution.py:81
  272.2 39.0 %collective-permute-start.2 = (bf16[2,1,8,80,768]{4,3,2,1,0:T(8,128)(2,1)}, bf16[2,1,8,80,768]{4,3,2,1,0:T(8,128)(2,1)}, u32[]{:S(2)}, u32[]{:S(2)}) collective-permute-start(bf16[2,1,8,80,768]{4,3,2,1,0:T(8,128)(2,1)} %get-tuple-element.8), channel_id=1, source_target_pairs={{0,8},{8,16},{16,24},{24,32},{32,40},{40,48},{48,56},{56,64},{64,7... | collective-permute-start | bytes 5898248 | tf_op jit(solution)/shard_map/ppermute | solution.py:78
  290.7 1.3 copy-start.4
Sparse Core Ops, SparseCore 0:
  33.7 164.6 all-gather.1

commit v17 on v16

--- a/solution.py
+++ b/solution.py
@@ -68,10 +68,12 @@
     group_cols = inner // GROUPS
     tiled = (frame_count // TT, TT, row_count // TH, TH, width, group_cols)
     groups = []
+    queries = []
     for group in range(GROUPS):
         start = group * group_cols
-        stacked = project_kv(modulated, full_weight, start, group_cols, k_gain)
-        stacked = stacked.reshape(2, *tiled)
+        projected = project_qkv(modulated, full_weight, start, group_cols, q_gain, k_gain)
+        queries.append(projected[0].reshape(frame_count, row_count, width, group_cols))
+        stacked = projected[1:].reshape(2, *tiled)
         rows_done = with_halo(stacked, (("height", 3),), 1)
         rows_done = rows_done.reshape(2, frame_count, row_count + 2 * TH, width, group_cols)
         count = lax.axis_size("tm")
@@ -80,7 +82,6 @@
         )
         after = lax.ppermute(rows_done[:, :TT], "tm", [(i + 1, i) for i in range(count - 1)])
         groups.append((rows_done, before, after))
-    query = project(modulated, full_weight, 0, inner, q_gain)
     frames_ext = frame_count + 2 * TT
     rows_ext = row_count + 2 * TH
     frame_block = lax.axis_index("tm")
@@ -121,7 +122,6 @@
     query_lo = (query_cols[None, :] - window[:, 2, None]).reshape(HEADS, query_n, 1)
     query_hi = (query_cols[None, :] + window[:, 2, None]).reshape(HEADS, query_n, 1)
     query_ok = query_valid.reshape(blocks, query_n, 1).astype(jnp.float32)
-    query_grid = query.reshape(frame_count, row_count, width, inner)
     assert frame_count == 2 * TT
     mask_rows = key_mask.reshape(HEADS, blocks, span_t, span_h, width)
     halo_masks, own_masks = [], []
@@ -138,7 +138,7 @@
     out = None
     for group, pieces in enumerate(groups):
         masks = (halo_mask, own_mask, query_lo, query_hi, halo_cols, own_cols, query_ok)
-        out = tile_attention(query_grid, pieces, masks, group, out)
+        out = tile_attention(queries[group], pieces, masks, group, out)
     return out
 
 
@@ -184,15 +184,17 @@
 
 
 def tile_attention(query, pieces, masks, group, out):
-    frames, rows, width, inner = query.shape
+    frames, rows, width, group_cols = query.shape
     middle, top, bottom = pieces
-    heads = middle.shape[-1] // HDIM
+    heads = group_cols // HDIM
+    out_shape = (frames, rows, width, masks[2].shape[0] * HDIM)
     first = group * heads
     assert rows // TH == ROW_TILES
     blocks = frames * ROW_TILES
     halo_mask, own_mask, query_lo, query_hi, halo_cols, own_cols, query_ok = masks
     query_n = TH * width
-    q_spec = pl.BlockSpec((frames, rows, width, HDIM), lambda h: (0, 0, 0, first + h))
+    q_spec = pl.BlockSpec((frames, rows, width, HDIM), lambda h: (0, 0, 0, h))
+    o_spec = pl.BlockSpec((frames, rows, width, HDIM), lambda h: (0, 0, 0, first + h))
 
     def piece_specs(piece):
         shape = (1, *piece.shape[1:-1], HDIM)
@@ -224,8 +226,8 @@
         kernel,
         grid=(heads,),
         in_specs=in_specs,
-        out_specs=q_spec,
-        out_shape=jax.ShapeDtypeStruct(query.shape, jnp.bfloat16),
+        out_specs=o_spec,
+        out_shape=jax.ShapeDtypeStruct(out_shape, jnp.bfloat16),
         input_output_aliases=aliases,
     )(*operands)
 
@@ -359,6 +361,41 @@
     )(x, w, gain.reshape(1, HDIM))
 
 
+def projection_qkv_kernel(x_ref, w_ref, qg_ref, kg_ref, o_ref):
+    acc = jnp.dot(x_ref[...], w_ref[...], preferred_element_type=jnp.float32)
+    third = pl.program_id(0) // (pl.num_programs(0) // 3)
+    normalize = third < 2
+    gain = jnp.where(third == 0, qg_ref[...], kg_ref[...])
+    for part in range(acc.shape[1] // HDIM):
+        piece = acc[:, part * HDIM : (part + 1) * HDIM]
+        power = jnp.mean(piece * piece, axis=-1, keepdims=True)
+        normed = jnp.where(normalize, piece * lax.rsqrt(power + EPS) * gain, piece)
+        o_ref[0, :, part * HDIM : (part + 1) * HDIM] = normed.astype(o_ref.dtype)
+
+
+def project_qkv(x, w, start, count, q_gain, k_gain):
+    tokens, features = x.shape
+    cols = PROJECT_COLS
+    inner = w.shape[1] // 3
+    steps = count // cols
+
+    def weight_block(j):
+        return (0, (j // steps) * (inner // cols) + start // cols + j % steps)
+
+    return pl.pallas_call(
+        projection_qkv_kernel,
+        grid=(3 * steps,),
+        in_specs=[
+            pl.BlockSpec((tokens, features), lambda j: (0, 0)),
+            pl.BlockSpec((features, cols), weight_block),
+            pl.BlockSpec((1, HDIM), lambda j: (0, 0)),
+            pl.BlockSpec((1, HDIM), lambda j: (0, 0)),
+        ],
+        out_specs=pl.BlockSpec((1, tokens, cols), lambda j: (j // steps, 0, j % steps)),
+        out_shape=jax.ShapeDtypeStruct((3, tokens, count), jnp.bfloat16),
+    )(x, w, q_gain.reshape(1, HDIM), k_gain.reshape(1, HDIM))
+
+
 def solution(mesh):
     in_specs = (
         P("tm", "height", None, None),

time: 341 us -> 368 us (1.079)
  waiting for transfers between devices: 162 us -> 189 us
  local copies, waits for them, and re-layouts: 17.3 us -> 23.2 us
    ppermute x2, waiting for transfers between devices: 0.01 us -> 23.7 us  [per_device(): lax.ppermute(rows_done[:, :TT], 'tm', [(i + 1, i) for i in range(count -...]
    slice x0 -> x4, local copies, waits for them, and re-layouts: none -> 7.86 us  [the longest x2 4.45 us: per_device(): projected[0].reshape(frame_count, row_count, width, group_cols)]
    pallas_call x5 -> x4, Pallas kernels: 73.9 us -> 71 us  [the longest x2 38.8 us: tile_attention(): pl.pallas_call(kernel, grid=(heads,), in_specs=in_specs, out_specs=o_spec...]
  transfers between devices with their start and end apart: 9 -> 9, of which waited for: 3 -> 5; matrix products, arithmetic and copies ran while one was open for 9% -> 9% of each run, Pallas kernels for 13% -> 10%
where the time goes in v17:
time: 368 us; the launch traced here: 367 us
  waiting for transfers between devices  189 us (51%)
  Pallas kernels  98 us (27%)
  starting transfers between devices  25.3 us (7%)
  local copies, waits for them, and re-layouts  23.2 us (6%)
  other arithmetic  17.8 us (5%)
  between operations  13.8 us (4%)
    all_gather x1, waiting for transfers between devices, per_device(): full_weight = lax.all_gather(band_weight, 'tm', axis=0, tiled=True)  154 us
    pallas_call x2, Pallas kernels, tile_attention(): pl.pallas_call(kernel, grid=(heads,), in_specs=in_specs, out_specs=o_spec...  38.8 us
    pallas_call x2, Pallas kernels, project_qkv(): pl.pallas_call(projection_qkv_kernel, grid=(3 * steps,), in_specs=[pl.Blo...  32.2 us
    pallas_call x1, Pallas kernels, band_gather(): pl.pallas_call(band_gather_kernel, in_specs=[pl.BlockSpec(memory_space=pl...  27 us
    ppermute x2, waiting for transfers between devices, per_device(): lax.ppermute(rows_done[:, :TT], 'tm', [(i + 1, i) for i in range(count -...  23.7 us
    ppermute x2, starting transfers between devices, with_halo(): lax.ppermute(head, axis, [((i + 1) % count, i) for i in range(ends)])  10.5 us
    ppermute x2, waiting for transfers between devices, with_halo(): lax.ppermute(tail, axis, [(i, (i + 1) % count) for i in range(ends)])  7.59 us
  transfers between devices with their start and end apart: 9, of which 5 were waited for; matrix products, arithmetic and copies ran while one was open for 9% of the time, Pallas kernels for 10%

profile of v17, /device:TPU:6, one launch (start us, length us, event | category | flops | bytes accessed | tf_op | source)
XLA Modules:
  0.0 366.9 jit_solution(10593453854838085703)
XLA Ops:
  6.5 27.0 %shard_map.82 = bf16[8,24,4608]{2,1,0:T(8,128)(2,1)} custom-call(bf16[24,4608]{1,0:T(8,128)(2,1)} %w_ref.1), custom_call_target="tpu_custom_call" | custom-call | tf_op jit(solution)/shard_map/pallas_call | solution.py:313
  33.6 2.7 convert_reduce_fusion
  36.5 3.3 multiply_reduce_fusion
  39.9 4.9 %fusion.3.x_ref = bf16[640,3072]{1,0:T(8,128)(2,1)} fusion(bf16[2,4,80,3072]{3,2,1,0:T(8,128)(2,1)} %param.8, f32[3072]{0:T(1024)S(1)} %copy-done.7, f32[3072]{0:T(1024)S(1)} %broadcast_add_fusion.1, f32[640]{0:T(1024)S(1)} %rsqrt.12, f32[640]{0:T(1024)S(1)} %div.33), kind=kLoop, calls=%fused_computation.4 | loop fusion | flops 11796480 | bytes 7894016 | tf_op jit(solution)/shard_map/convert_element_type | solution.py:44
  44.8 153.6 %all-gather.2.cloned.1.call-done.w_ref = bf16[3072,4608]{1,0:T(8,128)(2,1)} async-done(((bf16[192,4608]{1,0:T(8,128)(2,1)}), bf16[3072,4608]{1,0:T(8,128)(2,1)}) %all-gather.2.cloned.1.call-update) | async-done | bytes 28311568 | tf_op jit(solution)/shard_map/all_gather | solution.py:66
  198.4 16.1 %shard_map.83 = bf16[3,640,768]{2,1,0:T(8,128)(2,1)} custom-call(bf16[640,3072]{1,0:T(8,128)(2,1)} %fusion.3.x_ref, bf16[3072,4608]{1,0:T(8,128)(2,1)} %all-gather.2.cloned.1.call-done.w_ref, f32[1,128]{1,0:T(1,128)} %bitcast.62, f32[1,128]{1,0:T(1,128)} %bitcast.64), custom_call_target="tpu_custom_call" | custom-call | tf_op jit(solution)/shard_map/pallas_call | solution.py:385
  217.6 3.4 collective-permute-start
  221.1 4.5 %collective-permute-start.1 = (bf16[2,2,1,1,2,80,768]{6,5,4,3,1,0,2:T(8,128)(2,1)}, bf16[2,2,1,1,2,80,768]{6,5,4,3,1,0,2:T(8,128)(2,1)}, u32[]{:S(2)}, u32[]{:S(2)}) collective-permute-start(bf16[2,2,1,1,2,80,768]{6,5,4,3,1,0,2:T(8,128)(2,1)} %get-tuple-element.12), channel_id=1, source_target_pairs={{1,0},{2,1},{3,2},{4,3},{5,4},{6,5},{7,6},{9,8},{10,9},{11,10},{12... | collective-permute-start | bytes 2949128 | tf_op jit(solution)/shard_map/ppermute | solution.py:31
  225.7 16.1 %shard_map.84 = bf16[3,640,768]{2,1,0:T(8,128)(2,1)} custom-call(bf16[640,3072]{1,0:T(8,128)(2,1)} %fusion.3.x_ref, bf16[3072,4608]{1,0:T(8,128)(2,1)} %all-gather.2.cloned.1.call-done.w_ref, f32[1,128]{1,0:T(1,128)} %bitcast.63, f32[1,128]{1,0:T(1,128)} %bitcast.65), custom_call_target="tpu_custom_call" | custom-call | tf_op jit(solution)/shard_map/pallas_call | solution.py:385
  246.2 1.9 collective-permute-start.4
  248.1 6.0 %collective-permute-start.5 = (bf16[2,2,1,1,2,80,768]{6,5,4,3,1,0,2:T(8,128)(2,1)}, bf16[2,2,1,1,2,80,768]{6,5,4,3,1,0,2:T(8,128)(2,1)}, u32[]{:S(2)}, u32[]{:S(2)}) collective-permute-start(bf16[2,2,1,1,2,80,768]{6,5,4,3,1,0,2:T(8,128)(2,1)} %get-tuple-element.10), channel_id=1, source_target_pairs={{1,0},{2,1},{3,2},{4,3},{5,4},{6,5},{7,6},{9,8},{10,9},{11,10},{12... | collective-permute-start | bytes 2949128 | tf_op jit(solution)/shard_map/ppermute | solution.py:31
  258.1 2.2 fusion.11
  261.3 3.0 collective-permute-start.3
  264.3 1.9 collective-permute-start.2
  266.3 7.6 %collective-permute-done.4 = bf16[2,2,1,1,2,80,768]{6,5,4,3,1,0,2:T(8,128)(2,1)} collective-permute-done((bf16[2,2,1,1,2,80,768]{6,5,4,3,1,0,2:T(8,128)(2,1)}, bf16[2,2,1,1,2,80,768]{6,5,4,3,1,0,2:T(8,128)(2,1)}, u32[]{:S(2)}, u32[]{:S(2)}) %collective-permute-start.4) | collective-permute-done | bytes 983072 | tf_op jit(solution)/shard_map/ppermute | solution.py:29
  276.8 2.4 fusion.10
  279.8 2.4 collective-permute-start.7
  282.2 2.1 collective-permute-start.6
  289.1 2.2 slice.112
  291.3 2.2 slice.126
  293.5 23.7 %collective-permute-done.7.bk_ref.bv_ref = bf16[2,1,8,80,768]{4,3,2,1,0:T(8,128)(2,1)} collective-permute-done((bf16[2,1,8,80,768]{4,3,2,1,0:T(8,128)(2,1)}, bf16[2,1,8,80,768]{4,3,2,1,0:T(8,128)(2,1)}, u32[]{:S(2)}, u32[]{:S(2)}) %collective-permute-start.7) | collective-permute-done | bytes 1966112 | tf_op jit(solution)/shard_map/ppermute | solution.py:83
  317.2 2.8 collective-permute-done.6.tk_ref.tv_ref
  320.0 19.4 %shard_map.85.refs_14_ = bf16[2,4,80,1536]{3,2,1,0:T(8,128)(2,1)} custom-call(bf16[2,4,80,768]{3,2,1,0:T(8,128)(2,1)} %bitcast.53, bf16[2,2,8,80,768]{4,3,2,1,0:T(8,128)(2,1)} %bitcast.45, bf16[2,2,8,80,768]{4,3,2,1,0:T(8,128)(2,1)} %bitcast.46, bf16[2,1,8,80,768]{4,3,2,1,0:T(8,128)(2,1)} %collective-permute-done.6.tk_ref.tv_ref, ...), custom_call_target="tpu_custom_call" | custom-call | tf_op jit(solution)/shard_map/pallas_call | solution.py:225
  340.7 19.4 %shard_map.86 = bf16[2,4,80,1536]{3,2,1,0:T(8,128)(2,1)} custom-call(bf16[2,4,80,768]{3,2,1,0:T(8,128)(2,1)} %bitcast.52, bf16[2,2,8,80,768]{4,3,2,1,0:T(8,128)(2,1)} %bitcast.42, bf16[2,2,8,80,768]{4,3,2,1,0:T(8,128)(2,1)} %bitcast.43, bf16[2,1,8,80,768]{4,3,2,1,0:T(8,128)(2,1)} %collective-permute-done.2.refs_3_.refs_4_, ...), custom_call_target="tpu_custom_call", output_to_operand_aliasing={{}: (14, {})} | custom-call | tf_op jit(solution)/shard_map/pallas_call | solution.py:225
  (67 shorter events, 22.2 us)
Async XLA Ops:
  6.5 191.9 %all-gather.2.cloned.1.call-start = ((), (), s32[]{:S(2)}) async-start(), calls=%async_computation | async-start | bytes 30081024 | tf_op jit(solution)/shard_map/all_gather | solution.py:66
  33.6 6.2 %copy-start.6 = (f32[3072]{0:T(1024)S(1)}, f32[3072]{0:T(1024)}, u32[]{:S(2)}) copy-start(f32[3072]{0:T(1024)} %param.9) | copy-start | bytes 36868
  33.6 6.2 %copy-start.7 = (f32[3072]{0:T(1024)S(1)}, f32[3072]{0:T(1024)}, u32[]{:S(2)}) copy-start(f32[3072]{0:T(1024)} %param.10) | copy-start | bytes 36868
  214.5 11.1 %copy-start.5 = (s32[32,32,80]{2,1,0:T(8,128)S(1)}, s32[32,32,80]{2,1,0:T(8,128)}, u32[]{:S(2)}) copy-start(s32[32,32,80]{2,1,0:T(8,128)} %param.15) | copy-start | bytes 983044
  217.6 38.9 %collective-permute-start = (bf16[2,2,1,1,2,80,768]{6,5,4,3,1,0,2:T(8,128)(2,1)}, bf16[2,2,1,1,2,80,768]{6,5,4,3,1,0,2:T(8,128)(2,1)S(1)}, u32[]{:S(2)}, u32[]{:S(2)}) collective-permute-start(bf16[2,2,1,1,2,80,768]{6,5,4,3,1,0,2:T(8,128)(2,1)} %get-tuple-element.11), channel_id=1, source_target_pairs={{0,1},{1,2},{2,3},{3,4},{4,5},{5,6},{6,7},{8,9},{9,10},{10,11},{11... | collective-permute-start | bytes 2949128 | tf_op jit(solution)/shard_map/ppermute | solution.py:29
  221.1 35.5 %collective-permute-start.1 = (bf16[2,2,1,1,2,80,768]{6,5,4,3,1,0,2:T(8,128)(2,1)}, bf16[2,2,1,1,2,80,768]{6,5,4,3,1,0,2:T(8,128)(2,1)}, u32[]{:S(2)}, u32[]{:S(2)}) collective-permute-start(bf16[2,2,1,1,2,80,768]{6,5,4,3,1,0,2:T(8,128)(2,1)} %get-tuple-element.12), channel_id=1, source_target_pairs={{1,0},{2,1},{3,2},{4,3},{5,4},{6,5},{7,6},{9,8},{10,9},{11,10},{12... | collective-permute-start | bytes 2949128 | tf_op jit(solution)/shard_map/ppermute | solution.py:31
  241.8 14.7 %copy-start.8 = (s32[12,3]{0,1:T(4,128)S(1)}, s32[12,3]{0,1:T(4,128)}, u32[]{:S(2)}) copy-start(s32[12,3]{0,1:T(4,128)} %param.14) | copy-start | bytes 436
  243.5 1.3 copy-start.2
  246.2 27.7 %collective-permute-start.4 = (bf16[2,2,1,1,2,80,768]{6,5,4,3,1,0,2:T(8,128)(2,1)}, bf16[2,2,1,1,2,80,768]{6,5,4,3,1,0,2:T(8,128)(2,1)}, u32[]{:S(2)}, u32[]{:S(2)}) collective-permute-start(bf16[2,2,1,1,2,80,768]{6,5,4,3,1,0,2:T(8,128)(2,1)} %get-tuple-element.9), channel_id=1, source_target_pairs={{0,1},{1,2},{2,3},{3,4},{4,5},{5,6},{6,7},{8,9},{9,10},{10,11},{11... | collective-permute-start | bytes 2949128 | tf_op jit(solution)/shard_map/ppermute | solution.py:29
  248.1 26.9 %collective-permute-start.5 = (bf16[2,2,1,1,2,80,768]{6,5,4,3,1,0,2:T(8,128)(2,1)}, bf16[2,2,1,1,2,80,768]{6,5,4,3,1,0,2:T(8,128)(2,1)}, u32[]{:S(2)}, u32[]{:S(2)}) collective-permute-start(bf16[2,2,1,1,2,80,768]{6,5,4,3,1,0,2:T(8,128)(2,1)} %get-tuple-element.10), channel_id=1, source_target_pairs={{1,0},{2,1},{3,2},{4,3},{5,4},{6,5},{7,6},{9,8},{10,9},{11,10},{12... | collective-permute-start | bytes 2949128 | tf_op jit(solution)/shard_map/ppermute | solution.py:31
  258.1 3.3 copy-start
  258.1 17.0 %copy-start.3 = (bf16[2,640,768]{2,1,0:T(8,128)(2,1)S(1)}, bf16[2,640,768]{2,1,0:T(8,128)(2,1)}, u32[]{:S(2)}) copy-start(bf16[2,640,768]{2,1,0:T(8,128)(2,1)} %copy-done.2) | copy-start | bytes 5898244
  261.3 78.0 %collective-permute-start.3 = (bf16[2,1,8,80,768]{4,3,2,1,0:T(8,128)(2,1)}, bf16[2,1,8,80,768]{4,3,2,1,0:T(8,128)(2,1)S(1)}, u32[]{:S(2)}, u32[]{:S(2)}) collective-permute-start(bf16[2,1,8,80,768]{4,3,2,1,0:T(8,128)(2,1)} %get-tuple-element.7), channel_id=1, source_target_pairs={{8,0},{16,8},{24,16},{32,24},{40,32},{48,40},{56,48},{64,56},{72,6... | collective-permute-start | bytes 5898248 | tf_op jit(solution)/shard_map/ppermute | solution.py:83
  264.3 75.1 %collective-permute-start.2 = (bf16[2,1,8,80,768]{4,3,2,1,0:T(8,128)(2,1)}, bf16[2,1,8,80,768]{4,3,2,1,0:T(8,128)(2,1)}, u32[]{:S(2)}, u32[]{:S(2)}) collective-permute-start(bf16[2,1,8,80,768]{4,3,2,1,0:T(8,128)(2,1)} %get-tuple-element.8), channel_id=1, source_target_pairs={{0,8},{8,16},{16,24},{24,32},{32,40},{40,48},{48,56},{56,64},{64,7... | collective-permute-start | bytes 5898248 | tf_op jit(solution)/shard_map/ppermute | solution.py:80
  276.8 3.1 copy-start.1
  279.8 37.3 %collective-permute-start.7 = (bf16[2,1,8,80,768]{4,3,2,1,0:T(8,128)(2,1)}, bf16[2,1,8,80,768]{4,3,2,1,0:T(8,128)(2,1)}, u32[]{:S(2)}, u32[]{:S(2)}) collective-permute-start(bf16[2,1,8,80,768]{4,3,2,1,0:T(8,128)(2,1)} %get-tuple-element.5), channel_id=1, source_target_pairs={{8,0},{16,8},{24,16},{32,24},{40,32},{48,40},{56,48},{64,56},{72,6... | collective-permute-start | bytes 5898248 | tf_op jit(solution)/shard_map/ppermute | solution.py:83
  282.2 37.8 %collective-permute-start.6 = (bf16[2,1,8,80,768]{4,3,2,1,0:T(8,128)(2,1)}, bf16[2,1,8,80,768]{4,3,2,1,0:T(8,128)(2,1)}, u32[]{:S(2)}, u32[]{:S(2)}) collective-permute-start(bf16[2,1,8,80,768]{4,3,2,1,0:T(8,128)(2,1)} %get-tuple-element.6), channel_id=1, source_target_pairs={{0,8},{8,16},{16,24},{24,32},{32,40},{40,48},{48,56},{56,64},{64,7... | collective-permute-start | bytes 5898248 | tf_op jit(solution)/shard_map/ppermute | solution.py:80
  339.4 1.3 copy-start.4
Sparse Core Ops, SparseCore 0:
  33.7 164.6 all-gather.1

commit v18 on v16

--- a/solution.py
+++ b/solution.py
@@ -80,7 +80,6 @@
         )
         after = lax.ppermute(rows_done[:, :TT], "tm", [(i + 1, i) for i in range(count - 1)])
         groups.append((rows_done, before, after))
-    query = project(modulated, full_weight, 0, inner, q_gain)
     frames_ext = frame_count + 2 * TT
     rows_ext = row_count + 2 * TH
     frame_block = lax.axis_index("tm")
@@ -121,7 +120,6 @@
     query_lo = (query_cols[None, :] - window[:, 2, None]).reshape(HEADS, query_n, 1)
     query_hi = (query_cols[None, :] + window[:, 2, None]).reshape(HEADS, query_n, 1)
     query_ok = query_valid.reshape(blocks, query_n, 1).astype(jnp.float32)
-    query_grid = query.reshape(frame_count, row_count, width, inner)
     assert frame_count == 2 * TT
     mask_rows = key_mask.reshape(HEADS, blocks, span_t, span_h, width)
     halo_masks, own_masks = [], []
@@ -138,7 +136,9 @@
     out = None
     for group, pieces in enumerate(groups):
         masks = (halo_mask, own_mask, query_lo, query_hi, halo_cols, own_cols, query_ok)
-        out = tile_attention(query_grid, pieces, masks, group, out)
+        query = project(modulated, full_weight, group * group_cols, group_cols, q_gain)
+        query = query.reshape(frame_count, row_count, width, group_cols)
+        out = tile_attention(query, pieces, masks, group, out)
     return out
 
 
@@ -184,15 +184,17 @@
 
 
 def tile_attention(query, pieces, masks, group, out):
-    frames, rows, width, inner = query.shape
+    frames, rows, width, group_cols = query.shape
     middle, top, bottom = pieces
-    heads = middle.shape[-1] // HDIM
+    heads = group_cols // HDIM
+    out_shape = (frames, rows, width, masks[2].shape[0] * HDIM)
     first = group * heads
     assert rows // TH == ROW_TILES
     blocks = frames * ROW_TILES
     halo_mask, own_mask, query_lo, query_hi, halo_cols, own_cols, query_ok = masks
     query_n = TH * width
-    q_spec = pl.BlockSpec((frames, rows, width, HDIM), lambda h: (0, 0, 0, first + h))
+    q_spec = pl.BlockSpec((frames, rows, width, HDIM), lambda h: (0, 0, 0, h))
+    o_spec = pl.BlockSpec((frames, rows, width, HDIM), lambda h: (0, 0, 0, first + h))
 
     def piece_specs(piece):
         shape = (1, *piece.shape[1:-1], HDIM)
@@ -224,8 +226,8 @@
         kernel,
         grid=(heads,),
         in_specs=in_specs,
-        out_specs=q_spec,
-        out_shape=jax.ShapeDtypeStruct(query.shape, jnp.bfloat16),
+        out_specs=o_spec,
+        out_shape=jax.ShapeDtypeStruct(out_shape, jnp.bfloat16),
         input_output_aliases=aliases,
     )(*operands)
 

time: 341 us -> 358 us (1.050)
  waiting for transfers between devices: 162 us -> 178 us
    ppermute x2, waiting for transfers between devices: 0.01 us -> 13.2 us  [per_device(): lax.ppermute(rows_done[:, :TT], 'tm', [(i + 1, i) for i in range(count -...]
    pallas_call x1 -> x2, Pallas kernels: 11.7 us -> 14.9 us  [project(): pl.pallas_call(functools.partial(projection_kernel, normalize=normalize),...]
  transfers between devices with their start and end apart: 9 -> 9, of which waited for: 3 -> 5; matrix products, arithmetic and copies ran while one was open for 9% -> 8% of each run, Pallas kernels for 13% -> 13%
where the time goes in v18:
time: 358 us; the launch traced here: 357 us
  waiting for transfers between devices  178 us (50%)
  Pallas kernels  104 us (29%)
  starting transfers between devices  25.3 us (7%)
  other arithmetic  17.8 us (5%)
  local copies, waits for them, and re-layouts  17.3 us (5%)
  between operations  13.8 us (4%)
    all_gather x1, waiting for transfers between devices, per_device(): full_weight = lax.all_gather(band_weight, 'tm', axis=0, tiled=True)  154 us
    pallas_call x2, Pallas kernels, tile_attention(): pl.pallas_call(kernel, grid=(heads,), in_specs=in_specs, out_specs=o_spec...  38.7 us
    pallas_call x1, Pallas kernels, band_gather(): pl.pallas_call(band_gather_kernel, in_specs=[pl.BlockSpec(memory_space=pl...  27 us
    pallas_call x2, Pallas kernels, project_kv(): pl.pallas_call(projection_kv_kernel, grid=(2 * steps,), in_specs=[pl.Bloc...  23.6 us
    pallas_call x2, Pallas kernels, project(): pl.pallas_call(functools.partial(projection_kernel, normalize=normalize),...  14.9 us
    ppermute x2, waiting for transfers between devices, per_device(): lax.ppermute(rows_done[:, :TT], 'tm', [(i + 1, i) for i in range(count -...  13.2 us
    ppermute x2, starting transfers between devices, with_halo(): lax.ppermute(head, axis, [((i + 1) % count, i) for i in range(ends)])  10.5 us
    ppermute x2, waiting for transfers between devices, with_halo(): lax.ppermute(tail, axis, [(i, (i + 1) % count) for i in range(ends)])  7.59 us
  transfers between devices with their start and end apart: 9, of which 5 were waited for; matrix products, arithmetic and copies ran while one was open for 8% of the time, Pallas kernels for 13%

profile of v18, /device:TPU:6, one launch (start us, length us, event | category | flops | bytes accessed | tf_op | source)
XLA Modules:
  0.0 356.8 jit_solution(17573439606240932902)
XLA Ops:
  6.5 27.0 %shard_map.82 = bf16[8,24,4608]{2,1,0:T(8,128)(2,1)} custom-call(bf16[24,4608]{1,0:T(8,128)(2,1)} %w_ref.1), custom_call_target="tpu_custom_call" | custom-call | tf_op jit(solution)/shard_map/pallas_call | solution.py:313
  33.6 2.7 convert_reduce_fusion
  36.5 3.3 multiply_reduce_fusion
  39.9 4.9 %fusion.3.x_ref = bf16[640,3072]{1,0:T(8,128)(2,1)} fusion(bf16[2,4,80,3072]{3,2,1,0:T(8,128)(2,1)} %param.8, f32[3072]{0:T(1024)S(1)} %copy-done.7, f32[3072]{0:T(1024)S(1)} %broadcast_add_fusion.1, f32[640]{0:T(1024)S(1)} %rsqrt.12, f32[640]{0:T(1024)S(1)} %div.33), kind=kLoop, calls=%fused_computation.4 | loop fusion | flops 11796480 | bytes 7894016 | tf_op jit(solution)/shard_map/convert_element_type | solution.py:44
  44.8 153.6 %all-gather.2.cloned.1.call-done.w_ref = bf16[3072,4608]{1,0:T(8,128)(2,1)} async-done(((bf16[192,4608]{1,0:T(8,128)(2,1)}), bf16[3072,4608]{1,0:T(8,128)(2,1)}) %all-gather.2.cloned.1.call-update) | async-done | bytes 28311568 | tf_op jit(solution)/shard_map/all_gather | solution.py:66
  198.4 11.7 %shard_map.84 = bf16[2,640,768]{2,1,0:T(8,128)(2,1)} custom-call(bf16[640,3072]{1,0:T(8,128)(2,1)} %fusion.3.x_ref, bf16[3072,4608]{1,0:T(8,128)(2,1)} %all-gather.2.cloned.1.call-done.w_ref, f32[1,128]{1,0:T(1,128)} %bitcast.62), custom_call_target="tpu_custom_call" | custom-call | tf_op jit(solution)/shard_map/pallas_call | solution.py:351
  210.1 3.0 fusion.13
  213.1 3.4 collective-permute-start
  216.5 4.5 %collective-permute-start.1 = (bf16[2,2,1,1,2,80,768]{6,5,4,3,1,0,2:T(8,128)(2,1)}, bf16[2,2,1,1,2,80,768]{6,5,4,3,1,0,2:T(8,128)(2,1)}, u32[]{:S(2)}, u32[]{:S(2)}) collective-permute-start(bf16[2,2,1,1,2,80,768]{6,5,4,3,1,0,2:T(8,128)(2,1)} %get-tuple-element.12), channel_id=1, source_target_pairs={{1,0},{2,1},{3,2},{4,3},{5,4},{6,5},{7,6},{9,8},{10,9},{11,10},{12... | collective-permute-start | bytes 2949128 | tf_op jit(solution)/shard_map/ppermute | solution.py:31
  221.2 11.8 %shard_map.86 = bf16[2,640,768]{2,1,0:T(8,128)(2,1)} custom-call(bf16[640,3072]{1,0:T(8,128)(2,1)} %fusion.3.x_ref, bf16[3072,4608]{1,0:T(8,128)(2,1)} %all-gather.2.cloned.1.call-done.w_ref, f32[1,128]{1,0:T(1,128)} %bitcast.63), custom_call_target="tpu_custom_call" | custom-call | tf_op jit(solution)/shard_map/pallas_call | solution.py:351
  233.0 3.1 fusion.12
  238.0 6.0 %collective-permute-start.5 = (bf16[2,2,1,1,2,80,768]{6,5,4,3,1,0,2:T(8,128)(2,1)}, bf16[2,2,1,1,2,80,768]{6,5,4,3,1,0,2:T(8,128)(2,1)}, u32[]{:S(2)}, u32[]{:S(2)}) collective-permute-start(bf16[2,2,1,1,2,80,768]{6,5,4,3,1,0,2:T(8,128)(2,1)} %get-tuple-element.10), channel_id=1, source_target_pairs={{1,0},{2,1},{3,2},{4,3},{5,4},{6,5},{7,6},{9,8},{10,9},{11,10},{12... | collective-permute-start | bytes 2949128 | tf_op jit(solution)/shard_map/ppermute | solution.py:31
  248.0 2.2 fusion.11
  251.3 3.0 collective-permute-start.3
  256.2 7.6 %collective-permute-done.4 = bf16[2,2,1,1,2,80,768]{6,5,4,3,1,0,2:T(8,128)(2,1)} collective-permute-done((bf16[2,2,1,1,2,80,768]{6,5,4,3,1,0,2:T(8,128)(2,1)}, bf16[2,2,1,1,2,80,768]{6,5,4,3,1,0,2:T(8,128)(2,1)}, u32[]{:S(2)}, u32[]{:S(2)}) %collective-permute-start.4) | collective-permute-done | bytes 983072 | tf_op jit(solution)/shard_map/ppermute | solution.py:29
  266.7 2.3 fusion.10
  269.7 2.4 collective-permute-start.7
  272.1 2.1 collective-permute-start.6
  279.0 7.5 %shard_map.85 = bf16[640,768]{1,0:T(8,128)(2,1)} custom-call(bf16[640,3072]{1,0:T(8,128)(2,1)} %fusion.3.x_ref, bf16[3072,4608]{1,0:T(8,128)(2,1)} %all-gather.2.cloned.1.call-done.w_ref, f32[1,128]{1,0:T(1,128)} %bitcast.64), custom_call_target="tpu_custom_call" | custom-call | tf_op jit(solution)/shard_map/pallas_call | solution.py:254
  286.4 7.5 %shard_map.83 = bf16[640,768]{1,0:T(8,128)(2,1)} custom-call(bf16[640,3072]{1,0:T(8,128)(2,1)} %fusion.3.x_ref, bf16[3072,4608]{1,0:T(8,128)(2,1)} %all-gather.2.cloned.1.call-done.w_ref, f32[1,128]{1,0:T(1,128)} %bitcast.65), custom_call_target="tpu_custom_call" | custom-call | tf_op jit(solution)/shard_map/pallas_call | solution.py:254
  293.9 13.2 %collective-permute-done.7.bk_ref.bv_ref = bf16[2,1,8,80,768]{4,3,2,1,0:T(8,128)(2,1)} collective-permute-done((bf16[2,1,8,80,768]{4,3,2,1,0:T(8,128)(2,1)}, bf16[2,1,8,80,768]{4,3,2,1,0:T(8,128)(2,1)}, u32[]{:S(2)}, u32[]{:S(2)}) %collective-permute-start.7) | collective-permute-done | bytes 1966112 | tf_op jit(solution)/shard_map/ppermute | solution.py:81
  307.1 2.8 collective-permute-done.6.tk_ref.tv_ref
  309.9 19.4 %shard_map.87.refs_14_ = bf16[2,4,80,1536]{3,2,1,0:T(8,128)(2,1)} custom-call(bf16[2,4,80,768]{3,2,1,0:T(8,128)(2,1)} %bitcast.53, bf16[2,2,8,80,768]{4,3,2,1,0:T(8,128)(2,1)} %bitcast.45, bf16[2,2,8,80,768]{4,3,2,1,0:T(8,128)(2,1)} %bitcast.46, bf16[2,1,8,80,768]{4,3,2,1,0:T(8,128)(2,1)} %collective-permute-done.6.tk_ref.tv_ref, ...), custom_call_target="tpu_custom_call" | custom-call | tf_op jit(solution)/shard_map/pallas_call | solution.py:225
  330.6 19.4 %shard_map.88 = bf16[2,4,80,1536]{3,2,1,0:T(8,128)(2,1)} custom-call(bf16[2,4,80,768]{3,2,1,0:T(8,128)(2,1)} %bitcast.52, bf16[2,2,8,80,768]{4,3,2,1,0:T(8,128)(2,1)} %bitcast.42, bf16[2,2,8,80,768]{4,3,2,1,0:T(8,128)(2,1)} %bitcast.43, bf16[2,1,8,80,768]{4,3,2,1,0:T(8,128)(2,1)} %collective-permute-done.2.refs_3_.refs_4_, ...), custom_call_target="tpu_custom_call", output_to_operand_aliasing={{}: (14, {})} | custom-call | tf_op jit(solution)/shard_map/pallas_call | solution.py:225
  (65 shorter events, 18.6 us)
Async XLA Ops:
  6.5 191.9 %all-gather.2.cloned.1.call-start = ((), (), s32[]{:S(2)}) async-start(), calls=%async_computation | async-start | bytes 30081024 | tf_op jit(solution)/shard_map/all_gather | solution.py:66
  33.6 6.2 %copy-start.6 = (f32[3072]{0:T(1024)S(1)}, f32[3072]{0:T(1024)}, u32[]{:S(2)}) copy-start(f32[3072]{0:T(1024)} %param.9) | copy-start | bytes 36868
  33.6 6.2 %copy-start.7 = (f32[3072]{0:T(1024)S(1)}, f32[3072]{0:T(1024)}, u32[]{:S(2)}) copy-start(f32[3072]{0:T(1024)} %param.10) | copy-start | bytes 36868
  210.1 10.9 %copy-start.5 = (s32[32,32,80]{2,1,0:T(8,128)S(1)}, s32[32,32,80]{2,1,0:T(8,128)}, u32[]{:S(2)}) copy-start(s32[32,32,80]{2,1,0:T(8,128)} %param.15) | copy-start | bytes 983044
  213.1 33.3 %collective-permute-start = (bf16[2,2,1,1,2,80,768]{6,5,4,3,1,0,2:T(8,128)(2,1)}, bf16[2,2,1,1,2,80,768]{6,5,4,3,1,0,2:T(8,128)(2,1)S(1)}, u32[]{:S(2)}, u32[]{:S(2)}) collective-permute-start(bf16[2,2,1,1,2,80,768]{6,5,4,3,1,0,2:T(8,128)(2,1)} %get-tuple-element.11), channel_id=1, source_target_pairs={{0,1},{1,2},{2,3},{3,4},{4,5},{5,6},{6,7},{8,9},{9,10},{10,11},{11... | collective-permute-start | bytes 2949128 | tf_op jit(solution)/shard_map/ppermute | solution.py:29
  216.5 29.9 %collective-permute-start.1 = (bf16[2,2,1,1,2,80,768]{6,5,4,3,1,0,2:T(8,128)(2,1)}, bf16[2,2,1,1,2,80,768]{6,5,4,3,1,0,2:T(8,128)(2,1)}, u32[]{:S(2)}, u32[]{:S(2)}) collective-permute-start(bf16[2,2,1,1,2,80,768]{6,5,4,3,1,0,2:T(8,128)(2,1)} %get-tuple-element.12), channel_id=1, source_target_pairs={{1,0},{2,1},{3,2},{4,3},{5,4},{6,5},{7,6},{9,8},{10,9},{11,10},{12... | collective-permute-start | bytes 2949128 | tf_op jit(solution)/shard_map/ppermute | solution.py:31
  233.0 13.4 %copy-start.8 = (s32[12,3]{0,1:T(4,128)S(1)}, s32[12,3]{0,1:T(4,128)}, u32[]{:S(2)}) copy-start(s32[12,3]{0,1:T(4,128)} %param.14) | copy-start | bytes 436
  233.0 13.4 %copy-start.2 = (bf16[2,640,768]{2,1,0:T(8,128)(2,1)S(1)}, bf16[2,640,768]{2,1,0:T(8,128)(2,1)}, u32[]{:S(2)}) copy-start(bf16[2,640,768]{2,1,0:T(8,128)(2,1)} %shard_map.84) | copy-start | bytes 5898244
  236.1 27.7 %collective-permute-start.4 = (bf16[2,2,1,1,2,80,768]{6,5,4,3,1,0,2:T(8,128)(2,1)}, bf16[2,2,1,1,2,80,768]{6,5,4,3,1,0,2:T(8,128)(2,1)}, u32[]{:S(2)}, u32[]{:S(2)}) collective-permute-start(bf16[2,2,1,1,2,80,768]{6,5,4,3,1,0,2:T(8,128)(2,1)} %get-tuple-element.9), channel_id=1, source_target_pairs={{0,1},{1,2},{2,3},{3,4},{4,5},{5,6},{6,7},{8,9},{9,10},{10,11},{11... | collective-permute-start | bytes 2949128 | tf_op jit(solution)/shard_map/ppermute | solution.py:29
  238.0 26.9 %collective-permute-start.5 = (bf16[2,2,1,1,2,80,768]{6,5,4,3,1,0,2:T(8,128)(2,1)}, bf16[2,2,1,1,2,80,768]{6,5,4,3,1,0,2:T(8,128)(2,1)}, u32[]{:S(2)}, u32[]{:S(2)}) collective-permute-start(bf16[2,2,1,1,2,80,768]{6,5,4,3,1,0,2:T(8,128)(2,1)} %get-tuple-element.10), channel_id=1, source_target_pairs={{1,0},{2,1},{3,2},{4,3},{5,4},{6,5},{7,6},{9,8},{10,9},{11,10},{12... | collective-permute-start | bytes 2949128 | tf_op jit(solution)/shard_map/ppermute | solution.py:31
  248.0 3.3 copy-start
  248.0 16.9 %copy-start.3 = (bf16[2,640,768]{2,1,0:T(8,128)(2,1)S(1)}, bf16[2,640,768]{2,1,0:T(8,128)(2,1)}, u32[]{:S(2)}) copy-start(bf16[2,640,768]{2,1,0:T(8,128)(2,1)} %shard_map.86) | copy-start | bytes 5898244
  251.3 78.0 %collective-permute-start.3 = (bf16[2,1,8,80,768]{4,3,2,1,0:T(8,128)(2,1)}, bf16[2,1,8,80,768]{4,3,2,1,0:T(8,128)(2,1)S(1)}, u32[]{:S(2)}, u32[]{:S(2)}) collective-permute-start(bf16[2,1,8,80,768]{4,3,2,1,0:T(8,128)(2,1)} %get-tuple-element.7), channel_id=1, source_target_pairs={{8,0},{16,8},{24,16},{32,24},{40,32},{48,40},{56,48},{64,56},{72,6... | collective-permute-start | bytes 5898248 | tf_op jit(solution)/shard_map/ppermute | solution.py:81
  254.2 75.0 %collective-permute-start.2 = (bf16[2,1,8,80,768]{4,3,2,1,0:T(8,128)(2,1)}, bf16[2,1,8,80,768]{4,3,2,1,0:T(8,128)(2,1)}, u32[]{:S(2)}, u32[]{:S(2)}) collective-permute-start(bf16[2,1,8,80,768]{4,3,2,1,0:T(8,128)(2,1)} %get-tuple-element.8), channel_id=1, source_target_pairs={{0,8},{8,16},{16,24},{24,32},{32,40},{40,48},{48,56},{56,64},{64,7... | collective-permute-start | bytes 5898248 | tf_op jit(solution)/shard_map/ppermute | solution.py:78
  266.7 3.0 copy-start.1
  269.7 37.4 %collective-permute-start.7 = (bf16[2,1,8,80,768]{4,3,2,1,0:T(8,128)(2,1)}, bf16[2,1,8,80,768]{4,3,2,1,0:T(8,128)(2,1)}, u32[]{:S(2)}, u32[]{:S(2)}) collective-permute-start(bf16[2,1,8,80,768]{4,3,2,1,0:T(8,128)(2,1)} %get-tuple-element.5), channel_id=1, source_target_pairs={{8,0},{16,8},{24,16},{32,24},{40,32},{48,40},{56,48},{64,56},{72,6... | collective-permute-start | bytes 5898248 | tf_op jit(solution)/shard_map/ppermute | solution.py:81
  272.1 37.8 %collective-permute-start.6 = (bf16[2,1,8,80,768]{4,3,2,1,0:T(8,128)(2,1)}, bf16[2,1,8,80,768]{4,3,2,1,0:T(8,128)(2,1)}, u32[]{:S(2)}, u32[]{:S(2)}) collective-permute-start(bf16[2,1,8,80,768]{4,3,2,1,0:T(8,128)(2,1)} %get-tuple-element.6), channel_id=1, source_target_pairs={{0,8},{8,16},{16,24},{24,32},{32,40},{40,48},{48,56},{56,64},{64,7... | collective-permute-start | bytes 5898248 | tf_op jit(solution)/shard_map/ppermute | solution.py:78
  329.3 1.3 copy-start.4
Sparse Core Ops, SparseCore 0:
  33.7 164.6 all-gather.1

commit v19 on v16

--- a/solution.py
+++ b/solution.py
@@ -68,19 +68,21 @@
     group_cols = inner // GROUPS
     tiled = (frame_count // TT, TT, row_count // TH, TH, width, group_cols)
     groups = []
+    query = project(modulated, full_weight, 0, inner, q_gain)
     for group in range(GROUPS):
         start = group * group_cols
         stacked = project_kv(modulated, full_weight, start, group_cols, k_gain)
         stacked = stacked.reshape(2, *tiled)
         rows_done = with_halo(stacked, (("height", 3),), 1)
         rows_done = rows_done.reshape(2, frame_count, row_count + 2 * TH, width, group_cols)
+        if group == 0:
+            rows_done, query = lax.optimization_barrier((rows_done, query))
         count = lax.axis_size("tm")
         before = lax.ppermute(
             rows_done[:, frame_count - TT :], "tm", [(i, i + 1) for i in range(count - 1)]
         )
         after = lax.ppermute(rows_done[:, :TT], "tm", [(i + 1, i) for i in range(count - 1)])
         groups.append((rows_done, before, after))
-    query = project(modulated, full_weight, 0, inner, q_gain)
     frames_ext = frame_count + 2 * TT
     rows_ext = row_count + 2 * TH
     frame_block = lax.axis_index("tm")

time: 341 us -> 374 us (1.097)
  waiting for transfers between devices: 162 us -> 189 us
  starting transfers between devices: 25.3 us -> 32.6 us
    ppermute x2, waiting for transfers between devices: 0.01 us -> 21.7 us  [per_device(): lax.ppermute(rows_done[:, frame_count - TT:], 'tm', [(i, i + 1) for i in...]
    ppermute x2, starting transfers between devices: 5.33 us -> 14.7 us  [per_device(): lax.ppermute(rows_done[:, :TT], 'tm', [(i + 1, i) for i in range(count -...]
    ppermute x2, waiting for transfers between devices: 1.18 us -> 5.49 us  [with_halo(): lax.ppermute(head, axis, [((i + 1) % count, i) for i in range(ends)])]
  transfers between devices with their start and end apart: 9 -> 9, of which waited for: 3 -> 5; matrix products, arithmetic and copies ran while one was open for 9% -> 7% of each run, Pallas kernels for 13% -> 12%
where the time goes in v19:
time: 374 us; the launch traced here: 370 us
  waiting for transfers between devices  189 us (51%)
  Pallas kernels  101 us (27%)
  starting transfers between devices  32.6 us (9%)
  other arithmetic  18.7 us (5%)
  local copies, waits for them, and re-layouts  15.4 us (4%)
  between operations  13.8 us (4%)
    all_gather x1, waiting for transfers between devices, per_device(): full_weight = lax.all_gather(band_weight, 'tm', axis=0, tiled=True)  154 us
    pallas_call x2, Pallas kernels, tile_attention(): pl.pallas_call(kernel, grid=(heads,), in_specs=in_specs, out_specs=q_spec...  38.6 us
    pallas_call x1, Pallas kernels, band_gather(): pl.pallas_call(band_gather_kernel, in_specs=[pl.BlockSpec(memory_space=pl...  27 us
    pallas_call x2, Pallas kernels, project_kv(): pl.pallas_call(projection_kv_kernel, grid=(2 * steps,), in_specs=[pl.Bloc...  23.5 us
    ppermute x2, waiting for transfers between devices, per_device(): lax.ppermute(rows_done[:, frame_count - TT:], 'tm', [(i, i + 1) for i in...  21.7 us
    ppermute x2, starting transfers between devices, per_device(): lax.ppermute(rows_done[:, :TT], 'tm', [(i + 1, i) for i in range(count -...  14.7 us
    pallas_call x1, Pallas kernels, project(): pl.pallas_call(functools.partial(projection_kernel, normalize=normalize),...  11.8 us
    ppermute x2, starting transfers between devices, with_halo(): lax.ppermute(head, axis, [((i + 1) % count, i) for i in range(ends)])  10.3 us
  transfers between devices with their start and end apart: 9, of which 5 were waited for; matrix products, arithmetic and copies ran while one was open for 7% of the time, Pallas kernels for 12%

profile of v19, /device:TPU:6, one launch (start us, length us, event | category | flops | bytes accessed | tf_op | source)
XLA Modules:
  0.0 370.5 jit_solution(14182462416389911902)
XLA Ops:
  6.5 27.0 %shard_map.82 = bf16[8,24,4608]{2,1,0:T(8,128)(2,1)} custom-call(bf16[24,4608]{1,0:T(8,128)(2,1)} %w_ref.1), custom_call_target="tpu_custom_call" | custom-call | tf_op jit(solution)/shard_map/pallas_call | solution.py:313
  33.6 2.7 convert_reduce_fusion
  36.5 3.3 multiply_reduce_fusion
  39.9 4.9 %fusion.3.x_ref = bf16[640,3072]{1,0:T(8,128)(2,1)} fusion(bf16[2,4,80,3072]{3,2,1,0:T(8,128)(2,1)} %param.8, f32[3072]{0:T(1024)S(1)} %copy-done.7, f32[3072]{0:T(1024)S(1)} %broadcast_add_fusion.1, f32[640]{0:T(1024)S(1)} %rsqrt.12, f32[640]{0:T(1024)S(1)} %div.33), kind=kLoop, calls=%fused_computation.4 | loop fusion | flops 11796480 | bytes 7894016 | tf_op jit(solution)/shard_map/convert_element_type | solution.py:44
  44.8 153.6 %all-gather.2.cloned.1.call-done.w_ref = bf16[3072,4608]{1,0:T(8,128)(2,1)} async-done(((bf16[192,4608]{1,0:T(8,128)(2,1)}), bf16[3072,4608]{1,0:T(8,128)(2,1)}) %all-gather.2.cloned.1.call-update) | async-done | bytes 28311568 | tf_op jit(solution)/shard_map/all_gather | solution.py:66
  198.4 11.8 %shard_map.83 = bf16[2,640,768]{2,1,0:T(8,128)(2,1)} custom-call(bf16[640,3072]{1,0:T(8,128)(2,1)} %fusion.3.x_ref, bf16[3072,4608]{1,0:T(8,128)(2,1)} %all-gather.2.cloned.1.call-done.w_ref, f32[1,128]{1,0:T(1,128)} %bitcast.61), custom_call_target="tpu_custom_call" | custom-call | tf_op jit(solution)/shard_map/pallas_call | solution.py:351
  210.2 2.9 fusion.13
  213.1 4.2 %collective-permute-start.1 = (bf16[2,2,1,1,2,80,768]{6,5,4,3,1,0,2:T(8,128)(2,1)}, bf16[2,2,1,1,2,80,768]{6,5,4,3,1,0,2:T(8,128)(2,1)S(1)}, u32[]{:S(2)}, u32[]{:S(2)}) collective-permute-start(bf16[2,2,1,1,2,80,768]{6,5,4,3,1,0,2:T(8,128)(2,1)} %get-tuple-element.16), channel_id=1, source_target_pairs={{1,0},{2,1},{3,2},{4,3},{5,4},{6,5},{7,6},{9,8},{10,9},{11,10},{12... | collective-permute-start | bytes 2949128 | tf_op jit(solution)/shard_map/ppermute | solution.py:31
  217.3 1.9 collective-permute-start
  219.3 11.8 %shard_map.85 = bf16[2,640,768]{2,1,0:T(8,128)(2,1)} custom-call(bf16[640,3072]{1,0:T(8,128)(2,1)} %fusion.3.x_ref, bf16[3072,4608]{1,0:T(8,128)(2,1)} %all-gather.2.cloned.1.call-done.w_ref, f32[1,128]{1,0:T(1,128)} %bitcast.62), custom_call_target="tpu_custom_call" | custom-call | tf_op jit(solution)/shard_map/pallas_call | solution.py:351
  231.1 3.0 fusion.12
  234.0 6.0 %collective-permute-start.3 = (bf16[2,2,1,1,2,80,768]{6,5,4,3,1,0,2:T(8,128)(2,1)}, bf16[2,2,1,1,2,80,768]{6,5,4,3,1,0,2:T(8,128)(2,1)}, u32[]{:S(2)}, u32[]{:S(2)}) collective-permute-start(bf16[2,2,1,1,2,80,768]{6,5,4,3,1,0,2:T(8,128)(2,1)} %get-tuple-element.14), channel_id=1, source_target_pairs={{1,0},{2,1},{3,2},{4,3},{5,4},{6,5},{7,6},{9,8},{10,9},{11,10},{12... | collective-permute-start | bytes 2949128 | tf_op jit(solution)/shard_map/ppermute | solution.py:31
  240.1 1.9 collective-permute-start.2
  242.2 11.8 %shard_map.84 = bf16[640,1536]{1,0:T(8,128)(2,1)} custom-call(bf16[640,3072]{1,0:T(8,128)(2,1)} %fusion.3.x_ref, bf16[3072,4608]{1,0:T(8,128)(2,1)} %all-gather.2.cloned.1.call-done.w_ref, f32[1,128]{1,0:T(1,128)} %bitcast.63), custom_call_target="tpu_custom_call" | custom-call | tf_op jit(solution)/shard_map/pallas_call | solution.py:254
  255.8 5.5 %collective-permute-done.3 = bf16[2,2,1,1,2,80,768]{6,5,4,3,1,0,2:T(8,128)(2,1)} collective-permute-done((bf16[2,2,1,1,2,80,768]{6,5,4,3,1,0,2:T(8,128)(2,1)}, bf16[2,2,1,1,2,80,768]{6,5,4,3,1,0,2:T(8,128)(2,1)}, u32[]{:S(2)}, u32[]{:S(2)}) %collective-permute-start.3) | collective-permute-done | bytes 983072 | tf_op jit(solution)/shard_map/ppermute | solution.py:31
  261.2 6.2 %collective-permute-done.2 = bf16[2,2,1,1,2,80,768]{6,5,4,3,1,0,2:T(8,128)(2,1)} collective-permute-done((bf16[2,2,1,1,2,80,768]{6,5,4,3,1,0,2:T(8,128)(2,1)}, bf16[2,2,1,1,2,80,768]{6,5,4,3,1,0,2:T(8,128)(2,1)}, u32[]{:S(2)}, u32[]{:S(2)}) %collective-permute-start.2) | collective-permute-done | bytes 983072 | tf_op jit(solution)/shard_map/ppermute | solution.py:29
  269.2 2.4 fusion.11
  272.3 1.9 collective-permute-start.4
  274.2 7.3 %collective-permute-start.5 = (bf16[2,1,8,80,768]{4,3,2,1,0:T(8,128)(2,1)}, bf16[2,1,8,80,768]{4,3,2,1,0:T(8,128)(2,1)}, u32[]{:S(2)}, u32[]{:S(2)}) collective-permute-start(bf16[2,1,8,80,768]{4,3,2,1,0:T(8,128)(2,1)} %get-tuple-element.11), channel_id=1, source_target_pairs={{8,0},{16,8},{24,16},{32,24},{40,32},{48,40},{56,48},{64,56},{72,6... | collective-permute-start | bytes 5898248 | tf_op jit(solution)/shard_map/ppermute | solution.py:84
  281.5 2.2 fusion.10
  285.5 7.4 %collective-permute-start.7 = (bf16[2,1,8,80,768]{4,3,2,1,0:T(8,128)(2,1)}, bf16[2,1,8,80,768]{4,3,2,1,0:T(8,128)(2,1)}, u32[]{:S(2)}, u32[]{:S(2)}) collective-permute-start(bf16[2,1,8,80,768]{4,3,2,1,0:T(8,128)(2,1)} %get-tuple-element.9), channel_id=1, source_target_pairs={{8,0},{16,8},{24,16},{32,24},{40,32},{48,40},{56,48},{64,56},{72,6... | collective-permute-start | bytes 5898248 | tf_op jit(solution)/shard_map/ppermute | solution.py:84
  301.4 21.7 %collective-permute-done.6.tk_ref.tv_ref = bf16[2,1,8,80,768]{4,3,2,1,0:T(8,128)(2,1)S(1)} collective-permute-done((bf16[2,1,8,80,768]{4,3,2,1,0:T(8,128)(2,1)}, bf16[2,1,8,80,768]{4,3,2,1,0:T(8,128)(2,1)S(1)}, u32[]{:S(2)}, u32[]{:S(2)}) %collective-permute-start.6) | collective-permute-done | bytes 1966112 | tf_op jit(solution)/shard_map/ppermute | solution.py:81
  325.0 19.3 %shard_map.86.refs_14_ = bf16[2,4,80,1536]{3,2,1,0:T(8,128)(2,1)} custom-call(bf16[2,4,80,1536]{3,2,1,0:T(8,128)(2,1)} %bitcast.50, bf16[2,2,8,80,768]{4,3,2,1,0:T(8,128)(2,1)} %bitcast.41, bf16[2,2,8,80,768]{4,3,2,1,0:T(8,128)(2,1)} %bitcast.42, bf16[2,1,8,80,768]{4,3,2,1,0:T(8,128)(2,1)} %copy-done.4, bf16[2,1,8,80,768]{4,3,2,1,0:T(8,128)(2,1)} %copy-done.4, ...), custom_call_target="tpu_custom_call" | custom-call | tf_op jit(solution)/shard_map/pallas_call | solution.py:225
  344.2 19.4 %shard_map.87 = bf16[2,4,80,1536]{3,2,1,0:T(8,128)(2,1)} custom-call(bf16[2,4,80,1536]{3,2,1,0:T(8,128)(2,1)} %bitcast.51, bf16[2,2,8,80,768]{4,3,2,1,0:T(8,128)(2,1)} %bitcast.44, bf16[2,2,8,80,768]{4,3,2,1,0:T(8,128)(2,1)} %bitcast.45, bf16[2,1,8,80,768]{4,3,2,1,0:T(8,128)(2,1)} %collective-permute-done.4.refs_3_.refs_4_, ...), custom_call_target="tpu_custom_call", output_to_operand_aliasing={{}: (14, {})} | custom-call | tf_op jit(solution)/shard_map/pallas_call | solution.py:225
  (64 shorter events, 16.4 us)
Async XLA Ops:
  6.5 191.9 %all-gather.2.cloned.1.call-start = ((), (), s32[]{:S(2)}) async-start(), calls=%async_computation | async-start | bytes 30081024 | tf_op jit(solution)/shard_map/all_gather | solution.py:66
  33.6 6.2 %copy-start.6 = (f32[3072]{0:T(1024)S(1)}, f32[3072]{0:T(1024)}, u32[]{:S(2)}) copy-start(f32[3072]{0:T(1024)} %param.9) | copy-start | bytes 36868
  33.6 6.2 %copy-start.7 = (f32[3072]{0:T(1024)S(1)}, f32[3072]{0:T(1024)}, u32[]{:S(2)}) copy-start(f32[3072]{0:T(1024)} %param.10) | copy-start | bytes 36868
  213.1 40.9 %collective-permute-start.1 = (bf16[2,2,1,1,2,80,768]{6,5,4,3,1,0,2:T(8,128)(2,1)}, bf16[2,2,1,1,2,80,768]{6,5,4,3,1,0,2:T(8,128)(2,1)S(1)}, u32[]{:S(2)}, u32[]{:S(2)}) collective-permute-start(bf16[2,2,1,1,2,80,768]{6,5,4,3,1,0,2:T(8,128)(2,1)} %get-tuple-element.16), channel_id=1, source_target_pairs={{1,0},{2,1},{3,2},{4,3},{5,4},{6,5},{7,6},{9,8},{10,9},{11,10},{12... | collective-permute-start | bytes 2949128 | tf_op jit(solution)/shard_map/ppermute | solution.py:31
  217.3 36.7 %collective-permute-start = (bf16[2,2,1,1,2,80,768]{6,5,4,3,1,0,2:T(8,128)(2,1)}, bf16[2,2,1,1,2,80,768]{6,5,4,3,1,0,2:T(8,128)(2,1)}, u32[]{:S(2)}, u32[]{:S(2)}) collective-permute-start(bf16[2,2,1,1,2,80,768]{6,5,4,3,1,0,2:T(8,128)(2,1)} %get-tuple-element.15), channel_id=1, source_target_pairs={{0,1},{1,2},{2,3},{3,4},{4,5},{5,6},{6,7},{8,9},{9,10},{10,11},{11... | collective-permute-start | bytes 2949128 | tf_op jit(solution)/shard_map/ppermute | solution.py:29
  231.0 11.0 %copy-start.5 = (s32[32,32,80]{2,1,0:T(8,128)S(1)}, s32[32,32,80]{2,1,0:T(8,128)}, u32[]{:S(2)}) copy-start(s32[32,32,80]{2,1,0:T(8,128)} %param.15) | copy-start | bytes 983044
  231.0 11.1 %copy-start.8 = (s32[12,3]{0,1:T(4,128)S(1)}, s32[12,3]{0,1:T(4,128)}, u32[]{:S(2)}) copy-start(s32[12,3]{0,1:T(4,128)} %param.14) | copy-start | bytes 436
  234.0 27.2 %collective-permute-start.3 = (bf16[2,2,1,1,2,80,768]{6,5,4,3,1,0,2:T(8,128)(2,1)}, bf16[2,2,1,1,2,80,768]{6,5,4,3,1,0,2:T(8,128)(2,1)}, u32[]{:S(2)}, u32[]{:S(2)}) collective-permute-start(bf16[2,2,1,1,2,80,768]{6,5,4,3,1,0,2:T(8,128)(2,1)} %get-tuple-element.14), channel_id=1, source_target_pairs={{1,0},{2,1},{3,2},{4,3},{5,4},{6,5},{7,6},{9,8},{10,9},{11,10},{12... | collective-permute-start | bytes 2949128 | tf_op jit(solution)/shard_map/ppermute | solution.py:31
  240.1 27.4 %collective-permute-start.2 = (bf16[2,2,1,1,2,80,768]{6,5,4,3,1,0,2:T(8,128)(2,1)}, bf16[2,2,1,1,2,80,768]{6,5,4,3,1,0,2:T(8,128)(2,1)}, u32[]{:S(2)}, u32[]{:S(2)}) collective-permute-start(bf16[2,2,1,1,2,80,768]{6,5,4,3,1,0,2:T(8,128)(2,1)} %get-tuple-element.13), channel_id=1, source_target_pairs={{0,1},{1,2},{2,3},{3,4},{4,5},{5,6},{6,7},{8,9},{9,10},{10,11},{11... | collective-permute-start | bytes 2949128 | tf_op jit(solution)/shard_map/ppermute | solution.py:29
  242.2 11.8 %copy-start.2 = (bf16[2,640,768]{2,1,0:T(8,128)(2,1)S(1)}, bf16[2,640,768]{2,1,0:T(8,128)(2,1)}, u32[]{:S(2)}) copy-start(bf16[2,640,768]{2,1,0:T(8,128)(2,1)} %shard_map.83) | copy-start | bytes 5898244
  254.1 13.4 %copy-start.3 = (bf16[2,640,768]{2,1,0:T(8,128)(2,1)S(1)}, bf16[2,640,768]{2,1,0:T(8,128)(2,1)}, u32[]{:S(2)}) copy-start(bf16[2,640,768]{2,1,0:T(8,128)(2,1)} %shard_map.85) | copy-start | bytes 5898244
  255.7 25.7 %copy-start = (bf16[2,2,1,4,2,80,768]{6,5,4,3,1,0,2:T(8,128)(2,1)}, bf16[2,2,1,4,2,80,768]{6,5,4,3,1,0,2:T(8,128)(2,1)S(1)}, u32[]{:S(2)}) copy-start(bf16[2,2,1,4,2,80,768]{6,5,4,3,1,0,2:T(8,128)(2,1)S(1)} %pad_maximum_fusion) | copy-start | bytes 11796484
  269.2 3.1 copy-start.1
  272.3 72.0 %collective-permute-start.4 = (bf16[2,1,8,80,768]{4,3,2,1,0:T(8,128)(2,1)}, bf16[2,1,8,80,768]{4,3,2,1,0:T(8,128)(2,1)}, u32[]{:S(2)}, u32[]{:S(2)}) collective-permute-start(bf16[2,1,8,80,768]{4,3,2,1,0:T(8,128)(2,1)} %get-tuple-element.12), channel_id=1, source_target_pairs={{0,8},{8,16},{16,24},{24,32},{32,40},{40,48},{48,56},{56,64},{64,7... | collective-permute-start | bytes 5898248 | tf_op jit(solution)/shard_map/ppermute | solution.py:81
  274.2 70.1 %collective-permute-start.5 = (bf16[2,1,8,80,768]{4,3,2,1,0:T(8,128)(2,1)}, bf16[2,1,8,80,768]{4,3,2,1,0:T(8,128)(2,1)}, u32[]{:S(2)}, u32[]{:S(2)}) collective-permute-start(bf16[2,1,8,80,768]{4,3,2,1,0:T(8,128)(2,1)} %get-tuple-element.11), channel_id=1, source_target_pairs={{8,0},{16,8},{24,16},{32,24},{40,32},{48,40},{56,48},{64,56},{72,6... | collective-permute-start | bytes 5898248 | tf_op jit(solution)/shard_map/ppermute | solution.py:84
  283.6 39.5 %collective-permute-start.6 = (bf16[2,1,8,80,768]{4,3,2,1,0:T(8,128)(2,1)}, bf16[2,1,8,80,768]{4,3,2,1,0:T(8,128)(2,1)S(1)}, u32[]{:S(2)}, u32[]{:S(2)}) collective-permute-start(bf16[2,1,8,80,768]{4,3,2,1,0:T(8,128)(2,1)} %get-tuple-element.10), channel_id=1, source_target_pairs={{0,8},{8,16},{16,24},{24,32},{32,40},{40,48},{48,56},{56,64},{64,7... | collective-permute-start | bytes 5898248 | tf_op jit(solution)/shard_map/ppermute | solution.py:81
  285.5 39.4 %collective-permute-start.7 = (bf16[2,1,8,80,768]{4,3,2,1,0:T(8,128)(2,1)}, bf16[2,1,8,80,768]{4,3,2,1,0:T(8,128)(2,1)}, u32[]{:S(2)}, u32[]{:S(2)}) collective-permute-start(bf16[2,1,8,80,768]{4,3,2,1,0:T(8,128)(2,1)} %get-tuple-element.9), channel_id=1, source_target_pairs={{8,0},{16,8},{24,16},{32,24},{40,32},{48,40},{56,48},{64,56},{72,6... | collective-permute-start | bytes 5898248 | tf_op jit(solution)/shard_map/ppermute | solution.py:84
  323.1 1.9 copy-start.4
Sparse Core Ops, SparseCore 0:
  33.7 164.6 all-gather.1
